TPU v7x, 256 devices: a whole 4x4x8 slice. The times are simulated.
256 devices in a mesh: pool: 16 (over z, core), tensor: 16 (over y, x).
Axes of the slice: x: 4, y: 4, z: 8, core: 2. Of those that a mesh axis runs over, the one named last changes fastest.
Arguments:
- hidden: bfloat16 [8192, 14336], P('pool', 'tensor'), may hold values from -6 to 6
- down_weight: bfloat16 [14336, 8192], P('tensor', 'pool'), may hold values from -0.046875 to 0.046875
- adapter_shrink: bfloat16 [32, 14336, 64], P('pool', 'tensor'), may hold values from -0.046875 to 0.046875
- adapter_expand: bfloat16 [32, 8192, 64], P('pool', 'tensor'), may hold values from -0.75 to 0.75
- block_adapter: int32 [64], P('pool'), may hold values from 0 to 31, as said below
- block_rows: int32 [64], P('pool'), may hold values from 1 to 128, 6144 in all
Outputs:
- projected: bfloat16 [8192, 8192], P(('pool', 'tensor'))
Inputs may be any that keep to these rules, and one draw needn't show every extreme that they name: `block_adapter`: within each aligned run of 4 blocks (the rows of one pool index) no two blocks name adapters with the same a // 2. `block_rows`: some block is full.
All inputs are finite; a program needn't handle non-finite values.
Results may differ from a plain program's by a relative error of at most 0.02.
Values may be sent and summed in bfloat16 or wider, within the bound.
A program may use at most 128 MiB of HBM per device.

v0:
```python
import jax
import jax.numpy as jnp
from jax import lax
from jax.sharding import PartitionSpec as P

BLOCK = 128


adapter_scale_factor = 0.5


def shards(hidden, down_weight, adapter_shrink, adapter_expand, block_adapter, block_rows):
    input_rows, feat = hidden.shape
    block_count = block_adapter.shape[0]
    column_span = adapter_expand.shape[1]
    tensor_pos = lax.axis_index("tensor")
    tensor_count = lax.axis_size("tensor")
    own_rows = input_rows // tensor_count
    blocks = hidden.reshape(block_count, BLOCK, feat)
    partial_value = jnp.dot(
        hidden,
        lax.all_gather(down_weight, "pool", axis=1, tiled=True),
        preferred_element_type=jnp.float32,
    )
    total = lax.psum_scatter(
        partial_value.astype(jnp.bfloat16), "tensor", scatter_dimension=0, tiled=True
    ).astype(jnp.float32)
    shrink_piece = lax.all_gather(adapter_shrink, "pool", axis=0, tiled=True)
    expand_piece = lax.all_gather(adapter_expand, "pool", axis=0, tiled=True)
    idents = jnp.arange(shrink_piece.shape[0], dtype=jnp.int32)
    pick = (block_adapter[:, None] == idents[None, :]).astype(jnp.bfloat16)
    first = jnp.einsum("bk,kfr->bfr", pick, shrink_piece, preferred_element_type=jnp.float32)
    second = jnp.einsum("bk,kcr->bcr", pick, expand_piece, preferred_element_type=jnp.float32)
    shrink = jnp.einsum(
        "bnf,bfr->bnr", blocks, first.astype(jnp.bfloat16), preferred_element_type=jnp.float32
    )
    summed_shrink = lax.psum(shrink.astype(jnp.bfloat16), "tensor")
    enlarged_rows = jnp.einsum(
        "bnr,bcr->bnc",
        summed_shrink,
        second.astype(jnp.bfloat16),
        preferred_element_type=jnp.float32,
    )
    adapter_delta_columns = (
        (adapter_scale_factor * enlarged_rows).astype(jnp.bfloat16).reshape(input_rows, column_span)
    )
    delta_mine = lax.all_to_all(
        adapter_delta_columns, "tensor", split_axis=0, concat_axis=1, tiled=True
    )
    total = total + delta_mine.astype(jnp.float32)
    row_ids = tensor_pos * own_rows + jnp.arange(own_rows, dtype=jnp.int32)
    owning = (row_ids // BLOCK)[:, None] == jnp.arange(block_count, dtype=jnp.int32)[None, :]
    lengths = jnp.sum(jnp.where(owning, block_rows[None, :], 0), axis=1)
    valid = (row_ids % BLOCK < lengths).astype(jnp.float32)
    return (total * valid[:, None]).astype(jnp.bfloat16)


def solution(mesh):
    in_specs = (
        P("pool", "tensor"),
        P("tensor", "pool"),
        P("pool", "tensor", None),
        P("pool", "tensor", None),
        P("pool"),
        P("pool"),
    )
    out_specs = P(("pool", "tensor"), None)
    return jax.shard_map(shards, mesh=mesh, in_specs=in_specs, out_specs=out_specs, check_vma=False)
```

profile of v0, /device:TPU:0, one launch (start us, length us, event | category | flops | bytes accessed | tf_op | source)
XLA Modules:
  0.0 372.6 jit_solution(14904361085306204502)
XLA Ops:
  6.5 0.0 copy-start
  6.5 0.0 all-gather.6.cloned.1.call-start
  6.5 0.7 all-gather.6.cloned.1.call-update
  7.3 0.0 all-gather.4.cloned.1.call-start
  7.3 0.7 all-gather.4.cloned.1.call-update
  8.0 0.0 all-gather.8.cloned.1.call-start
  8.1 0.7 all-gather.8.cloned.1.call-update
  8.7 0.0 all-reduce.2.cloned.1.call-start
  8.8 43.3 %all-gather.6.cloned.1.call-done = bf16[32,896,64]{1,2,0:T(8,128)(2,1)} async-done(((bf16[2,896,64]{1,2,0:T(8,128)(2,1)}), bf16[32,896,64]{1,2,0:T(8,128)(2,1)}) %all-gather.6.cloned.1.call-update) | async-done | bytes 3670032 | tf_op jit(solution)/shard_map/all_gather | solution.py:28
  52.0 5.0 %fusion.5 = bf16[4,896,64]{1,0,2:T(4,128)(2,1)S(1)} fusion(bf16[32,896,64]{1,2,0:T(8,128)(2,1)} %all-gather.6.cloned.1.call-done, s32[4]{0:T(128)} %param.10), kind=kOutput, calls=%fused_computation.7 | convolution fusion | flops 14909568 | bytes 4128784 | tf_op jit(solution)/shard_map/bk,kfr->bfr/dot_general | solution.py:32
  57.1 0.0 copy-done
  57.1 1.1 fusion.11
  58.2 0.0 all-reduce.2.cloned.1.call-update
  58.2 0.0 reduce-scatter.2.cloned.1.call-start
  58.2 79.8 %all-gather.4.cloned.1.call-done = bf16[896,8192]{1,0:T(8,128)(2,1)} async-done(((bf16[896,512]{1,0:T(8,128)(2,1)}), bf16[896,8192]{1,0:T(8,128)(2,1)}) %all-gather.4.cloned.1.call-update) | async-done | bytes 14680080 | tf_op jit(solution)/shard_map/all_gather | solution.py:22
  138.1 16.5 %convolution_convert_fusion = bf16[512,8192]{1,0:T(8,128)(2,1)} fusion(bf16[512,896]{1,0:T(8,128)(2,1)S(1)} %copy-done, bf16[896,8192]{1,0:T(8,128)(2,1)} %all-gather.4.cloned.1.call-done), kind=kOutput, calls=%fused_computation | convolution fusion | flops 7520387072 | bytes 23986176 | tf_op jit(solution)/shard_map/dot_general | solution.py:20
  154.6 0.0 copy-start.1
  154.6 0.0 reduce-scatter.2.cloned.1.call-update
  154.6 0.0 copy-start.2
  154.6 23.6 %all-gather.8.cloned.1.call-done = bf16[32,512,64]{1,2,0:T(8,128)(2,1)} async-done(((bf16[2,512,64]{1,2,0:T(8,128)(2,1)}), bf16[32,512,64]{1,2,0:T(8,128)(2,1)}) %all-gather.8.cloned.1.call-update) | async-done | bytes 2097168 | tf_op jit(solution)/shard_map/all_gather | solution.py:29
  178.2 0.0 copy-done.1
  178.2 2.9 fusion.8
  181.1 89.5 %all-reduce.2.cloned.1.call-done = bf16[4,128,64]{1,2,0:T(8,128)(2,1)} async-done(((bf16[4,128,64]{1,2,0:T(8,128)(2,1)}), bf16[4,128,64]{1,2,0:T(8,128)(2,1)}) %all-reduce.2.cloned.1.call-update) | async-done | bytes 65552 | tf_op jit(solution)/shard_map/psum | solution.py:37
  270.6 2.0 fusion.4
  272.6 5.0 %all-to-all-start = ((bf16[16,32,512]{2,1,0:T(8,128)(2,1)}), bf16[16,32,512]{2,1,0:T(8,128)(2,1)S(1)}, u32[]{:S(2)}, u32[]{:S(2)}) async-start(bf16[16,32,512]{2,1,0:T(8,128)(2,1)} %bitcast.3), calls=%async_computation.1 | async-start | bytes 1048576 | tf_op jit(solution)/shard_map/all_to_all | solution.py:47
  277.6 0.0 copy-done.2
  277.6 0.1 select_reduce_fusion
  277.7 10.0 %all-to-all-done = bf16[16,32,512]{2,1,0:T(8,128)(2,1)S(1)} async-done(((bf16[16,32,512]{2,1,0:T(8,128)(2,1)}), bf16[16,32,512]{2,1,0:T(8,128)(2,1)S(1)}, u32[]{:S(2)}, u32[]{:S(2)}) %all-to-all-start) | async-done | bytes 524320 | tf_op jit(solution)/shard_map/all_to_all | solution.py:47
  287.7 0.1 convert_bitcast_fusion
  287.8 0.1 copy.14
  287.9 76.2 %reduce-scatter.2.cloned.1.call-done = bf16[32,8192]{1,0:T(8,128)(2,1)} async-done(((bf16[512,8192]{1,0:T(8,128)(2,1)}), bf16[32,8192]{1,0:T(8,128)(2,1)}) %reduce-scatter.2.cloned.1.call-update) | async-done | bytes 524304 | tf_op jit(solution)/shard_map/reduce_scatter | solution.py:25
  364.1 2.0 multiply_convert_fusion
  (2 shorter events, 0.0 us)
Async XLA Ops:
  6.5 50.5 %copy-start = (bf16[512,896]{1,0:T(8,128)(2,1)S(1)}, bf16[512,896]{1,0:T(8,128)(2,1)}, u32[]{:S(2)}) copy-start(bf16[512,896]{1,0:T(8,128)(2,1)} %param.6) | copy-start | bytes 2752516
  6.5 45.5 %all-gather.6.cloned.1.call-start = ((), (), s32[]{:S(2)}) async-start(), calls=%async_computation.4 | async-start | bytes 3899392 | tf_op jit(solution)/shard_map/all_gather | solution.py:28
  7.3 130.8 %all-gather.4.cloned.1.call-start = ((), (), s32[]{:S(2)}) async-start(), calls=%async_computation.2 | async-start | bytes 15597568 | tf_op jit(solution)/shard_map/all_gather | solution.py:22
  8.0 170.2 %all-gather.8.cloned.1.call-start = ((), (), s32[]{:S(2)}) async-start(), calls=%async_computation.6 | async-start | bytes 2228224 | tf_op jit(solution)/shard_map/all_gather | solution.py:29
  8.7 261.9 %all-reduce.2.cloned.1.call-start = ((), (), s32[]{:S(2)}) async-start(), calls=%async_computation.5 | async-start | bytes 131072 | tf_op jit(solution)/shard_map/psum | solution.py:37
  58.2 305.9 %reduce-scatter.2.cloned.1.call-start = ((), (), s32[]{:S(2)}) async-start(), calls=%async_computation.3 | async-start | bytes 8912896 | tf_op jit(solution)/shard_map/reduce_scatter | solution.py:25
  154.6 23.7 %copy-start.1 = (s32[4]{0:T(128)S(1)}, s32[4]{0:T(128)}, u32[]{:S(2)}) copy-start(s32[4]{0:T(128)} %param.10) | copy-start | bytes 52
  154.6 123.0 %copy-start.2 = (s32[4]{0:T(128)S(1)}, s32[4]{0:T(128)}, u32[]{:S(2)}) copy-start(s32[4]{0:T(128)} %param.11) | copy-start | bytes 52
  272.6 15.1 %all-to-all-start = ((bf16[16,32,512]{2,1,0:T(8,128)(2,1)}), bf16[16,32,512]{2,1,0:T(8,128)(2,1)S(1)}, u32[]{:S(2)}, u32[]{:S(2)}) async-start(bf16[16,32,512]{2,1,0:T(8,128)(2,1)} %bitcast.3), calls=%async_computation.1 | async-start | bytes 1048576 | tf_op jit(solution)/shard_map/all_to_all | solution.py:47
Sparse Core Ops, SparseCore 0:
  9.2 42.8 all-gather.5
  53.9 84.1 all-gather.3
  139.9 38.2 all-gather.7
  181.3 89.3 all-reduce.1
  274.6 89.4 reduce-scatter.1
where the time goes:
time: 375 us; the launch traced here: 373 us
  waiting for transfers between devices  325 us (87%)
  matrix products  27.4 us (7%)
  between operations  13.2 us (4%)
  starting transfers between devices  5.12 us (1%)
    psum x1, waiting for transfers between devices, shards(): summed_shrink = lax.psum(shrink.astype(jnp.bfloat16), 'tensor')  89.5 us
    all_gather x1, waiting for transfers between devices, shards(): lax.all_gather(down_weight, 'pool', axis=1, tiled=True)  79.8 us
    reduce_scatter x1, waiting for transfers between devices, shards(): lax.psum_scatter(partial_value.astype(jnp.bfloat16), 'tensor', scatter_di...  76.2 us
    all_gather x1, waiting for transfers between devices, shards(): shrink_piece = lax.all_gather(adapter_shrink, 'pool', axis=0, tiled=True)  43.3 us
    all_gather x1, waiting for transfers between devices, shards(): expand_piece = lax.all_gather(adapter_expand, 'pool', axis=0, tiled=True)  23.6 us
    dot_general x1, matrix products, shards(): jnp.dot(hidden, lax.all_gather(down_weight, 'pool', axis=1, tiled=True),...  16.5 us
    all_to_all x1, waiting for transfers between devices, shards(): lax.all_to_all(adapter_delta_columns, 'tensor', split_axis=0, concat_axis...  9.96 us
  transfers between devices with their start and end apart: 6, of which 6 were waited for; matrix products, arithmetic and copies ran while one was open for 7% of the time, Pallas kernels for 0%

commit v1 on v0

v1 whole, which is shorter than its diff:
```python
import jax
import jax.numpy as jnp
from jax import lax
from jax.sharding import PartitionSpec as P

BLOCK = 128


adapter_scale_factor = 0.5


def tensor_allsum(x, count):
    step = 1
    while step < count:
        perm = [(i, i ^ step) for i in range(count)]
        x = x + lax.ppermute(x, "tensor", perm)
        step *= 2
    return x


def shards(hidden, down_weight, adapter_shrink, adapter_expand, block_adapter, block_rows):
    input_rows, feat = hidden.shape
    block_count = block_adapter.shape[0]
    pool_count = lax.axis_size("pool")
    tensor_pos = lax.axis_index("tensor")
    tensor_count = lax.axis_size("tensor")
    own_rows = input_rows // tensor_count
    held, _, rank = adapter_shrink.shape
    column_span = adapter_expand.shape[1]
    width = down_weight.shape[1]

    shrink_rows = held * feat * rank // width
    expand_rows = held * column_span * rank // width
    pack = jnp.concatenate(
        [
            down_weight,
            adapter_shrink.reshape(shrink_rows, width),
            adapter_expand.reshape(expand_rows, width),
        ],
        axis=0,
    )
    gathered = lax.all_gather(pack, "pool", axis=0, tiled=False)
    w_all = gathered[:, :feat, :]
    shrink_all = gathered[:, feat:feat + shrink_rows, :].reshape(pool_count * held, feat, rank)
    expand_all = gathered[:, feat + shrink_rows:, :].reshape(pool_count * held, column_span, rank)

    first = jnp.take(shrink_all, block_adapter, axis=0)
    second = jnp.take(expand_all, block_adapter, axis=0)
    blocks = hidden.reshape(block_count, BLOCK, feat)
    shrink = jnp.einsum("bnf,bfr->bnr", blocks, first, preferred_element_type=jnp.float32)
    summed_shrink = tensor_allsum(shrink, tensor_count).astype(jnp.bfloat16)
    enlarged_rows = jnp.einsum(
        "bnr,bcr->bnc", summed_shrink, second, preferred_element_type=jnp.float32
    )
    delta = (adapter_scale_factor * enlarged_rows).astype(jnp.bfloat16).reshape(input_rows, column_span)

    partial_value = jnp.einsum("if,pfj->ipj", hidden, w_all, preferred_element_type=jnp.float32)
    chunk_ids = jnp.arange(pool_count, dtype=jnp.int32)[None, :, None]
    partial_value = partial_value + jnp.where(
        chunk_ids == tensor_pos, delta.astype(jnp.float32)[:, None, :], 0.0
    )
    partial_value = partial_value.astype(jnp.bfloat16).reshape(input_rows, pool_count * width)
    total = lax.psum_scatter(partial_value, "tensor", scatter_dimension=0, tiled=True)

    row_ids = tensor_pos * own_rows + jnp.arange(own_rows, dtype=jnp.int32)
    owning = (row_ids // BLOCK)[:, None] == jnp.arange(block_count, dtype=jnp.int32)[None, :]
    lengths = jnp.sum(jnp.where(owning, block_rows[None, :], 0), axis=1)
    valid = row_ids % BLOCK < lengths
    return jnp.where(valid[:, None], total, jnp.zeros_like(total))


def solution(mesh):
    in_specs = (
        P("pool", "tensor"),
        P("tensor", "pool"),
        P("pool", "tensor", None),
        P("pool", "tensor", None),
        P("pool"),
        P("pool"),
    )
    out_specs = P(("pool", "tensor"), None)
    return jax.shard_map(shards, mesh=mesh, in_specs=in_specs, out_specs=out_specs, check_vma=False)
```

time: 375 us -> 312 us (0.83)
  waiting for transfers between devices: 325 us -> 211 us
  local copies, waits for them, and re-layouts: 0.1 us -> 49.9 us
  matrix products: 27.4 us -> 19.7 us
  starting transfers between devices: 5.12 us -> 9.51 us
    psum x1 -> x0, waiting for transfers between devices: 89.5 us -> none  [shards(): summed_shrink = lax.psum(shrink.astype(jnp.bfloat16), 'tensor')]
    reshape x0 -> x7, local copies, waits for them, and re-layouts: none -> 37.2 us  [the longest x2 18.1 us: shards(): gathered[:, feat:feat + shrink_rows, :]]
    all_gather x3 -> x1, waiting for transfers between devices: 147 us -> 114 us  [shards(): gathered = lax.all_gather(pack, 'pool', axis=0, tiled=False)]
    ppermute x0 -> x4, waiting for transfers between devices: none -> 11.2 us  [tensor_allsum(): x = x + lax.ppermute(x, 'tensor', perm)]
    reduce_scatter x1, waiting for transfers between devices: 76.2 us -> 86.3 us  [shards(): lax.psum_scatter(partial_value, 'tensor', scatter_dimension=0, tiled=True)]
    all_to_all x1 -> x0, waiting for transfers between devices: 9.96 us -> none  [shards(): lax.all_to_all(adapter_delta_columns, 'tensor', split_axis=0, concat_axis...]
    ppermute x0 -> x4, starting transfers between devices: none -> 9.47 us  [tensor_allsum(): x = x + lax.ppermute(x, 'tensor', perm)]
    dot_general x5 -> x3, matrix products: 27.4 us -> 19.7 us  [the longest x1 18.9 us: shards(): jnp.einsum('if,pfj->ipj', hidden, w_all, preferred_element_type=jnp.float32)]
  transfers between devices with their start and end apart: 6 -> 6, of which waited for: 6 -> 5; matrix products, arithmetic and copies ran while one was open for 7% -> 3% of each run, Pallas kernels for 0% -> 0%
where the time goes in v1:
time: 312 us; the launch traced here: 309 us
  waiting for transfers between devices  211 us (68%)
  local copies, waits for them, and re-layouts  49.9 us (16%)
  matrix products  19.7 us (6%)
  between operations  13.6 us (4%)
  starting transfers between devices  9.51 us (3%)
  other arithmetic  4.61 us (1%)
    all_gather x1, waiting for transfers between devices, shards(): gathered = lax.all_gather(pack, 'pool', axis=0, tiled=False)  114 us
    reduce_scatter x1, waiting for transfers between devices, shards(): lax.psum_scatter(partial_value, 'tensor', scatter_dimension=0, tiled=True)  86.3 us
    dot_general x1, matrix products, shards(): jnp.einsum('if,pfj->ipj', hidden, w_all, preferred_element_type=jnp.float32)  18.9 us
    reshape x2, local copies, waits for them, and re-layouts, shards(): gathered[:, feat:feat + shrink_rows, :]  18.1 us
    reshape x1, local copies, waits for them, and re-layouts, shards(): partial_value.astype(jnp.bfloat16).reshape(input_rows, pool_count * width)  11.4 us
    ppermute x4, waiting for transfers between devices, tensor_allsum(): x = x + lax.ppermute(x, 'tensor', perm)  11.2 us
    ppermute x4, starting transfers between devices, tensor_allsum(): x = x + lax.ppermute(x, 'tensor', perm)  9.47 us
    reshape x2, local copies, waits for them, and re-layouts, shards(): gathered[:, feat + shrink_rows:, :]  7.18 us
  transfers between devices with their start and end apart: 6, of which 5 were waited for; matrix products, arithmetic and copies ran while one was open for 3% of the time, Pallas kernels for 0%

profile of v1, /device:TPU:0, one launch (start us, length us, event | category | flops | bytes accessed | tf_op | source)
XLA Modules:
  0.0 308.8 jit_solution(6284889642570586211)
XLA Ops:
  6.5 0.0 copy-start
  6.5 0.0 copy-start.2
  6.5 0.0 all-gather.3.cloned.1.call-start
  6.5 1.3 copy.16
  7.8 0.3 reshape.72
  8.1 1.1 copy.17
  9.2 0.2 reshape.73
  9.4 2.3 pad_maximum_fusion
  11.8 0.0 all-gather.3.cloned.1.call-update
  11.8 0.0 reduce-scatter.2.cloned.1.call-start
  11.8 0.0 copy-done.2
  11.9 114.0 %all-gather.3.cloned.1.call-done = bf16[19968,512]{1,0:T(8,128)(2,1)} async-done(((bf16[1248,512]{1,0:T(8,128)(2,1)}), bf16[19968,512]{1,0:T(8,128)(2,1)}) %all-gather.3.cloned.1.call-update) | async-done | bytes 20447248 | tf_op jit(solution)/shard_map/all_gather | solution.py:42
  125.9 4.3 %slice.17 = bf16[16,224,512]{2,1,0:T(8,128)(2,1)} slice(bf16[16,1248,512]{2,1,0:T(8,128)(2,1)} %bitcast.18), slice={[0:16], [896:1120], [0:512]} | slice | bytes 7340032 | tf_op jit(solution)/shard_map/slice | solution.py:44
  130.1 10.1 %reshape.74 = bf16[32,896,64]{2,1,0:T(8,128)(2,1)} reshape(bf16[16,224,512]{2,1,0:T(8,128)(2,1)} %slice.17) | data formatting | bytes 7340032 | tf_op jit(solution)/shard_map/reshape | solution.py:44
  140.2 8.0 %copy.19 = bf16[32,896,64]{1,2,0:T(8,128)(2,1)} copy(bf16[32,896,64]{2,1,0:T(8,128)(2,1)} %reshape.74) | data formatting | bytes 7340032 | tf_op jit(solution)/shard_map/reshape | solution.py:44
  148.2 2.7 gather_fusion
  150.9 0.0 copy-done
  150.9 0.5 convolution_bitcast_fusion
  151.4 1.6 collective-permute-start
  153.0 4.2 %collective-permute-done = f32[4,128,64]{1,2,0:T(8,128)S(1)} collective-permute-done((f32[4,128,64]{1,2,0:T(8,128)S(1)}, f32[4,128,64]{1,2,0:T(8,128)S(1)}, u32[]{:S(2)}, u32[]{:S(2)}) %collective-permute-start) | collective-permute-done | bytes 131104 | tf_op jit(solution)/shard_map/ppermute | solution.py:16
  157.2 3.1 collective-permute-start.1
  160.3 3.5 %collective-permute-done.1 = f32[4,128,64]{1,2,0:T(8,128)S(1)} collective-permute-done((f32[4,128,64]{1,2,0:T(8,128)S(1)}, f32[4,128,64]{1,2,0:T(8,128)S(1)}, u32[]{:S(2)}, u32[]{:S(2)}) %collective-permute-start.1) | collective-permute-done | bytes 131104 | tf_op jit(solution)/shard_map/ppermute | solution.py:16
  163.8 1.6 collective-permute-start.2
  165.4 3.5 %collective-permute-done.2 = f32[4,128,64]{1,2,0:T(8,128)S(1)} collective-permute-done((f32[4,128,64]{1,2,0:T(8,128)S(1)}, f32[4,128,64]{1,2,0:T(8,128)S(1)}, u32[]{:S(2)}, u32[]{:S(2)}) %collective-permute-start.2) | collective-permute-done | bytes 131104 | tf_op jit(solution)/shard_map/ppermute | solution.py:16
  168.9 3.3 %collective-permute-start.3 = (f32[4,128,64]{1,2,0:T(8,128)S(1)}, f32[4,128,64]{1,2,0:T(8,128)S(1)}, u32[]{:S(2)}, u32[]{:S(2)}) collective-permute-start(f32[4,128,64]{1,2,0:T(8,128)S(1)} %add.57), channel_id=1, source_target_pairs={{0,8},{1,9},{2,10},{3,11},{4,12},{5,13},{6,14},{7,15},{8,0},{9,1},... | collective-permute-start | bytes 393224 | tf_op jit(solution)/shard_map/ppermute | solution.py:16
  172.1 1.8 slice.18
  173.9 3.6 %reshape.76 = bf16[32,512,64]{2,1,0:T(8,128)(2,1)} reshape(bf16[16,128,512]{2,1,0:T(8,128)(2,1)S(1)} %slice.18) | data formatting | bytes 4194304 | tf_op jit(solution)/shard_map/reshape | solution.py:45
  177.6 3.5 %copy.20 = bf16[32,512,64]{1,2,0:T(8,128)(2,1)S(1)} copy(bf16[32,512,64]{2,1,0:T(8,128)(2,1)} %reshape.76) | data formatting | bytes 4194304 | tf_op jit(solution)/shard_map/reshape | solution.py:45
  181.1 0.6 gather_fusion.1
  181.7 0.0 collective-permute-done.3
  181.7 0.4 fusion.5
  182.1 0.2 bitcast_convert_fusion
  182.2 0.3 copy.21
  182.6 18.9 %fusion = bf16[512,16,512]{0,2,1:T(8,128)(2,1)} fusion(f32[512,512]{0,1:T(8,128)S(1)} %copy.21, pred[16]{0:T(512)(128)(4,1)S(1)} %iota_compare_fusion.1, bf16[16,1248,512]{2,1,0:T(8,128)(2,1)} %bitcast.20, bf16[512,896]{1,0:T(8,128)(2,1)S(1)} %copy-done), kind=kOutput, calls=%fused_computation.3 | convolution fusion | flops 7528775680 | bytes 25034768 | tf_op jit(solution)/shard_map/if,pfj->ipj/dot_general | solution.py:57
  201.4 11.4 %copy.22 = bf16[512,8192]{1,0:T(8,128)(2,1)} copy(bf16[512,8192]{0,1:T(8,128)(2,1)} %bitcast.17) | data formatting | bytes 16777216 | tf_op jit(solution)/shard_map/reshape | solution.py:62
  212.8 0.0 copy-start.1
  212.8 0.0 copy-start.3
  212.8 0.0 reduce-scatter.2.cloned.1.call-update
  212.9 0.7 copy-done.3
  213.6 0.1 select_reduce_fusion
  213.7 86.3 %reduce-scatter.2.cloned.1.call-done = bf16[32,8192]{1,0:T(8,128)(2,1)} async-done(((bf16[512,8192]{1,0:T(8,128)(2,1)}), bf16[32,8192]{1,0:T(8,128)(2,1)}) %reduce-scatter.2.cloned.1.call-update) | async-done | bytes 524304 | tf_op jit(solution)/shard_map/reduce_scatter | solution.py:63
  300.0 1.9 broadcast_select_fusion
  301.9 0.0 copy-done.1
  (9 shorter events, 0.1 us)
Async XLA Ops:
  6.5 144.4 %copy-start = (bf16[512,896]{1,0:T(8,128)(2,1)S(1)}, bf16[512,896]{1,0:T(8,128)(2,1)}, u32[]{:S(2)}) copy-start(bf16[512,896]{1,0:T(8,128)(2,1)} %param.6) | copy-start | bytes 2752516
  6.5 5.3 %copy-start.2 = (s32[4]{0:T(128)S(1)}, s32[4]{0:T(128)}, u32[]{:S(2)}) copy-start(s32[4]{0:T(128)} %param.10) | copy-start | bytes 52
  6.5 119.3 %all-gather.3.cloned.1.call-start = ((), (), s32[]{:S(2)}) async-start(), calls=%async_computation.2 | async-start | bytes 21725184 | tf_op jit(solution)/shard_map/all_gather | solution.py:42
  11.8 288.2 %reduce-scatter.2.cloned.1.call-start = ((), (), s32[]{:S(2)}) async-start(), calls=%async_computation.1 | async-start | bytes 8912896 | tf_op jit(solution)/shard_map/reduce_scatter | solution.py:63
  151.4 5.7 %collective-permute-start = (f32[4,128,64]{1,2,0:T(8,128)S(1)}, f32[4,128,64]{1,2,0:T(8,128)S(1)}, u32[]{:S(2)}, u32[]{:S(2)}) collective-permute-start(f32[4,128,64]{1,2,0:T(8,128)S(1)} %convolution_bitcast_fusion), channel_id=1, source_target_pairs={{0,1},{1,0},{2,3},{3,2},{4,5},{5,4},{6,7},{7,6},{8,9},{9,8},{10,11... | collective-permute-start | bytes 393224 | tf_op jit(solution)/shard_map/ppermute | solution.py:16
  157.2 6.6 %collective-permute-start.1 = (f32[4,128,64]{1,2,0:T(8,128)S(1)}, f32[4,128,64]{1,2,0:T(8,128)S(1)}, u32[]{:S(2)}, u32[]{:S(2)}) collective-permute-start(f32[4,128,64]{1,2,0:T(8,128)S(1)} %add.55), channel_id=1, source_target_pairs={{0,2},{1,3},{2,0},{3,1},{4,6},{5,7},{6,4},{7,5},{8,10},{9,11},{10,... | collective-permute-start | bytes 393224 | tf_op jit(solution)/shard_map/ppermute | solution.py:16
  163.8 5.1 %collective-permute-start.2 = (f32[4,128,64]{1,2,0:T(8,128)S(1)}, f32[4,128,64]{1,2,0:T(8,128)S(1)}, u32[]{:S(2)}, u32[]{:S(2)}) collective-permute-start(f32[4,128,64]{1,2,0:T(8,128)S(1)} %add.56), channel_id=1, source_target_pairs={{0,4},{1,5},{2,6},{3,7},{4,0},{5,1},{6,2},{7,3},{8,12},{9,13},{10,... | collective-permute-start | bytes 393224 | tf_op jit(solution)/shard_map/ppermute | solution.py:16
  168.9 12.8 %collective-permute-start.3 = (f32[4,128,64]{1,2,0:T(8,128)S(1)}, f32[4,128,64]{1,2,0:T(8,128)S(1)}, u32[]{:S(2)}, u32[]{:S(2)}) collective-permute-start(f32[4,128,64]{1,2,0:T(8,128)S(1)} %add.57), channel_id=1, source_target_pairs={{0,8},{1,9},{2,10},{3,11},{4,12},{5,13},{6,14},{7,15},{8,0},{9,1},... | collective-permute-start | bytes 393224 | tf_op jit(solution)/shard_map/ppermute | solution.py:16
  212.8 89.1 %copy-start.1 = (bf16[512,896]{1,0:T(8,128)(2,1)S(1)}, bf16[512,896]{1,0:T(8,128)(2,1)}, u32[]{:S(2)}) copy-start(bf16[512,896]{1,0:T(8,128)(2,1)} %param.6) | copy-start | bytes 2752516
  212.8 0.7 copy-start.3
Sparse Core Ops, SparseCore 0:
  11.9 113.9 all-gather.2
  213.0 86.9 reduce-scatter.1

commit v2 on v1

--- a/solution.py
+++ b/solution.py
@@ -1,6 +1,10 @@
+import functools
+
 import jax
 import jax.numpy as jnp
 from jax import lax
+from jax.experimental import pallas as pl
+from jax.experimental.pallas import tpu as pltpu
 from jax.sharding import PartitionSpec as P
 
 BLOCK = 128
@@ -16,6 +20,49 @@
         x = x + lax.ppermute(x, "tensor", perm)
         step *= 2
     return x
+
+
+def scatter_kernel(count, rows, part_ref, recv_ref, send_sems, recv_sems):
+    me = lax.axis_index("tensor")
+    pool_me = lax.axis_index("pool")
+    barrier = pltpu.get_barrier_semaphore()
+    for d in range(1, count):
+        other = lax.rem(me + d, count)
+        pl.semaphore_signal(
+            barrier, 1, device_id=(pool_me, other), device_id_type=pl.DeviceIdType.MESH
+        )
+    pl.semaphore_wait(barrier, count - 1)
+    copies = []
+    for d in range(1, count):
+        target = lax.rem(me + d, count)
+        start = pl.multiple_of(target * rows, rows)
+        copy = pltpu.make_async_remote_copy(
+            src_ref=part_ref.at[:, pl.ds(start, rows), :],
+            dst_ref=recv_ref.at[d - 1],
+            send_sem=send_sems.at[d - 1],
+            recv_sem=recv_sems.at[d - 1],
+            device_id=(pool_me, target),
+            device_id_type=pl.DeviceIdType.MESH,
+        )
+        copy.start()
+        copies.append(copy)
+    for copy in copies:
+        copy.wait()
+
+
+def scatter_rows(partial_value, count, rows):
+    chunks, _, width = partial_value.shape
+    return pl.pallas_call(
+        functools.partial(scatter_kernel, count, rows),
+        out_shape=jax.ShapeDtypeStruct((count - 1, chunks, rows, width), partial_value.dtype),
+        in_specs=[pl.BlockSpec(memory_space=pl.ANY)],
+        out_specs=pl.BlockSpec(memory_space=pl.ANY),
+        scratch_shapes=[
+            pltpu.SemaphoreType.DMA((count - 1,)),
+            pltpu.SemaphoreType.DMA((count - 1,)),
+        ],
+        compiler_params=pltpu.CompilerParams(collective_id=0, has_side_effects=True),
+    )(partial_value)
 
 
 def shards(hidden, down_weight, adapter_shrink, adapter_expand, block_adapter, block_rows):
@@ -41,11 +88,15 @@
     )
     gathered = lax.all_gather(pack, "pool", axis=0, tiled=False)
     w_all = gathered[:, :feat, :]
-    shrink_all = gathered[:, feat:feat + shrink_rows, :].reshape(pool_count * held, feat, rank)
-    expand_all = gathered[:, feat + shrink_rows:, :].reshape(pool_count * held, column_span, rank)
+    shrink_all = gathered[:, feat:feat + shrink_rows, :].reshape(
+        pool_count * held, shrink_rows // held, width
+    )
+    expand_all = gathered[:, feat + shrink_rows:, :].reshape(
+        pool_count * held, expand_rows // held, width
+    )
 
-    first = jnp.take(shrink_all, block_adapter, axis=0)
-    second = jnp.take(expand_all, block_adapter, axis=0)
+    first = jnp.take(shrink_all, block_adapter, axis=0).reshape(block_count, feat, rank)
+    second = jnp.take(expand_all, block_adapter, axis=0).reshape(block_count, column_span, rank)
     blocks = hidden.reshape(block_count, BLOCK, feat)
     shrink = jnp.einsum("bnf,bfr->bnr", blocks, first, preferred_element_type=jnp.float32)
     summed_shrink = tensor_allsum(shrink, tensor_count).astype(jnp.bfloat16)
@@ -54,19 +105,22 @@
     )
     delta = (adapter_scale_factor * enlarged_rows).astype(jnp.bfloat16).reshape(input_rows, column_span)
 
-    partial_value = jnp.einsum("if,pfj->ipj", hidden, w_all, preferred_element_type=jnp.float32)
-    chunk_ids = jnp.arange(pool_count, dtype=jnp.int32)[None, :, None]
+    partial_value = jnp.einsum("if,pfj->pij", hidden, w_all, preferred_element_type=jnp.float32)
+    chunk_ids = jnp.arange(pool_count, dtype=jnp.int32)[:, None, None]
     partial_value = partial_value + jnp.where(
-        chunk_ids == tensor_pos, delta.astype(jnp.float32)[:, None, :], 0.0
+        chunk_ids == tensor_pos, delta.astype(jnp.float32)[None, :, :], 0.0
     )
-    partial_value = partial_value.astype(jnp.bfloat16).reshape(input_rows, pool_count * width)
-    total = lax.psum_scatter(partial_value, "tensor", scatter_dimension=0, tiled=True)
+    partial_value = partial_value.astype(jnp.bfloat16)
+    received = scatter_rows(partial_value, tensor_count, own_rows)
+    own = lax.dynamic_slice_in_dim(partial_value, tensor_pos * own_rows, own_rows, axis=1)
+    total = own.astype(jnp.float32) + jnp.sum(received.astype(jnp.float32), axis=0)
+    total = jnp.transpose(total, (1, 0, 2)).reshape(own_rows, pool_count * width)
 
     row_ids = tensor_pos * own_rows + jnp.arange(own_rows, dtype=jnp.int32)
     owning = (row_ids // BLOCK)[:, None] == jnp.arange(block_count, dtype=jnp.int32)[None, :]
     lengths = jnp.sum(jnp.where(owning, block_rows[None, :], 0), axis=1)
     valid = row_ids % BLOCK < lengths
-    return jnp.where(valid[:, None], total, jnp.zeros_like(total))
+    return jnp.where(valid[:, None], total, 0.0).astype(jnp.bfloat16)
 
 
 def solution(mesh):

time: 312 us -> 311 us (level)
  Pallas kernels: 0 us -> 121 us
  waiting for transfers between devices: 211 us -> 125 us
  local copies, waits for them, and re-layouts: 49.9 us -> 12.8 us
  other arithmetic: 4.61 us -> 11.2 us
    pallas_call x0 -> x1, Pallas kernels: none -> 121 us  [scatter_rows(): pl.pallas_call(functools.partial(scatter_kernel, count, rows), out_shape=...]
    reduce_scatter x1 -> x0, waiting for transfers between devices: 86.3 us -> none  [shards(): lax.psum_scatter(partial_value, 'tensor', scatter_dimension=0, tiled=True)]
    reshape x5 -> x1, local copies, waits for them, and re-layouts: 36.7 us -> 0.04 us  [shards(): jnp.transpose(total, (1, 0, 2)).reshape(own_rows, pool_count * width)]
    reduce_sum x0 -> x1, other arithmetic: none -> 5.01 us  [shards(): jnp.sum(received.astype(jnp.float32), axis=0)]
  transfers between devices with their start and end apart: 6 -> 5, of which waited for: 5 -> 5; matrix products, arithmetic and copies ran while one was open for 3% -> 1% of each run, Pallas kernels for 0% -> 0%
where the time goes in v2:
time: 311 us; the launch traced here: 309 us
  waiting for transfers between devices  125 us (40%)
  Pallas kernels  121 us (39%)
  matrix products  17.2 us (6%)
  between operations  13.5 us (4%)
  local copies, waits for them, and re-layouts  12.8 us (4%)
  other arithmetic  11.2 us (4%)
  starting transfers between devices  9.29 us (3%)
    pallas_call x1, Pallas kernels, scatter_rows(): pl.pallas_call(functools.partial(scatter_kernel, count, rows), out_shape=...  121 us
    all_gather x1, waiting for transfers between devices, shards(): gathered = lax.all_gather(pack, 'pool', axis=0, tiled=False)  113 us
    dot_general x1, matrix products, shards(): jnp.einsum('if,pfj->pij', hidden, w_all, preferred_element_type=jnp.float32)  16.3 us
    ppermute x4, waiting for transfers between devices, tensor_allsum(): x = x + lax.ppermute(x, 'tensor', perm)  11.8 us
    ppermute x4, starting transfers between devices, tensor_allsum(): x = x + lax.ppermute(x, 'tensor', perm)  9.29 us
  transfers between devices with their start and end apart: 5, of which 5 were waited for; matrix products, arithmetic and copies ran while one was open for 1% of the time, Pallas kernels for 0%

profile of v2, /device:TPU:0, one launch (start us, length us, event | category | flops | bytes accessed | tf_op | source)
XLA Modules:
  0.0 309.4 jit_solution(397679873091492838)
XLA Ops:
  6.5 0.0 copy-start
  6.5 0.0 all-gather.3.cloned.1.call-start
  6.5 1.3 copy.12
  7.8 0.3 reshape.76
  8.1 1.1 copy.13
  9.2 0.2 reshape.77
  9.4 0.0 copy-start.1
  9.4 2.3 pad_maximum_fusion
  11.7 0.0 all-gather.3.cloned.1.call-update
  11.8 0.7 compare_select_fusion
  12.4 0.7 compare_and_fusion
  13.1 112.8 %all-gather.3.cloned.1.call-done = bf16[19968,512]{1,0:T(8,128)(2,1)} async-done(((bf16[1248,512]{1,0:T(8,128)(2,1)}), bf16[19968,512]{1,0:T(8,128)(2,1)}) %all-gather.3.cloned.1.call-update) | async-done | bytes 20447248 | tf_op jit(solution)/shard_map/all_gather | solution.py:89
  125.8 4.2 %slice.17 = bf16[16,224,512]{2,1,0:T(8,128)(2,1)} slice(bf16[16,1248,512]{2,1,0:T(8,128)(2,1)} %bitcast.25), slice={[0:16], [896:1120], [0:512]} | slice | bytes 7340032 | tf_op jit(solution)/shard_map/slice | solution.py:91
  130.0 2.6 gather_fusion
  132.7 0.5 gather.13
  133.1 0.0 copy-done
  133.1 0.6 convolution_bitcast_fusion
  133.7 1.6 collective-permute-start
  135.3 4.2 %collective-permute-done = f32[4,128,64]{1,2,0:T(8,128)S(1)} collective-permute-done((f32[4,128,64]{1,2,0:T(8,128)S(1)}, f32[4,128,64]{1,2,0:T(8,128)S(1)}, u32[]{:S(2)}, u32[]{:S(2)}) %collective-permute-start) | collective-permute-done | bytes 131104 | tf_op jit(solution)/shard_map/ppermute | solution.py:20
  139.5 3.1 collective-permute-start.1
  142.6 3.5 %collective-permute-done.1 = f32[4,128,64]{1,2,0:T(8,128)S(1)} collective-permute-done((f32[4,128,64]{1,2,0:T(8,128)S(1)}, f32[4,128,64]{1,2,0:T(8,128)S(1)}, u32[]{:S(2)}, u32[]{:S(2)}) %collective-permute-start.1) | collective-permute-done | bytes 131104 | tf_op jit(solution)/shard_map/ppermute | solution.py:20
  146.1 1.6 collective-permute-start.2
  147.7 0.0 copy-done.1
  147.7 0.1 select_reduce_fusion
  147.8 3.4 %collective-permute-done.2 = f32[4,128,64]{1,2,0:T(8,128)S(1)} collective-permute-done((f32[4,128,64]{1,2,0:T(8,128)S(1)}, f32[4,128,64]{1,2,0:T(8,128)S(1)}, u32[]{:S(2)}, u32[]{:S(2)}) %collective-permute-start.2) | collective-permute-done | bytes 131104 | tf_op jit(solution)/shard_map/ppermute | solution.py:20
  151.2 3.1 %collective-permute-start.3 = (f32[4,128,64]{1,2,0:T(8,128)S(1)}, f32[4,128,64]{1,2,0:T(8,128)S(1)}, u32[]{:S(2)}, u32[]{:S(2)}) collective-permute-start(f32[4,128,64]{1,2,0:T(8,128)S(1)} %add.61), channel_id=1, source_target_pairs={{0,8},{1,9},{2,10},{3,11},{4,12},{5,13},{6,14},{7,15},{8,0},{9,1},... | collective-permute-start | bytes 393224 | tf_op jit(solution)/shard_map/ppermute | solution.py:20
  154.3 1.8 slice.18
  156.1 0.6 gather_fusion.1
  156.7 0.3 gather.15
  156.9 0.8 collective-permute-done.3
  157.7 0.4 fusion.5
  158.1 0.2 bitcast_convert_fusion
  158.3 16.3 %fusion.part_ref = bf16[16,512,512]{2,1,0:T(8,128)(2,1)} fusion(f32[512,512]{1,0:T(8,128)S(1)} %bitcast_convert_fusion, pred[16]{0:T(512)(128)(4,1)S(1)} %iota_compare_fusion.1, bf16[16,1248,512]{2,1,0:T(8,128)(2,1)} %bitcast.27, bf16[512,896]{1,0:T(8,128)(2,1)S(1)} %copy-done), kind=kOutput, calls=%fused_computation.3 | convolution fusion | flops 7528775680 | bytes 25034768 | tf_op jit(solution)/shard_map/if,pfj->pij/dot_general | solution.py:108
  174.5 120.7 %shard_map.64 = bf16[15,16,32,512]{3,2,1,0:T(8,128)(2,1)} custom-call(bf16[16,512,512]{2,1,0:T(8,128)(2,1)} %fusion.part_ref), custom_call_target="tpu_custom_call" | custom-call | tf_op jit(solution)/shard_map/pallas_call | solution.py:55
  295.3 5.0 %convert_reduce_fusion = f32[16,32,512]{2,1,0:T(8,128)S(1)} fusion(bf16[15,16,32,512]{3,2,1,0:T(8,128)(2,1)} %shard_map.64), kind=kLoop, calls=%fused_computation.4 | loop fusion | flops 7602176 | bytes 8912896 | tf_op jit(solution)/shard_map/reduce_sum | solution.py:116
  300.3 1.3 add_bitcast_fusion
  301.6 0.9 select_convert_fusion
  (8 shorter events, 0.1 us)
Async XLA Ops:
  6.5 126.6 %copy-start = (bf16[512,896]{1,0:T(8,128)(2,1)S(1)}, bf16[512,896]{1,0:T(8,128)(2,1)}, u32[]{:S(2)}) copy-start(bf16[512,896]{1,0:T(8,128)(2,1)} %param.6) | copy-start | bytes 2752516
  6.5 119.3 %all-gather.3.cloned.1.call-start = ((), (), s32[]{:S(2)}) async-start(), calls=%async_computation | async-start | bytes 21725184 | tf_op jit(solution)/shard_map/all_gather | solution.py:89
  9.4 138.3 %copy-start.1 = (s32[4]{0:T(128)S(1)}, s32[4]{0:T(128)}, u32[]{:S(2)}) copy-start(s32[4]{0:T(128)} %param.11) | copy-start | bytes 52
  133.7 5.7 %collective-permute-start = (f32[4,128,64]{1,2,0:T(8,128)S(1)}, f32[4,128,64]{1,2,0:T(8,128)S(1)}, u32[]{:S(2)}, u32[]{:S(2)}) collective-permute-start(f32[4,128,64]{1,2,0:T(8,128)S(1)} %convolution_bitcast_fusion), channel_id=1, source_target_pairs={{0,1},{1,0},{2,3},{3,2},{4,5},{5,4},{6,7},{7,6},{8,9},{9,8},{10,11... | collective-permute-start | bytes 393224 | tf_op jit(solution)/shard_map/ppermute | solution.py:20
  139.5 6.6 %collective-permute-start.1 = (f32[4,128,64]{1,2,0:T(8,128)S(1)}, f32[4,128,64]{1,2,0:T(8,128)S(1)}, u32[]{:S(2)}, u32[]{:S(2)}) collective-permute-start(f32[4,128,64]{1,2,0:T(8,128)S(1)} %add.59), channel_id=1, source_target_pairs={{0,2},{1,3},{2,0},{3,1},{4,6},{5,7},{6,4},{7,5},{8,10},{9,11},{10,... | collective-permute-start | bytes 393224 | tf_op jit(solution)/shard_map/ppermute | solution.py:20
  146.1 5.1 %collective-permute-start.2 = (f32[4,128,64]{1,2,0:T(8,128)S(1)}, f32[4,128,64]{1,2,0:T(8,128)S(1)}, u32[]{:S(2)}, u32[]{:S(2)}) collective-permute-start(f32[4,128,64]{1,2,0:T(8,128)S(1)} %add.60), channel_id=1, source_target_pairs={{0,4},{1,5},{2,6},{3,7},{4,0},{5,1},{6,2},{7,3},{8,12},{9,13},{10,... | collective-permute-start | bytes 393224 | tf_op jit(solution)/shard_map/ppermute | solution.py:20
  151.2 6.6 %collective-permute-start.3 = (f32[4,128,64]{1,2,0:T(8,128)S(1)}, f32[4,128,64]{1,2,0:T(8,128)S(1)}, u32[]{:S(2)}, u32[]{:S(2)}) collective-permute-start(f32[4,128,64]{1,2,0:T(8,128)S(1)} %add.61), channel_id=1, source_target_pairs={{0,8},{1,9},{2,10},{3,11},{4,12},{5,13},{6,14},{7,15},{8,0},{9,1},... | collective-permute-start | bytes 393224 | tf_op jit(solution)/shard_map/ppermute | solution.py:20
Sparse Core Ops, SparseCore 0:
  11.9 113.9 all-gather.2

commit v3 on v2

--- a/solution.py
+++ b/solution.py
@@ -75,25 +75,38 @@
     held, _, rank = adapter_shrink.shape
     column_span = adapter_expand.shape[1]
     width = down_weight.shape[1]
+    half = width // 2
 
-    shrink_rows = held * feat * rank // width
-    expand_rows = held * column_span * rank // width
+    w_first = lax.all_gather(down_weight[:, :half], "pool", axis=0, tiled=False)
+    part_first = jnp.einsum(
+        "if,pfj->pij", hidden, w_first, preferred_element_type=jnp.float32
+    ).astype(jnp.bfloat16)
+    received = scatter_rows(part_first, tensor_count, own_rows)
+    own = lax.dynamic_slice_in_dim(part_first, tensor_pos * own_rows, own_rows, axis=1)
+    sum_first = own.astype(jnp.float32) + jnp.sum(received.astype(jnp.float32), axis=0)
+
+    shrink_rows = held * feat * rank // half
+    expand_rows = held * column_span * rank // half
     pack = jnp.concatenate(
         [
-            down_weight,
-            adapter_shrink.reshape(shrink_rows, width),
-            adapter_expand.reshape(expand_rows, width),
+            down_weight[:, half:],
+            adapter_shrink.reshape(shrink_rows, half),
+            adapter_expand.reshape(expand_rows, half),
         ],
         axis=0,
     )
     gathered = lax.all_gather(pack, "pool", axis=0, tiled=False)
-    w_all = gathered[:, :feat, :]
+    w_second = gathered[:, :feat, :]
     shrink_all = gathered[:, feat:feat + shrink_rows, :].reshape(
-        pool_count * held, shrink_rows // held, width
+        pool_count * held, shrink_rows // held, half
     )
     expand_all = gathered[:, feat + shrink_rows:, :].reshape(
-        pool_count * held, expand_rows // held, width
+        pool_count * held, expand_rows // held, half
     )
+    part_second = jnp.einsum(
+        "if,pfj->pij", hidden, w_second, preferred_element_type=jnp.float32
+    ).astype(jnp.bfloat16)
+    sum_second = lax.psum_scatter(part_second, "tensor", scatter_dimension=1, tiled=True)
 
     first = jnp.take(shrink_all, block_adapter, axis=0).reshape(block_count, feat, rank)
     second = jnp.take(expand_all, block_adapter, axis=0).reshape(block_count, column_span, rank)
@@ -104,17 +117,11 @@
         "bnr,bcr->bnc", summed_shrink, second, preferred_element_type=jnp.float32
     )
     delta = (adapter_scale_factor * enlarged_rows).astype(jnp.bfloat16).reshape(input_rows, column_span)
+    delta_mine = lax.all_to_all(delta, "tensor", split_axis=0, concat_axis=1, tiled=True)
 
-    partial_value = jnp.einsum("if,pfj->pij", hidden, w_all, preferred_element_type=jnp.float32)
-    chunk_ids = jnp.arange(pool_count, dtype=jnp.int32)[:, None, None]
-    partial_value = partial_value + jnp.where(
-        chunk_ids == tensor_pos, delta.astype(jnp.float32)[None, :, :], 0.0
-    )
-    partial_value = partial_value.astype(jnp.bfloat16)
-    received = scatter_rows(partial_value, tensor_count, own_rows)
-    own = lax.dynamic_slice_in_dim(partial_value, tensor_pos * own_rows, own_rows, axis=1)
-    total = own.astype(jnp.float32) + jnp.sum(received.astype(jnp.float32), axis=0)
+    total = jnp.concatenate([sum_first, sum_second.astype(jnp.float32)], axis=2)
     total = jnp.transpose(total, (1, 0, 2)).reshape(own_rows, pool_count * width)
+    total = total + delta_mine.astype(jnp.float32)
 
     row_ids = tensor_pos * own_rows + jnp.arange(own_rows, dtype=jnp.int32)
     owning = (row_ids // BLOCK)[:, None] == jnp.arange(block_count, dtype=jnp.int32)[None, :]

time: 311 us -> 296 us (0.952)
  Pallas kernels: 121 us -> 80.2 us
  waiting for transfers between devices: 125 us -> 146 us
  other arithmetic: 11.2 us -> 7.22 us
    reduce_scatter x0 -> x1, waiting for transfers between devices: none -> 41.5 us  [shards(): lax.psum_scatter(part_second, 'tensor', scatter_dimension=1, tiled=True)]
    pallas_call x1, Pallas kernels: 121 us -> 80.2 us  [scatter_rows(): pl.pallas_call(functools.partial(scatter_kernel, count, rows), out_shape=...]
    all_gather x1, waiting for transfers between devices: 113 us -> 78.7 us  [shards(): gathered = lax.all_gather(pack, 'pool', axis=0, tiled=False)]
    all_gather x0 -> x1, waiting for transfers between devices: none -> 12.9 us  [shards(): w_first = lax.all_gather(down_weight[:, :half], 'pool', axis=0, tiled=False)]
    all_to_all x0 -> x1, starting transfers between devices: none -> 3.84 us  [shards(): lax.all_to_all(delta, 'tensor', split_axis=0, concat_axis=1, tiled=True)]
    dot_general x1 -> x2, matrix products: 16.3 us -> 18.3 us  [the longest x1 9.19 us: shards(): jnp.einsum('if,pfj->pij', hidden, w_second, preferred_element_type=jnp.fl...]
  transfers between devices with their start and end apart: 5 -> 8, of which waited for: 5 -> 6; matrix products, arithmetic and copies ran while one was open for 1% -> 12% of each run, Pallas kernels for 0% -> 27%
where the time goes in v3:
time: 296 us; the launch traced here: 294 us
  waiting for transfers between devices  146 us (49%)
  Pallas kernels  80.2 us (27%)
  matrix products  20.1 us (7%)
  local copies, waits for them, and re-layouts  15.4 us (5%)
  between operations  13.3 us (4%)
  starting transfers between devices  12.2 us (4%)
  other arithmetic  7.22 us (2%)
    pallas_call x1, Pallas kernels, scatter_rows(): pl.pallas_call(functools.partial(scatter_kernel, count, rows), out_shape=...  80.2 us
    all_gather x1, waiting for transfers between devices, shards(): gathered = lax.all_gather(pack, 'pool', axis=0, tiled=False)  78.7 us
    reduce_scatter x1, waiting for transfers between devices, shards(): lax.psum_scatter(part_second, 'tensor', scatter_dimension=1, tiled=True)  41.5 us
    all_gather x1, waiting for transfers between devices, shards(): w_first = lax.all_gather(down_weight[:, :half], 'pool', axis=0, tiled=False)  12.9 us
    ppermute x4, waiting for transfers between devices, tensor_allsum(): x = x + lax.ppermute(x, 'tensor', perm)  12.2 us
    dot_general x1, matrix products, shards(): jnp.einsum('if,pfj->pij', hidden, w_second, preferred_element_type=jnp.fl...  9.19 us
    dot_general x1, matrix products, shards(): jnp.einsum('if,pfj->pij', hidden, w_first, preferred_element_type=jnp.flo...  9.1 us
    ppermute x4, starting transfers between devices, tensor_allsum(): x = x + lax.ppermute(x, 'tensor', perm)  8.26 us
  transfers between devices with their start and end apart: 8, of which 6 were waited for; matrix products, arithmetic and copies ran while one was open for 12% of the time, Pallas kernels for 27%

profile of v3, /device:TPU:0, one launch (start us, length us, event | category | flops | bytes accessed | tf_op | source)
XLA Modules:
  0.0 294.4 jit_solution(2384483574248481309)
XLA Ops:
  6.5 0.0 copy-start
  6.5 0.0 all-gather.7.cloned.1.call-start
  6.5 1.2 copy.21
  7.7 0.2 reshape.69
  7.9 1.2 copy.20
  9.1 0.3 reshape.68
  9.5 2.0 fusion.17
  11.4 0.9 pad_maximum_fusion
  12.4 0.0 all-gather.7.cloned.1.call-update
  12.4 0.0 all-gather.5.cloned.1.call-start
  12.4 0.7 all-gather.5.cloned.1.call-update
  13.2 0.0 reduce-scatter.2.cloned.1.call-start
  13.2 78.7 %all-gather.7.cloned.1.call-done = bf16[25600,256]{1,0:T(8,128)(2,1)} async-done(((bf16[1600,256]{1,0:T(8,128)(2,1)}), bf16[25600,256]{1,0:T(8,128)(2,1)}) %all-gather.7.cloned.1.call-update) | async-done | bytes 13107216 | tf_op jit(solution)/shard_map/all_gather | solution.py:98
  91.9 0.0 copy-done
  91.9 9.2 %convert_bitcast_fusion = bf16[16,512,256]{2,1,0:T(8,128)(2,1)} fusion(bf16[16,1600,256]{2,1,0:T(8,128)(2,1)} %bitcast.28, bf16[512,896]{1,0:T(8,128)(2,1)S(1)} %copy-done), kind=kOutput, calls=%fused_computation.5 | convolution fusion | flops 3760193536 | bytes 12451840 | tf_op jit(solution)/shard_map/if,pfj->pij/dot_general | solution.py:106
  101.1 0.0 copy-start.1
  101.1 0.0 reduce-scatter.2.cloned.1.call-update
  101.1 0.6 copy-done.1
  101.8 4.3 %slice.25 = bf16[16,448,256]{2,1,0:T(8,128)(2,1)} slice(bf16[16,1600,256]{2,1,0:T(8,128)(2,1)} %bitcast.29), slice={[0:16], [896:1344], [0:256]} | slice | bytes 7340032 | tf_op jit(solution)/shard_map/slice | solution.py:100
  106.1 0.0 copy-start.2
  106.1 2.6 gather_fusion
  108.7 0.4 gather.13
  109.1 0.6 convolution_bitcast_fusion
  109.7 1.6 collective-permute-start
  111.3 4.4 %collective-permute-done = f32[4,128,64]{1,2,0:T(8,128)S(1)} collective-permute-done((f32[4,128,64]{1,2,0:T(8,128)S(1)}, f32[4,128,64]{1,2,0:T(8,128)S(1)}, u32[]{:S(2)}, u32[]{:S(2)}) %collective-permute-start) | collective-permute-done | bytes 131104 | tf_op jit(solution)/shard_map/ppermute | solution.py:20
  115.7 2.9 collective-permute-start.1
  118.6 0.0 copy-done.2
  118.6 0.1 select_reduce_fusion
  118.7 3.9 %collective-permute-done.1 = f32[4,128,64]{1,2,0:T(8,128)S(1)} collective-permute-done((f32[4,128,64]{1,2,0:T(8,128)S(1)}, f32[4,128,64]{1,2,0:T(8,128)S(1)}, u32[]{:S(2)}, u32[]{:S(2)}) %collective-permute-start.1) | collective-permute-done | bytes 131104 | tf_op jit(solution)/shard_map/ppermute | solution.py:20
  122.6 1.1 collective-permute-start.2
  123.8 3.9 %collective-permute-done.2 = f32[4,128,64]{1,2,0:T(8,128)S(1)} collective-permute-done((f32[4,128,64]{1,2,0:T(8,128)S(1)}, f32[4,128,64]{1,2,0:T(8,128)S(1)}, u32[]{:S(2)}, u32[]{:S(2)}) %collective-permute-start.2) | collective-permute-done | bytes 131104 | tf_op jit(solution)/shard_map/ppermute | solution.py:20
  127.7 2.7 collective-permute-start.3
  130.4 12.9 %all-gather.5.cloned.1.call-done = bf16[14336,256]{1,0:T(8,128)(2,1)} async-done(((bf16[896,256]{1,0:T(8,128)(2,1)}), bf16[14336,256]{1,0:T(8,128)(2,1)}) %all-gather.5.cloned.1.call-update) | async-done | bytes 7340048 | tf_op jit(solution)/shard_map/all_gather | solution.py:80
  143.3 9.1 %convolution_convert_fusion = bf16[16,256,512]{1,2,0:T(8,128)(2,1)} fusion(bf16[16,896,256]{2,1,0:T(8,128)(2,1)} %bitcast.32, bf16[512,896]{1,0:T(8,128)(2,1)S(1)} %copy-done), kind=kOutput, calls=%fused_computation.6 | convolution fusion | flops 3760193536 | bytes 12451840 | tf_op jit(solution)/shard_map/if,pfj->pij/dot_general | solution.py:81
  152.4 80.2 %shard_map.64 = bf16[15,16,32,256]{3,2,1,0:T(8,128)(2,1)} custom-call(bf16[16,512,256]{2,1,0:T(8,128)(2,1)} %bitcast.25), custom_call_target="tpu_custom_call" | custom-call | tf_op jit(solution)/shard_map/pallas_call | solution.py:55
  232.6 1.7 slice.26
  234.3 0.6 gather_fusion.1
  234.9 0.2 gather.15
  235.2 0.0 collective-permute-done.3
  235.2 1.2 fusion.4
  236.3 3.8 %all-to-all-start = ((bf16[16,32,512]{2,1,0:T(8,128)(2,1)}), bf16[16,32,512]{2,1,0:T(8,128)(2,1)S(1)}, u32[]{:S(2)}, u32[]{:S(2)}) async-start(bf16[16,32,512]{2,1,0:T(8,128)(2,1)} %bitcast.10), calls=%async_computation.1 | async-start | bytes 1048576 | tf_op jit(solution)/shard_map/all_to_all | solution.py:120
  240.2 3.0 %convert_reduce_fusion = f32[16,32,256]{2,1,0:T(8,128)S(1)} fusion(bf16[15,16,32,256]{3,2,1,0:T(8,128)(2,1)} %shard_map.64), kind=kLoop, calls=%fused_computation.2 | loop fusion | flops 3801088 | bytes 4456448 | tf_op jit(solution)/shard_map/reduce_sum | solution.py:86
  243.2 1.0 bitcast_add_fusion
  244.2 41.5 %reduce-scatter.2.cloned.1.call-done = bf16[16,32,256]{2,1,0:T(8,128)(2,1)} async-done(((bf16[16,512,256]{2,1,0:T(8,128)(2,1)}), bf16[16,32,256]{2,1,0:T(8,128)(2,1)}) %reduce-scatter.2.cloned.1.call-update) | async-done | bytes 262160 | tf_op jit(solution)/shard_map/reduce_scatter | solution.py:109
  285.7 1.0 convert_element_type.44
  286.7 0.0 all-to-all-done
  286.7 0.1 fusion.5
  286.9 0.9 select_convert_fusion
  (9 shorter events, 0.1 us)
Async XLA Ops:
  6.5 85.4 %copy-start = (bf16[512,896]{1,0:T(8,128)(2,1)S(1)}, bf16[512,896]{1,0:T(8,128)(2,1)}, u32[]{:S(2)}) copy-start(bf16[512,896]{1,0:T(8,128)(2,1)} %param.6) | copy-start | bytes 2752516
  6.5 85.4 %all-gather.7.cloned.1.call-start = ((), (), s32[]{:S(2)}) async-start(), calls=%async_computation.4 | async-start | bytes 13926400 | tf_op jit(solution)/shard_map/all_gather | solution.py:98
  12.4 130.9 %all-gather.5.cloned.1.call-start = ((), (), s32[]{:S(2)}) async-start(), calls=%async_computation.3 | async-start | bytes 7798784 | tf_op jit(solution)/shard_map/all_gather | solution.py:80
  13.2 272.6 %reduce-scatter.2.cloned.1.call-start = ((), (), s32[]{:S(2)}) async-start(), calls=%async_computation.2 | async-start | bytes 4456448 | tf_op jit(solution)/shard_map/reduce_scatter | solution.py:109
  101.1 0.7 copy-start.1
  106.1 12.6 %copy-start.2 = (s32[4]{0:T(128)S(1)}, s32[4]{0:T(128)}, u32[]{:S(2)}) copy-start(s32[4]{0:T(128)} %param.11) | copy-start | bytes 52
  109.7 6.0 %collective-permute-start = (f32[4,128,64]{1,2,0:T(8,128)S(1)}, f32[4,128,64]{1,2,0:T(8,128)S(1)}, u32[]{:S(2)}, u32[]{:S(2)}) collective-permute-start(f32[4,128,64]{1,2,0:T(8,128)S(1)} %convolution_bitcast_fusion), channel_id=1, source_target_pairs={{0,1},{1,0},{2,3},{3,2},{4,5},{5,4},{6,7},{7,6},{8,9},{9,8},{10,11... | collective-permute-start | bytes 393224 | tf_op jit(solution)/shard_map/ppermute | solution.py:20
  115.7 6.9 %collective-permute-start.1 = (f32[4,128,64]{1,2,0:T(8,128)S(1)}, f32[4,128,64]{1,2,0:T(8,128)S(1)}, u32[]{:S(2)}, u32[]{:S(2)}) collective-permute-start(f32[4,128,64]{1,2,0:T(8,128)S(1)} %add.69), channel_id=1, source_target_pairs={{0,2},{1,3},{2,0},{3,1},{4,6},{5,7},{6,4},{7,5},{8,10},{9,11},{10,... | collective-permute-start | bytes 393224 | tf_op jit(solution)/shard_map/ppermute | solution.py:20
  122.6 5.1 %collective-permute-start.2 = (f32[4,128,64]{1,2,0:T(8,128)S(1)}, f32[4,128,64]{1,2,0:T(8,128)S(1)}, u32[]{:S(2)}, u32[]{:S(2)}) collective-permute-start(f32[4,128,64]{1,2,0:T(8,128)S(1)} %add.70), channel_id=1, source_target_pairs={{0,4},{1,5},{2,6},{3,7},{4,0},{5,1},{6,2},{7,3},{8,12},{9,13},{10,... | collective-permute-start | bytes 393224 | tf_op jit(solution)/shard_map/ppermute | solution.py:20
  127.7 107.4 %collective-permute-start.3 = (f32[4,128,64]{1,2,0:T(8,128)S(1)}, f32[4,128,64]{1,2,0:T(8,128)S(1)}, u32[]{:S(2)}, u32[]{:S(2)}) collective-permute-start(f32[4,128,64]{1,2,0:T(8,128)S(1)} %add.71), channel_id=1, source_target_pairs={{0,8},{1,9},{2,10},{3,11},{4,12},{5,13},{6,14},{7,15},{8,0},{9,1},... | collective-permute-start | bytes 393224 | tf_op jit(solution)/shard_map/ppermute | solution.py:20
  236.3 50.4 %all-to-all-start = ((bf16[16,32,512]{2,1,0:T(8,128)(2,1)}), bf16[16,32,512]{2,1,0:T(8,128)(2,1)S(1)}, u32[]{:S(2)}, u32[]{:S(2)}) async-start(bf16[16,32,512]{2,1,0:T(8,128)(2,1)} %bitcast.10), calls=%async_computation.1 | async-start | bytes 1048576 | tf_op jit(solution)/shard_map/all_to_all | solution.py:120
Sparse Core Ops, SparseCore 0:
  12.5 79.3 all-gather.6
  93.7 49.5 all-gather.4
  146.9 138.7 reduce-scatter.1

commit v4 on v2

--- a/solution.py
+++ b/solution.py
@@ -65,35 +65,64 @@
     )(partial_value)
 
 
+def tensor_shift(x, side, step, along_y):
+    perm = []
+    for yy in range(side):
+        for xx in range(side):
+            if along_y:
+                perm.append((yy * side + xx, ((yy + step) % side) * side + xx))
+            else:
+                perm.append((yy * side + xx, yy * side + (xx + step) % side))
+    return lax.ppermute(x, "tensor", perm)
+
+
 def shards(hidden, down_weight, adapter_shrink, adapter_expand, block_adapter, block_rows):
     input_rows, feat = hidden.shape
     block_count = block_adapter.shape[0]
     pool_count = lax.axis_size("pool")
     tensor_pos = lax.axis_index("tensor")
     tensor_count = lax.axis_size("tensor")
+    side = 4
+    quarter = pool_count // side
+    my_y = tensor_pos // side
+    my_x = tensor_pos % side
     own_rows = input_rows // tensor_count
     held, _, rank = adapter_shrink.shape
     column_span = adapter_expand.shape[1]
     width = down_weight.shape[1]
 
+    pairs = []
+    for p1 in range(pool_count):
+        for y1 in range(side):
+            for x1 in range(side):
+                p2 = (p1 % quarter) * side + y1
+                y2 = p1 // quarter
+                pairs.append((p1 * tensor_count + y1 * side + x1, p2 * tensor_count + y2 * side + x1))
+    moved = lax.ppermute(down_weight, ("pool", "tensor"), pairs)
+
     shrink_rows = held * feat * rank // width
     expand_rows = held * column_span * rank // width
     pack = jnp.concatenate(
         [
-            down_weight,
+            moved,
             adapter_shrink.reshape(shrink_rows, width),
             adapter_expand.reshape(expand_rows, width),
         ],
         axis=0,
     )
     gathered = lax.all_gather(pack, "pool", axis=0, tiled=False)
-    w_all = gathered[:, :feat, :]
+    w_quarter = gathered[:, :feat, :].reshape(quarter, side, feat, width)
     shrink_all = gathered[:, feat:feat + shrink_rows, :].reshape(
         pool_count * held, shrink_rows // held, width
     )
     expand_all = gathered[:, feat + shrink_rows:, :].reshape(
         pool_count * held, expand_rows // held, width
     )
+
+    pieces = [hidden] + [tensor_shift(hidden, side, s, True) for s in range(1, side)]
+    by_shift = jnp.stack(pieces, axis=0)
+    order = (my_y - jnp.arange(side, dtype=jnp.int32)) % side
+    hidden_column = jnp.take(by_shift, order, axis=0)
 
     first = jnp.take(shrink_all, block_adapter, axis=0).reshape(block_count, feat, rank)
     second = jnp.take(expand_all, block_adapter, axis=0).reshape(block_count, column_span, rank)
@@ -105,22 +134,36 @@
     )
     delta = (adapter_scale_factor * enlarged_rows).astype(jnp.bfloat16).reshape(input_rows, column_span)
 
-    partial_value = jnp.einsum("if,pfj->pij", hidden, w_all, preferred_element_type=jnp.float32)
-    chunk_ids = jnp.arange(pool_count, dtype=jnp.int32)[:, None, None]
+    partial_value = jnp.einsum(
+        "yif,ayfj->aij", hidden_column, w_quarter, preferred_element_type=jnp.float32
+    )
+    chunk_ids = jnp.arange(quarter, dtype=jnp.int32)[:, None, None]
     partial_value = partial_value + jnp.where(
-        chunk_ids == tensor_pos, delta.astype(jnp.float32)[None, :, :], 0.0
+        chunk_ids == my_x, delta.astype(jnp.float32)[None, :, :], 0.0
     )
-    partial_value = partial_value.astype(jnp.bfloat16)
-    received = scatter_rows(partial_value, tensor_count, own_rows)
-    own = lax.dynamic_slice_in_dim(partial_value, tensor_pos * own_rows, own_rows, axis=1)
-    total = own.astype(jnp.float32) + jnp.sum(received.astype(jnp.float32), axis=0)
-    total = jnp.transpose(total, (1, 0, 2)).reshape(own_rows, pool_count * width)
+    partial_value = partial_value.astype(jnp.bfloat16).reshape(
+        quarter, side, side, own_rows, width
+    )
+
+    total = lax.dynamic_index_in_dim(partial_value, my_x, axis=2, keepdims=False).astype(jnp.float32)
+    for s in range(1, side):
+        piece = lax.dynamic_index_in_dim(partial_value, (my_x + s) % side, axis=2, keepdims=False)
+        total = total + tensor_shift(piece, side, s, False).astype(jnp.float32)
+    total = total.astype(jnp.bfloat16)
+
+    got = [lax.dynamic_index_in_dim(total, my_y, axis=1, keepdims=False)]
+    for s in range(1, side):
+        piece = lax.dynamic_index_in_dim(total, (my_y + s) % side, axis=1, keepdims=False)
+        got.append(tensor_shift(piece, side, s, True))
+    by_shift = jnp.stack(got, axis=0)
+    result = jnp.take(by_shift, order, axis=0)
+    result = jnp.transpose(result, (2, 0, 1, 3)).reshape(own_rows, pool_count * width)
 
     row_ids = tensor_pos * own_rows + jnp.arange(own_rows, dtype=jnp.int32)
     owning = (row_ids // BLOCK)[:, None] == jnp.arange(block_count, dtype=jnp.int32)[None, :]
     lengths = jnp.sum(jnp.where(owning, block_rows[None, :], 0), axis=1)
     valid = row_ids % BLOCK < lengths
-    return jnp.where(valid[:, None], total, 0.0).astype(jnp.bfloat16)
+    return jnp.where(valid[:, None], result, jnp.zeros_like(result))
 
 
 def solution(mesh):

time: 311 us -> 280 us (0.900)
  Pallas kernels: 121 us -> 0 us
  starting transfers between devices: 9.29 us -> 56.8 us
  waiting for transfers between devices: 125 us -> 150 us
  local copies, waits for them, and re-layouts: 12.8 us -> 34.2 us
  other arithmetic: 11.2 us -> 7.41 us
    pallas_call x1 -> x0, Pallas kernels: 121 us -> none  [scatter_rows(): pl.pallas_call(functools.partial(scatter_kernel, count, rows), out_shape=...]
    ppermute x0 -> x10, starting transfers between devices: none -> 47.5 us  [the longest x9 45.6 us: tensor_shift(): return lax.ppermute(x, 'tensor', perm)]
    ppermute x0 -> x10, waiting for transfers between devices: none -> 29.4 us  [the longest x9 29.4 us: tensor_shift(): return lax.ppermute(x, 'tensor', perm)]
    slice x0 -> x1, local copies, waits for them, and re-layouts: none -> 13.3 us  [shards(): w_quarter = gathered[:, :feat, :].reshape(quarter, side, feat, width)]
    gather x0 -> x2, local copies, waits for them, and re-layouts: none -> 5.44 us  [the longest x1 4.86 us: shards(): hidden_column = jnp.take(by_shift, order, axis=0)]
    reduce_sum x1 -> x0, other arithmetic: 5.01 us -> none  [shards(): jnp.sum(received.astype(jnp.float32), axis=0)]
    dot_general x1, matrix products: 16.3 us -> 12.2 us  [shards(): jnp.einsum('yif,ayfj->aij', hidden_column, w_quarter, preferred_element_t...]
    another operation x0 -> x2, other arithmetic: none -> 3.2 us  [the longest x1 3.13 us: shards(): by_shift = jnp.stack(pieces, axis=0)]
  transfers between devices with their start and end apart: 5 -> 15, of which waited for: 5 -> 9; matrix products, arithmetic and copies ran while one was open for 1% -> 13% of each run, Pallas kernels for 0% -> 0%
where the time goes in v4:
time: 280 us; the launch traced here: 277 us
  waiting for transfers between devices  150 us (54%)
  starting transfers between devices  56.8 us (20%)
  local copies, waits for them, and re-layouts  34.2 us (12%)
  matrix products  14.4 us (5%)
  between operations  13.7 us (5%)
  other arithmetic  7.41 us (3%)
    all_gather x1, waiting for transfers between devices, shards(): gathered = lax.all_gather(pack, 'pool', axis=0, tiled=False)  110 us
    ppermute x9, starting transfers between devices, tensor_shift(): return lax.ppermute(x, 'tensor', perm)  45.6 us
    ppermute x9, waiting for transfers between devices, tensor_shift(): return lax.ppermute(x, 'tensor', perm)  29.4 us
    slice x1, local copies, waits for them, and re-layouts, shards(): w_quarter = gathered[:, :feat, :].reshape(quarter, side, feat, width)  13.3 us
    dot_general x1, matrix products, shards(): jnp.einsum('yif,ayfj->aij', hidden_column, w_quarter, preferred_element_t...  12.2 us
    ppermute x4, waiting for transfers between devices, tensor_allsum(): x = x + lax.ppermute(x, 'tensor', perm)  11.1 us
    ppermute x4, starting transfers between devices, tensor_allsum(): x = x + lax.ppermute(x, 'tensor', perm)  9.28 us
  transfers between devices with their start and end apart: 15, of which 9 were waited for; matrix products, arithmetic and copies ran while one was open for 13% of the time, Pallas kernels for 0%

profile of v4, /device:TPU:0, one launch (start us, length us, event | category | flops | bytes accessed | tf_op | source)
XLA Modules:
  0.0 276.9 jit_solution(2473084373672934417)
XLA Ops:
  6.5 2.0 collective-permute-start
  8.5 1.1 copy.17
  9.6 0.2 reshape.140
  9.8 1.2 copy.16
  11.0 0.3 reshape.139
  11.3 1.1 pad_maximum_fusion.1
  12.5 37.5 %collective-permute-start.3 = (bf16[512,896]{1,0:T(8,128)(2,1)S(1)}, bf16[512,896]{1,0:T(8,128)(2,1)S(1)}, u32[]{:S(2)}, u32[]{:S(2)}) collective-permute-start(bf16[512,896]{1,0:T(8,128)(2,1)S(1)} %copy-done), channel_id=1, source_target_pairs={{0,12},{1,13},{2,14},{3,15},{4,0},{5,1},{6,2},{7,3},{8,4},{9,5},{1... | collective-permute-start | bytes 2752520 | tf_op jit(solution)/shard_map/ppermute | solution.py:76
  50.0 1.0 collective-permute-start.1
  51.0 110.0 %all-gather.3.cloned.1.call-done = bf16[19968,512]{1,0:T(8,128)(2,1)} async-done(((bf16[1248,512]{1,0:T(8,128)(2,1)}), bf16[19968,512]{1,0:T(8,128)(2,1)}) %all-gather.3.cloned.1.call-update) | async-done | bytes 20447248 | tf_op jit(solution)/shard_map/all_gather | solution.py:113
  161.0 4.2 %slice.21 = bf16[16,224,512]{2,1,0:T(8,128)(2,1)} slice(bf16[16,1248,512]{2,1,0:T(8,128)(2,1)} %bitcast.53), slice={[0:16], [896:1120], [0:512]} | slice | bytes 7340032 | tf_op jit(solution)/shard_map/slice | solution.py:115
  165.2 2.6 gather_fusion.1
  167.8 1.4 gather.22
  169.2 1.8 convolution_bitcast_fusion
  171.0 1.6 collective-permute-start.4
  172.5 4.2 %collective-permute-done.4 = f32[4,128,64]{1,2,0:T(8,128)S(1)} collective-permute-done((f32[4,128,64]{1,2,0:T(8,128)S(1)}, f32[4,128,64]{1,2,0:T(8,128)S(1)}, u32[]{:S(2)}, u32[]{:S(2)}) %collective-permute-start.4) | collective-permute-done | bytes 131104 | tf_op jit(solution)/shard_map/ppermute | solution.py:20
  176.7 3.1 %collective-permute-start.5 = (f32[4,128,64]{1,2,0:T(8,128)S(1)}, f32[4,128,64]{1,2,0:T(8,128)S(1)}, u32[]{:S(2)}, u32[]{:S(2)}) collective-permute-start(f32[4,128,64]{1,2,0:T(8,128)S(1)} %add.168), channel_id=1, source_target_pairs={{0,2},{1,3},{2,0},{3,1},{4,6},{5,7},{6,4},{7,5},{8,10},{9,11},{10,... | collective-permute-start | bytes 393224 | tf_op jit(solution)/shard_map/ppermute | solution.py:20
  179.8 3.5 %collective-permute-done.5 = f32[4,128,64]{1,2,0:T(8,128)S(1)} collective-permute-done((f32[4,128,64]{1,2,0:T(8,128)S(1)}, f32[4,128,64]{1,2,0:T(8,128)S(1)}, u32[]{:S(2)}, u32[]{:S(2)}) %collective-permute-start.5) | collective-permute-done | bytes 131104 | tf_op jit(solution)/shard_map/ppermute | solution.py:20
  183.3 1.6 collective-permute-start.6
  185.0 3.4 %collective-permute-done.6 = f32[4,128,64]{1,2,0:T(8,128)S(1)} collective-permute-done((f32[4,128,64]{1,2,0:T(8,128)S(1)}, f32[4,128,64]{1,2,0:T(8,128)S(1)}, u32[]{:S(2)}, u32[]{:S(2)}) %collective-permute-start.6) | collective-permute-done | bytes 131104 | tf_op jit(solution)/shard_map/ppermute | solution.py:20
  188.4 3.1 %collective-permute-start.7 = (f32[4,128,64]{1,2,0:T(8,128)S(1)}, f32[4,128,64]{1,2,0:T(8,128)S(1)}, u32[]{:S(2)}, u32[]{:S(2)}) collective-permute-start(f32[4,128,64]{1,2,0:T(8,128)S(1)} %add.170), channel_id=1, source_target_pairs={{0,8},{1,9},{2,10},{3,11},{4,12},{5,13},{6,14},{7,15},{8,0},{9,1},... | collective-permute-start | bytes 393224 | tf_op jit(solution)/shard_map/ppermute | solution.py:20
  191.5 3.1 %pad_maximum_fusion = bf16[4,512,896]{2,1,0:T(8,128)(2,1)} fusion(bf16[1,512,896]{2,1,0:T(8,128)(2,1)S(1)} %bitcast.63, bf16[1,512,896]{2,1,0:T(8,128)(2,1)S(1)} %bitcast.64, bf16[1,512,896]{2,1,0:T(8,128)(2,1)} %bitcast.3, bf16[1,512,896]{2,1,0:T(8,128)(2,1)S(1)} %bitcast.62), kind=kLoop, calls=%fused_computation.6 | loop fusion | flops 5505024 | bytes 7340032 | tf_op jit(solution)/shard_map/stack | solution.py:123
  194.6 4.9 %gather_fusion = bf16[4,512,896]{2,1,0:T(8,128)(2,1)} fusion(bf16[4,512,896]{2,1,0:T(8,128)(2,1)} %pad_maximum_fusion, s32[1024]{0:T(1024)S(1)} %pad_clamp_fusion.1), kind=kCustom, calls=%fused_computation | custom fusion | bytes 7340048 | tf_op jit(solution)/shard_map/jit(_take)/gather | solution.py:125
  199.5 1.8 slice.22
  201.3 13.3 %slice.20 = bf16[16,896,512]{2,1,0:T(8,128)(2,1)} slice(bf16[16,1248,512]{2,1,0:T(8,128)(2,1)} %bitcast.55), slice={[0:16], [0:896], [0:512]} | slice | bytes 29360128 | tf_op jit(solution)/shard_map/slice | solution.py:114
  214.6 0.6 gather_fusion.2
  215.2 0.3 gather.24
  215.5 0.4 fusion.8
  215.8 0.2 bitcast_convert_fusion
  216.0 12.2 %fusion = bf16[4,512,512]{2,1,0:T(8,128)(2,1)S(1)} fusion(f32[512,512]{1,0:T(8,128)S(1)} %bitcast_convert_fusion, pred[4]{0:T(512)(128)(4,1)S(1)} %get-tuple-element.13, bf16[4,4,896,512]{3,2,1,0:T(8,128)(2,1)} %bitcast.56, bf16[4,512,896]{2,1,0:T(8,128)(2,1)} %gather_fusion, pred[4]{0:T(512)(128)(4,1)S(1)} %get-tuple-element.12), kind=kOutput, calls=%fused_computation.5 | convolution fusion | flops 7521173504 | bytes 21495816 | tf_op jit(solution)/shard_map/yif,ayfj->aij/dot_general | solution.py:137
  228.3 1.0 dynamic-slice_bitcast_fusion.2
  229.2 2.7 collective-permute-start.10
  231.9 0.9 collective-permute-start.9
  232.8 0.9 collective-permute-start.8
  233.6 0.1 select_reduce_fusion
  233.7 18.0 %collective-permute-done.10 = bf16[4,4,32,512]{3,2,1,0:T(8,128)(2,1)} collective-permute-done((bf16[4,4,32,512]{3,2,1,0:T(8,128)(2,1)}, bf16[4,4,32,512]{3,2,1,0:T(8,128)(2,1)}, u32[]{:S(2)}, u32[]{:S(2)}) %collective-permute-start.10) | collective-permute-done | bytes 524320 | tf_op jit(solution)/shard_map/ppermute | solution.py:76
  251.7 3.5 %collective-permute-done.8 = bf16[4,4,32,512]{3,2,1,0:T(8,128)(2,1)} collective-permute-done((bf16[4,4,32,512]{3,2,1,0:T(8,128)(2,1)S(1)}, bf16[4,4,32,512]{3,2,1,0:T(8,128)(2,1)}, u32[]{:S(2)}, u32[]{:S(2)}) %collective-permute-start.8) | collective-permute-done | bytes 524320 | tf_op jit(solution)/shard_map/ppermute | solution.py:76
  255.2 1.7 fusion.11
  256.9 1.2 collective-permute-start.13
  258.2 1.5 collective-permute-start.12
  259.7 3.7 %collective-permute-done.13 = bf16[4,32,512]{2,1,0:T(8,128)(2,1)S(1)} collective-permute-done((bf16[4,32,512]{2,1,0:T(8,128)(2,1)S(1)}, bf16[4,32,512]{2,1,0:T(8,128)(2,1)S(1)}, u32[]{:S(2)}, u32[]{:S(2)}) %collective-permute-start.13) | collective-permute-done | bytes 131104 | tf_op jit(solution)/shard_map/ppermute | solution.py:76
  263.4 2.7 collective-permute-done.12
  266.1 1.5 collective-permute-done.11
  267.6 0.1 pad_maximum_fusion.2
  267.7 0.6 gather_fusion.3
  268.3 0.1 select_bitcast_fusion
  268.4 0.4 copy.20
  268.8 0.4 reshape.146
  269.2 0.9 broadcast_select_fusion
  (28 shorter events, 0.2 us)
Async XLA Ops:
  6.5 5.9 %copy-start = (bf16[512,896]{1,0:T(8,128)(2,1)S(1)}, bf16[512,896]{1,0:T(8,128)(2,1)}, u32[]{:S(2)}) copy-start(bf16[512,896]{1,0:T(8,128)(2,1)} %param.6) | copy-start | bytes 2752516
  6.5 44.4 %copy-start.1 = (s32[4]{0:T(128)S(1)}, s32[4]{0:T(128)}, u32[]{:S(2)}) copy-start(s32[4]{0:T(128)} %param.10) | copy-start | bytes 52
  6.5 154.4 %all-gather.3.cloned.1.call-start = ((), (), s32[]{:S(2)}) async-start(), calls=%async_computation | async-start | bytes 21725184 | tf_op jit(solution)/shard_map/all_gather | solution.py:113
  6.5 4.8 %collective-permute-start = (bf16[896,512]{1,0:T(8,128)(2,1)}, bf16[896,512]{1,0:T(8,128)(2,1)S(1)}, u32[]{:S(2)}, u32[]{:S(2)}) collective-permute-start(bf16[896,512]{1,0:T(8,128)(2,1)} %param.7), channel_id=1, source_target_pairs={{0,0},{1,1},{2,2},{3,3},{4,16},{5,17},{6,18},{7,19},{8,32},{9,33},... | collective-permute-start | bytes 2752520 | tf_op jit(solution)/shard_map/ppermute | solution.py:101
  12.5 179.0 %collective-permute-start.3 = (bf16[512,896]{1,0:T(8,128)(2,1)S(1)}, bf16[512,896]{1,0:T(8,128)(2,1)S(1)}, u32[]{:S(2)}, u32[]{:S(2)}) collective-permute-start(bf16[512,896]{1,0:T(8,128)(2,1)S(1)} %copy-done), channel_id=1, source_target_pairs={{0,12},{1,13},{2,14},{3,15},{4,0},{5,1},{6,2},{7,3},{8,4},{9,5},{1... | collective-permute-start | bytes 2752520 | tf_op jit(solution)/shard_map/ppermute | solution.py:76
  50.0 141.5 %collective-permute-start.2 = (bf16[512,896]{1,0:T(8,128)(2,1)S(1)}, bf16[512,896]{1,0:T(8,128)(2,1)S(1)}, u32[]{:S(2)}, u32[]{:S(2)}) collective-permute-start(bf16[512,896]{1,0:T(8,128)(2,1)S(1)} %copy-done), channel_id=1, source_target_pairs={{0,8},{1,9},{2,10},{3,11},{4,12},{5,13},{6,14},{7,15},{8,0},{9,1},... | collective-permute-start | bytes 2752520 | tf_op jit(solution)/shard_map/ppermute | solution.py:76
  50.0 141.5 %collective-permute-start.1 = (bf16[512,896]{1,0:T(8,128)(2,1)S(1)}, bf16[512,896]{1,0:T(8,128)(2,1)}, u32[]{:S(2)}, u32[]{:S(2)}) collective-permute-start(bf16[512,896]{1,0:T(8,128)(2,1)S(1)} %copy-done), channel_id=1, source_target_pairs={{0,4},{1,5},{2,6},{3,7},{4,8},{5,9},{6,10},{7,11},{8,12},{9,13},{1... | collective-permute-start | bytes 2752520 | tf_op jit(solution)/shard_map/ppermute | solution.py:76
  171.0 5.7 %collective-permute-start.4 = (f32[4,128,64]{1,2,0:T(8,128)S(1)}, f32[4,128,64]{1,2,0:T(8,128)S(1)}, u32[]{:S(2)}, u32[]{:S(2)}) collective-permute-start(f32[4,128,64]{1,2,0:T(8,128)S(1)} %convolution_bitcast_fusion), channel_id=1, source_target_pairs={{0,1},{1,0},{2,3},{3,2},{4,5},{5,4},{6,7},{7,6},{8,9},{9,8},{10,11... | collective-permute-start | bytes 393224 | tf_op jit(solution)/shard_map/ppermute | solution.py:20
  176.7 6.6 %collective-permute-start.5 = (f32[4,128,64]{1,2,0:T(8,128)S(1)}, f32[4,128,64]{1,2,0:T(8,128)S(1)}, u32[]{:S(2)}, u32[]{:S(2)}) collective-permute-start(f32[4,128,64]{1,2,0:T(8,128)S(1)} %add.168), channel_id=1, source_target_pairs={{0,2},{1,3},{2,0},{3,1},{4,6},{5,7},{6,4},{7,5},{8,10},{9,11},{10,... | collective-permute-start | bytes 393224 | tf_op jit(solution)/shard_map/ppermute | solution.py:20
  183.3 5.1 %collective-permute-start.6 = (f32[4,128,64]{1,2,0:T(8,128)S(1)}, f32[4,128,64]{1,2,0:T(8,128)S(1)}, u32[]{:S(2)}, u32[]{:S(2)}) collective-permute-start(f32[4,128,64]{1,2,0:T(8,128)S(1)} %add.169), channel_id=1, source_target_pairs={{0,4},{1,5},{2,6},{3,7},{4,0},{5,1},{6,2},{7,3},{8,12},{9,13},{10,... | collective-permute-start | bytes 393224 | tf_op jit(solution)/shard_map/ppermute | solution.py:20
  188.4 27.1 %collective-permute-start.7 = (f32[4,128,64]{1,2,0:T(8,128)S(1)}, f32[4,128,64]{1,2,0:T(8,128)S(1)}, u32[]{:S(2)}, u32[]{:S(2)}) collective-permute-start(f32[4,128,64]{1,2,0:T(8,128)S(1)} %add.170), channel_id=1, source_target_pairs={{0,8},{1,9},{2,10},{3,11},{4,12},{5,13},{6,14},{7,15},{8,0},{9,1},... | collective-permute-start | bytes 393224 | tf_op jit(solution)/shard_map/ppermute | solution.py:20
  216.0 17.6 %copy-start.2 = (s32[4]{0:T(128)S(1)}, s32[4]{0:T(128)}, u32[]{:S(2)}) copy-start(s32[4]{0:T(128)} %param.11) | copy-start | bytes 52
  229.2 22.5 %collective-permute-start.10 = (bf16[4,4,32,512]{3,2,1,0:T(8,128)(2,1)}, bf16[4,4,32,512]{3,2,1,0:T(8,128)(2,1)}, u32[]{:S(2)}, u32[]{:S(2)}) collective-permute-start(bf16[4,4,32,512]{3,2,1,0:T(8,128)(2,1)} %get-tuple-element.6), channel_id=1, source_target_pairs={{0,3},{1,0},{2,1},{3,2},{4,7},{5,4},{6,5},{7,6},{8,11},{9,8},{10,9... | collective-permute-start | bytes 1572872 | tf_op jit(solution)/shard_map/ppermute | solution.py:76
  231.9 19.8 %collective-permute-start.9 = (bf16[4,4,32,512]{3,2,1,0:T(8,128)(2,1)S(1)}, bf16[4,4,32,512]{3,2,1,0:T(8,128)(2,1)}, u32[]{:S(2)}, u32[]{:S(2)}) collective-permute-start(bf16[4,4,32,512]{3,2,1,0:T(8,128)(2,1)S(1)} %get-tuple-element.7), channel_id=1, source_target_pairs={{0,2},{1,3},{2,0},{3,1},{4,6},{5,7},{6,4},{7,5},{8,10},{9,11},{10,... | collective-permute-start | bytes 1572872 | tf_op jit(solution)/shard_map/ppermute | solution.py:76
  232.8 22.4 %collective-permute-start.8 = (bf16[4,4,32,512]{3,2,1,0:T(8,128)(2,1)S(1)}, bf16[4,4,32,512]{3,2,1,0:T(8,128)(2,1)}, u32[]{:S(2)}, u32[]{:S(2)}) collective-permute-start(bf16[4,4,32,512]{3,2,1,0:T(8,128)(2,1)S(1)} %get-tuple-element.5), channel_id=1, source_target_pairs={{0,1},{1,2},{2,3},{3,0},{4,5},{5,6},{6,7},{7,4},{8,9},{9,10},{10,1... | collective-permute-start | bytes 1572872 | tf_op jit(solution)/shard_map/ppermute | solution.py:76
  256.9 6.4 %collective-permute-start.13 = (bf16[4,32,512]{2,1,0:T(8,128)(2,1)S(1)}, bf16[4,32,512]{2,1,0:T(8,128)(2,1)S(1)}, u32[]{:S(2)}, u32[]{:S(2)}) collective-permute-start(bf16[4,32,512]{2,1,0:T(8,128)(2,1)S(1)} %get-tuple-element.9), channel_id=1, source_target_pairs={{0,12},{1,13},{2,14},{3,15},{4,0},{5,1},{6,2},{7,3},{8,4},{9,5},{1... | collective-permute-start | bytes 393224 | tf_op jit(solution)/shard_map/ppermute | solution.py:76
  258.2 7.9 %collective-permute-start.12 = (bf16[4,32,512]{2,1,0:T(8,128)(2,1)S(1)}, bf16[4,32,512]{2,1,0:T(8,128)(2,1)S(1)}, u32[]{:S(2)}, u32[]{:S(2)}) collective-permute-start(bf16[4,32,512]{2,1,0:T(8,128)(2,1)S(1)} %get-tuple-element.10), channel_id=1, source_target_pairs={{0,8},{1,9},{2,10},{3,11},{4,12},{5,13},{6,14},{7,15},{8,0},{9,1},... | collective-permute-start | bytes 393224 | tf_op jit(solution)/shard_map/ppermute | solution.py:76
  259.7 8.0 %collective-permute-start.11 = (bf16[4,32,512]{2,1,0:T(8,128)(2,1)S(1)}, bf16[4,32,512]{2,1,0:T(8,128)(2,1)S(1)}, u32[]{:S(2)}, u32[]{:S(2)}) collective-permute-start(bf16[4,32,512]{2,1,0:T(8,128)(2,1)S(1)} %get-tuple-element.11), channel_id=1, source_target_pairs={{0,4},{1,5},{2,6},{3,7},{4,8},{5,9},{6,10},{7,11},{8,12},{9,13},{1... | collective-permute-start | bytes 393224 | tf_op jit(solution)/shard_map/ppermute | solution.py:76
Sparse Core Ops, SparseCore 0:
  12.6 148.3 all-gather.2

commit v5 on v4

--- a/solution.py
+++ b/solution.py
@@ -111,7 +111,8 @@
         axis=0,
     )
     gathered = lax.all_gather(pack, "pool", axis=0, tiled=False)
-    w_quarter = gathered[:, :feat, :].reshape(quarter, side, feat, width)
+    plane_rows = gathered.shape[1]
+    w_quarter = gathered.reshape(quarter, side, plane_rows, width)
     shrink_all = gathered[:, feat:feat + shrink_rows, :].reshape(
         pool_count * held, shrink_rows // held, width
     )
@@ -123,6 +124,7 @@
     by_shift = jnp.stack(pieces, axis=0)
     order = (my_y - jnp.arange(side, dtype=jnp.int32)) % side
     hidden_column = jnp.take(by_shift, order, axis=0)
+    hidden_column = jnp.pad(hidden_column, ((0, 0), (0, 0), (0, plane_rows - feat)))
 
     first = jnp.take(shrink_all, block_adapter, axis=0).reshape(block_count, feat, rank)
     second = jnp.take(expand_all, block_adapter, axis=0).reshape(block_count, column_span, rank)
@@ -137,10 +139,6 @@
     partial_value = jnp.einsum(
         "yif,ayfj->aij", hidden_column, w_quarter, preferred_element_type=jnp.float32
     )
-    chunk_ids = jnp.arange(quarter, dtype=jnp.int32)[:, None, None]
-    partial_value = partial_value + jnp.where(
-        chunk_ids == my_x, delta.astype(jnp.float32)[None, :, :], 0.0
-    )
     partial_value = partial_value.astype(jnp.bfloat16).reshape(
         quarter, side, side, own_rows, width
     )
@@ -149,7 +147,14 @@
     for s in range(1, side):
         piece = lax.dynamic_index_in_dim(partial_value, (my_x + s) % side, axis=2, keepdims=False)
         total = total + tensor_shift(piece, side, s, False).astype(jnp.float32)
-    total = total.astype(jnp.bfloat16)
+    delta_rows = delta.reshape(side, side, own_rows, column_span)
+    sent = [lax.dynamic_index_in_dim(delta_rows, my_x, axis=1, keepdims=False)]
+    for s in range(1, side):
+        piece = lax.dynamic_index_in_dim(delta_rows, (my_x + s) % side, axis=1, keepdims=False)
+        sent.append(tensor_shift(piece, side, s, False))
+    order_x = (my_x - jnp.arange(side, dtype=jnp.int32)) % side
+    delta_here = jnp.take(jnp.stack(sent, axis=0), order_x, axis=0)
+    total = (total + delta_here.astype(jnp.float32)).astype(jnp.bfloat16)
 
     got = [lax.dynamic_index_in_dim(total, my_y, axis=1, keepdims=False)]
     for s in range(1, side):

time: 280 us -> 275 us (0.982)
  waiting for transfers between devices: 150 us -> 142 us
  local copies, waits for them, and re-layouts: 34.2 us -> 28 us
  starting transfers between devices: 56.8 us -> 61.3 us
  matrix products: 14.4 us -> 18.3 us
    slice x1 -> x0, local copies, waits for them, and re-layouts: 13.3 us -> none  [shards(): w_quarter = gathered[:, :feat, :].reshape(quarter, side, feat, width)]
    ppermute x4, waiting for transfers between devices: 11.1 us -> 1.75 us  [tensor_allsum(): x = x + lax.ppermute(x, 'tensor', perm)]
    gather x1 -> x2, local copies, waits for them, and re-layouts: 4.86 us -> 10.9 us  [shards(): hidden_column = jnp.take(by_shift, order, axis=0)]
    ppermute x9 -> x12, starting transfers between devices: 45.6 us -> 50.4 us  [tensor_shift(): return lax.ppermute(x, 'tensor', perm)]
    dot_general x1, matrix products: 12.2 us -> 16.2 us  [shards(): jnp.einsum('yif,ayfj->aij', hidden_column, w_quarter, preferred_element_t...]
    ppermute x9 -> x12, waiting for transfers between devices: 29.4 us -> 30.6 us  [tensor_shift(): return lax.ppermute(x, 'tensor', perm)]
  transfers between devices with their start and end apart: 15 -> 18, of which waited for: 9 -> 7; matrix products, arithmetic and copies ran while one was open for 13% -> 19% of each run, Pallas kernels for 0% -> 0%
where the time goes in v5:
time: 275 us; the launch traced here: 273 us
  waiting for transfers between devices  142 us (52%)
  starting transfers between devices  61.3 us (22%)
  local copies, waits for them, and re-layouts  28 us (10%)
  matrix products  18.3 us (7%)
  between operations  13.7 us (5%)
  other arithmetic  9.96 us (4%)
    all_gather x1, waiting for transfers between devices, shards(): gathered = lax.all_gather(pack, 'pool', axis=0, tiled=False)  109 us
    ppermute x12, starting transfers between devices, tensor_shift(): return lax.ppermute(x, 'tensor', perm)  50.4 us
    ppermute x12, waiting for transfers between devices, tensor_shift(): return lax.ppermute(x, 'tensor', perm)  30.6 us
    dot_general x1, matrix products, shards(): jnp.einsum('yif,ayfj->aij', hidden_column, w_quarter, preferred_element_t...  16.2 us
    gather x2, local copies, waits for them, and re-layouts, shards(): hidden_column = jnp.take(by_shift, order, axis=0)  10.9 us
    ppermute x4, starting transfers between devices, tensor_allsum(): x = x + lax.ppermute(x, 'tensor', perm)  8.89 us
  transfers between devices with their start and end apart: 18, of which 7 were waited for; matrix products, arithmetic and copies ran while one was open for 19% of the time, Pallas kernels for 0%

profile of v5, /device:TPU:0, one launch (start us, length us, event | category | flops | bytes accessed | tf_op | source)
XLA Modules:
  0.0 273.0 jit_solution(21301793387212232)
XLA Ops:
  6.5 2.0 collective-permute-start
  8.5 1.2 copy.18
  9.7 0.3 reshape.132
  10.0 1.1 copy.19
  11.1 0.2 reshape.133
  11.3 1.1 pad_maximum_fusion.1
  12.5 19.0 %collective-permute-start.1 = (bf16[512,896]{1,0:T(8,128)(2,1)S(1)}, bf16[512,896]{1,0:T(8,128)(2,1)S(1)}, u32[]{:S(2)}, u32[]{:S(2)}) collective-permute-start(bf16[512,896]{1,0:T(8,128)(2,1)S(1)} %copy-done), channel_id=1, source_target_pairs={{0,4},{1,5},{2,6},{3,7},{4,8},{5,9},{6,10},{7,11},{8,12},{9,13},{1... | collective-permute-start | bytes 2752520 | tf_op jit(solution)/shard_map/ppermute | solution.py:76
  31.5 20.0 %collective-permute-start.2 = (bf16[512,896]{1,0:T(8,128)(2,1)S(1)}, bf16[512,896]{1,0:T(8,128)(2,1)S(1)}, u32[]{:S(2)}, u32[]{:S(2)}) collective-permute-start(bf16[512,896]{1,0:T(8,128)(2,1)S(1)} %copy-done), channel_id=1, source_target_pairs={{0,8},{1,9},{2,10},{3,11},{4,12},{5,13},{6,14},{7,15},{8,0},{9,1},... | collective-permute-start | bytes 2752520 | tf_op jit(solution)/shard_map/ppermute | solution.py:76
  51.7 109.3 %all-gather.3.cloned.1.call-done = bf16[19968,512]{1,0:T(8,128)(2,1)} async-done(((bf16[1248,512]{1,0:T(8,128)(2,1)}), bf16[19968,512]{1,0:T(8,128)(2,1)}) %all-gather.3.cloned.1.call-update) | async-done | bytes 20447248 | tf_op jit(solution)/shard_map/all_gather | solution.py:113
  160.9 4.2 %slice.18 = bf16[16,224,512]{2,1,0:T(8,128)(2,1)} slice(bf16[16,1248,512]{2,1,0:T(8,128)(2,1)} %bitcast.65), slice={[0:16], [896:1120], [0:512]} | slice | bytes 7340032 | tf_op jit(solution)/shard_map/slice | solution.py:116
  165.2 2.6 gather_fusion.1
  167.8 1.4 gather.21
  169.2 1.8 convolution_bitcast_fusion
  170.9 1.6 collective-permute-start.7
  172.5 3.1 %pad_maximum_fusion = bf16[4,512,896]{2,1,0:T(8,128)(2,1)} fusion(bf16[1,512,896]{2,1,0:T(8,128)(2,1)} %bitcast.4, bf16[1,512,896]{2,1,0:T(8,128)(2,1)S(1)} %bitcast.71, bf16[1,512,896]{2,1,0:T(8,128)(2,1)S(1)} %bitcast.70, bf16[1,512,896]{2,1,0:T(8,128)(2,1)S(1)} %bitcast.69), kind=kLoop, calls=%fused_computation.9 | loop fusion | flops 5505024 | bytes 7340032 | tf_op jit(solution)/shard_map/stack | solution.py:124
  175.6 4.9 %gather_fusion = bf16[4,512,896]{2,1,0:T(8,128)(2,1)} fusion(bf16[4,512,896]{2,1,0:T(8,128)(2,1)} %pad_maximum_fusion, s32[1024]{0:T(1024)S(1)} %pad_clamp_fusion.3), kind=kCustom, calls=%fused_computation.2 | custom fusion | bytes 7340048 | tf_op jit(solution)/shard_map/jit(_take)/gather | solution.py:126
  180.6 6.0 %copy.20 = bf16[4,512,896]{1,2,0:T(8,128)(2,1)} copy(bf16[4,512,896]{2,1,0:T(8,128)(2,1)} %gather_fusion) | data formatting | bytes 7340032 | tf_op jit(solution)/shard_map/jit(_take)/gather | solution.py:126
  186.5 2.8 %collective-permute-start.8 = (f32[4,128,64]{1,2,0:T(8,128)S(1)}, f32[4,128,64]{1,2,0:T(8,128)S(1)}, u32[]{:S(2)}, u32[]{:S(2)}) collective-permute-start(f32[4,128,64]{1,2,0:T(8,128)S(1)} %add.198), channel_id=1, source_target_pairs={{0,2},{1,3},{2,0},{3,1},{4,6},{5,7},{6,4},{7,5},{8,10},{9,11},{10,... | collective-permute-start | bytes 393224 | tf_op jit(solution)/shard_map/ppermute | solution.py:20
  189.3 2.5 broadcast_select_fusion
  191.8 1.7 collective-permute-done.8
  193.5 1.8 collective-permute-start.9
  195.3 16.2 %bitcast_convert_fusion = bf16[4,512,512]{1,2,0:T(8,128)(2,1)} fusion(bf16[4,4,1248,512]{3,2,1,0:T(8,128)(2,1)} %bitcast.66, bf16[4,512,896]{1,2,0:T(8,128)(2,1)S(1)} %broadcast_select_fusion), kind=kOutput, calls=%fused_computation.8 | convolution fusion | flops 10470031360 | bytes 26214400 | tf_op jit(solution)/shard_map/yif,ayfj->aij/dot_general | solution.py:139
  211.5 1.8 slice.19
  213.3 0.6 gather_fusion.2
  213.8 0.3 gather.23
  214.2 2.8 %collective-permute-start.10 = (f32[4,128,64]{1,2,0:T(8,128)S(1)}, f32[4,128,64]{1,2,0:T(8,128)S(1)}, u32[]{:S(2)}, u32[]{:S(2)}) collective-permute-start(f32[4,128,64]{1,2,0:T(8,128)S(1)} %add.200), channel_id=1, source_target_pairs={{0,8},{1,9},{2,10},{3,11},{4,12},{5,13},{6,14},{7,15},{8,0},{9,1},... | collective-permute-start | bytes 393224 | tf_op jit(solution)/shard_map/ppermute | solution.py:20
  217.0 1.5 dynamic-slice_bitcast_fusion.2
  218.4 0.6 collective-permute-start.4
  219.1 3.0 %collective-permute-start.5 = (bf16[4,4,32,512]{3,2,1,0:T(8,128)(2,1)S(1)}, bf16[4,4,32,512]{3,2,1,0:T(8,128)(2,1)}, u32[]{:S(2)}, u32[]{:S(2)}) collective-permute-start(bf16[4,4,32,512]{3,2,1,0:T(8,128)(2,1)S(1)} %get-tuple-element.8), channel_id=1, source_target_pairs={{0,2},{1,3},{2,0},{3,1},{4,6},{5,7},{6,4},{7,5},{8,10},{9,11},{10,... | collective-permute-start | bytes 1572872 | tf_op jit(solution)/shard_map/ppermute | solution.py:76
  222.1 1.8 collective-permute-start.6
  223.8 0.4 fusion.5
  224.3 0.3 collective-permute-start.11
  224.6 1.3 collective-permute-start.12
  225.9 21.6 %collective-permute-done.11 = bf16[4,32,512]{2,1,0:T(8,128)(2,1)S(1)} collective-permute-done((bf16[4,32,512]{2,1,0:T(8,128)(2,1)S(1)}, bf16[4,32,512]{2,1,0:T(8,128)(2,1)S(1)}, u32[]{:S(2)}, u32[]{:S(2)}) %collective-permute-start.11) | collective-permute-done | bytes 131104 | tf_op jit(solution)/shard_map/ppermute | solution.py:76
  247.6 0.9 collective-permute-start.13
  248.6 0.7 collective-permute-done.12
  249.3 3.2 %collective-permute-done.13 = bf16[4,32,512]{2,1,0:T(8,128)(2,1)S(1)} collective-permute-done((bf16[4,32,512]{2,1,0:T(8,128)(2,1)S(1)}, bf16[4,32,512]{2,1,0:T(8,128)(2,1)S(1)}, u32[]{:S(2)}, u32[]{:S(2)}) %collective-permute-start.13) | collective-permute-done | bytes 131104 | tf_op jit(solution)/shard_map/ppermute | solution.py:76
  252.6 0.6 gather_fusion.3
  253.2 1.8 fusion.9
  255.1 0.3 collective-permute-start.14
  255.4 1.7 collective-permute-start.15
  257.2 1.5 collective-permute-start.16
  258.7 4.1 %collective-permute-done.14 = bf16[4,32,512]{2,1,0:T(8,128)(2,1)S(1)} collective-permute-done((bf16[4,32,512]{2,1,0:T(8,128)(2,1)S(1)}, bf16[4,32,512]{2,1,0:T(8,128)(2,1)S(1)}, u32[]{:S(2)}, u32[]{:S(2)}) %collective-permute-start.14) | collective-permute-done | bytes 131104 | tf_op jit(solution)/shard_map/ppermute | solution.py:76
  262.8 0.9 collective-permute-done.16
  263.8 0.6 gather_fusion.4
  264.5 0.4 copy.23
  264.9 0.4 reshape.139
  265.3 0.9 broadcast_select_fusion.1
  (42 shorter events, 0.7 us)
Async XLA Ops:
  6.5 5.9 %copy-start = (bf16[512,896]{1,0:T(8,128)(2,1)S(1)}, bf16[512,896]{1,0:T(8,128)(2,1)}, u32[]{:S(2)}) copy-start(bf16[512,896]{1,0:T(8,128)(2,1)} %param.8) | copy-start | bytes 2752516
  6.5 45.0 %copy-start.2 = (s32[4]{0:T(128)S(1)}, s32[4]{0:T(128)}, u32[]{:S(2)}) copy-start(s32[4]{0:T(128)} %param.12) | copy-start | bytes 52
  6.5 45.0 %copy-start.1 = (s32[4]{0:T(128)S(1)}, s32[4]{0:T(128)}, u32[]{:S(2)}) copy-start(s32[4]{0:T(128)} %param.13) | copy-start | bytes 52
  6.5 154.4 %all-gather.3.cloned.1.call-start = ((), (), s32[]{:S(2)}) async-start(), calls=%async_computation | async-start | bytes 21725184 | tf_op jit(solution)/shard_map/all_gather | solution.py:113
  6.5 4.8 %collective-permute-start = (bf16[896,512]{1,0:T(8,128)(2,1)}, bf16[896,512]{1,0:T(8,128)(2,1)S(1)}, u32[]{:S(2)}, u32[]{:S(2)}) collective-permute-start(bf16[896,512]{1,0:T(8,128)(2,1)} %param.9), channel_id=1, source_target_pairs={{0,0},{1,1},{2,2},{3,3},{4,16},{5,17},{6,18},{7,19},{8,32},{9,33},... | collective-permute-start | bytes 2752520 | tf_op jit(solution)/shard_map/ppermute | solution.py:101
  12.5 160.0 %collective-permute-start.1 = (bf16[512,896]{1,0:T(8,128)(2,1)S(1)}, bf16[512,896]{1,0:T(8,128)(2,1)S(1)}, u32[]{:S(2)}, u32[]{:S(2)}) collective-permute-start(bf16[512,896]{1,0:T(8,128)(2,1)S(1)} %copy-done), channel_id=1, source_target_pairs={{0,4},{1,5},{2,6},{3,7},{4,8},{5,9},{6,10},{7,11},{8,12},{9,13},{1... | collective-permute-start | bytes 2752520 | tf_op jit(solution)/shard_map/ppermute | solution.py:76
  31.5 141.0 %collective-permute-start.2 = (bf16[512,896]{1,0:T(8,128)(2,1)S(1)}, bf16[512,896]{1,0:T(8,128)(2,1)S(1)}, u32[]{:S(2)}, u32[]{:S(2)}) collective-permute-start(bf16[512,896]{1,0:T(8,128)(2,1)S(1)} %copy-done), channel_id=1, source_target_pairs={{0,8},{1,9},{2,10},{3,11},{4,12},{5,13},{6,14},{7,15},{8,0},{9,1},... | collective-permute-start | bytes 2752520 | tf_op jit(solution)/shard_map/ppermute | solution.py:76
  51.5 121.1 %collective-permute-start.3 = (bf16[512,896]{1,0:T(8,128)(2,1)S(1)}, bf16[512,896]{1,0:T(8,128)(2,1)}, u32[]{:S(2)}, u32[]{:S(2)}) collective-permute-start(bf16[512,896]{1,0:T(8,128)(2,1)S(1)} %copy-done), channel_id=1, source_target_pairs={{0,12},{1,13},{2,14},{3,15},{4,0},{5,1},{6,2},{7,3},{8,4},{9,5},{1... | collective-permute-start | bytes 2752520 | tf_op jit(solution)/shard_map/ppermute | solution.py:76
  170.9 15.6 %collective-permute-start.7 = (f32[4,128,64]{1,2,0:T(8,128)S(1)}, f32[4,128,64]{1,2,0:T(8,128)S(1)}, u32[]{:S(2)}, u32[]{:S(2)}) collective-permute-start(f32[4,128,64]{1,2,0:T(8,128)S(1)} %convolution_bitcast_fusion), channel_id=1, source_target_pairs={{0,1},{1,0},{2,3},{3,2},{4,5},{5,4},{6,7},{7,6},{8,9},{9,8},{10,11... | collective-permute-start | bytes 393224 | tf_op jit(solution)/shard_map/ppermute | solution.py:20
  186.5 7.0 %collective-permute-start.8 = (f32[4,128,64]{1,2,0:T(8,128)S(1)}, f32[4,128,64]{1,2,0:T(8,128)S(1)}, u32[]{:S(2)}, u32[]{:S(2)}) collective-permute-start(f32[4,128,64]{1,2,0:T(8,128)S(1)} %add.198), channel_id=1, source_target_pairs={{0,2},{1,3},{2,0},{3,1},{4,6},{5,7},{6,4},{7,5},{8,10},{9,11},{10,... | collective-permute-start | bytes 393224 | tf_op jit(solution)/shard_map/ppermute | solution.py:20
  193.5 20.6 %collective-permute-start.9 = (f32[4,128,64]{1,2,0:T(8,128)S(1)}, f32[4,128,64]{1,2,0:T(8,128)S(1)}, u32[]{:S(2)}, u32[]{:S(2)}) collective-permute-start(f32[4,128,64]{1,2,0:T(8,128)S(1)} %add.199), channel_id=1, source_target_pairs={{0,4},{1,5},{2,6},{3,7},{4,0},{5,1},{6,2},{7,3},{8,12},{9,13},{10,... | collective-permute-start | bytes 393224 | tf_op jit(solution)/shard_map/ppermute | solution.py:20
  214.2 9.7 %collective-permute-start.10 = (f32[4,128,64]{1,2,0:T(8,128)S(1)}, f32[4,128,64]{1,2,0:T(8,128)S(1)}, u32[]{:S(2)}, u32[]{:S(2)}) collective-permute-start(f32[4,128,64]{1,2,0:T(8,128)S(1)} %add.200), channel_id=1, source_target_pairs={{0,8},{1,9},{2,10},{3,11},{4,12},{5,13},{6,14},{7,15},{8,0},{9,1},... | collective-permute-start | bytes 393224 | tf_op jit(solution)/shard_map/ppermute | solution.py:20
  218.4 34.8 %collective-permute-start.4 = (bf16[4,4,32,512]{3,2,1,0:T(8,128)(2,1)S(1)}, bf16[4,4,32,512]{3,2,1,0:T(8,128)(2,1)S(1)}, u32[]{:S(2)}, u32[]{:S(2)}) collective-permute-start(bf16[4,4,32,512]{3,2,1,0:T(8,128)(2,1)S(1)} %get-tuple-element.6), channel_id=1, source_target_pairs={{0,1},{1,2},{2,3},{3,0},{4,5},{5,6},{6,7},{7,4},{8,9},{9,10},{10,1... | collective-permute-start | bytes 1572872 | tf_op jit(solution)/shard_map/ppermute | solution.py:76
  219.1 34.1 %collective-permute-start.5 = (bf16[4,4,32,512]{3,2,1,0:T(8,128)(2,1)S(1)}, bf16[4,4,32,512]{3,2,1,0:T(8,128)(2,1)}, u32[]{:S(2)}, u32[]{:S(2)}) collective-permute-start(bf16[4,4,32,512]{3,2,1,0:T(8,128)(2,1)S(1)} %get-tuple-element.8), channel_id=1, source_target_pairs={{0,2},{1,3},{2,0},{3,1},{4,6},{5,7},{6,4},{7,5},{8,10},{9,11},{10,... | collective-permute-start | bytes 1572872 | tf_op jit(solution)/shard_map/ppermute | solution.py:76
  222.1 31.2 %collective-permute-start.6 = (bf16[4,4,32,512]{3,2,1,0:T(8,128)(2,1)S(1)}, bf16[4,4,32,512]{3,2,1,0:T(8,128)(2,1)}, u32[]{:S(2)}, u32[]{:S(2)}) collective-permute-start(bf16[4,4,32,512]{3,2,1,0:T(8,128)(2,1)S(1)} %get-tuple-element.7), channel_id=1, source_target_pairs={{0,3},{1,0},{2,1},{3,2},{4,7},{5,4},{6,5},{7,6},{8,11},{9,8},{10,9... | collective-permute-start | bytes 1572872 | tf_op jit(solution)/shard_map/ppermute | solution.py:76
  224.3 23.3 %collective-permute-start.11 = (bf16[4,32,512]{2,1,0:T(8,128)(2,1)S(1)}, bf16[4,32,512]{2,1,0:T(8,128)(2,1)S(1)}, u32[]{:S(2)}, u32[]{:S(2)}) collective-permute-start(bf16[4,32,512]{2,1,0:T(8,128)(2,1)S(1)} %get-tuple-element.16), channel_id=1, source_target_pairs={{0,1},{1,2},{2,3},{3,0},{4,5},{5,6},{6,7},{7,4},{8,9},{9,10},{10,1... | collective-permute-start | bytes 393224 | tf_op jit(solution)/shard_map/ppermute | solution.py:76
  224.6 24.7 %collective-permute-start.12 = (bf16[4,32,512]{2,1,0:T(8,128)(2,1)S(1)}, bf16[4,32,512]{2,1,0:T(8,128)(2,1)S(1)}, u32[]{:S(2)}, u32[]{:S(2)}) collective-permute-start(bf16[4,32,512]{2,1,0:T(8,128)(2,1)S(1)} %get-tuple-element.15), channel_id=1, source_target_pairs={{0,2},{1,3},{2,0},{3,1},{4,6},{5,7},{6,4},{7,5},{8,10},{9,11},{10,... | collective-permute-start | bytes 393224 | tf_op jit(solution)/shard_map/ppermute | solution.py:76
  247.6 5.0 %collective-permute-start.13 = (bf16[4,32,512]{2,1,0:T(8,128)(2,1)S(1)}, bf16[4,32,512]{2,1,0:T(8,128)(2,1)S(1)}, u32[]{:S(2)}, u32[]{:S(2)}) collective-permute-start(bf16[4,32,512]{2,1,0:T(8,128)(2,1)S(1)} %get-tuple-element.14), channel_id=1, source_target_pairs={{0,3},{1,0},{2,1},{3,2},{4,7},{5,4},{6,5},{7,6},{8,11},{9,8},{10,9... | collective-permute-start | bytes 393224 | tf_op jit(solution)/shard_map/ppermute | solution.py:76
  255.1 7.7 %collective-permute-start.14 = (bf16[4,32,512]{2,1,0:T(8,128)(2,1)S(1)}, bf16[4,32,512]{2,1,0:T(8,128)(2,1)S(1)}, u32[]{:S(2)}, u32[]{:S(2)}) collective-permute-start(bf16[4,32,512]{2,1,0:T(8,128)(2,1)S(1)} %get-tuple-element.12), channel_id=1, source_target_pairs={{0,4},{1,5},{2,6},{3,7},{4,8},{5,9},{6,10},{7,11},{8,12},{9,13},{1... | collective-permute-start | bytes 393224 | tf_op jit(solution)/shard_map/ppermute | solution.py:76
  255.4 7.4 %collective-permute-start.15 = (bf16[4,32,512]{2,1,0:T(8,128)(2,1)S(1)}, bf16[4,32,512]{2,1,0:T(8,128)(2,1)S(1)}, u32[]{:S(2)}, u32[]{:S(2)}) collective-permute-start(bf16[4,32,512]{2,1,0:T(8,128)(2,1)S(1)} %get-tuple-element.11), channel_id=1, source_target_pairs={{0,8},{1,9},{2,10},{3,11},{4,12},{5,13},{6,14},{7,15},{8,0},{9,1},... | collective-permute-start | bytes 393224 | tf_op jit(solution)/shard_map/ppermute | solution.py:76
  257.2 6.5 %collective-permute-start.16 = (bf16[4,32,512]{2,1,0:T(8,128)(2,1)S(1)}, bf16[4,32,512]{2,1,0:T(8,128)(2,1)S(1)}, u32[]{:S(2)}, u32[]{:S(2)}) collective-permute-start(bf16[4,32,512]{2,1,0:T(8,128)(2,1)S(1)} %get-tuple-element.10), channel_id=1, source_target_pairs={{0,12},{1,13},{2,14},{3,15},{4,0},{5,1},{6,2},{7,3},{8,4},{9,5},{1... | collective-permute-start | bytes 393224 | tf_op jit(solution)/shard_map/ppermute | solution.py:76
Sparse Core Ops, SparseCore 0:
  12.6 148.3 all-gather.2

commit v6 on v4

--- a/solution.py
+++ b/solution.py
@@ -95,8 +95,8 @@
     for p1 in range(pool_count):
         for y1 in range(side):
             for x1 in range(side):
-                p2 = (p1 % quarter) * side + y1
-                y2 = p1 // quarter
+                y2 = p1 % side
+                p2 = (p1 // side) * side + (y2 - y1) % side
                 pairs.append((p1 * tensor_count + y1 * side + x1, p2 * tensor_count + y2 * side + x1))
     moved = lax.ppermute(down_weight, ("pool", "tensor"), pairs)
 
@@ -111,7 +111,8 @@
         axis=0,
     )
     gathered = lax.all_gather(pack, "pool", axis=0, tiled=False)
-    w_quarter = gathered[:, :feat, :].reshape(quarter, side, feat, width)
+    plane_rows = gathered.shape[1]
+    w_quarter = gathered.reshape(quarter, side, plane_rows, width)
     shrink_all = gathered[:, feat:feat + shrink_rows, :].reshape(
         pool_count * held, shrink_rows // held, width
     )
@@ -120,9 +121,7 @@
     )
 
     pieces = [hidden] + [tensor_shift(hidden, side, s, True) for s in range(1, side)]
-    by_shift = jnp.stack(pieces, axis=0)
-    order = (my_y - jnp.arange(side, dtype=jnp.int32)) % side
-    hidden_column = jnp.take(by_shift, order, axis=0)
+    hidden_column = jnp.pad(jnp.stack(pieces, axis=0), ((0, 0), (0, 0), (0, plane_rows - feat)))
 
     first = jnp.take(shrink_all, block_adapter, axis=0).reshape(block_count, feat, rank)
     second = jnp.take(expand_all, block_adapter, axis=0).reshape(block_count, column_span, rank)
@@ -135,11 +134,7 @@
     delta = (adapter_scale_factor * enlarged_rows).astype(jnp.bfloat16).reshape(input_rows, column_span)
 
     partial_value = jnp.einsum(
-        "yif,ayfj->aij", hidden_column, w_quarter, preferred_element_type=jnp.float32
-    )
-    chunk_ids = jnp.arange(quarter, dtype=jnp.int32)[:, None, None]
-    partial_value = partial_value + jnp.where(
-        chunk_ids == my_x, delta.astype(jnp.float32)[None, :, :], 0.0
+        "sif,asfj->aij", hidden_column, w_quarter, preferred_element_type=jnp.float32
     )
     partial_value = partial_value.astype(jnp.bfloat16).reshape(
         quarter, side, side, own_rows, width
@@ -155,9 +150,11 @@
     for s in range(1, side):
         piece = lax.dynamic_index_in_dim(total, (my_y + s) % side, axis=1, keepdims=False)
         got.append(tensor_shift(piece, side, s, True))
-    by_shift = jnp.stack(got, axis=0)
-    result = jnp.take(by_shift, order, axis=0)
-    result = jnp.transpose(result, (2, 0, 1, 3)).reshape(own_rows, pool_count * width)
+    order = (my_y - jnp.arange(side, dtype=jnp.int32)) % side
+    result = jnp.take(jnp.stack(got, axis=0), order, axis=0)
+    result = jnp.transpose(result, (2, 1, 0, 3)).reshape(own_rows, pool_count * width)
+    delta_mine = lax.all_to_all(delta, "tensor", split_axis=0, concat_axis=1, tiled=True)
+    result = (result.astype(jnp.float32) + delta_mine.astype(jnp.float32)).astype(jnp.bfloat16)
 
     row_ids = tensor_pos * own_rows + jnp.arange(own_rows, dtype=jnp.int32)
     owning = (row_ids // BLOCK)[:, None] == jnp.arange(block_count, dtype=jnp.int32)[None, :]

time: 280 us -> 246 us (0.88)
  local copies, waits for them, and re-layouts: 34.2 us -> 17.6 us
  starting transfers between devices: 56.8 us -> 45.7 us
  waiting for transfers between devices: 150 us -> 144 us
  matrix products: 14.4 us -> 17.8 us
    ppermute x9, waiting for transfers between devices: 29.4 us -> 0.02 us  [tensor_shift(): return lax.ppermute(x, 'tensor', perm)]
    ppermute x9, starting transfers between devices: 45.6 us -> 30.1 us  [tensor_shift(): return lax.ppermute(x, 'tensor', perm)]
    ppermute x4, waiting for transfers between devices: 11.1 us -> 25.2 us  [tensor_allsum(): x = x + lax.ppermute(x, 'tensor', perm)]
    slice x1 -> x0, local copies, waits for them, and re-layouts: 13.3 us -> none  [shards(): w_quarter = gathered[:, :feat, :].reshape(quarter, side, feat, width)]
    all_to_all x0 -> x1, waiting for transfers between devices: none -> 7.86 us  [shards(): lax.all_to_all(delta, 'tensor', split_axis=0, concat_axis=1, tiled=True)]
    all_to_all x0 -> x1, starting transfers between devices: none -> 5.23 us  [shards(): lax.all_to_all(delta, 'tensor', split_axis=0, concat_axis=1, tiled=True)]
    gather x2 -> x1, local copies, waits for them, and re-layouts: 5.44 us -> 0.58 us  [shards(): result = jnp.take(jnp.stack(got, axis=0), order, axis=0)]
    dot_general x1, matrix products: 12.2 us -> 16 us  [shards(): jnp.einsum('sif,asfj->aij', hidden_column, w_quarter, preferred_element_t...]
  transfers between devices with their start and end apart: 15 -> 16, of which waited for: 9 -> 4; matrix products, arithmetic and copies ran while one was open for 13% -> 15% of each run, Pallas kernels for 0% -> 0%
where the time goes in v6:
time: 246 us; the launch traced here: 244 us
  waiting for transfers between devices  144 us (59%)
  starting transfers between devices  45.7 us (19%)
  matrix products  17.8 us (7%)
  local copies, waits for them, and re-layouts  17.6 us (7%)
  between operations  13.7 us (6%)
  other arithmetic  5.94 us (2%)
    all_gather x1, waiting for transfers between devices, shards(): gathered = lax.all_gather(pack, 'pool', axis=0, tiled=False)  111 us
    ppermute x9, starting transfers between devices, tensor_shift(): return lax.ppermute(x, 'tensor', perm)  30.1 us
    ppermute x4, waiting for transfers between devices, tensor_allsum(): x = x + lax.ppermute(x, 'tensor', perm)  25.2 us
    dot_general x1, matrix products, shards(): jnp.einsum('sif,asfj->aij', hidden_column, w_quarter, preferred_element_t...  16 us
    ppermute x4, starting transfers between devices, tensor_allsum(): x = x + lax.ppermute(x, 'tensor', perm)  8.38 us
    all_to_all x1, waiting for transfers between devices, shards(): lax.all_to_all(delta, 'tensor', split_axis=0, concat_axis=1, tiled=True)  7.86 us
    all_to_all x1, starting transfers between devices, shards(): lax.all_to_all(delta, 'tensor', split_axis=0, concat_axis=1, tiled=True)  5.23 us
  transfers between devices with their start and end apart: 16, of which 4 were waited for; matrix products, arithmetic and copies ran while one was open for 15% of the time, Pallas kernels for 0%

profile of v6, /device:TPU:0, one launch (start us, length us, event | category | flops | bytes accessed | tf_op | source)
XLA Modules:
  0.0 244.3 jit_solution(16637460248513450245)
XLA Ops:
  6.5 2.0 collective-permute-start
  8.5 1.1 copy.32
  9.6 0.2 reshape.134
  9.8 1.2 copy.31
  11.0 0.3 reshape.133
  11.3 1.1 pad_maximum_fusion
  12.5 0.5 copy.33
  13.0 11.6 %collective-permute-start.3 = (bf16[512,896]{0,1:T(8,128)(2,1)S(1)}, bf16[512,896]{0,1:T(8,128)(2,1)}, u32[]{:S(2)}, u32[]{:S(2)}) collective-permute-start(bf16[512,896]{0,1:T(8,128)(2,1)S(1)} %copy.33), channel_id=1, source_target_pairs={{0,12},{1,13},{2,14},{3,15},{4,0},{5,1},{6,2},{7,3},{8,4},{9,5},{1... | collective-permute-start | bytes 2752520 | tf_op jit(solution)/shard_map/ppermute | solution.py:76
  24.6 10.4 %collective-permute-start.2 = (bf16[512,896]{0,1:T(8,128)(2,1)S(1)}, bf16[512,896]{0,1:T(8,128)(2,1)}, u32[]{:S(2)}, u32[]{:S(2)}) collective-permute-start(bf16[512,896]{0,1:T(8,128)(2,1)S(1)} %copy.33), channel_id=1, source_target_pairs={{0,8},{1,9},{2,10},{3,11},{4,12},{5,13},{6,14},{7,15},{8,0},{9,1},... | collective-permute-start | bytes 2752520 | tf_op jit(solution)/shard_map/ppermute | solution.py:76
  35.0 1.3 collective-permute-start.1
  36.4 110.6 %all-gather.3.cloned.1.call-done = bf16[19968,512]{1,0:T(8,128)(2,1)} async-done(((bf16[1248,512]{1,0:T(8,128)(2,1)}), bf16[19968,512]{1,0:T(8,128)(2,1)}) %all-gather.3.cloned.1.call-update) | async-done | bytes 20447248 | tf_op jit(solution)/shard_map/all_gather | solution.py:113
  146.9 4.2 %slice.14 = bf16[16,224,512]{2,1,0:T(8,128)(2,1)} slice(bf16[16,1248,512]{2,1,0:T(8,128)(2,1)} %bitcast.58), slice={[0:16], [896:1120], [0:512]} | slice | bytes 7340032 | tf_op jit(solution)/shard_map/slice | solution.py:116
  151.1 2.6 %gather_fusion.1 = bf16[4,112,512]{2,1,0:T(8,128)(2,1)S(1)} fusion(bf16[32,112,512]{2,1,0:T(8,128)(2,1)} %bitcast.53, s32[1024]{0:T(1024)S(1)} %pad_clamp_fusion), kind=kCustom, calls=%fused_computation.1 | custom fusion | bytes 917520 | tf_op jit(solution)/shard_map/jit(_take)/gather | solution.py:126
  153.7 0.5 gather.18
  154.2 0.6 convolution_bitcast_fusion
  154.8 1.6 collective-permute-start.10
  156.4 16.0 %bitcast_convert_fusion = bf16[4,512,512]{1,2,0:T(8,128)(2,1)S(1)} fusion(bf16[4,4,1248,512]{3,2,1,0:T(8,128)(2,1)} %bitcast.59, bf16[1,512,896]{1,2,0:T(8,128)(2,1)} %bitcast.4, bf16[1,512,896]{1,2,0:T(8,128)(2,1)} %bitcast.3, bf16[1,512,896]{1,2,0:T(8,128)(2,1)} %bitcast.2, bf16[1,512,896]{1,2,0:T(8,128)(2,1)S(1)} %bitcast.62), kind=kOutput, calls=%fused_computation.18 | convolution fusion | flops 10503258112 | bytes 26214400 | tf_op jit(solution)/shard_map/sif,asfj->aij/dot_general | solution.py:136
  172.4 1.3 copy-done
  173.8 0.9 dynamic-slice_bitcast_fusion.2
  174.7 2.1 collective-permute-start.6
  176.7 0.6 collective-permute-start.5
  177.3 1.4 collective-permute-start.4
  178.8 2.1 collective-permute-start.11
  181.0 0.1 select_reduce_fusion
  181.0 24.8 %collective-permute-done.11 = f32[4,128,64]{1,2,0:T(8,128)S(1)} collective-permute-done((f32[4,128,64]{1,2,0:T(8,128)S(1)}, f32[4,128,64]{1,2,0:T(8,128)S(1)}, u32[]{:S(2)}, u32[]{:S(2)}) %collective-permute-start.11) | collective-permute-done | bytes 131104 | tf_op jit(solution)/shard_map/ppermute | solution.py:20
  205.9 1.6 collective-permute-start.12
  207.4 0.6 fusion.32
  208.0 1.8 slice.15
  209.8 0.6 gather_fusion.2
  210.4 0.3 gather.20
  210.7 0.3 collective-permute-done.12
  211.0 0.9 add.193
  212.0 3.1 %collective-permute-start.13 = (f32[4,128,64]{1,2,0:T(8,128)S(1)}, f32[4,128,64]{1,2,0:T(8,128)S(1)}, u32[]{:S(2)}, u32[]{:S(2)}) collective-permute-start(f32[4,128,64]{1,2,0:T(8,128)S(1)} %add.193), channel_id=1, source_target_pairs={{0,8},{1,9},{2,10},{3,11},{4,12},{5,13},{6,14},{7,15},{8,0},{9,1},... | collective-permute-start | bytes 393224 | tf_op jit(solution)/shard_map/ppermute | solution.py:20
  215.1 1.9 fusion.24
  217.0 0.1 dynamic-slice_bitcast_fusion.6
  217.0 1.2 collective-permute-start.9
  218.2 1.5 collective-permute-start.8
  219.7 1.2 fusion.21
  220.9 5.2 %all-to-all-start = ((bf16[16,32,512]{2,1,0:T(8,128)(2,1)}), bf16[16,32,512]{2,1,0:T(8,128)(2,1)S(1)}, u32[]{:S(2)}, u32[]{:S(2)}) async-start(bf16[16,32,512]{2,1,0:T(8,128)(2,1)} %bitcast.29), calls=%async_computation | async-start | bytes 1048576 | tf_op jit(solution)/shard_map/all_to_all | solution.py:156
  226.2 0.1 pad_maximum_fusion.1
  226.3 0.6 gather_fusion
  226.9 0.1 convert_bitcast_fusion.1
  227.0 0.7 copy.37
  227.7 0.7 reshape.141
  228.4 7.9 %all-to-all-done = bf16[16,32,512]{2,1,0:T(8,128)(2,1)S(1)} async-done(((bf16[16,32,512]{2,1,0:T(8,128)(2,1)}), bf16[16,32,512]{2,1,0:T(8,128)(2,1)S(1)}, u32[]{:S(2)}, u32[]{:S(2)}) %all-to-all-start) | async-done | bytes 524320 | tf_op jit(solution)/shard_map/all_to_all | solution.py:156
  236.3 0.1 convert_bitcast_fusion
  236.4 0.1 copy.44
  236.5 0.9 fusion.27
  (32 shorter events, 0.2 us)
Async XLA Ops:
  6.5 5.9 %copy-start.1 = (bf16[512,896]{1,0:T(8,128)(2,1)S(1)}, bf16[512,896]{1,0:T(8,128)(2,1)}, u32[]{:S(2)}) copy-start(bf16[512,896]{1,0:T(8,128)(2,1)} %param.6) | copy-start | bytes 2752516
  6.5 29.8 %copy-start.2 = (s32[4]{0:T(128)S(1)}, s32[4]{0:T(128)}, u32[]{:S(2)}) copy-start(s32[4]{0:T(128)} %param.10) | copy-start | bytes 52
  6.5 140.4 %all-gather.3.cloned.1.call-start = ((), (), s32[]{:S(2)}) async-start(), calls=%async_computation.1 | async-start | bytes 21725184 | tf_op jit(solution)/shard_map/all_gather | solution.py:113
  6.5 4.8 %collective-permute-start = (bf16[896,512]{1,0:T(8,128)(2,1)}, bf16[896,512]{1,0:T(8,128)(2,1)S(1)}, u32[]{:S(2)}, u32[]{:S(2)}) collective-permute-start(bf16[896,512]{1,0:T(8,128)(2,1)} %param.7), channel_id=1, source_target_pairs={{0,0},{1,1},{2,2},{3,3},{4,48},{5,49},{6,50},{7,51},{8,32},{9,33},... | collective-permute-start | bytes 2752520 | tf_op jit(solution)/shard_map/ppermute | solution.py:101
  13.0 143.4 %collective-permute-start.3 = (bf16[512,896]{0,1:T(8,128)(2,1)S(1)}, bf16[512,896]{0,1:T(8,128)(2,1)}, u32[]{:S(2)}, u32[]{:S(2)}) collective-permute-start(bf16[512,896]{0,1:T(8,128)(2,1)S(1)} %copy.33), channel_id=1, source_target_pairs={{0,12},{1,13},{2,14},{3,15},{4,0},{5,1},{6,2},{7,3},{8,4},{9,5},{1... | collective-permute-start | bytes 2752520 | tf_op jit(solution)/shard_map/ppermute | solution.py:76
  24.6 131.7 %collective-permute-start.2 = (bf16[512,896]{0,1:T(8,128)(2,1)S(1)}, bf16[512,896]{0,1:T(8,128)(2,1)}, u32[]{:S(2)}, u32[]{:S(2)}) collective-permute-start(bf16[512,896]{0,1:T(8,128)(2,1)S(1)} %copy.33), channel_id=1, source_target_pairs={{0,8},{1,9},{2,10},{3,11},{4,12},{5,13},{6,14},{7,15},{8,0},{9,1},... | collective-permute-start | bytes 2752520 | tf_op jit(solution)/shard_map/ppermute | solution.py:76
  35.0 121.4 %collective-permute-start.1 = (bf16[512,896]{0,1:T(8,128)(2,1)S(1)}, bf16[512,896]{0,1:T(8,128)(2,1)}, u32[]{:S(2)}, u32[]{:S(2)}) collective-permute-start(bf16[512,896]{0,1:T(8,128)(2,1)S(1)} %copy.33), channel_id=1, source_target_pairs={{0,4},{1,5},{2,6},{3,7},{4,8},{5,9},{6,10},{7,11},{8,12},{9,13},{1... | collective-permute-start | bytes 2752520 | tf_op jit(solution)/shard_map/ppermute | solution.py:76
  154.8 24.0 %collective-permute-start.10 = (f32[4,128,64]{1,2,0:T(8,128)S(1)}, f32[4,128,64]{1,2,0:T(8,128)S(1)}, u32[]{:S(2)}, u32[]{:S(2)}) collective-permute-start(f32[4,128,64]{1,2,0:T(8,128)S(1)} %convolution_bitcast_fusion), channel_id=1, source_target_pairs={{0,1},{1,0},{2,3},{3,2},{4,5},{5,4},{6,7},{7,6},{8,9},{9,8},{10,11... | collective-permute-start | bytes 393224 | tf_op jit(solution)/shard_map/ppermute | solution.py:20
  156.4 24.6 %copy-start.4 = (s32[4]{0:T(128)S(1)}, s32[4]{0:T(128)}, u32[]{:S(2)}) copy-start(s32[4]{0:T(128)} %param.11) | copy-start | bytes 52
  172.4 1.3 copy-start
  174.7 40.4 %collective-permute-start.6 = (bf16[4,4,32,512]{3,2,1,0:T(8,128)(2,1)}, bf16[4,4,32,512]{3,2,1,0:T(8,128)(2,1)}, u32[]{:S(2)}, u32[]{:S(2)}) collective-permute-start(bf16[4,4,32,512]{3,2,1,0:T(8,128)(2,1)} %get-tuple-element.6), channel_id=1, source_target_pairs={{0,3},{1,0},{2,1},{3,2},{4,7},{5,4},{6,5},{7,6},{8,11},{9,8},{10,9... | collective-permute-start | bytes 1572872 | tf_op jit(solution)/shard_map/ppermute | solution.py:76
  176.7 38.3 %collective-permute-start.5 = (bf16[4,4,32,512]{3,2,1,0:T(8,128)(2,1)S(1)}, bf16[4,4,32,512]{3,2,1,0:T(8,128)(2,1)}, u32[]{:S(2)}, u32[]{:S(2)}) collective-permute-start(bf16[4,4,32,512]{3,2,1,0:T(8,128)(2,1)S(1)} %get-tuple-element.7), channel_id=1, source_target_pairs={{0,2},{1,3},{2,0},{3,1},{4,6},{5,7},{6,4},{7,5},{8,10},{9,11},{10,... | collective-permute-start | bytes 1572872 | tf_op jit(solution)/shard_map/ppermute | solution.py:76
  177.3 37.7 %collective-permute-start.4 = (bf16[4,4,32,512]{3,2,1,0:T(8,128)(2,1)S(1)}, bf16[4,4,32,512]{3,2,1,0:T(8,128)(2,1)}, u32[]{:S(2)}, u32[]{:S(2)}) collective-permute-start(bf16[4,4,32,512]{3,2,1,0:T(8,128)(2,1)S(1)} %get-tuple-element.5), channel_id=1, source_target_pairs={{0,1},{1,2},{2,3},{3,0},{4,5},{5,6},{6,7},{7,4},{8,9},{9,10},{10,1... | collective-permute-start | bytes 1572872 | tf_op jit(solution)/shard_map/ppermute | solution.py:76
  178.8 27.1 %collective-permute-start.11 = (f32[4,128,64]{1,2,0:T(8,128)S(1)}, f32[4,128,64]{1,2,0:T(8,128)S(1)}, u32[]{:S(2)}, u32[]{:S(2)}) collective-permute-start(f32[4,128,64]{1,2,0:T(8,128)S(1)} %add.191), channel_id=1, source_target_pairs={{0,2},{1,3},{2,0},{3,1},{4,6},{5,7},{6,4},{7,5},{8,10},{9,11},{10,... | collective-permute-start | bytes 393224 | tf_op jit(solution)/shard_map/ppermute | solution.py:20
  205.9 5.2 %collective-permute-start.12 = (f32[4,128,64]{1,2,0:T(8,128)S(1)}, f32[4,128,64]{1,2,0:T(8,128)}, u32[]{:S(2)}, u32[]{:S(2)}) collective-permute-start(f32[4,128,64]{1,2,0:T(8,128)S(1)} %add.192), channel_id=1, source_target_pairs={{0,4},{1,5},{2,6},{3,7},{4,0},{5,1},{6,2},{7,3},{8,12},{9,13},{10,... | collective-permute-start | bytes 393224 | tf_op jit(solution)/shard_map/ppermute | solution.py:20
  212.0 7.8 %collective-permute-start.13 = (f32[4,128,64]{1,2,0:T(8,128)S(1)}, f32[4,128,64]{1,2,0:T(8,128)S(1)}, u32[]{:S(2)}, u32[]{:S(2)}) collective-permute-start(f32[4,128,64]{1,2,0:T(8,128)S(1)} %add.193), channel_id=1, source_target_pairs={{0,8},{1,9},{2,10},{3,11},{4,12},{5,13},{6,14},{7,15},{8,0},{9,1},... | collective-permute-start | bytes 393224 | tf_op jit(solution)/shard_map/ppermute | solution.py:20
  217.0 9.2 %collective-permute-start.9 = (bf16[4,32,512]{2,1,0:T(8,128)(2,1)S(1)}, bf16[4,32,512]{2,1,0:T(8,128)(2,1)S(1)}, u32[]{:S(2)}, u32[]{:S(2)}) collective-permute-start(bf16[4,32,512]{2,1,0:T(8,128)(2,1)S(1)} %get-tuple-element.9), channel_id=1, source_target_pairs={{0,12},{1,13},{2,14},{3,15},{4,0},{5,1},{6,2},{7,3},{8,4},{9,5},{1... | collective-permute-start | bytes 393224 | tf_op jit(solution)/shard_map/ppermute | solution.py:76
  218.2 7.9 %collective-permute-start.8 = (bf16[4,32,512]{2,1,0:T(8,128)(2,1)S(1)}, bf16[4,32,512]{2,1,0:T(8,128)(2,1)S(1)}, u32[]{:S(2)}, u32[]{:S(2)}) collective-permute-start(bf16[4,32,512]{2,1,0:T(8,128)(2,1)S(1)} %get-tuple-element.10), channel_id=1, source_target_pairs={{0,8},{1,9},{2,10},{3,11},{4,12},{5,13},{6,14},{7,15},{8,0},{9,1},... | collective-permute-start | bytes 393224 | tf_op jit(solution)/shard_map/ppermute | solution.py:76
  219.7 6.5 %collective-permute-start.7 = (bf16[4,32,512]{2,1,0:T(8,128)(2,1)S(1)}, bf16[4,32,512]{2,1,0:T(8,128)(2,1)S(1)}, u32[]{:S(2)}, u32[]{:S(2)}) collective-permute-start(bf16[4,32,512]{2,1,0:T(8,128)(2,1)S(1)} %get-tuple-element.11), channel_id=1, source_target_pairs={{0,4},{1,5},{2,6},{3,7},{4,8},{5,9},{6,10},{7,11},{8,12},{9,13},{1... | collective-permute-start | bytes 393224 | tf_op jit(solution)/shard_map/ppermute | solution.py:76
  220.9 15.4 %all-to-all-start = ((bf16[16,32,512]{2,1,0:T(8,128)(2,1)}), bf16[16,32,512]{2,1,0:T(8,128)(2,1)S(1)}, u32[]{:S(2)}, u32[]{:S(2)}) async-start(bf16[16,32,512]{2,1,0:T(8,128)(2,1)} %bitcast.29), calls=%async_computation | async-start | bytes 1048576 | tf_op jit(solution)/shard_map/all_to_all | solution.py:156
  226.3 10.2 %copy-start.3 = (pred[32]{0:T(512)(128)(4,1)S(1)}, pred[32]{0:T(512)(128)(4,1)}, u32[]{:S(2)}) copy-start(pred[32]{0:T(512)(128)(4,1)} %fusion.32) | copy-start | bytes 100
Sparse Core Ops, SparseCore 0:
  12.6 134.3 all-gather.2

commit v7 on v6

--- a/solution.py
+++ b/solution.py
@@ -22,26 +22,27 @@
     return x
 
 
-def scatter_kernel(count, rows, part_ref, recv_ref, send_sems, recv_sems):
+def x_reduce_kernel(side, part_ref, recv_ref, send_sems, recv_sems):
     me = lax.axis_index("tensor")
     pool_me = lax.axis_index("pool")
+    my_y = me // side
+    my_x = me % side
     barrier = pltpu.get_barrier_semaphore()
-    for d in range(1, count):
-        other = lax.rem(me + d, count)
+    for s in range(1, side):
+        other = my_y * side + lax.rem(my_x + s, side)
         pl.semaphore_signal(
             barrier, 1, device_id=(pool_me, other), device_id_type=pl.DeviceIdType.MESH
         )
-    pl.semaphore_wait(barrier, count - 1)
+    pl.semaphore_wait(barrier, side - 1)
     copies = []
-    for d in range(1, count):
-        target = lax.rem(me + d, count)
-        start = pl.multiple_of(target * rows, rows)
+    for s in range(1, side):
+        target_x = lax.rem(my_x + s, side)
         copy = pltpu.make_async_remote_copy(
-            src_ref=part_ref.at[:, pl.ds(start, rows), :],
-            dst_ref=recv_ref.at[d - 1],
-            send_sem=send_sems.at[d - 1],
-            recv_sem=recv_sems.at[d - 1],
-            device_id=(pool_me, target),
+            src_ref=part_ref.at[:, pl.ds(target_x, 1)],
+            dst_ref=recv_ref.at[s - 1],
+            send_sem=send_sems.at[s - 1],
+            recv_sem=recv_sems.at[s - 1],
+            device_id=(pool_me, my_y * side + target_x),
             device_id_type=pl.DeviceIdType.MESH,
         )
         copy.start()
@@ -50,16 +51,16 @@
         copy.wait()
 
 
-def scatter_rows(partial_value, count, rows):
-    chunks, _, width = partial_value.shape
+def x_reduce_send(partial_value, side):
+    groups, _, rows, width = partial_value.shape
     return pl.pallas_call(
-        functools.partial(scatter_kernel, count, rows),
-        out_shape=jax.ShapeDtypeStruct((count - 1, chunks, rows, width), partial_value.dtype),
+        functools.partial(x_reduce_kernel, side),
+        out_shape=jax.ShapeDtypeStruct((side - 1, groups, 1, rows, width), partial_value.dtype),
         in_specs=[pl.BlockSpec(memory_space=pl.ANY)],
         out_specs=pl.BlockSpec(memory_space=pl.ANY),
         scratch_shapes=[
-            pltpu.SemaphoreType.DMA((count - 1,)),
-            pltpu.SemaphoreType.DMA((count - 1,)),
+            pltpu.SemaphoreType.DMA((side - 1,)),
+            pltpu.SemaphoreType.DMA((side - 1,)),
         ],
         compiler_params=pltpu.CompilerParams(collective_id=0, has_side_effects=True),
     )(partial_value)
@@ -137,14 +138,13 @@
         "sif,asfj->aij", hidden_column, w_quarter, preferred_element_type=jnp.float32
     )
     partial_value = partial_value.astype(jnp.bfloat16).reshape(
-        quarter, side, side, own_rows, width
+        quarter * side, side, own_rows, width
     )
 
-    total = lax.dynamic_index_in_dim(partial_value, my_x, axis=2, keepdims=False).astype(jnp.float32)
-    for s in range(1, side):
-        piece = lax.dynamic_index_in_dim(partial_value, (my_x + s) % side, axis=2, keepdims=False)
-        total = total + tensor_shift(piece, side, s, False).astype(jnp.float32)
-    total = total.astype(jnp.bfloat16)
+    received = x_reduce_send(partial_value, side)
+    total = lax.dynamic_index_in_dim(partial_value, my_x, axis=1, keepdims=False).astype(jnp.float32)
+    total = total + jnp.sum(received[:, :, 0].astype(jnp.float32), axis=0)
+    total = total.astype(jnp.bfloat16).reshape(quarter, side, own_rows, width)
 
     got = [lax.dynamic_index_in_dim(total, my_y, axis=1, keepdims=False)]
     for s in range(1, side):

time: 246 us -> 247 us (level)
  Pallas kernels: 0 us -> 26.1 us
  waiting for transfers between devices: 144 us -> 122 us
    pallas_call x0 -> x1, Pallas kernels: none -> 26.1 us  [x_reduce_send(): pl.pallas_call(functools.partial(x_reduce_kernel, side), out_shape=jax.Sh...]
    ppermute x4, waiting for transfers between devices: 25.2 us -> 4.13 us  [tensor_allsum(): x = x + lax.ppermute(x, 'tensor', perm)]
    ppermute x9 -> x6, starting transfers between devices: 30.1 us -> 26.6 us  [tensor_shift(): return lax.ppermute(x, 'tensor', perm)]
  transfers between devices with their start and end apart: 16 -> 13, of which waited for: 4 -> 4; matrix products, arithmetic and copies ran while one was open for 15% -> 15% of each run, Pallas kernels for 0% -> 11%
where the time goes in v7:
time: 247 us; the launch traced here: 246 us
  waiting for transfers between devices  122 us (49%)
  starting transfers between devices  43.3 us (18%)
  Pallas kernels  26.1 us (11%)
  matrix products  18.7 us (8%)
  local copies, waits for them, and re-layouts  16.4 us (7%)
  between operations  13.7 us (6%)
  other arithmetic  5.23 us (2%)
    all_gather x1, waiting for transfers between devices, shards(): gathered = lax.all_gather(pack, 'pool', axis=0, tiled=False)  110 us
    ppermute x6, starting transfers between devices, tensor_shift(): return lax.ppermute(x, 'tensor', perm)  26.6 us
    pallas_call x1, Pallas kernels, x_reduce_send(): pl.pallas_call(functools.partial(x_reduce_kernel, side), out_shape=jax.Sh...  26.1 us
    dot_general x1, matrix products, shards(): jnp.einsum('sif,asfj->aij', hidden_column, w_quarter, preferred_element_t...  16.9 us
    ppermute x4, starting transfers between devices, tensor_allsum(): x = x + lax.ppermute(x, 'tensor', perm)  9.49 us
    all_to_all x1, waiting for transfers between devices, shards(): lax.all_to_all(delta, 'tensor', split_axis=0, concat_axis=1, tiled=True)  7.86 us
    all_to_all x1, starting transfers between devices, shards(): lax.all_to_all(delta, 'tensor', split_axis=0, concat_axis=1, tiled=True)  5.21 us
  transfers between devices with their start and end apart: 13, of which 4 were waited for; matrix products, arithmetic and copies ran while one was open for 15% of the time, Pallas kernels for 11%

profile of v7, /device:TPU:0, one launch (start us, length us, event | category | flops | bytes accessed | tf_op | source)
XLA Modules:
  0.0 245.9 jit_solution(14401876811360419615)
XLA Ops:
  6.5 2.0 collective-permute-start
  8.5 1.1 copy.32
  9.6 0.2 reshape.138
  9.8 1.2 copy.31
  11.0 0.3 reshape.137
  11.3 0.0 collective-permute-done
  11.3 1.2 pad_maximum_fusion
  12.5 0.0 all-gather.3.cloned.1.call-update
  12.5 0.5 copy.33
  13.0 11.6 %collective-permute-start.3 = (bf16[512,896]{0,1:T(8,128)(2,1)S(1)}, bf16[512,896]{0,1:T(8,128)(2,1)}, u32[]{:S(2)}, u32[]{:S(2)}) collective-permute-start(bf16[512,896]{0,1:T(8,128)(2,1)S(1)} %copy.33), channel_id=1, source_target_pairs={{0,12},{1,13},{2,14},{3,15},{4,0},{5,1},{6,2},{7,3},{8,4},{9,5},{1... | collective-permute-start | bytes 2752520 | tf_op jit(solution)/shard_map/ppermute | solution.py:77
  24.7 10.4 %collective-permute-start.2 = (bf16[512,896]{0,1:T(8,128)(2,1)S(1)}, bf16[512,896]{0,1:T(8,128)(2,1)}, u32[]{:S(2)}, u32[]{:S(2)}) collective-permute-start(bf16[512,896]{0,1:T(8,128)(2,1)S(1)} %copy.33), channel_id=1, source_target_pairs={{0,8},{1,9},{2,10},{3,11},{4,12},{5,13},{6,14},{7,15},{8,0},{9,1},... | collective-permute-start | bytes 2752520 | tf_op jit(solution)/shard_map/ppermute | solution.py:77
  35.1 1.3 collective-permute-start.1
  36.4 0.1 select_reduce_fusion
  36.5 110.4 %all-gather.3.cloned.1.call-done = bf16[19968,512]{1,0:T(8,128)(2,1)} async-done(((bf16[1248,512]{1,0:T(8,128)(2,1)}), bf16[19968,512]{1,0:T(8,128)(2,1)}) %all-gather.3.cloned.1.call-update) | async-done | bytes 20447248 | tf_op jit(solution)/shard_map/all_gather | solution.py:114
  147.0 4.2 %slice.14 = bf16[16,224,512]{2,1,0:T(8,128)(2,1)} slice(bf16[16,1248,512]{2,1,0:T(8,128)(2,1)} %bitcast.56), slice={[0:16], [896:1120], [0:512]} | slice | bytes 7340032 | tf_op jit(solution)/shard_map/slice | solution.py:117
  151.2 2.6 %gather_fusion.1 = bf16[4,112,512]{2,1,0:T(8,128)(2,1)S(1)} fusion(bf16[32,112,512]{2,1,0:T(8,128)(2,1)} %bitcast.49, s32[1024]{0:T(1024)S(1)} %pad_clamp_fusion), kind=kCustom, calls=%fused_computation.1 | custom fusion | bytes 917520 | tf_op jit(solution)/shard_map/jit(_take)/gather | solution.py:127
  153.8 0.5 gather.18
  154.2 0.6 convolution_bitcast_fusion
  154.9 1.6 collective-permute-start.7
  156.4 0.6 fusion.30
  157.0 3.6 %collective-permute-done.7 = f32[4,128,64]{1,2,0:T(8,128)S(1)} collective-permute-done((f32[4,128,64]{1,2,0:T(8,128)S(1)}, f32[4,128,64]{1,2,0:T(8,128)S(1)}, u32[]{:S(2)}, u32[]{:S(2)}) %collective-permute-start.7) | collective-permute-done | bytes 131104 | tf_op jit(solution)/shard_map/ppermute | solution.py:20
  160.6 3.1 %collective-permute-start.8 = (f32[4,128,64]{1,2,0:T(8,128)S(1)}, f32[4,128,64]{1,2,0:T(8,128)S(1)}, u32[]{:S(2)}, u32[]{:S(2)}) collective-permute-start(f32[4,128,64]{1,2,0:T(8,128)S(1)} %add.148), channel_id=1, source_target_pairs={{0,2},{1,3},{2,0},{3,1},{4,6},{5,7},{6,4},{7,5},{8,10},{9,11},{10,... | collective-permute-start | bytes 393224 | tf_op jit(solution)/shard_map/ppermute | solution.py:20
  163.7 0.0 collective-permute-done.1
  163.7 16.9 %bitcast_convert_fusion = bf16[4,512,512]{1,2,0:T(8,128)(2,1)} fusion(bf16[4,4,1248,512]{3,2,1,0:T(8,128)(2,1)} %bitcast.57, bf16[1,512,896]{1,2,0:T(8,128)(2,1)} %bitcast.4, bf16[1,512,896]{1,2,0:T(8,128)(2,1)} %bitcast.3, bf16[1,512,896]{1,2,0:T(8,128)(2,1)} %bitcast.2, bf16[1,512,896]{1,2,0:T(8,128)(2,1)S(1)} %bitcast.60), kind=kOutput, calls=%fused_computation.18 | convolution fusion | flops 10503258112 | bytes 26214400 | tf_op jit(solution)/shard_map/sif,asfj->aij/dot_general | solution.py:137
  180.6 26.1 %shard_map.64 = bf16[3,16,1,32,512]{4,3,2,1,0:T(8,128)(2,1)} custom-call(bf16[16,4,32,512]{3,2,1,0:T(8,128)(2,1)} %bitcast.52), custom_call_target="tpu_custom_call" | custom-call | tf_op jit(solution)/shard_map/pallas_call | solution.py:56
  206.8 1.8 collective-permute-start.9
  208.5 1.8 convert_reduce_fusion
  210.3 1.1 constant_dynamic-slice_fusion
  211.4 0.5 collective-permute-done.9
  212.0 3.1 %collective-permute-start.10 = (f32[4,128,64]{1,2,0:T(8,128)S(1)}, f32[4,128,64]{1,2,0:T(8,128)S(1)}, u32[]{:S(2)}, u32[]{:S(2)}) collective-permute-start(f32[4,128,64]{1,2,0:T(8,128)S(1)} %add.150), channel_id=1, source_target_pairs={{0,8},{1,9},{2,10},{3,11},{4,12},{5,13},{6,14},{7,15},{8,0},{9,1},... | collective-permute-start | bytes 393224 | tf_op jit(solution)/shard_map/ppermute | solution.py:20
  215.1 0.2 fusion.22
  215.3 1.8 slice.15
  217.1 0.1 dynamic-slice_bitcast_fusion.3
  217.2 1.2 collective-permute-start.6
  218.4 2.1 collective-permute-start.5
  220.5 0.6 gather_fusion.2
  221.1 0.3 gather.20
  221.4 1.2 fusion.21
  222.5 5.2 %all-to-all-start = ((bf16[16,32,512]{2,1,0:T(8,128)(2,1)}), bf16[16,32,512]{2,1,0:T(8,128)(2,1)S(1)}, u32[]{:S(2)}, u32[]{:S(2)}) async-start(bf16[16,32,512]{2,1,0:T(8,128)(2,1)} %bitcast.27), calls=%async_computation | async-start | bytes 1048576 | tf_op jit(solution)/shard_map/all_to_all | solution.py:156
  227.8 0.1 pad_maximum_fusion.1
  227.9 0.6 gather_fusion
  228.5 0.1 convert_bitcast_fusion.1
  228.6 0.7 copy.37
  229.3 0.7 reshape.145
  230.0 7.9 %all-to-all-done = bf16[16,32,512]{2,1,0:T(8,128)(2,1)S(1)} async-done(((bf16[16,32,512]{2,1,0:T(8,128)(2,1)}), bf16[16,32,512]{2,1,0:T(8,128)(2,1)S(1)}, u32[]{:S(2)}, u32[]{:S(2)}) %all-to-all-start) | async-done | bytes 524320 | tf_op jit(solution)/shard_map/all_to_all | solution.py:156
  237.9 0.1 convert_bitcast_fusion
  238.0 0.1 copy.44
  238.1 0.9 fusion.25
  (26 shorter events, 0.1 us)
Async XLA Ops:
  6.5 6.0 %copy-start = (bf16[512,896]{1,0:T(8,128)(2,1)S(1)}, bf16[512,896]{1,0:T(8,128)(2,1)}, u32[]{:S(2)}) copy-start(bf16[512,896]{1,0:T(8,128)(2,1)} %param.6) | copy-start | bytes 2752516
  6.5 29.8 %copy-start.3 = (s32[4]{0:T(128)S(1)}, s32[4]{0:T(128)}, u32[]{:S(2)}) copy-start(s32[4]{0:T(128)} %param.11) | copy-start | bytes 52
  6.5 29.9 %copy-start.1 = (s32[4]{0:T(128)S(1)}, s32[4]{0:T(128)}, u32[]{:S(2)}) copy-start(s32[4]{0:T(128)} %param.10) | copy-start | bytes 52
  6.5 140.4 %all-gather.3.cloned.1.call-start = ((), (), s32[]{:S(2)}) async-start(), calls=%async_computation.1 | async-start | bytes 21725184 | tf_op jit(solution)/shard_map/all_gather | solution.py:114
  6.5 4.8 %collective-permute-start = (bf16[896,512]{1,0:T(8,128)(2,1)}, bf16[896,512]{1,0:T(8,128)(2,1)S(1)}, u32[]{:S(2)}, u32[]{:S(2)}) collective-permute-start(bf16[896,512]{1,0:T(8,128)(2,1)} %param.7), channel_id=1, source_target_pairs={{0,0},{1,1},{2,2},{3,3},{4,48},{5,49},{6,50},{7,51},{8,32},{9,33},... | collective-permute-start | bytes 2752520 | tf_op jit(solution)/shard_map/ppermute | solution.py:102
  13.0 150.6 %collective-permute-start.3 = (bf16[512,896]{0,1:T(8,128)(2,1)S(1)}, bf16[512,896]{0,1:T(8,128)(2,1)}, u32[]{:S(2)}, u32[]{:S(2)}) collective-permute-start(bf16[512,896]{0,1:T(8,128)(2,1)S(1)} %copy.33), channel_id=1, source_target_pairs={{0,12},{1,13},{2,14},{3,15},{4,0},{5,1},{6,2},{7,3},{8,4},{9,5},{1... | collective-permute-start | bytes 2752520 | tf_op jit(solution)/shard_map/ppermute | solution.py:77
  24.7 139.0 %collective-permute-start.2 = (bf16[512,896]{0,1:T(8,128)(2,1)S(1)}, bf16[512,896]{0,1:T(8,128)(2,1)}, u32[]{:S(2)}, u32[]{:S(2)}) collective-permute-start(bf16[512,896]{0,1:T(8,128)(2,1)S(1)} %copy.33), channel_id=1, source_target_pairs={{0,8},{1,9},{2,10},{3,11},{4,12},{5,13},{6,14},{7,15},{8,0},{9,1},... | collective-permute-start | bytes 2752520 | tf_op jit(solution)/shard_map/ppermute | solution.py:77
  35.1 128.6 %collective-permute-start.1 = (bf16[512,896]{0,1:T(8,128)(2,1)S(1)}, bf16[512,896]{0,1:T(8,128)(2,1)}, u32[]{:S(2)}, u32[]{:S(2)}) collective-permute-start(bf16[512,896]{0,1:T(8,128)(2,1)S(1)} %copy.33), channel_id=1, source_target_pairs={{0,4},{1,5},{2,6},{3,7},{4,8},{5,9},{6,10},{7,11},{8,12},{9,13},{1... | collective-permute-start | bytes 2752520 | tf_op jit(solution)/shard_map/ppermute | solution.py:77
  154.9 5.7 %collective-permute-start.7 = (f32[4,128,64]{1,2,0:T(8,128)S(1)}, f32[4,128,64]{1,2,0:T(8,128)S(1)}, u32[]{:S(2)}, u32[]{:S(2)}) collective-permute-start(f32[4,128,64]{1,2,0:T(8,128)S(1)} %convolution_bitcast_fusion), channel_id=1, source_target_pairs={{0,1},{1,0},{2,3},{3,2},{4,5},{5,4},{6,7},{7,6},{8,9},{9,8},{10,11... | collective-permute-start | bytes 393224 | tf_op jit(solution)/shard_map/ppermute | solution.py:20
  160.6 46.1 %collective-permute-start.8 = (f32[4,128,64]{1,2,0:T(8,128)S(1)}, f32[4,128,64]{1,2,0:T(8,128)S(1)}, u32[]{:S(2)}, u32[]{:S(2)}) collective-permute-start(f32[4,128,64]{1,2,0:T(8,128)S(1)} %add.148), channel_id=1, source_target_pairs={{0,2},{1,3},{2,0},{3,1},{4,6},{5,7},{6,4},{7,5},{8,10},{9,11},{10,... | collective-permute-start | bytes 393224 | tf_op jit(solution)/shard_map/ppermute | solution.py:20
  206.8 5.2 %collective-permute-start.9 = (f32[4,128,64]{1,2,0:T(8,128)S(1)}, f32[4,128,64]{1,2,0:T(8,128)S(1)}, u32[]{:S(2)}, u32[]{:S(2)}) collective-permute-start(f32[4,128,64]{1,2,0:T(8,128)S(1)} %add.149), channel_id=1, source_target_pairs={{0,4},{1,5},{2,6},{3,7},{4,0},{5,1},{6,2},{7,3},{8,12},{9,13},{10,... | collective-permute-start | bytes 393224 | tf_op jit(solution)/shard_map/ppermute | solution.py:20
  212.0 9.3 %collective-permute-start.10 = (f32[4,128,64]{1,2,0:T(8,128)S(1)}, f32[4,128,64]{1,2,0:T(8,128)S(1)}, u32[]{:S(2)}, u32[]{:S(2)}) collective-permute-start(f32[4,128,64]{1,2,0:T(8,128)S(1)} %add.150), channel_id=1, source_target_pairs={{0,8},{1,9},{2,10},{3,11},{4,12},{5,13},{6,14},{7,15},{8,0},{9,1},... | collective-permute-start | bytes 393224 | tf_op jit(solution)/shard_map/ppermute | solution.py:20
  217.2 10.6 %collective-permute-start.6 = (bf16[4,32,512]{2,1,0:T(8,128)(2,1)S(1)}, bf16[4,32,512]{2,1,0:T(8,128)(2,1)S(1)}, u32[]{:S(2)}, u32[]{:S(2)}) collective-permute-start(bf16[4,32,512]{2,1,0:T(8,128)(2,1)S(1)} %get-tuple-element.6), channel_id=1, source_target_pairs={{0,12},{1,13},{2,14},{3,15},{4,0},{5,1},{6,2},{7,3},{8,4},{9,5},{1... | collective-permute-start | bytes 393224 | tf_op jit(solution)/shard_map/ppermute | solution.py:77
  218.4 9.4 %collective-permute-start.5 = (bf16[4,32,512]{2,1,0:T(8,128)(2,1)S(1)}, bf16[4,32,512]{2,1,0:T(8,128)(2,1)S(1)}, u32[]{:S(2)}, u32[]{:S(2)}) collective-permute-start(bf16[4,32,512]{2,1,0:T(8,128)(2,1)S(1)} %get-tuple-element.7), channel_id=1, source_target_pairs={{0,8},{1,9},{2,10},{3,11},{4,12},{5,13},{6,14},{7,15},{8,0},{9,1},... | collective-permute-start | bytes 393224 | tf_op jit(solution)/shard_map/ppermute | solution.py:77
  220.5 7.3 %collective-permute-start.4 = (bf16[4,32,512]{2,1,0:T(8,128)(2,1)S(1)}, bf16[4,32,512]{2,1,0:T(8,128)(2,1)S(1)}, u32[]{:S(2)}, u32[]{:S(2)}) collective-permute-start(bf16[4,32,512]{2,1,0:T(8,128)(2,1)S(1)} %get-tuple-element.8), channel_id=1, source_target_pairs={{0,4},{1,5},{2,6},{3,7},{4,8},{5,9},{6,10},{7,11},{8,12},{9,13},{1... | collective-permute-start | bytes 393224 | tf_op jit(solution)/shard_map/ppermute | solution.py:77
  222.5 15.4 %all-to-all-start = ((bf16[16,32,512]{2,1,0:T(8,128)(2,1)}), bf16[16,32,512]{2,1,0:T(8,128)(2,1)S(1)}, u32[]{:S(2)}, u32[]{:S(2)}) async-start(bf16[16,32,512]{2,1,0:T(8,128)(2,1)} %bitcast.27), calls=%async_computation | async-start | bytes 1048576 | tf_op jit(solution)/shard_map/all_to_all | solution.py:156
  227.9 10.2 %copy-start.2 = (pred[32]{0:T(512)(128)(4,1)S(1)}, pred[32]{0:T(512)(128)(4,1)}, u32[]{:S(2)}) copy-start(pred[32]{0:T(512)(128)(4,1)} %fusion.30) | copy-start | bytes 100
Sparse Core Ops, SparseCore 0:
  12.6 134.3 all-gather.2

commit v8 on v7

v8 whole, which is shorter than its diff:
```python
import functools

import jax
import jax.numpy as jnp
from jax import lax
from jax.experimental import pallas as pl
from jax.experimental.pallas import tpu as pltpu
from jax.sharding import PartitionSpec as P

BLOCK = 128


adapter_scale_factor = 0.5


def tensor_shift(x, side, step, along_y):
    perm = []
    for yy in range(side):
        for xx in range(side):
            if along_y:
                perm.append((yy * side + xx, ((yy + step) % side) * side + xx))
            else:
                perm.append((yy * side + xx, yy * side + (xx + step) % side))
    return lax.ppermute(x, "tensor", perm)


def tensor_allsum(x, side):
    for along_y in (False, True):
        x = x + sum(tensor_shift(x, side, s, along_y) for s in range(1, side))
    return x


def y_reduce_kernel(side, part_ref, recv_ref, send_sems, recv_sems):
    me = lax.axis_index("tensor")
    pool_me = lax.axis_index("pool")
    my_y = me // side
    my_x = me % side
    barrier = pltpu.get_barrier_semaphore()
    for s in range(1, side):
        other = lax.rem(my_y + s, side) * side + my_x
        pl.semaphore_signal(
            barrier, 1, device_id=(pool_me, other), device_id_type=pl.DeviceIdType.MESH
        )
    pl.semaphore_wait(barrier, side - 1)
    copies = []
    for s in range(1, side):
        target_y = lax.rem(my_y + s, side)
        copy = pltpu.make_async_remote_copy(
            src_ref=part_ref.at[:, pl.ds(target_y, 1)],
            dst_ref=recv_ref.at[s - 1],
            send_sem=send_sems.at[s - 1],
            recv_sem=recv_sems.at[s - 1],
            device_id=(pool_me, target_y * side + my_x),
            device_id_type=pl.DeviceIdType.MESH,
        )
        copy.start()
        copies.append(copy)
    for copy in copies:
        copy.wait()


def y_reduce_send(partial_value, side):
    groups, _, rows, width = partial_value.shape
    return pl.pallas_call(
        functools.partial(y_reduce_kernel, side),
        out_shape=jax.ShapeDtypeStruct((side - 1, groups, 1, rows, width), partial_value.dtype),
        in_specs=[pl.BlockSpec(memory_space=pl.ANY)],
        out_specs=pl.BlockSpec(memory_space=pl.ANY),
        scratch_shapes=[
            pltpu.SemaphoreType.DMA((side - 1,)),
            pltpu.SemaphoreType.DMA((side - 1,)),
        ],
        compiler_params=pltpu.CompilerParams(collective_id=0, has_side_effects=True),
    )(partial_value)


def shards(hidden, down_weight, adapter_shrink, adapter_expand, block_adapter, block_rows):
    input_rows, feat = hidden.shape
    block_count = block_adapter.shape[0]
    pool_count = lax.axis_size("pool")
    tensor_pos = lax.axis_index("tensor")
    tensor_count = lax.axis_size("tensor")
    side = 4
    quarter = pool_count // side
    my_y = tensor_pos // side
    my_x = tensor_pos % side
    own_rows = input_rows // tensor_count
    held, _, rank = adapter_shrink.shape
    column_span = adapter_expand.shape[1]
    width = down_weight.shape[1]

    pairs = []
    for p1 in range(pool_count):
        for y1 in range(side):
            for x1 in range(side):
                x2 = p1 % side
                p2 = (p1 // side) * side + (x2 - x1) % side
                pairs.append((p1 * tensor_count + y1 * side + x1, p2 * tensor_count + y1 * side + x2))
    moved = lax.ppermute(down_weight, ("pool", "tensor"), pairs)

    shrink_rows = held * feat * rank // width
    expand_rows = held * column_span * rank // width
    pack = jnp.concatenate(
        [
            moved,
            adapter_shrink.reshape(shrink_rows, width),
            adapter_expand.reshape(expand_rows, width),
        ],
        axis=0,
    )
    gathered = lax.all_gather(pack, "pool", axis=0, tiled=False)
    plane_rows = gathered.shape[1]
    w_quarter = gathered.reshape(quarter, side, plane_rows, width)
    shrink_all = gathered[:, feat:feat + shrink_rows, :].reshape(
        pool_count * held, shrink_rows // held, width
    )
    expand_all = gathered[:, feat + shrink_rows:, :].reshape(
        pool_count * held, expand_rows // held, width
    )

    pieces = [hidden] + [tensor_shift(hidden, side, s, False) for s in range(1, side)]
    hidden_column = jnp.pad(jnp.stack(pieces, axis=0), ((0, 0), (0, 0), (0, plane_rows - feat)))

    first = jnp.take(shrink_all, block_adapter, axis=0).reshape(block_count, feat, rank)
    second = jnp.take(expand_all, block_adapter, axis=0).reshape(block_count, column_span, rank)
    blocks = hidden.reshape(block_count, BLOCK, feat)
    shrink = jnp.einsum("bnf,bfr->bnr", blocks, first, preferred_element_type=jnp.float32)
    summed_shrink = tensor_allsum(shrink, side).astype(jnp.bfloat16)
    enlarged_rows = jnp.einsum(
        "bnr,bcr->bnc", summed_shrink, second, preferred_element_type=jnp.float32
    )
    delta = (adapter_scale_factor * enlarged_rows).astype(jnp.bfloat16).reshape(input_rows, column_span)

    partial_value = jnp.einsum(
        "sif,asfj->aij", hidden_column, w_quarter, preferred_element_type=jnp.float32
    )
    chunk_ids = jnp.arange(quarter, dtype=jnp.int32)[:, None, None]
    partial_value = partial_value + jnp.where(
        chunk_ids == my_y, delta.astype(jnp.float32)[None, :, :], 0.0
    )
    partial_value = partial_value.astype(jnp.bfloat16).reshape(
        quarter, side, side, own_rows, width
    )
    partial_value = jnp.transpose(partial_value, (0, 2, 1, 3, 4)).reshape(
        quarter * side, side, own_rows, width
    )

    received = y_reduce_send(partial_value, side)
    total = lax.dynamic_index_in_dim(partial_value, my_y, axis=1, keepdims=False).astype(jnp.float32)
    total = total + jnp.sum(received[:, :, 0].astype(jnp.float32), axis=0)
    total = total.astype(jnp.bfloat16).reshape(quarter, side, own_rows, width)

    got = [lax.dynamic_index_in_dim(total, my_x, axis=1, keepdims=False)]
    for s in range(1, side):
        piece = lax.dynamic_index_in_dim(total, (my_x + s) % side, axis=1, keepdims=False)
        got.append(tensor_shift(piece, side, s, False))
    order = (my_x - jnp.arange(side, dtype=jnp.int32)) % side
    result = jnp.take(jnp.stack(got, axis=0), order, axis=0)
    result = jnp.transpose(result, (2, 1, 0, 3)).reshape(own_rows, pool_count * width)

    row_ids = tensor_pos * own_rows + jnp.arange(own_rows, dtype=jnp.int32)
    owning = (row_ids // BLOCK)[:, None] == jnp.arange(block_count, dtype=jnp.int32)[None, :]
    lengths = jnp.sum(jnp.where(owning, block_rows[None, :], 0), axis=1)
    valid = row_ids % BLOCK < lengths
    return jnp.where(valid[:, None], result, jnp.zeros_like(result))


def solution(mesh):
    in_specs = (
        P("pool", "tensor"),
        P("tensor", "pool"),
        P("pool", "tensor", None),
        P("pool", "tensor", None),
        P("pool"),
        P("pool"),
    )
    out_specs = P(("pool", "tensor"), None)
    return jax.shard_map(shards, mesh=mesh, in_specs=in_specs, out_specs=out_specs, check_vma=False)
```

time: 247 us -> 276 us (1.12)
  waiting for transfers between devices: 122 us -> 169 us
  starting transfers between devices: 43.3 us -> 21.3 us
    ppermute x6 -> x12, waiting for transfers between devices: 0.02 us -> 34.7 us  [tensor_shift(): return lax.ppermute(x, 'tensor', perm)]
    all_gather x1, waiting for transfers between devices: 110 us -> 134 us  [shards(): gathered = lax.all_gather(pack, 'pool', axis=0, tiled=False)]
    ppermute x4 -> x0, starting transfers between devices: 9.49 us -> none  [tensor_allsum(): x = x + lax.ppermute(x, 'tensor', perm)]
    all_to_all x1 -> x0, waiting for transfers between devices: 7.86 us -> none  [shards(): lax.all_to_all(delta, 'tensor', split_axis=0, concat_axis=1, tiled=True)]
    ppermute x6 -> x12, starting transfers between devices: 26.6 us -> 19.3 us  [tensor_shift(): return lax.ppermute(x, 'tensor', perm)]
    all_to_all x1 -> x0, starting transfers between devices: 5.21 us -> none  [shards(): lax.all_to_all(delta, 'tensor', split_axis=0, concat_axis=1, tiled=True)]
    ppermute x4 -> x0, waiting for transfers between devices: 4.13 us -> none  [tensor_allsum(): x = x + lax.ppermute(x, 'tensor', perm)]
  transfers between devices with their start and end apart: 13 -> 14, of which waited for: 4 -> 9; matrix products, arithmetic and copies ran while one was open for 15% -> 3% of each run, Pallas kernels for 11% -> 0%
where the time goes in v8:
time: 276 us; the launch traced here: 274 us
  waiting for transfers between devices  169 us (61%)
  Pallas kernels  27.1 us (10%)
  starting transfers between devices  21.3 us (8%)
  matrix products  20.7 us (8%)
  local copies, waits for them, and re-layouts  17.2 us (6%)
  between operations  13.7 us (5%)
  other arithmetic  5.1 us (2%)
    all_gather x1, waiting for transfers between devices, shards(): gathered = lax.all_gather(pack, 'pool', axis=0, tiled=False)  134 us
    ppermute x12, waiting for transfers between devices, tensor_shift(): return lax.ppermute(x, 'tensor', perm)  34.7 us
    pallas_call x1, Pallas kernels, y_reduce_send(): pl.pallas_call(functools.partial(y_reduce_kernel, side), out_shape=jax.Sh...  27.1 us
    ppermute x12, starting transfers between devices, tensor_shift(): return lax.ppermute(x, 'tensor', perm)  19.3 us
    dot_general x1, matrix products, shards(): jnp.einsum('sif,asfj->aij', hidden_column, w_quarter, preferred_element_t...  18.8 us
  transfers between devices with their start and end apart: 14, of which 9 were waited for; matrix products, arithmetic and copies ran while one was open for 3% of the time, Pallas kernels for 0%

profile of v8, /device:TPU:0, one launch (start us, length us, event | category | flops | bytes accessed | tf_op | source)
XLA Modules:
  0.0 274.3 jit_solution(877050461721787167)
XLA Ops:
  6.5 2.0 collective-permute-start
  8.5 1.2 copy.31
  9.7 0.3 reshape.146
  10.0 1.1 copy.32
  11.1 0.2 reshape.147
  11.3 1.2 pad_maximum_fusion
  12.5 134.5 %all-gather.3.cloned.1.call-done = bf16[19968,512]{1,0:T(8,128)(2,1)} async-done(((bf16[1248,512]{1,0:T(8,128)(2,1)}), bf16[19968,512]{1,0:T(8,128)(2,1)}) %all-gather.3.cloned.1.call-update) | async-done | bytes 20447248 | tf_op jit(solution)/shard_map/all_gather | solution.py:111
  147.0 4.3 %slice.14 = bf16[16,224,512]{2,1,0:T(8,128)(2,1)} slice(bf16[16,1248,512]{2,1,0:T(8,128)(2,1)} %bitcast.59), slice={[0:16], [896:1120], [0:512]} | slice | bytes 7340032 | tf_op jit(solution)/shard_map/slice | solution.py:114
  151.3 2.6 gather_fusion
  153.9 0.5 gather.17
  154.4 0.6 convolution_bitcast_fusion
  155.0 1.5 collective-permute-start.4
  156.6 2.7 collective-permute-start.5
  159.3 1.5 collective-permute-start.6
  160.7 0.5 copy.33
  161.3 0.6 collective-permute-start.1
  161.9 0.9 collective-permute-start.2
  162.8 1.9 collective-permute-start.3
  164.7 1.7 collective-permute-done.5
  166.4 1.6 collective-permute-start.7
  168.1 2.7 %collective-permute-start.8 = (f32[4,128,64]{1,2,0:T(8,128)S(1)}, f32[4,128,64]{1,2,0:T(8,128)}, u32[]{:S(2)}, u32[]{:S(2)}) collective-permute-start(f32[4,128,64]{1,2,0:T(8,128)S(1)} %add_add_fusion), channel_id=1, source_target_pairs={{0,8},{1,9},{2,10},{3,11},{4,12},{5,13},{6,14},{7,15},{8,0},{9,1},... | collective-permute-start | bytes 393224 | tf_op jit(solution)/shard_map/ppermute | solution.py:24
  170.8 3.2 %collective-permute-done.7 = f32[4,128,64]{1,2,0:T(8,128)S(1)} collective-permute-done((f32[4,128,64]{1,2,0:T(8,128)S(1)}, f32[4,128,64]{1,2,0:T(8,128)S(1)}, u32[]{:S(2)}, u32[]{:S(2)}) %collective-permute-start.7) | collective-permute-done | bytes 131104 | tf_op jit(solution)/shard_map/ppermute | solution.py:24
  174.1 0.8 collective-permute-start.9
  174.9 0.5 iota_compare_fusion.2
  175.4 1.7 slice.15
  177.2 0.6 gather_fusion.1
  177.7 0.3 gather.19
  178.0 1.1 collective-permute-done.9
  179.1 1.3 fusion.22
  180.5 0.1 bitcast_convert_fusion
  180.7 5.5 %collective-permute-done.1 = bf16[512,896]{0,1:T(8,128)(2,1)} collective-permute-done((bf16[512,896]{0,1:T(8,128)(2,1)S(1)}, bf16[512,896]{0,1:T(8,128)(2,1)}, u32[]{:S(2)}, u32[]{:S(2)}) %collective-permute-start.1) | collective-permute-done | bytes 917536 | tf_op jit(solution)/shard_map/ppermute | solution.py:24
  186.1 19.0 %collective-permute-done.2 = bf16[512,896]{0,1:T(8,128)(2,1)} collective-permute-done((bf16[512,896]{0,1:T(8,128)(2,1)S(1)}, bf16[512,896]{0,1:T(8,128)(2,1)}, u32[]{:S(2)}, u32[]{:S(2)}) %collective-permute-start.2) | collective-permute-done | bytes 917536 | tf_op jit(solution)/shard_map/ppermute | solution.py:24
  205.1 18.8 %fusion.18 = bf16[4,512,512]{2,1,0:T(8,128)(2,1)S(1)} fusion(bf16[4,4,1248,512]{3,2,1,0:T(8,128)(2,1)} %bitcast.61, bf16[1,512,896]{1,2,0:T(8,128)(2,1)} %bitcast.4, bf16[1,512,896]{1,2,0:T(8,128)(2,1)} %bitcast.3, bf16[1,512,896]{1,2,0:T(8,128)(2,1)} %bitcast.2, bf16[1,512,896]{1,2,0:T(8,128)(2,1)S(1)} %bitcast.63, ...), kind=kOutput, calls=%fused_computation.19 | convolution fusion | flops 10505355264 | bytes 27262980 | tf_op jit(solution)/shard_map/sif,asfj->aij/dot_general | solution.py:134
  223.9 1.5 copy.39
  225.4 27.1 %shard_map.64 = bf16[3,16,1,32,512]{4,3,2,1,0:T(8,128)(2,1)} custom-call(bf16[16,4,32,512]{3,2,1,0:T(8,128)(2,1)} %bitcast.52), custom_call_target="tpu_custom_call" | custom-call | tf_op jit(solution)/shard_map/pallas_call | solution.py:64
  252.4 1.8 convert_reduce_fusion
  254.3 1.1 constant_dynamic-slice_fusion
  255.4 0.2 fusion.23
  255.6 1.3 collective-permute-start.10
  256.9 2.9 %collective-permute-start.11 = (bf16[4,32,512]{2,1,0:T(8,128)(2,1)S(1)}, bf16[4,32,512]{2,1,0:T(8,128)(2,1)S(1)}, u32[]{:S(2)}, u32[]{:S(2)}) collective-permute-start(bf16[4,32,512]{2,1,0:T(8,128)(2,1)S(1)} %get-tuple-element.7), channel_id=1, source_target_pairs={{0,2},{1,3},{2,0},{3,1},{4,6},{5,7},{6,4},{7,5},{8,10},{9,11},{10,... | collective-permute-start | bytes 393224 | tf_op jit(solution)/shard_map/ppermute | solution.py:24
  259.8 1.0 collective-permute-start.12
  260.8 2.5 collective-permute-done.10
  263.3 1.6 collective-permute-done.11
  265.0 0.6 gather_fusion.2
  265.6 0.1 select_bitcast_fusion
  265.7 0.4 copy.40
  266.1 0.4 reshape.154
  266.5 0.9 broadcast_select_fusion
  (25 shorter events, 0.4 us)
Async XLA Ops:
  6.5 6.0 %copy-start.1 = (s32[4]{0:T(128)S(1)}, s32[4]{0:T(128)}, u32[]{:S(2)}) copy-start(s32[4]{0:T(128)} %param.10) | copy-start | bytes 52
  6.5 140.5 %all-gather.3.cloned.1.call-start = ((), (), s32[]{:S(2)}) async-start(), calls=%async_computation | async-start | bytes 21725184 | tf_op jit(solution)/shard_map/all_gather | solution.py:111
  6.5 4.8 %collective-permute-start = (bf16[896,512]{1,0:T(8,128)(2,1)}, bf16[896,512]{1,0:T(8,128)(2,1)S(1)}, u32[]{:S(2)}, u32[]{:S(2)}) collective-permute-start(bf16[896,512]{1,0:T(8,128)(2,1)} %param.7), channel_id=1, source_target_pairs={{0,0},{1,48},{2,32},{3,16},{4,4},{5,52},{6,36},{7,20},{8,8},{9,56}... | collective-permute-start | bytes 2752520 | tf_op jit(solution)/shard_map/ppermute | solution.py:99
  147.0 7.4 %copy-start = (bf16[512,896]{1,0:T(8,128)(2,1)S(1)}, bf16[512,896]{1,0:T(8,128)(2,1)}, u32[]{:S(2)}) copy-start(bf16[512,896]{1,0:T(8,128)(2,1)} %param.6) | copy-start | bytes 2752516
  151.3 16.7 %copy-start.2 = (s32[4]{0:T(128)S(1)}, s32[4]{0:T(128)}, u32[]{:S(2)}) copy-start(s32[4]{0:T(128)} %param.11) | copy-start | bytes 52
  155.0 7.8 %collective-permute-start.4 = (f32[4,128,64]{1,2,0:T(8,128)S(1)}, f32[4,128,64]{1,2,0:T(8,128)S(1)}, u32[]{:S(2)}, u32[]{:S(2)}) collective-permute-start(f32[4,128,64]{1,2,0:T(8,128)S(1)} %convolution_bitcast_fusion), channel_id=1, source_target_pairs={{0,1},{1,2},{2,3},{3,0},{4,5},{5,6},{6,7},{7,4},{8,9},{9,10},{10,1... | collective-permute-start | bytes 393224 | tf_op jit(solution)/shard_map/ppermute | solution.py:24
  156.6 9.8 %collective-permute-start.5 = (f32[4,128,64]{1,2,0:T(8,128)S(1)}, f32[4,128,64]{1,2,0:T(8,128)S(1)}, u32[]{:S(2)}, u32[]{:S(2)}) collective-permute-start(f32[4,128,64]{1,2,0:T(8,128)S(1)} %convolution_bitcast_fusion), channel_id=1, source_target_pairs={{0,2},{1,3},{2,0},{3,1},{4,6},{5,7},{6,4},{7,5},{8,10},{9,11},{10,... | collective-permute-start | bytes 393224 | tf_op jit(solution)/shard_map/ppermute | solution.py:24
  159.3 7.1 %collective-permute-start.6 = (f32[4,128,64]{1,2,0:T(8,128)S(1)}, f32[4,128,64]{1,2,0:T(8,128)S(1)}, u32[]{:S(2)}, u32[]{:S(2)}) collective-permute-start(f32[4,128,64]{1,2,0:T(8,128)S(1)} %convolution_bitcast_fusion), channel_id=1, source_target_pairs={{0,3},{1,0},{2,1},{3,2},{4,7},{5,4},{6,5},{7,6},{8,11},{9,8},{10,9... | collective-permute-start | bytes 393224 | tf_op jit(solution)/shard_map/ppermute | solution.py:24
  161.3 24.9 %collective-permute-start.1 = (bf16[512,896]{0,1:T(8,128)(2,1)S(1)}, bf16[512,896]{0,1:T(8,128)(2,1)}, u32[]{:S(2)}, u32[]{:S(2)}) collective-permute-start(bf16[512,896]{0,1:T(8,128)(2,1)S(1)} %copy.33), channel_id=1, source_target_pairs={{0,1},{1,2},{2,3},{3,0},{4,5},{5,6},{6,7},{7,4},{8,9},{9,10},{10,1... | collective-permute-start | bytes 2752520 | tf_op jit(solution)/shard_map/ppermute | solution.py:24
  161.9 43.2 %collective-permute-start.2 = (bf16[512,896]{0,1:T(8,128)(2,1)S(1)}, bf16[512,896]{0,1:T(8,128)(2,1)}, u32[]{:S(2)}, u32[]{:S(2)}) collective-permute-start(bf16[512,896]{0,1:T(8,128)(2,1)S(1)} %copy.33), channel_id=1, source_target_pairs={{0,2},{1,3},{2,0},{3,1},{4,6},{5,7},{6,4},{7,5},{8,10},{9,11},{10,... | collective-permute-start | bytes 2752520 | tf_op jit(solution)/shard_map/ppermute | solution.py:24
  162.8 42.3 %collective-permute-start.3 = (bf16[512,896]{0,1:T(8,128)(2,1)S(1)}, bf16[512,896]{0,1:T(8,128)(2,1)}, u32[]{:S(2)}, u32[]{:S(2)}) collective-permute-start(bf16[512,896]{0,1:T(8,128)(2,1)S(1)} %copy.33), channel_id=1, source_target_pairs={{0,3},{1,0},{2,1},{3,2},{4,7},{5,4},{6,5},{7,6},{8,11},{9,8},{10,9... | collective-permute-start | bytes 2752520 | tf_op jit(solution)/shard_map/ppermute | solution.py:24
  166.4 7.7 %collective-permute-start.7 = (f32[4,128,64]{1,2,0:T(8,128)S(1)}, f32[4,128,64]{1,2,0:T(8,128)S(1)}, u32[]{:S(2)}, u32[]{:S(2)}) collective-permute-start(f32[4,128,64]{1,2,0:T(8,128)S(1)} %add_add_fusion), channel_id=1, source_target_pairs={{0,4},{1,5},{2,6},{3,7},{4,8},{5,9},{6,10},{7,11},{8,12},{9,13},{1... | collective-permute-start | bytes 393224 | tf_op jit(solution)/shard_map/ppermute | solution.py:24
  168.1 9.9 %collective-permute-start.8 = (f32[4,128,64]{1,2,0:T(8,128)S(1)}, f32[4,128,64]{1,2,0:T(8,128)}, u32[]{:S(2)}, u32[]{:S(2)}) collective-permute-start(f32[4,128,64]{1,2,0:T(8,128)S(1)} %add_add_fusion), channel_id=1, source_target_pairs={{0,8},{1,9},{2,10},{3,11},{4,12},{5,13},{6,14},{7,15},{8,0},{9,1},... | collective-permute-start | bytes 393224 | tf_op jit(solution)/shard_map/ppermute | solution.py:24
  174.1 5.1 %collective-permute-start.9 = (f32[4,128,64]{1,2,0:T(8,128)S(1)}, f32[4,128,64]{1,2,0:T(8,128)}, u32[]{:S(2)}, u32[]{:S(2)}) collective-permute-start(f32[4,128,64]{1,2,0:T(8,128)S(1)} %add_add_fusion), channel_id=1, source_target_pairs={{0,12},{1,13},{2,14},{3,15},{4,0},{5,1},{6,2},{7,3},{8,4},{9,5},{1... | collective-permute-start | bytes 393224 | tf_op jit(solution)/shard_map/ppermute | solution.py:24
  255.6 7.7 %collective-permute-start.10 = (bf16[4,32,512]{2,1,0:T(8,128)(2,1)S(1)}, bf16[4,32,512]{2,1,0:T(8,128)(2,1)S(1)}, u32[]{:S(2)}, u32[]{:S(2)}) collective-permute-start(bf16[4,32,512]{2,1,0:T(8,128)(2,1)S(1)} %get-tuple-element.8), channel_id=1, source_target_pairs={{0,1},{1,2},{2,3},{3,0},{4,5},{5,6},{6,7},{7,4},{8,9},{9,10},{10,1... | collective-permute-start | bytes 393224 | tf_op jit(solution)/shard_map/ppermute | solution.py:24
  256.9 7.9 %collective-permute-start.11 = (bf16[4,32,512]{2,1,0:T(8,128)(2,1)S(1)}, bf16[4,32,512]{2,1,0:T(8,128)(2,1)S(1)}, u32[]{:S(2)}, u32[]{:S(2)}) collective-permute-start(bf16[4,32,512]{2,1,0:T(8,128)(2,1)S(1)} %get-tuple-element.7), channel_id=1, source_target_pairs={{0,2},{1,3},{2,0},{3,1},{4,6},{5,7},{6,4},{7,5},{8,10},{9,11},{10,... | collective-permute-start | bytes 393224 | tf_op jit(solution)/shard_map/ppermute | solution.py:24
  259.8 5.1 %collective-permute-start.12 = (bf16[4,32,512]{2,1,0:T(8,128)(2,1)S(1)}, bf16[4,32,512]{2,1,0:T(8,128)(2,1)S(1)}, u32[]{:S(2)}, u32[]{:S(2)}) collective-permute-start(bf16[4,32,512]{2,1,0:T(8,128)(2,1)S(1)} %get-tuple-element.6), channel_id=1, source_target_pairs={{0,3},{1,0},{2,1},{3,2},{4,7},{5,4},{6,5},{7,6},{8,11},{9,8},{10,9... | collective-permute-start | bytes 393224 | tf_op jit(solution)/shard_map/ppermute | solution.py:24
Sparse Core Ops, SparseCore 0:
  12.6 134.3 all-gather.2

commit v9 on v8

--- a/solution.py
+++ b/solution.py
@@ -108,6 +108,8 @@
         ],
         axis=0,
     )
+    pieces = [hidden] + [tensor_shift(hidden, side, s, False) for s in range(1, side)]
+    pack, pieces = lax.optimization_barrier((pack, pieces))
     gathered = lax.all_gather(pack, "pool", axis=0, tiled=False)
     plane_rows = gathered.shape[1]
     w_quarter = gathered.reshape(quarter, side, plane_rows, width)
@@ -118,7 +120,6 @@
         pool_count * held, expand_rows // held, width
     )
 
-    pieces = [hidden] + [tensor_shift(hidden, side, s, False) for s in range(1, side)]
     hidden_column = jnp.pad(jnp.stack(pieces, axis=0), ((0, 0), (0, 0), (0, plane_rows - feat)))
 
     first = jnp.take(shrink_all, block_adapter, axis=0).reshape(block_count, feat, rank)

time: 276 us -> 291 us (1.054)
  waiting for transfers between devices: 169 us -> 180 us
    ppermute x12, waiting for transfers between devices: 34.7 us -> 51.8 us  [tensor_shift(): return lax.ppermute(x, 'tensor', perm)]
    all_gather x1, waiting for transfers between devices: 134 us -> 129 us  [shards(): gathered = lax.all_gather(pack, 'pool', axis=0, tiled=False)]
where the time goes in v9:
time: 291 us; the launch traced here: 289 us
  waiting for transfers between devices  180 us (62%)
  Pallas kernels  26.6 us (9%)
  starting transfers between devices  23.9 us (8%)
  matrix products  20.7 us (7%)
  local copies, waits for them, and re-layouts  18.7 us (6%)
  between operations  13.7 us (5%)
  other arithmetic  5.11 us (2%)
    all_gather x1, waiting for transfers between devices, shards(): gathered = lax.all_gather(pack, 'pool', axis=0, tiled=False)  129 us
    ppermute x12, waiting for transfers between devices, tensor_shift(): return lax.ppermute(x, 'tensor', perm)  51.8 us
    pallas_call x1, Pallas kernels, y_reduce_send(): pl.pallas_call(functools.partial(y_reduce_kernel, side), out_shape=jax.Sh...  26.6 us
    ppermute x12, starting transfers between devices, tensor_shift(): return lax.ppermute(x, 'tensor', perm)  21.9 us
    dot_general x1, matrix products, shards(): jnp.einsum('sif,asfj->aij', hidden_column, w_quarter, preferred_element_t...  18.8 us
  transfers between devices with their start and end apart: 14, of which 9 were waited for; matrix products, arithmetic and copies ran while one was open for 3% of the time, Pallas kernels for 0%

profile of v9, /device:TPU:0, one launch (start us, length us, event | category | flops | bytes accessed | tf_op | source)
XLA Modules:
  0.0 289.1 jit_solution(13583500572416550186)
XLA Ops:
  6.5 2.0 collective-permute-start
  8.5 1.5 copy.33
  10.0 1.2 collective-permute-start.1
  11.2 2.2 collective-permute-start.2
  13.4 2.5 collective-permute-start.3
  15.9 1.2 copy.31
  17.1 0.3 reshape.146
  17.4 1.1 copy.32
  18.5 0.2 reshape.147
  18.7 1.2 pad_maximum_fusion
  19.9 21.0 %collective-permute-done.1 = bf16[512,896]{0,1:T(8,128)(2,1)S(1)} collective-permute-done((bf16[512,896]{0,1:T(8,128)(2,1)S(1)}, bf16[512,896]{0,1:T(8,128)(2,1)S(1)}, u32[]{:S(2)}, u32[]{:S(2)}) %collective-permute-start.1) | collective-permute-done | bytes 917536 | tf_op jit(solution)/shard_map/ppermute | solution.py:24
  40.8 21.2 %collective-permute-done.2 = bf16[512,896]{0,1:T(8,128)(2,1)} collective-permute-done((bf16[512,896]{0,1:T(8,128)(2,1)S(1)}, bf16[512,896]{0,1:T(8,128)(2,1)}, u32[]{:S(2)}, u32[]{:S(2)}) %collective-permute-start.2) | collective-permute-done | bytes 917536 | tf_op jit(solution)/shard_map/ppermute | solution.py:24
  62.2 128.5 %all-gather.3.cloned.1.call-done = bf16[19968,512]{1,0:T(8,128)(2,1)} async-done(((bf16[1248,512]{1,0:T(8,128)(2,1)}), bf16[19968,512]{1,0:T(8,128)(2,1)}) %all-gather.3.cloned.1.call-update) | async-done | bytes 20447248 | tf_op jit(solution)/shard_map/all_gather | solution.py:113
  190.7 4.3 %slice.14 = bf16[16,224,512]{2,1,0:T(8,128)(2,1)} slice(bf16[16,1248,512]{2,1,0:T(8,128)(2,1)} %bitcast.60), slice={[0:16], [896:1120], [0:512]} | slice | bytes 7340032 | tf_op jit(solution)/shard_map/slice | solution.py:116
  195.0 2.6 gather_fusion
  197.6 0.5 gather.17
  198.1 0.6 convolution_bitcast_fusion
  198.7 1.5 collective-permute-start.4
  200.2 2.7 collective-permute-start.5
  202.9 1.5 collective-permute-start.6
  204.5 1.2 collective-permute-done.4
  205.6 3.7 %collective-permute-done.5 = f32[4,128,64]{1,2,0:T(8,128)S(1)} collective-permute-done((f32[4,128,64]{1,2,0:T(8,128)S(1)}, f32[4,128,64]{1,2,0:T(8,128)S(1)}, u32[]{:S(2)}, u32[]{:S(2)}) %collective-permute-start.5) | collective-permute-done | bytes 131104 | tf_op jit(solution)/shard_map/ppermute | solution.py:24
  209.4 1.6 collective-permute-start.7
  211.0 2.7 collective-permute-start.8
  213.7 1.4 collective-permute-start.9
  215.2 0.5 iota_compare_fusion.2
  215.7 0.5 copy.36
  216.3 1.8 slice.15
  218.1 0.6 gather_fusion.1
  218.6 0.3 gather.19
  218.9 0.5 collective-permute-done.8
  219.4 1.3 fusion.22
  220.9 18.8 %fusion.18 = bf16[4,512,512]{2,1,0:T(8,128)(2,1)S(1)} fusion(bf16[4,4,1248,512]{3,2,1,0:T(8,128)(2,1)} %bitcast.62, bf16[1,512,896]{1,2,0:T(8,128)(2,1)} %bitcast.4, bf16[1,512,896]{1,2,0:T(8,128)(2,1)} %bitcast.3, bf16[1,512,896]{1,2,0:T(8,128)(2,1)} %bitcast.67, bf16[1,512,896]{1,2,0:T(8,128)(2,1)S(1)} %bitcast.63, ...), kind=kOutput, calls=%fused_computation.19 | convolution fusion | flops 10505355264 | bytes 27262980 | tf_op jit(solution)/shard_map/sif,asfj->aij/dot_general | solution.py:135
  239.7 1.5 copy.39
  241.2 26.6 %shard_map.64 = bf16[3,16,1,32,512]{4,3,2,1,0:T(8,128)(2,1)} custom-call(bf16[16,4,32,512]{3,2,1,0:T(8,128)(2,1)} %bitcast.52), custom_call_target="tpu_custom_call" | custom-call | tf_op jit(solution)/shard_map/pallas_call | solution.py:64
  267.8 1.8 convert_reduce_fusion
  269.6 1.1 constant_dynamic-slice_fusion
  270.7 0.2 fusion.23
  271.0 1.3 collective-permute-start.10
  272.3 2.6 collective-permute-start.11
  274.8 0.7 collective-permute-start.12
  275.6 2.1 collective-permute-done.10
  277.7 1.5 collective-permute-done.11
  279.2 0.6 collective-permute-done.12
  279.9 0.6 gather_fusion.2
  280.6 0.4 copy.40
  281.0 0.4 reshape.154
  281.4 0.9 broadcast_select_fusion
  (28 shorter events, 0.6 us)
Async XLA Ops:
  6.5 55.6 %copy-start.1 = (s32[4]{0:T(128)S(1)}, s32[4]{0:T(128)}, u32[]{:S(2)}) copy-start(s32[4]{0:T(128)} %param.10) | copy-start | bytes 52
  6.5 184.2 %all-gather.3.cloned.1.call-start = ((), (), s32[]{:S(2)}) async-start(), calls=%async_computation | async-start | bytes 21725184 | tf_op jit(solution)/shard_map/all_gather | solution.py:113
  6.5 12.2 %collective-permute-start = (bf16[896,512]{1,0:T(8,128)(2,1)}, bf16[896,512]{1,0:T(8,128)(2,1)S(1)}, u32[]{:S(2)}, u32[]{:S(2)}) collective-permute-start(bf16[896,512]{1,0:T(8,128)(2,1)} %param.7), channel_id=1, source_target_pairs={{0,0},{1,48},{2,32},{3,16},{4,4},{5,52},{6,36},{7,20},{8,8},{9,56}... | collective-permute-start | bytes 2752520 | tf_op jit(solution)/shard_map/ppermute | solution.py:99
  10.0 30.9 %collective-permute-start.1 = (bf16[512,896]{0,1:T(8,128)(2,1)S(1)}, bf16[512,896]{0,1:T(8,128)(2,1)S(1)}, u32[]{:S(2)}, u32[]{:S(2)}) collective-permute-start(bf16[512,896]{0,1:T(8,128)(2,1)S(1)} %copy.33), channel_id=1, source_target_pairs={{0,1},{1,2},{2,3},{3,0},{4,5},{5,6},{6,7},{7,4},{8,9},{9,10},{10,1... | collective-permute-start | bytes 2752520 | tf_op jit(solution)/shard_map/ppermute | solution.py:24
  11.2 50.9 %collective-permute-start.2 = (bf16[512,896]{0,1:T(8,128)(2,1)S(1)}, bf16[512,896]{0,1:T(8,128)(2,1)}, u32[]{:S(2)}, u32[]{:S(2)}) collective-permute-start(bf16[512,896]{0,1:T(8,128)(2,1)S(1)} %copy.33), channel_id=1, source_target_pairs={{0,2},{1,3},{2,0},{3,1},{4,6},{5,7},{6,4},{7,5},{8,10},{9,11},{10,... | collective-permute-start | bytes 2752520 | tf_op jit(solution)/shard_map/ppermute | solution.py:24
  13.4 48.7 %collective-permute-start.3 = (bf16[512,896]{0,1:T(8,128)(2,1)S(1)}, bf16[512,896]{0,1:T(8,128)(2,1)}, u32[]{:S(2)}, u32[]{:S(2)}) collective-permute-start(bf16[512,896]{0,1:T(8,128)(2,1)S(1)} %copy.33), channel_id=1, source_target_pairs={{0,3},{1,0},{2,1},{3,2},{4,7},{5,4},{6,5},{7,6},{8,11},{9,8},{10,9... | collective-permute-start | bytes 2752520 | tf_op jit(solution)/shard_map/ppermute | solution.py:24
  40.8 168.5 %copy-start.2 = (bf16[512,896]{0,1:T(8,128)(2,1)}, bf16[512,896]{0,1:T(8,128)(2,1)S(1)}, u32[]{:S(2)}) copy-start(bf16[512,896]{0,1:T(8,128)(2,1)S(1)} %collective-permute-done.1) | copy-start | bytes 2752516
  190.7 7.4 %copy-start = (bf16[512,896]{1,0:T(8,128)(2,1)S(1)}, bf16[512,896]{1,0:T(8,128)(2,1)}, u32[]{:S(2)}) copy-start(bf16[512,896]{1,0:T(8,128)(2,1)} %param.6) | copy-start | bytes 2752516
  190.7 13.7 %copy-start.3 = (s32[4]{0:T(128)S(1)}, s32[4]{0:T(128)}, u32[]{:S(2)}) copy-start(s32[4]{0:T(128)} %param.11) | copy-start | bytes 52
  198.7 6.9 %collective-permute-start.4 = (f32[4,128,64]{1,2,0:T(8,128)S(1)}, f32[4,128,64]{1,2,0:T(8,128)S(1)}, u32[]{:S(2)}, u32[]{:S(2)}) collective-permute-start(f32[4,128,64]{1,2,0:T(8,128)S(1)} %convolution_bitcast_fusion), channel_id=1, source_target_pairs={{0,1},{1,2},{2,3},{3,0},{4,5},{5,6},{6,7},{7,4},{8,9},{9,10},{10,1... | collective-permute-start | bytes 393224 | tf_op jit(solution)/shard_map/ppermute | solution.py:24
  200.2 9.1 %collective-permute-start.5 = (f32[4,128,64]{1,2,0:T(8,128)S(1)}, f32[4,128,64]{1,2,0:T(8,128)S(1)}, u32[]{:S(2)}, u32[]{:S(2)}) collective-permute-start(f32[4,128,64]{1,2,0:T(8,128)S(1)} %convolution_bitcast_fusion), channel_id=1, source_target_pairs={{0,2},{1,3},{2,0},{3,1},{4,6},{5,7},{6,4},{7,5},{8,10},{9,11},{10,... | collective-permute-start | bytes 393224 | tf_op jit(solution)/shard_map/ppermute | solution.py:24
  202.9 6.5 %collective-permute-start.6 = (f32[4,128,64]{1,2,0:T(8,128)S(1)}, f32[4,128,64]{1,2,0:T(8,128)S(1)}, u32[]{:S(2)}, u32[]{:S(2)}) collective-permute-start(f32[4,128,64]{1,2,0:T(8,128)S(1)} %convolution_bitcast_fusion), channel_id=1, source_target_pairs={{0,3},{1,0},{2,1},{3,2},{4,7},{5,4},{6,5},{7,6},{8,11},{9,8},{10,9... | collective-permute-start | bytes 393224 | tf_op jit(solution)/shard_map/ppermute | solution.py:24
  209.4 9.5 %collective-permute-start.7 = (f32[4,128,64]{1,2,0:T(8,128)S(1)}, f32[4,128,64]{1,2,0:T(8,128)S(1)}, u32[]{:S(2)}, u32[]{:S(2)}) collective-permute-start(f32[4,128,64]{1,2,0:T(8,128)S(1)} %add_add_fusion), channel_id=1, source_target_pairs={{0,4},{1,5},{2,6},{3,7},{4,8},{5,9},{6,10},{7,11},{8,12},{9,13},{1... | collective-permute-start | bytes 393224 | tf_op jit(solution)/shard_map/ppermute | solution.py:24
  211.0 8.5 %collective-permute-start.8 = (f32[4,128,64]{1,2,0:T(8,128)S(1)}, f32[4,128,64]{1,2,0:T(8,128)}, u32[]{:S(2)}, u32[]{:S(2)}) collective-permute-start(f32[4,128,64]{1,2,0:T(8,128)S(1)} %add_add_fusion), channel_id=1, source_target_pairs={{0,8},{1,9},{2,10},{3,11},{4,12},{5,13},{6,14},{7,15},{8,0},{9,1},... | collective-permute-start | bytes 393224 | tf_op jit(solution)/shard_map/ppermute | solution.py:24
  213.7 5.7 %collective-permute-start.9 = (f32[4,128,64]{1,2,0:T(8,128)S(1)}, f32[4,128,64]{1,2,0:T(8,128)}, u32[]{:S(2)}, u32[]{:S(2)}) collective-permute-start(f32[4,128,64]{1,2,0:T(8,128)S(1)} %add_add_fusion), channel_id=1, source_target_pairs={{0,12},{1,13},{2,14},{3,15},{4,0},{5,1},{6,2},{7,3},{8,4},{9,5},{1... | collective-permute-start | bytes 393224 | tf_op jit(solution)/shard_map/ppermute | solution.py:24
  271.0 6.8 %collective-permute-start.10 = (bf16[4,32,512]{2,1,0:T(8,128)(2,1)S(1)}, bf16[4,32,512]{2,1,0:T(8,128)(2,1)S(1)}, u32[]{:S(2)}, u32[]{:S(2)}) collective-permute-start(bf16[4,32,512]{2,1,0:T(8,128)(2,1)S(1)} %get-tuple-element.18), channel_id=1, source_target_pairs={{0,1},{1,2},{2,3},{3,0},{4,5},{5,6},{6,7},{7,4},{8,9},{9,10},{10,1... | collective-permute-start | bytes 393224 | tf_op jit(solution)/shard_map/ppermute | solution.py:24
  272.3 6.9 %collective-permute-start.11 = (bf16[4,32,512]{2,1,0:T(8,128)(2,1)S(1)}, bf16[4,32,512]{2,1,0:T(8,128)(2,1)S(1)}, u32[]{:S(2)}, u32[]{:S(2)}) collective-permute-start(bf16[4,32,512]{2,1,0:T(8,128)(2,1)S(1)} %get-tuple-element.17), channel_id=1, source_target_pairs={{0,2},{1,3},{2,0},{3,1},{4,6},{5,7},{6,4},{7,5},{8,10},{9,11},{10,... | collective-permute-start | bytes 393224 | tf_op jit(solution)/shard_map/ppermute | solution.py:24
  274.8 5.0 %collective-permute-start.12 = (bf16[4,32,512]{2,1,0:T(8,128)(2,1)S(1)}, bf16[4,32,512]{2,1,0:T(8,128)(2,1)S(1)}, u32[]{:S(2)}, u32[]{:S(2)}) collective-permute-start(bf16[4,32,512]{2,1,0:T(8,128)(2,1)S(1)} %get-tuple-element.16), channel_id=1, source_target_pairs={{0,3},{1,0},{2,1},{3,2},{4,7},{5,4},{6,5},{7,6},{8,11},{9,8},{10,9... | collective-permute-start | bytes 393224 | tf_op jit(solution)/shard_map/ppermute | solution.py:24
Sparse Core Ops, SparseCore 0:
  62.2 128.4 all-gather.2

commit v10 on v6

--- a/solution.py
+++ b/solution.py
@@ -13,12 +13,20 @@
 adapter_scale_factor = 0.5
 
 
-def tensor_allsum(x, count):
-    step = 1
-    while step < count:
-        perm = [(i, i ^ step) for i in range(count)]
-        x = x + lax.ppermute(x, "tensor", perm)
-        step *= 2
+def tensor_shift(x, side, step, along_y):
+    perm = []
+    for yy in range(side):
+        for xx in range(side):
+            if along_y:
+                perm.append((yy * side + xx, ((yy + step) % side) * side + xx))
+            else:
+                perm.append((yy * side + xx, yy * side + (xx + step) % side))
+    return lax.ppermute(x, "tensor", perm)
+
+
+def tensor_allsum(x, side):
+    for along_y in (False, True):
+        x = x + sum(tensor_shift(x, side, s, along_y) for s in range(1, side))
     return x
 
 
@@ -63,17 +71,6 @@
         ],
         compiler_params=pltpu.CompilerParams(collective_id=0, has_side_effects=True),
     )(partial_value)
-
-
-def tensor_shift(x, side, step, along_y):
-    perm = []
-    for yy in range(side):
-        for xx in range(side):
-            if along_y:
-                perm.append((yy * side + xx, ((yy + step) % side) * side + xx))
-            else:
-                perm.append((yy * side + xx, yy * side + (xx + step) % side))
-    return lax.ppermute(x, "tensor", perm)
 
 
 def shards(hidden, down_weight, adapter_shrink, adapter_expand, block_adapter, block_rows):
@@ -121,30 +118,32 @@
     )
 
     pieces = [hidden] + [tensor_shift(hidden, side, s, True) for s in range(1, side)]
-    hidden_column = jnp.pad(jnp.stack(pieces, axis=0), ((0, 0), (0, 0), (0, plane_rows - feat)))
+    hidden_column = jnp.stack(pieces, axis=0).reshape(side, side, side, own_rows, feat)
+    hidden_column = jnp.transpose(hidden_column, (2, 0, 1, 3, 4)).reshape(
+        side, side, side * own_rows, feat
+    )
+    hidden_column = jnp.pad(hidden_column, ((0, 0), (0, 0), (0, 0), (0, plane_rows - feat)))
 
     first = jnp.take(shrink_all, block_adapter, axis=0).reshape(block_count, feat, rank)
     second = jnp.take(expand_all, block_adapter, axis=0).reshape(block_count, column_span, rank)
     blocks = hidden.reshape(block_count, BLOCK, feat)
     shrink = jnp.einsum("bnf,bfr->bnr", blocks, first, preferred_element_type=jnp.float32)
-    summed_shrink = tensor_allsum(shrink, tensor_count).astype(jnp.bfloat16)
+    summed_shrink = tensor_allsum(shrink, side).astype(jnp.bfloat16)
     enlarged_rows = jnp.einsum(
         "bnr,bcr->bnc", summed_shrink, second, preferred_element_type=jnp.float32
     )
     delta = (adapter_scale_factor * enlarged_rows).astype(jnp.bfloat16).reshape(input_rows, column_span)
 
-    partial_value = jnp.einsum(
-        "sif,asfj->aij", hidden_column, w_quarter, preferred_element_type=jnp.float32
-    )
-    partial_value = partial_value.astype(jnp.bfloat16).reshape(
-        quarter, side, side, own_rows, width
-    )
+    def rows_for(owner_x):
+        rows = lax.dynamic_index_in_dim(hidden_column, owner_x, axis=0, keepdims=False)
+        piece = jnp.einsum("sif,asfj->aij", rows, w_quarter, preferred_element_type=jnp.float32)
+        return piece.astype(jnp.bfloat16).reshape(quarter, side, own_rows, width)
 
-    total = lax.dynamic_index_in_dim(partial_value, my_x, axis=2, keepdims=False).astype(jnp.float32)
+    total = None
     for s in range(1, side):
-        piece = lax.dynamic_index_in_dim(partial_value, (my_x + s) % side, axis=2, keepdims=False)
-        total = total + tensor_shift(piece, side, s, False).astype(jnp.float32)
-    total = total.astype(jnp.bfloat16)
+        arrived = tensor_shift(rows_for((my_x + s) % side), side, s, False).astype(jnp.float32)
+        total = arrived if total is None else total + arrived
+    total = (total + rows_for(my_x).astype(jnp.float32)).astype(jnp.bfloat16)
 
     got = [lax.dynamic_index_in_dim(total, my_y, axis=1, keepdims=False)]
     for s in range(1, side):

time: 246 us -> 235 us (0.955)
  waiting for transfers between devices: 144 us -> 123 us
  matrix products: 17.8 us -> 21.3 us
  local copies, waits for them, and re-layouts: 17.6 us -> 20.4 us
    ppermute x9 -> x15, waiting for transfers between devices: 0.02 us -> 48.5 us  [tensor_shift(): return lax.ppermute(x, 'tensor', perm)]
    all_gather x1, waiting for transfers between devices: 111 us -> 67.6 us  [shards(): gathered = lax.all_gather(pack, 'pool', axis=0, tiled=False)]
    ppermute x4 -> x0, waiting for transfers between devices: 25.2 us -> none  [tensor_allsum(): x = x + lax.ppermute(x, 'tensor', perm)]
    ppermute x9 -> x15, starting transfers between devices: 30.1 us -> 41.5 us  [tensor_shift(): return lax.ppermute(x, 'tensor', perm)]
    ppermute x4 -> x0, starting transfers between devices: 8.38 us -> none  [tensor_allsum(): x = x + lax.ppermute(x, 'tensor', perm)]
    dot_general x1 -> x4, matrix products: 16 us -> 18.9 us  [rows_for(): jnp.einsum('sif,asfj->aij', rows, w_quarter, preferred_element_type=jnp.f...]
  transfers between devices with their start and end apart: 16 -> 18, of which waited for: 4 -> 8; matrix products, arithmetic and copies ran while one was open for 15% -> 15% of each run, Pallas kernels for 0% -> 0%
where the time goes in v10:
time: 235 us; the launch traced here: 234 us
  waiting for transfers between devices  123 us (52%)
  starting transfers between devices  48.1 us (20%)
  matrix products  21.3 us (9%)
  local copies, waits for them, and re-layouts  20.4 us (9%)
  between operations  13.8 us (6%)
  other arithmetic  7.04 us (3%)
    all_gather x1, waiting for transfers between devices, shards(): gathered = lax.all_gather(pack, 'pool', axis=0, tiled=False)  67.6 us
    ppermute x15, waiting for transfers between devices, tensor_shift(): return lax.ppermute(x, 'tensor', perm)  48.5 us
    ppermute x15, starting transfers between devices, tensor_shift(): return lax.ppermute(x, 'tensor', perm)  41.5 us
    dot_general x4, matrix products, rows_for(): jnp.einsum('sif,asfj->aij', rows, w_quarter, preferred_element_type=jnp.f...  18.9 us
    all_to_all x1, waiting for transfers between devices, shards(): lax.all_to_all(delta, 'tensor', split_axis=0, concat_axis=1, tiled=True)  6.77 us
  transfers between devices with their start and end apart: 18, of which 8 were waited for; matrix products, arithmetic and copies ran while one was open for 15% of the time, Pallas kernels for 0%

profile of v10, /device:TPU:0, one launch (start us, length us, event | category | flops | bytes accessed | tf_op | source)
XLA Modules:
  0.0 233.6 jit_solution(5770144097390535090)
XLA Ops:
  6.5 2.0 collective-permute-start
  8.5 1.1 copy.30
  9.8 1.2 copy.29
  11.0 0.3 reshape.152
  11.3 1.2 pad_maximum_fusion
  12.6 11.6 %collective-permute-start.3 = (bf16[512,896]{1,0:T(8,128)(2,1)S(1)}, bf16[512,896]{1,0:T(8,128)(2,1)S(1)}, u32[]{:S(2)}, u32[]{:S(2)}) collective-permute-start(bf16[512,896]{1,0:T(8,128)(2,1)S(1)} %copy-done.1), channel_id=1, source_target_pairs={{0,12},{1,13},{2,14},{3,15},{4,0},{5,1},{6,2},{7,3},{8,4},{9,5},{1... | collective-permute-start | bytes 2752520 | tf_op jit(solution)/shard_map/ppermute | solution.py:24
  24.2 10.4 %collective-permute-start.2 = (bf16[512,896]{1,0:T(8,128)(2,1)S(1)}, bf16[512,896]{1,0:T(8,128)(2,1)S(1)}, u32[]{:S(2)}, u32[]{:S(2)}) collective-permute-start(bf16[512,896]{1,0:T(8,128)(2,1)S(1)} %copy-done.1), channel_id=1, source_target_pairs={{0,8},{1,9},{2,10},{3,11},{4,12},{5,13},{6,14},{7,15},{8,0},{9,1},... | collective-permute-start | bytes 2752520 | tf_op jit(solution)/shard_map/ppermute | solution.py:24
  34.6 1.3 collective-permute-start.1
  36.2 5.8 %collective-permute-done.3 = bf16[512,896]{1,0:T(8,128)(2,1)S(1)} collective-permute-done((bf16[512,896]{1,0:T(8,128)(2,1)S(1)}, bf16[512,896]{1,0:T(8,128)(2,1)S(1)}, u32[]{:S(2)}, u32[]{:S(2)}) %collective-permute-start.3) | collective-permute-done | bytes 917536 | tf_op jit(solution)/shard_map/ppermute | solution.py:24
  42.0 13.4 %collective-permute-done.2 = bf16[512,896]{1,0:T(8,128)(2,1)S(1)} collective-permute-done((bf16[512,896]{1,0:T(8,128)(2,1)S(1)}, bf16[512,896]{1,0:T(8,128)(2,1)S(1)}, u32[]{:S(2)}, u32[]{:S(2)}) %collective-permute-start.2) | collective-permute-done | bytes 917536 | tf_op jit(solution)/shard_map/ppermute | solution.py:24
  55.4 20.1 %collective-permute-done.1 = bf16[512,896]{1,0:T(8,128)(2,1)} collective-permute-done((bf16[512,896]{1,0:T(8,128)(2,1)S(1)}, bf16[512,896]{1,0:T(8,128)(2,1)}, u32[]{:S(2)}, u32[]{:S(2)}) %collective-permute-start.1) | collective-permute-done | bytes 917536 | tf_op jit(solution)/shard_map/ppermute | solution.py:24
  75.5 1.6 maximum_bitcast_fusion
  77.2 2.3 copy.31
  79.4 67.6 %all-gather.3.cloned.1.call-done = bf16[19968,512]{1,0:T(8,128)(2,1)} async-done(((bf16[1248,512]{1,0:T(8,128)(2,1)}), bf16[19968,512]{1,0:T(8,128)(2,1)}) %all-gather.3.cloned.1.call-update) | async-done | bytes 20447248 | tf_op jit(solution)/shard_map/all_gather | solution.py:110
  147.0 4.3 %slice.14 = bf16[16,224,512]{2,1,0:T(8,128)(2,1)} slice(bf16[16,1248,512]{2,1,0:T(8,128)(2,1)} %bitcast.103), slice={[0:16], [896:1120], [0:512]} | slice | bytes 7340032 | tf_op jit(solution)/shard_map/slice | solution.py:113
  151.3 2.6 %gather_fusion.1 = bf16[4,112,512]{2,1,0:T(8,128)(2,1)S(1)} fusion(bf16[32,112,512]{2,1,0:T(8,128)(2,1)} %bitcast.119, s32[1024]{0:T(1024)S(1)} %pad_clamp_fusion), kind=kCustom, calls=%fused_computation.1 | custom fusion | bytes 917520 | tf_op jit(solution)/shard_map/jit(_take)/gather | solution.py:127
  153.9 0.5 gather.18
  154.4 1.3 convolution_bitcast_fusion.4
  155.7 2.7 %collective-permute-start.12 = (f32[4,128,64]{1,2,0:T(8,128)}, f32[4,128,64]{1,2,0:T(8,128)S(1)}, u32[]{:S(2)}, u32[]{:S(2)}) collective-permute-start(f32[4,128,64]{1,2,0:T(8,128)} %convolution_bitcast_fusion.4), channel_id=1, source_target_pairs={{0,3},{1,0},{2,1},{3,2},{4,7},{5,4},{6,5},{7,6},{8,11},{9,8},{10,9... | collective-permute-start | bytes 393224 | tf_op jit(solution)/shard_map/ppermute | solution.py:24
  158.4 2.3 collective-permute-start.11
  160.7 10.2 %fusion.14 = bf16[4,512,128]{1,2,0:T(8,128)(2,1)S(1)} fusion(bf16[4,4,1248,512]{3,2,1,0:T(8,128)(2,1)} %bitcast.104, s32[]{:T(128)S(6)} %select_n.155, bf16[4,4,128,896]{3,2,1,0:T(8,128)(2,1)} %bitcast.111), kind=kOutput, calls=%fused_computation.19 | convolution fusion | flops 2617507840 | bytes 24641540 | tf_op jit(solution)/shard_map/sif,asfj->aij/dot_general | solution.py:139
  170.9 1.4 collective-permute-start.6
  172.5 1.0 copy-done
  173.5 2.9 %fusion.11 = bf16[4,512,128]{1,2,0:T(8,128)(2,1)S(1)} fusion(bf16[4,4,1248,512]{3,2,1,0:T(8,128)(2,1)S(1)} %bitcast.107, s32[]{:T(128)S(6)} %select_n.153, bf16[4,4,128,896]{3,2,1,0:T(8,128)(2,1)S(1)} %bitcast.112), kind=kOutput, calls=%fused_computation.18 | convolution fusion | flops 2617507840 | bytes 24641540 | tf_op jit(solution)/shard_map/sif,asfj->aij/dot_general | solution.py:139
  176.4 1.6 collective-permute-start.5
  178.0 2.9 %fusion.8 = bf16[4,512,128]{1,2,0:T(8,128)(2,1)S(1)} fusion(bf16[4,4,1248,512]{3,2,1,0:T(8,128)(2,1)S(1)} %bitcast.108, s32[]{:T(128)S(6)} %select_n.151, bf16[4,4,128,896]{3,2,1,0:T(8,128)(2,1)S(1)} %bitcast.113), kind=kOutput, calls=%fused_computation.17 | convolution fusion | flops 2617507840 | bytes 24641540 | tf_op jit(solution)/shard_map/sif,asfj->aij/dot_general | solution.py:139
  180.9 0.7 copy-done.2
  181.6 0.5 collective-permute-start.4
  182.1 2.9 %fusion.21 = f32[4,512,128]{1,2,0:T(8,128)S(1)} fusion(bf16[4,4,1248,512]{3,2,1,0:T(8,128)(2,1)S(1)} %bitcast.109, s32[]{:T(128)S(6)} %select_n.156, bf16[4,4,128,896]{3,2,1,0:T(8,128)(2,1)S(1)} %bitcast.114), kind=kOutput, calls=%fused_computation.22 | convolution fusion | flops 2617769984 | bytes 25165828 | tf_op jit(solution)/shard_map/sif,asfj->aij/dot_general | solution.py:139
  185.0 1.5 slice.15
  186.6 2.2 gather_fusion.2
  189.0 1.1 add_add_fusion
  190.2 2.8 %collective-permute-start.15 = (f32[4,128,64]{1,2,0:T(8,128)S(1)}, f32[4,128,64]{1,2,0:T(8,128)S(1)}, u32[]{:S(2)}, u32[]{:S(2)}) collective-permute-start(f32[4,128,64]{1,2,0:T(8,128)S(1)} %add_add_fusion), channel_id=1, source_target_pairs={{0,12},{1,13},{2,14},{3,15},{4,0},{5,1},{6,2},{7,3},{8,4},{9,5},{1... | collective-permute-start | bytes 393224 | tf_op jit(solution)/shard_map/ppermute | solution.py:24
  193.0 2.3 collective-permute-start.14
  195.3 7.3 %collective-permute-done.4 = bf16[4,4,32,512]{3,2,1,0:T(8,128)(2,1)} collective-permute-done((bf16[4,4,32,512]{3,2,1,0:T(8,128)(2,1)S(1)}, bf16[4,4,32,512]{3,2,1,0:T(8,128)(2,1)}, u32[]{:S(2)}, u32[]{:S(2)}) %collective-permute-start.4) | collective-permute-done | bytes 524320 | tf_op jit(solution)/shard_map/ppermute | solution.py:24
  202.6 1.7 add_convert_fusion.1
  204.3 2.8 %collective-permute-start.9 = (bf16[4,32,512]{2,1,0:T(8,128)(2,1)S(1)}, bf16[4,32,512]{2,1,0:T(8,128)(2,1)S(1)}, u32[]{:S(2)}, u32[]{:S(2)}) collective-permute-start(bf16[4,32,512]{2,1,0:T(8,128)(2,1)S(1)} %get-tuple-element.6), channel_id=1, source_target_pairs={{0,12},{1,13},{2,14},{3,15},{4,0},{5,1},{6,2},{7,3},{8,4},{9,5},{1... | collective-permute-start | bytes 393224 | tf_op jit(solution)/shard_map/ppermute | solution.py:24
  207.2 0.8 collective-permute-start.8
  208.0 0.9 collective-permute-start.7
  208.9 1.2 fusion.20
  210.0 4.7 %all-to-all-start = ((bf16[16,32,512]{2,1,0:T(8,128)(2,1)}), bf16[16,32,512]{2,1,0:T(8,128)(2,1)S(1)}, u32[]{:S(2)}, u32[]{:S(2)}) async-start(bf16[16,32,512]{2,1,0:T(8,128)(2,1)} %bitcast.45), calls=%async_computation | async-start | bytes 1048576 | tf_op jit(solution)/shard_map/all_to_all | solution.py:155
  214.8 0.3 collective-permute-done.8
  215.1 1.5 collective-permute-done.7
  216.7 0.6 gather_fusion
  217.4 0.7 copy.36
  218.1 0.7 reshape.163
  218.8 6.8 %all-to-all-done = bf16[16,32,512]{2,1,0:T(8,128)(2,1)S(1)} async-done(((bf16[16,32,512]{2,1,0:T(8,128)(2,1)}), bf16[16,32,512]{2,1,0:T(8,128)(2,1)S(1)}, u32[]{:S(2)}, u32[]{:S(2)}) %all-to-all-start) | async-done | bytes 524320 | tf_op jit(solution)/shard_map/all_to_all | solution.py:155
  225.8 0.9 fusion.26
  (48 shorter events, 1.4 us)
Async XLA Ops:
  6.5 6.0 %copy-start.1 = (bf16[512,896]{1,0:T(8,128)(2,1)S(1)}, bf16[512,896]{1,0:T(8,128)(2,1)}, u32[]{:S(2)}) copy-start(bf16[512,896]{1,0:T(8,128)(2,1)} %param.6) | copy-start | bytes 2752516
  6.5 29.5 %copy-start.3 = (s32[4]{0:T(128)S(1)}, s32[4]{0:T(128)}, u32[]{:S(2)}) copy-start(s32[4]{0:T(128)} %param.10) | copy-start | bytes 52
  6.5 29.6 %copy-start.4 = (s32[4]{0:T(128)S(1)}, s32[4]{0:T(128)}, u32[]{:S(2)}) copy-start(s32[4]{0:T(128)} %param.11) | copy-start | bytes 52
  6.5 140.5 %all-gather.3.cloned.1.call-start = ((), (), s32[]{:S(2)}) async-start(), calls=%async_computation.1 | async-start | bytes 21725184 | tf_op jit(solution)/shard_map/all_gather | solution.py:110
  6.5 4.8 %collective-permute-start = (bf16[896,512]{1,0:T(8,128)(2,1)}, bf16[896,512]{1,0:T(8,128)(2,1)S(1)}, u32[]{:S(2)}, u32[]{:S(2)}) collective-permute-start(bf16[896,512]{1,0:T(8,128)(2,1)} %param.7), channel_id=1, source_target_pairs={{0,0},{1,1},{2,2},{3,3},{4,48},{5,49},{6,50},{7,51},{8,32},{9,33},... | collective-permute-start | bytes 2752520 | tf_op jit(solution)/shard_map/ppermute | solution.py:98
  12.6 29.5 %collective-permute-start.3 = (bf16[512,896]{1,0:T(8,128)(2,1)S(1)}, bf16[512,896]{1,0:T(8,128)(2,1)S(1)}, u32[]{:S(2)}, u32[]{:S(2)}) collective-permute-start(bf16[512,896]{1,0:T(8,128)(2,1)S(1)} %copy-done.1), channel_id=1, source_target_pairs={{0,12},{1,13},{2,14},{3,15},{4,0},{5,1},{6,2},{7,3},{8,4},{9,5},{1... | collective-permute-start | bytes 2752520 | tf_op jit(solution)/shard_map/ppermute | solution.py:24
  24.2 31.2 %collective-permute-start.2 = (bf16[512,896]{1,0:T(8,128)(2,1)S(1)}, bf16[512,896]{1,0:T(8,128)(2,1)S(1)}, u32[]{:S(2)}, u32[]{:S(2)}) collective-permute-start(bf16[512,896]{1,0:T(8,128)(2,1)S(1)} %copy-done.1), channel_id=1, source_target_pairs={{0,8},{1,9},{2,10},{3,11},{4,12},{5,13},{6,14},{7,15},{8,0},{9,1},... | collective-permute-start | bytes 2752520 | tf_op jit(solution)/shard_map/ppermute | solution.py:24
  34.6 41.0 %collective-permute-start.1 = (bf16[512,896]{1,0:T(8,128)(2,1)S(1)}, bf16[512,896]{1,0:T(8,128)(2,1)}, u32[]{:S(2)}, u32[]{:S(2)}) collective-permute-start(bf16[512,896]{1,0:T(8,128)(2,1)S(1)} %copy-done.1), channel_id=1, source_target_pairs={{0,4},{1,5},{2,6},{3,7},{4,8},{5,9},{6,10},{7,11},{8,12},{9,13},{1... | collective-permute-start | bytes 2752520 | tf_op jit(solution)/shard_map/ppermute | solution.py:24
  154.4 17.9 %slice-start = ((s8[20447232]{0:T(1024)(128)(4,1)}), s8[4194304]{0:T(1024)(128)(4,1)S(1)}, s32[]{:S(2)}) async-start(s8[20447232]{0:T(1024)(128)(4,1)} %bitcast.105), calls=%async_computation.2 | async-start | bytes 8388608
  155.7 25.2 %collective-permute-start.12 = (f32[4,128,64]{1,2,0:T(8,128)}, f32[4,128,64]{1,2,0:T(8,128)S(1)}, u32[]{:S(2)}, u32[]{:S(2)}) collective-permute-start(f32[4,128,64]{1,2,0:T(8,128)} %convolution_bitcast_fusion.4), channel_id=1, source_target_pairs={{0,3},{1,0},{2,1},{3,2},{4,7},{5,4},{6,5},{7,6},{8,11},{9,8},{10,9... | collective-permute-start | bytes 393224 | tf_op jit(solution)/shard_map/ppermute | solution.py:24
  158.4 30.6 %collective-permute-start.10 = (f32[4,128,64]{1,2,0:T(8,128)}, f32[4,128,64]{1,2,0:T(8,128)}, u32[]{:S(2)}, u32[]{:S(2)}) collective-permute-start(f32[4,128,64]{1,2,0:T(8,128)} %convolution_bitcast_fusion.4), channel_id=1, source_target_pairs={{0,1},{1,2},{2,3},{3,0},{4,5},{5,6},{6,7},{7,4},{8,9},{9,10},{10,1... | collective-permute-start | bytes 393224 | tf_op jit(solution)/shard_map/ppermute | solution.py:24
  158.4 30.7 %collective-permute-start.11 = (f32[4,128,64]{1,2,0:T(8,128)}, f32[4,128,64]{1,2,0:T(8,128)}, u32[]{:S(2)}, u32[]{:S(2)}) collective-permute-start(f32[4,128,64]{1,2,0:T(8,128)} %convolution_bitcast_fusion.4), channel_id=1, source_target_pairs={{0,2},{1,3},{2,0},{3,1},{4,6},{5,7},{6,4},{7,5},{8,10},{9,11},{10,... | collective-permute-start | bytes 393224 | tf_op jit(solution)/shard_map/ppermute | solution.py:24
  160.7 11.6 %slice-start.1 = ((s8[20447232]{0:T(1024)(128)(4,1)}), s8[4194304]{0:T(1024)(128)(4,1)S(1)}, s32[]{:S(2)}) async-start(s8[20447232]{0:T(1024)(128)(4,1)} %bitcast.105), calls=%async_computation.3 | async-start | bytes 8388608
  160.7 11.6 %slice-start.2 = ((s8[20447232]{0:T(1024)(128)(4,1)}), s8[4194304]{0:T(1024)(128)(4,1)S(1)}, s32[]{:S(2)}) async-start(s8[20447232]{0:T(1024)(128)(4,1)} %bitcast.105), calls=%async_computation.4 | async-start | bytes 8388608
  160.7 11.6 %slice-start.3 = ((s8[20447232]{0:T(1024)(128)(4,1)}), s8[4194304]{0:T(1024)(128)(4,1)S(1)}, s32[]{:S(2)}) async-start(s8[20447232]{0:T(1024)(128)(4,1)} %bitcast.105), calls=%async_computation.5 | async-start | bytes 8388608
  160.7 11.8 %slice-start.4 = ((s8[20447232]{0:T(1024)(128)(4,1)}), s8[3670016]{0:T(1024)(128)(4,1)S(1)}, s32[]{:S(2)}) async-start(s8[20447232]{0:T(1024)(128)(4,1)} %bitcast.105), calls=%async_computation.6 | async-start | bytes 7340032
  160.7 12.8 %copy-start = (bf16[4,4,4,32,896]{4,3,2,1,0:T(8,128)(2,1)S(1)}, bf16[4,4,4,32,896]{4,3,2,1,0:T(8,128)(2,1)}, u32[]{:S(2)}) copy-start(bf16[4,4,4,32,896]{4,3,2,1,0:T(8,128)(2,1)} %copy.31) | copy-start | bytes 11010052
  170.9 22.1 %collective-permute-start.6 = (bf16[4,4,32,512]{3,2,1,0:T(8,128)(2,1)S(1)}, bf16[4,4,32,512]{3,2,1,0:T(8,128)(2,1)}, u32[]{:S(2)}, u32[]{:S(2)}) collective-permute-start(bf16[4,4,32,512]{3,2,1,0:T(8,128)(2,1)S(1)} %bitcast.117), channel_id=1, source_target_pairs={{0,3},{1,0},{2,1},{3,2},{4,7},{5,4},{6,5},{7,6},{8,11},{9,8},{10,9... | collective-permute-start | bytes 1572872 | tf_op jit(solution)/shard_map/ppermute | solution.py:24
  176.4 18.8 %collective-permute-start.5 = (bf16[4,4,32,512]{3,2,1,0:T(8,128)(2,1)S(1)}, bf16[4,4,32,512]{3,2,1,0:T(8,128)(2,1)}, u32[]{:S(2)}, u32[]{:S(2)}) collective-permute-start(bf16[4,4,32,512]{3,2,1,0:T(8,128)(2,1)S(1)} %bitcast.116), channel_id=1, source_target_pairs={{0,2},{1,3},{2,0},{3,1},{4,6},{5,7},{6,4},{7,5},{8,10},{9,11},{10,... | collective-permute-start | bytes 1572872 | tf_op jit(solution)/shard_map/ppermute | solution.py:24
  180.9 0.7 copy-start.2
  181.6 21.0 %collective-permute-start.4 = (bf16[4,4,32,512]{3,2,1,0:T(8,128)(2,1)S(1)}, bf16[4,4,32,512]{3,2,1,0:T(8,128)(2,1)}, u32[]{:S(2)}, u32[]{:S(2)}) collective-permute-start(bf16[4,4,32,512]{3,2,1,0:T(8,128)(2,1)S(1)} %bitcast.118), channel_id=1, source_target_pairs={{0,1},{1,2},{2,3},{3,0},{4,5},{5,6},{6,7},{7,4},{8,9},{9,10},{10,1... | collective-permute-start | bytes 1572872 | tf_op jit(solution)/shard_map/ppermute | solution.py:24
  190.2 17.8 %collective-permute-start.15 = (f32[4,128,64]{1,2,0:T(8,128)S(1)}, f32[4,128,64]{1,2,0:T(8,128)S(1)}, u32[]{:S(2)}, u32[]{:S(2)}) collective-permute-start(f32[4,128,64]{1,2,0:T(8,128)S(1)} %add_add_fusion), channel_id=1, source_target_pairs={{0,12},{1,13},{2,14},{3,15},{4,0},{5,1},{6,2},{7,3},{8,4},{9,5},{1... | collective-permute-start | bytes 393224 | tf_op jit(solution)/shard_map/ppermute | solution.py:24
  193.0 15.9 %collective-permute-start.13 = (f32[4,128,64]{1,2,0:T(8,128)S(1)}, f32[4,128,64]{1,2,0:T(8,128)S(1)}, u32[]{:S(2)}, u32[]{:S(2)}) collective-permute-start(f32[4,128,64]{1,2,0:T(8,128)S(1)} %add_add_fusion), channel_id=1, source_target_pairs={{0,4},{1,5},{2,6},{3,7},{4,8},{5,9},{6,10},{7,11},{8,12},{9,13},{1... | collective-permute-start | bytes 393224 | tf_op jit(solution)/shard_map/ppermute | solution.py:24
  193.0 15.9 %collective-permute-start.14 = (f32[4,128,64]{1,2,0:T(8,128)S(1)}, f32[4,128,64]{1,2,0:T(8,128)S(1)}, u32[]{:S(2)}, u32[]{:S(2)}) collective-permute-start(f32[4,128,64]{1,2,0:T(8,128)S(1)} %add_add_fusion), channel_id=1, source_target_pairs={{0,8},{1,9},{2,10},{3,11},{4,12},{5,13},{6,14},{7,15},{8,0},{9,1},... | collective-permute-start | bytes 393224 | tf_op jit(solution)/shard_map/ppermute | solution.py:24
  204.3 10.4 %collective-permute-start.9 = (bf16[4,32,512]{2,1,0:T(8,128)(2,1)S(1)}, bf16[4,32,512]{2,1,0:T(8,128)(2,1)S(1)}, u32[]{:S(2)}, u32[]{:S(2)}) collective-permute-start(bf16[4,32,512]{2,1,0:T(8,128)(2,1)S(1)} %get-tuple-element.6), channel_id=1, source_target_pairs={{0,12},{1,13},{2,14},{3,15},{4,0},{5,1},{6,2},{7,3},{8,4},{9,5},{1... | collective-permute-start | bytes 393224 | tf_op jit(solution)/shard_map/ppermute | solution.py:24
  207.2 7.9 %collective-permute-start.8 = (bf16[4,32,512]{2,1,0:T(8,128)(2,1)S(1)}, bf16[4,32,512]{2,1,0:T(8,128)(2,1)S(1)}, u32[]{:S(2)}, u32[]{:S(2)}) collective-permute-start(bf16[4,32,512]{2,1,0:T(8,128)(2,1)S(1)} %get-tuple-element.7), channel_id=1, source_target_pairs={{0,8},{1,9},{2,10},{3,11},{4,12},{5,13},{6,14},{7,15},{8,0},{9,1},... | collective-permute-start | bytes 393224 | tf_op jit(solution)/shard_map/ppermute | solution.py:24
  208.0 8.6 %collective-permute-start.7 = (bf16[4,32,512]{2,1,0:T(8,128)(2,1)S(1)}, bf16[4,32,512]{2,1,0:T(8,128)(2,1)S(1)}, u32[]{:S(2)}, u32[]{:S(2)}) collective-permute-start(bf16[4,32,512]{2,1,0:T(8,128)(2,1)S(1)} %get-tuple-element.8), channel_id=1, source_target_pairs={{0,4},{1,5},{2,6},{3,7},{4,8},{5,9},{6,10},{7,11},{8,12},{9,13},{1... | collective-permute-start | bytes 393224 | tf_op jit(solution)/shard_map/ppermute | solution.py:24
  210.0 15.6 %all-to-all-start = ((bf16[16,32,512]{2,1,0:T(8,128)(2,1)}), bf16[16,32,512]{2,1,0:T(8,128)(2,1)S(1)}, u32[]{:S(2)}, u32[]{:S(2)}) async-start(bf16[16,32,512]{2,1,0:T(8,128)(2,1)} %bitcast.45), calls=%async_computation | async-start | bytes 1048576 | tf_op jit(solution)/shard_map/all_to_all | solution.py:155
Sparse Core Ops, SparseCore 0:
  12.7 134.3 all-gather.2

commit v11 on v10

--- a/solution.py
+++ b/solution.py
@@ -110,13 +110,6 @@
     gathered = lax.all_gather(pack, "pool", axis=0, tiled=False)
     plane_rows = gathered.shape[1]
     w_quarter = gathered.reshape(quarter, side, plane_rows, width)
-    shrink_all = gathered[:, feat:feat + shrink_rows, :].reshape(
-        pool_count * held, shrink_rows // held, width
-    )
-    expand_all = gathered[:, feat + shrink_rows:, :].reshape(
-        pool_count * held, expand_rows // held, width
-    )
-
     pieces = [hidden] + [tensor_shift(hidden, side, s, True) for s in range(1, side)]
     hidden_column = jnp.stack(pieces, axis=0).reshape(side, side, side, own_rows, feat)
     hidden_column = jnp.transpose(hidden_column, (2, 0, 1, 3, 4)).reshape(
@@ -124,8 +117,24 @@
     )
     hidden_column = jnp.pad(hidden_column, ((0, 0), (0, 0), (0, 0), (0, plane_rows - feat)))
 
-    first = jnp.take(shrink_all, block_adapter, axis=0).reshape(block_count, feat, rank)
-    second = jnp.take(expand_all, block_adapter, axis=0).reshape(block_count, column_span, rank)
+    shrink_part = shrink_rows // held
+    expand_part = expand_rows // held
+    first = jnp.stack([
+        lax.dynamic_slice(
+            gathered,
+            (block_adapter[b] // held, feat + (block_adapter[b] % held) * shrink_part, 0),
+            (1, shrink_part, width),
+        )[0]
+        for b in range(block_count)
+    ]).reshape(block_count, feat, rank)
+    second = jnp.stack([
+        lax.dynamic_slice(
+            gathered,
+            (block_adapter[b] // held, feat + shrink_rows + (block_adapter[b] % held) * expand_part, 0),
+            (1, expand_part, width),
+        )[0]
+        for b in range(block_count)
+    ]).reshape(block_count, column_span, rank)
     blocks = hidden.reshape(block_count, BLOCK, feat)
     shrink = jnp.einsum("bnf,bfr->bnr", blocks, first, preferred_element_type=jnp.float32)
     summed_shrink = tensor_allsum(shrink, side).astype(jnp.bfloat16)

time: 235 us -> 237 us (level)
  local copies, waits for them, and re-layouts: 20.4 us -> 9.69 us
  between operations: 13.8 us -> 24 us
    gather x4 -> x0, local copies, waits for them, and re-layouts: 5.5 us -> none  [the longest x2 3.07 us: shards(): jnp.take(shrink_all, block_adapter, axis=0).reshape(block_count, feat, rank)]
    slice x2 -> x1, local copies, waits for them, and re-layouts: 5.82 us -> 0.65 us  [shards(): block_adapter[b] // held]
  transfers between devices with their start and end apart: 18 -> 18, of which waited for: 8 -> 6; matrix products, arithmetic and copies ran while one was open for 15% -> 14% of each run, Pallas kernels for 0% -> 0%
where the time goes in v11:
time: 237 us; the launch traced here: 236 us
  waiting for transfers between devices  124 us (52%)
  starting transfers between devices  49.8 us (21%)
  between operations  24 us (10%)
  matrix products  21.2 us (9%)
  local copies, waits for them, and re-layouts  9.69 us (4%)
  other arithmetic  7.12 us (3%)
    all_gather x1, waiting for transfers between devices, shards(): gathered = lax.all_gather(pack, 'pool', axis=0, tiled=False)  67.6 us
    ppermute x15, waiting for transfers between devices, tensor_shift(): return lax.ppermute(x, 'tensor', perm)  48.4 us
    ppermute x15, starting transfers between devices, tensor_shift(): return lax.ppermute(x, 'tensor', perm)  42.9 us
    dot_general x4, matrix products, rows_for(): jnp.einsum('sif,asfj->aij', rows, w_quarter, preferred_element_type=jnp.f...  18.9 us
    all_to_all x1, waiting for transfers between devices, shards(): lax.all_to_all(delta, 'tensor', split_axis=0, concat_axis=1, tiled=True)  7.86 us
    all_to_all x1, starting transfers between devices, shards(): lax.all_to_all(delta, 'tensor', split_axis=0, concat_axis=1, tiled=True)  5 us
  transfers between devices with their start and end apart: 18, of which 6 were waited for; matrix products, arithmetic and copies ran while one was open for 14% of the time, Pallas kernels for 0%

profile of v11, /device:TPU:0, one launch (start us, length us, event | category | flops | bytes accessed | tf_op | source)
XLA Modules:
  0.0 235.8 jit_solution(13146521420583806199)
XLA Ops:
  6.5 2.0 collective-permute-start
  8.5 1.1 copy.30
  9.6 0.2 reshape.144
  9.8 1.2 copy.29
  11.0 0.3 reshape.143
  11.3 1.2 pad_maximum_fusion
  12.6 11.6 %collective-permute-start.3 = (bf16[512,896]{1,0:T(8,128)(2,1)S(1)}, bf16[512,896]{1,0:T(8,128)(2,1)S(1)}, u32[]{:S(2)}, u32[]{:S(2)}) collective-permute-start(bf16[512,896]{1,0:T(8,128)(2,1)S(1)} %copy-done.1), channel_id=1, source_target_pairs={{0,12},{1,13},{2,14},{3,15},{4,0},{5,1},{6,2},{7,3},{8,4},{9,5},{1... | collective-permute-start | bytes 2752520 | tf_op jit(solution)/shard_map/ppermute | solution.py:24
  24.2 10.4 %collective-permute-start.2 = (bf16[512,896]{1,0:T(8,128)(2,1)S(1)}, bf16[512,896]{1,0:T(8,128)(2,1)S(1)}, u32[]{:S(2)}, u32[]{:S(2)}) collective-permute-start(bf16[512,896]{1,0:T(8,128)(2,1)S(1)} %copy-done.1), channel_id=1, source_target_pairs={{0,8},{1,9},{2,10},{3,11},{4,12},{5,13},{6,14},{7,15},{8,0},{9,1},... | collective-permute-start | bytes 2752520 | tf_op jit(solution)/shard_map/ppermute | solution.py:24
  34.6 1.3 collective-permute-start.1
  35.9 0.7 fusion.37
  46.9 0.1 select_reduce_fusion
  47.0 8.4 %collective-permute-done.2 = bf16[512,896]{1,0:T(8,128)(2,1)S(1)} collective-permute-done((bf16[512,896]{1,0:T(8,128)(2,1)S(1)}, bf16[512,896]{1,0:T(8,128)(2,1)S(1)}, u32[]{:S(2)}, u32[]{:S(2)}) %collective-permute-start.2) | collective-permute-done | bytes 917536 | tf_op jit(solution)/shard_map/ppermute | solution.py:24
  55.4 20.1 %collective-permute-done.1 = bf16[512,896]{1,0:T(8,128)(2,1)} collective-permute-done((bf16[512,896]{1,0:T(8,128)(2,1)S(1)}, bf16[512,896]{1,0:T(8,128)(2,1)}, u32[]{:S(2)}, u32[]{:S(2)}) %collective-permute-start.1) | collective-permute-done | bytes 917536 | tf_op jit(solution)/shard_map/ppermute | solution.py:24
  75.5 1.6 maximum_bitcast_fusion
  77.1 2.3 copy.31
  79.4 67.6 %all-gather.3.cloned.1.call-done = bf16[19968,512]{1,0:T(8,128)(2,1)} async-done(((bf16[1248,512]{1,0:T(8,128)(2,1)}), bf16[19968,512]{1,0:T(8,128)(2,1)}) %all-gather.3.cloned.1.call-update) | async-done | bytes 20447248 | tf_op jit(solution)/shard_map/all_gather | solution.py:110
  147.0 1.1 constant_dynamic-slice_fusion.7
  148.2 0.5 reshape.150
  148.7 1.2 convolution_bitcast_fusion.4
  149.9 2.7 %collective-permute-start.12 = (f32[4,128,64]{1,2,0:T(8,128)}, f32[4,128,64]{1,2,0:T(8,128)S(1)}, u32[]{:S(2)}, u32[]{:S(2)}) collective-permute-start(f32[4,128,64]{1,2,0:T(8,128)} %convolution_bitcast_fusion.4), channel_id=1, source_target_pairs={{0,3},{1,0},{2,1},{3,2},{4,7},{5,4},{6,5},{7,6},{8,11},{9,8},{10,9... | collective-permute-start | bytes 393224 | tf_op jit(solution)/shard_map/ppermute | solution.py:24
  152.6 10.2 %fusion.14 = bf16[4,512,128]{1,2,0:T(8,128)(2,1)S(1)} fusion(bf16[4,4,1248,512]{3,2,1,0:T(8,128)(2,1)} %bitcast.108, s32[]{:T(128)S(6)} %select_n.219, bf16[4,4,128,896]{3,2,1,0:T(8,128)(2,1)} %bitcast.115), kind=kOutput, calls=%fused_computation.17 | convolution fusion | flops 2617507840 | bytes 24641540 | tf_op jit(solution)/shard_map/sif,asfj->aij/dot_general | solution.py:148
  162.8 3.5 %collective-permute-start.6 = (bf16[4,4,32,512]{3,2,1,0:T(8,128)(2,1)S(1)}, bf16[4,4,32,512]{3,2,1,0:T(8,128)(2,1)}, u32[]{:S(2)}, u32[]{:S(2)}) collective-permute-start(bf16[4,4,32,512]{3,2,1,0:T(8,128)(2,1)S(1)} %bitcast.121), channel_id=1, source_target_pairs={{0,3},{1,0},{2,1},{3,2},{4,7},{5,4},{6,5},{7,6},{8,11},{9,8},{10,9... | collective-permute-start | bytes 1572872 | tf_op jit(solution)/shard_map/ppermute | solution.py:24
  166.3 2.9 %fusion.11 = bf16[4,512,128]{1,2,0:T(8,128)(2,1)S(1)} fusion(bf16[4,4,1248,512]{3,2,1,0:T(8,128)(2,1)S(1)} %bitcast.111, s32[]{:T(128)S(6)} %select_n.217, bf16[4,4,128,896]{3,2,1,0:T(8,128)(2,1)S(1)} %bitcast.116), kind=kOutput, calls=%fused_computation.16 | convolution fusion | flops 2617507840 | bytes 24641540 | tf_op jit(solution)/shard_map/sif,asfj->aij/dot_general | solution.py:148
  169.2 1.5 collective-permute-start.5
  170.7 2.9 %fusion.8 = bf16[4,512,128]{1,2,0:T(8,128)(2,1)S(1)} fusion(bf16[4,4,1248,512]{3,2,1,0:T(8,128)(2,1)S(1)} %bitcast.112, s32[]{:T(128)S(6)} %select_n.215, bf16[4,4,128,896]{3,2,1,0:T(8,128)(2,1)S(1)} %bitcast.117), kind=kOutput, calls=%fused_computation.15 | convolution fusion | flops 2617507840 | bytes 24641540 | tf_op jit(solution)/shard_map/sif,asfj->aij/dot_general | solution.py:148
  173.6 1.8 collective-permute-start.4
  175.4 2.9 %fusion.21 = f32[4,512,128]{1,2,0:T(8,128)S(1)} fusion(bf16[4,4,1248,512]{3,2,1,0:T(8,128)(2,1)S(1)} %bitcast.113, s32[]{:T(128)S(6)} %select_n.220, bf16[4,4,128,896]{3,2,1,0:T(8,128)(2,1)S(1)} %bitcast.118), kind=kOutput, calls=%fused_computation.20 | convolution fusion | flops 2617769984 | bytes 25165828 | tf_op jit(solution)/shard_map/sif,asfj->aij/dot_general | solution.py:148
  178.4 0.9 collective-permute-start.11
  179.4 0.3 reshape.152
  179.7 18.5 %collective-permute-done.11 = f32[4,128,64]{1,2,0:T(8,128)} collective-permute-done((f32[4,128,64]{1,2,0:T(8,128)}, f32[4,128,64]{1,2,0:T(8,128)}, u32[]{:S(2)}, u32[]{:S(2)}) %collective-permute-start.11) | collective-permute-done | bytes 131104 | tf_op jit(solution)/shard_map/ppermute | solution.py:24
  198.2 1.1 add_add_fusion
  199.3 2.8 %collective-permute-start.15 = (f32[4,128,64]{1,2,0:T(8,128)S(1)}, f32[4,128,64]{1,2,0:T(8,128)S(1)}, u32[]{:S(2)}, u32[]{:S(2)}) collective-permute-start(f32[4,128,64]{1,2,0:T(8,128)S(1)} %add_add_fusion), channel_id=1, source_target_pairs={{0,12},{1,13},{2,14},{3,15},{4,0},{5,1},{6,2},{7,3},{8,4},{9,5},{1... | collective-permute-start | bytes 393224 | tf_op jit(solution)/shard_map/ppermute | solution.py:24
  202.2 2.3 collective-permute-start.14
  204.5 1.7 add_convert_fusion.1
  206.2 1.2 collective-permute-start.9
  207.4 2.7 %collective-permute-start.8 = (bf16[4,32,512]{2,1,0:T(8,128)(2,1)S(1)}, bf16[4,32,512]{2,1,0:T(8,128)(2,1)S(1)}, u32[]{:S(2)}, u32[]{:S(2)}) collective-permute-start(bf16[4,32,512]{2,1,0:T(8,128)(2,1)S(1)} %get-tuple-element.15), channel_id=1, source_target_pairs={{0,8},{1,9},{2,10},{3,11},{4,12},{5,13},{6,14},{7,15},{8,0},{9,1},... | collective-permute-start | bytes 393224 | tf_op jit(solution)/shard_map/ppermute | solution.py:24
  210.2 1.3 collective-permute-done.13
  211.5 1.2 fusion.20
  212.6 5.0 %all-to-all-start = ((bf16[16,32,512]{2,1,0:T(8,128)(2,1)}), bf16[16,32,512]{2,1,0:T(8,128)(2,1)S(1)}, u32[]{:S(2)}, u32[]{:S(2)}) async-start(bf16[16,32,512]{2,1,0:T(8,128)(2,1)} %bitcast.47), calls=%async_computation | async-start | bytes 1048576 | tf_op jit(solution)/shard_map/all_to_all | solution.py:164
  217.7 0.1 pad_maximum_fusion.1
  217.8 0.6 gather_fusion
  218.4 0.1 convert_bitcast_fusion.1
  218.5 0.7 copy.36
  219.2 0.7 reshape.154
  219.9 7.9 %all-to-all-done = bf16[16,32,512]{2,1,0:T(8,128)(2,1)S(1)} async-done(((bf16[16,32,512]{2,1,0:T(8,128)(2,1)}), bf16[16,32,512]{2,1,0:T(8,128)(2,1)S(1)}, u32[]{:S(2)}, u32[]{:S(2)}) %all-to-all-start) | async-done | bytes 524320 | tf_op jit(solution)/shard_map/all_to_all | solution.py:164
  227.8 0.1 convert_bitcast_fusion
  227.9 0.1 copy.46
  228.0 0.9 fusion.24
  (47 shorter events, 0.3 us)
Async XLA Ops:
  6.5 6.0 %copy-start.1 = (bf16[512,896]{1,0:T(8,128)(2,1)S(1)}, bf16[512,896]{1,0:T(8,128)(2,1)}, u32[]{:S(2)}) copy-start(bf16[512,896]{1,0:T(8,128)(2,1)} %param.6) | copy-start | bytes 2752516
  6.5 29.3 %copy-start.3 = (s32[4]{0:T(128)S(1)}, s32[4]{0:T(128)}, u32[]{:S(2)}) copy-start(s32[4]{0:T(128)} %param.10) | copy-start | bytes 52
  6.5 40.3 %copy-start.4 = (s32[4]{0:T(128)S(1)}, s32[4]{0:T(128)}, u32[]{:S(2)}) copy-start(s32[4]{0:T(128)} %param.11) | copy-start | bytes 52
  6.5 140.5 %all-gather.3.cloned.1.call-start = ((), (), s32[]{:S(2)}) async-start(), calls=%async_computation.1 | async-start | bytes 21725184 | tf_op jit(solution)/shard_map/all_gather | solution.py:110
  6.5 4.8 %collective-permute-start = (bf16[896,512]{1,0:T(8,128)(2,1)}, bf16[896,512]{1,0:T(8,128)(2,1)S(1)}, u32[]{:S(2)}, u32[]{:S(2)}) collective-permute-start(bf16[896,512]{1,0:T(8,128)(2,1)} %param.7), channel_id=1, source_target_pairs={{0,0},{1,1},{2,2},{3,3},{4,48},{5,49},{6,50},{7,51},{8,32},{9,33},... | collective-permute-start | bytes 2752520 | tf_op jit(solution)/shard_map/ppermute | solution.py:98
  12.6 34.4 %collective-permute-start.3 = (bf16[512,896]{1,0:T(8,128)(2,1)S(1)}, bf16[512,896]{1,0:T(8,128)(2,1)S(1)}, u32[]{:S(2)}, u32[]{:S(2)}) collective-permute-start(bf16[512,896]{1,0:T(8,128)(2,1)S(1)} %copy-done.1), channel_id=1, source_target_pairs={{0,12},{1,13},{2,14},{3,15},{4,0},{5,1},{6,2},{7,3},{8,4},{9,5},{1... | collective-permute-start | bytes 2752520 | tf_op jit(solution)/shard_map/ppermute | solution.py:24
  24.2 31.2 %collective-permute-start.2 = (bf16[512,896]{1,0:T(8,128)(2,1)S(1)}, bf16[512,896]{1,0:T(8,128)(2,1)S(1)}, u32[]{:S(2)}, u32[]{:S(2)}) collective-permute-start(bf16[512,896]{1,0:T(8,128)(2,1)S(1)} %copy-done.1), channel_id=1, source_target_pairs={{0,8},{1,9},{2,10},{3,11},{4,12},{5,13},{6,14},{7,15},{8,0},{9,1},... | collective-permute-start | bytes 2752520 | tf_op jit(solution)/shard_map/ppermute | solution.py:24
  34.6 41.0 %collective-permute-start.1 = (bf16[512,896]{1,0:T(8,128)(2,1)S(1)}, bf16[512,896]{1,0:T(8,128)(2,1)}, u32[]{:S(2)}, u32[]{:S(2)}) collective-permute-start(bf16[512,896]{1,0:T(8,128)(2,1)S(1)} %copy-done.1), channel_id=1, source_target_pairs={{0,4},{1,5},{2,6},{3,7},{4,8},{5,9},{6,10},{7,11},{8,12},{9,13},{1... | collective-permute-start | bytes 2752520 | tf_op jit(solution)/shard_map/ppermute | solution.py:24
  148.7 17.6 %slice-start = ((s8[20447232]{0:T(1024)(128)(4,1)}), s8[4194304]{0:T(1024)(128)(4,1)S(1)}, s32[]{:S(2)}) async-start(s8[20447232]{0:T(1024)(128)(4,1)} %bitcast.109), calls=%async_computation.2 | async-start | bytes 8388608
  149.9 28.5 %collective-permute-start.12 = (f32[4,128,64]{1,2,0:T(8,128)}, f32[4,128,64]{1,2,0:T(8,128)S(1)}, u32[]{:S(2)}, u32[]{:S(2)}) collective-permute-start(f32[4,128,64]{1,2,0:T(8,128)} %convolution_bitcast_fusion.4), channel_id=1, source_target_pairs={{0,3},{1,0},{2,1},{3,2},{4,7},{5,4},{6,5},{7,6},{8,11},{9,8},{10,9... | collective-permute-start | bytes 393224 | tf_op jit(solution)/shard_map/ppermute | solution.py:24
  152.5 27.2 %collective-permute-start.10 = (f32[4,128,64]{1,2,0:T(8,128)}, f32[4,128,64]{1,2,0:T(8,128)}, u32[]{:S(2)}, u32[]{:S(2)}) collective-permute-start(f32[4,128,64]{1,2,0:T(8,128)} %convolution_bitcast_fusion.4), channel_id=1, source_target_pairs={{0,1},{1,2},{2,3},{3,0},{4,5},{5,6},{6,7},{7,4},{8,9},{9,10},{10,1... | collective-permute-start | bytes 393224 | tf_op jit(solution)/shard_map/ppermute | solution.py:24
  152.5 13.7 %slice-start.1 = ((s8[20447232]{0:T(1024)(128)(4,1)}), s8[4194304]{0:T(1024)(128)(4,1)S(1)}, s32[]{:S(2)}) async-start(s8[20447232]{0:T(1024)(128)(4,1)} %bitcast.109), calls=%async_computation.3 | async-start | bytes 8388608
  152.5 13.7 %slice-start.2 = ((s8[20447232]{0:T(1024)(128)(4,1)}), s8[4194304]{0:T(1024)(128)(4,1)S(1)}, s32[]{:S(2)}) async-start(s8[20447232]{0:T(1024)(128)(4,1)} %bitcast.109), calls=%async_computation.4 | async-start | bytes 8388608
  152.6 13.7 %slice-start.3 = ((s8[20447232]{0:T(1024)(128)(4,1)}), s8[4194304]{0:T(1024)(128)(4,1)S(1)}, s32[]{:S(2)}) async-start(s8[20447232]{0:T(1024)(128)(4,1)} %bitcast.109), calls=%async_computation.5 | async-start | bytes 8388608
  152.6 13.7 %slice-start.4 = ((s8[20447232]{0:T(1024)(128)(4,1)}), s8[3670016]{0:T(1024)(128)(4,1)S(1)}, s32[]{:S(2)}) async-start(s8[20447232]{0:T(1024)(128)(4,1)} %bitcast.109), calls=%async_computation.6 | async-start | bytes 7340032
  152.6 13.7 %copy-start = (bf16[4,4,4,32,896]{4,3,2,1,0:T(8,128)(2,1)S(1)}, bf16[4,4,4,32,896]{4,3,2,1,0:T(8,128)(2,1)}, u32[]{:S(2)}) copy-start(bf16[4,4,4,32,896]{4,3,2,1,0:T(8,128)(2,1)} %copy.31) | copy-start | bytes 11010052
  162.8 39.4 %collective-permute-start.6 = (bf16[4,4,32,512]{3,2,1,0:T(8,128)(2,1)S(1)}, bf16[4,4,32,512]{3,2,1,0:T(8,128)(2,1)}, u32[]{:S(2)}, u32[]{:S(2)}) collective-permute-start(bf16[4,4,32,512]{3,2,1,0:T(8,128)(2,1)S(1)} %bitcast.121), channel_id=1, source_target_pairs={{0,3},{1,0},{2,1},{3,2},{4,7},{5,4},{6,5},{7,6},{8,11},{9,8},{10,9... | collective-permute-start | bytes 1572872 | tf_op jit(solution)/shard_map/ppermute | solution.py:24
  169.2 35.3 %collective-permute-start.5 = (bf16[4,4,32,512]{3,2,1,0:T(8,128)(2,1)S(1)}, bf16[4,4,32,512]{3,2,1,0:T(8,128)(2,1)}, u32[]{:S(2)}, u32[]{:S(2)}) collective-permute-start(bf16[4,4,32,512]{3,2,1,0:T(8,128)(2,1)S(1)} %bitcast.120), channel_id=1, source_target_pairs={{0,2},{1,3},{2,0},{3,1},{4,6},{5,7},{6,4},{7,5},{8,10},{9,11},{10,... | collective-permute-start | bytes 1572872 | tf_op jit(solution)/shard_map/ppermute | solution.py:24
  173.6 30.9 %collective-permute-start.4 = (bf16[4,4,32,512]{3,2,1,0:T(8,128)(2,1)S(1)}, bf16[4,4,32,512]{3,2,1,0:T(8,128)(2,1)}, u32[]{:S(2)}, u32[]{:S(2)}) collective-permute-start(bf16[4,4,32,512]{3,2,1,0:T(8,128)(2,1)S(1)} %bitcast.122), channel_id=1, source_target_pairs={{0,1},{1,2},{2,3},{3,0},{4,5},{5,6},{6,7},{7,4},{8,9},{9,10},{10,1... | collective-permute-start | bytes 1572872 | tf_op jit(solution)/shard_map/ppermute | solution.py:24
  178.4 1.0 copy-start.2
  178.4 19.8 %collective-permute-start.11 = (f32[4,128,64]{1,2,0:T(8,128)}, f32[4,128,64]{1,2,0:T(8,128)}, u32[]{:S(2)}, u32[]{:S(2)}) collective-permute-start(f32[4,128,64]{1,2,0:T(8,128)} %convolution_bitcast_fusion.4), channel_id=1, source_target_pairs={{0,2},{1,3},{2,0},{3,1},{4,6},{5,7},{6,4},{7,5},{8,10},{9,11},{10,... | collective-permute-start | bytes 393224 | tf_op jit(solution)/shard_map/ppermute | solution.py:24
  199.3 10.8 %collective-permute-start.15 = (f32[4,128,64]{1,2,0:T(8,128)S(1)}, f32[4,128,64]{1,2,0:T(8,128)S(1)}, u32[]{:S(2)}, u32[]{:S(2)}) collective-permute-start(f32[4,128,64]{1,2,0:T(8,128)S(1)} %add_add_fusion), channel_id=1, source_target_pairs={{0,12},{1,13},{2,14},{3,15},{4,0},{5,1},{6,2},{7,3},{8,4},{9,5},{1... | collective-permute-start | bytes 393224 | tf_op jit(solution)/shard_map/ppermute | solution.py:24
  202.2 9.3 %collective-permute-start.13 = (f32[4,128,64]{1,2,0:T(8,128)S(1)}, f32[4,128,64]{1,2,0:T(8,128)S(1)}, u32[]{:S(2)}, u32[]{:S(2)}) collective-permute-start(f32[4,128,64]{1,2,0:T(8,128)S(1)} %add_add_fusion), channel_id=1, source_target_pairs={{0,4},{1,5},{2,6},{3,7},{4,8},{5,9},{6,10},{7,11},{8,12},{9,13},{1... | collective-permute-start | bytes 393224 | tf_op jit(solution)/shard_map/ppermute | solution.py:24
  202.2 9.3 %collective-permute-start.14 = (f32[4,128,64]{1,2,0:T(8,128)S(1)}, f32[4,128,64]{1,2,0:T(8,128)S(1)}, u32[]{:S(2)}, u32[]{:S(2)}) collective-permute-start(f32[4,128,64]{1,2,0:T(8,128)S(1)} %add_add_fusion), channel_id=1, source_target_pairs={{0,8},{1,9},{2,10},{3,11},{4,12},{5,13},{6,14},{7,15},{8,0},{9,1},... | collective-permute-start | bytes 393224 | tf_op jit(solution)/shard_map/ppermute | solution.py:24
  206.2 11.5 %collective-permute-start.9 = (bf16[4,32,512]{2,1,0:T(8,128)(2,1)S(1)}, bf16[4,32,512]{2,1,0:T(8,128)(2,1)S(1)}, u32[]{:S(2)}, u32[]{:S(2)}) collective-permute-start(bf16[4,32,512]{2,1,0:T(8,128)(2,1)S(1)} %get-tuple-element.14), channel_id=1, source_target_pairs={{0,12},{1,13},{2,14},{3,15},{4,0},{5,1},{6,2},{7,3},{8,4},{9,5},{1... | collective-permute-start | bytes 393224 | tf_op jit(solution)/shard_map/ppermute | solution.py:24
  207.4 10.3 %collective-permute-start.8 = (bf16[4,32,512]{2,1,0:T(8,128)(2,1)S(1)}, bf16[4,32,512]{2,1,0:T(8,128)(2,1)S(1)}, u32[]{:S(2)}, u32[]{:S(2)}) collective-permute-start(bf16[4,32,512]{2,1,0:T(8,128)(2,1)S(1)} %get-tuple-element.15), channel_id=1, source_target_pairs={{0,8},{1,9},{2,10},{3,11},{4,12},{5,13},{6,14},{7,15},{8,0},{9,1},... | collective-permute-start | bytes 393224 | tf_op jit(solution)/shard_map/ppermute | solution.py:24
  210.1 7.5 %collective-permute-start.7 = (bf16[4,32,512]{2,1,0:T(8,128)(2,1)S(1)}, bf16[4,32,512]{2,1,0:T(8,128)(2,1)S(1)}, u32[]{:S(2)}, u32[]{:S(2)}) collective-permute-start(bf16[4,32,512]{2,1,0:T(8,128)(2,1)S(1)} %get-tuple-element.16), channel_id=1, source_target_pairs={{0,4},{1,5},{2,6},{3,7},{4,8},{5,9},{6,10},{7,11},{8,12},{9,13},{1... | collective-permute-start | bytes 393224 | tf_op jit(solution)/shard_map/ppermute | solution.py:24
  212.6 15.1 %all-to-all-start = ((bf16[16,32,512]{2,1,0:T(8,128)(2,1)}), bf16[16,32,512]{2,1,0:T(8,128)(2,1)S(1)}, u32[]{:S(2)}, u32[]{:S(2)}) async-start(bf16[16,32,512]{2,1,0:T(8,128)(2,1)} %bitcast.47), calls=%async_computation | async-start | bytes 1048576 | tf_op jit(solution)/shard_map/all_to_all | solution.py:164
Sparse Core Ops, SparseCore 0:
  12.7 134.3 all-gather.2

commit v12 on v10

--- a/solution.py
+++ b/solution.py
@@ -97,24 +97,28 @@
                 pairs.append((p1 * tensor_count + y1 * side + x1, p2 * tensor_count + y2 * side + x1))
     moved = lax.ppermute(down_weight, ("pool", "tensor"), pairs)
 
-    shrink_rows = held * feat * rank // width
-    expand_rows = held * column_span * rank // width
+    half = width // 2
+    shrink_rows = held * feat * rank // half
+    expand_rows = held * column_span * rank // half
     pack = jnp.concatenate(
         [
-            moved,
-            adapter_shrink.reshape(shrink_rows, width),
-            adapter_expand.reshape(expand_rows, width),
+            moved[:, :half],
+            adapter_shrink.reshape(shrink_rows, half),
+            adapter_expand.reshape(expand_rows, half),
         ],
         axis=0,
     )
     gathered = lax.all_gather(pack, "pool", axis=0, tiled=False)
     plane_rows = gathered.shape[1]
-    w_quarter = gathered.reshape(quarter, side, plane_rows, width)
+    w_first = gathered.reshape(quarter, side, plane_rows, half)
     shrink_all = gathered[:, feat:feat + shrink_rows, :].reshape(
-        pool_count * held, shrink_rows // held, width
+        pool_count * held, shrink_rows // held, half
     )
     expand_all = gathered[:, feat + shrink_rows:, :].reshape(
-        pool_count * held, expand_rows // held, width
+        pool_count * held, expand_rows // held, half
+    )
+    w_second = lax.all_gather(moved[:, half:], "pool", axis=0, tiled=False).reshape(
+        quarter, side, feat, half
     )
 
     pieces = [hidden] + [tensor_shift(hidden, side, s, True) for s in range(1, side)]
@@ -122,7 +126,7 @@
     hidden_column = jnp.transpose(hidden_column, (2, 0, 1, 3, 4)).reshape(
         side, side, side * own_rows, feat
     )
-    hidden_column = jnp.pad(hidden_column, ((0, 0), (0, 0), (0, 0), (0, plane_rows - feat)))
+    hidden_padded = jnp.pad(hidden_column, ((0, 0), (0, 0), (0, 0), (0, plane_rows - feat)))
 
     first = jnp.take(shrink_all, block_adapter, axis=0).reshape(block_count, feat, rank)
     second = jnp.take(expand_all, block_adapter, axis=0).reshape(block_count, column_span, rank)
@@ -134,16 +138,21 @@
     )
     delta = (adapter_scale_factor * enlarged_rows).astype(jnp.bfloat16).reshape(input_rows, column_span)
 
-    def rows_for(owner_x):
-        rows = lax.dynamic_index_in_dim(hidden_column, owner_x, axis=0, keepdims=False)
-        piece = jnp.einsum("sif,asfj->aij", rows, w_quarter, preferred_element_type=jnp.float32)
-        return piece.astype(jnp.bfloat16).reshape(quarter, side, own_rows, width)
+    def reduce_over_x(hidden_rows, w_half):
+        def rows_for(owner_x):
+            rows = lax.dynamic_index_in_dim(hidden_rows, owner_x, axis=0, keepdims=False)
+            piece = jnp.einsum("sif,asfj->aij", rows, w_half, preferred_element_type=jnp.float32)
+            return piece.astype(jnp.bfloat16).reshape(quarter, side, own_rows, half)
 
-    total = None
-    for s in range(1, side):
-        arrived = tensor_shift(rows_for((my_x + s) % side), side, s, False).astype(jnp.float32)
-        total = arrived if total is None else total + arrived
-    total = (total + rows_for(my_x).astype(jnp.float32)).astype(jnp.bfloat16)
+        summed = None
+        for s in range(1, side):
+            arrived = tensor_shift(rows_for((my_x + s) % side), side, s, False).astype(jnp.float32)
+            summed = arrived if summed is None else summed + arrived
+        return (summed + rows_for(my_x).astype(jnp.float32)).astype(jnp.bfloat16)
+
+    total = jnp.concatenate(
+        [reduce_over_x(hidden_padded, w_first), reduce_over_x(hidden_column, w_second)], axis=3
+    )
 
     got = [lax.dynamic_index_in_dim(total, my_y, axis=1, keepdims=False)]
     for s in range(1, side):

time: 235 us -> 246 us (1.047)
  matrix products: 21.3 us -> 36.8 us
  waiting for transfers between devices: 123 us -> 111 us
  starting transfers between devices: 48.1 us -> 58 us
  local copies, waits for them, and re-layouts: 20.4 us -> 17.8 us
    all_gather x1, waiting for transfers between devices: 67.6 us -> 51.3 us  [shards(): gathered = lax.all_gather(pack, 'pool', axis=0, tiled=False)]
    dot_general x4 -> x8, matrix products: 18.9 us -> 35 us  [rows_for(): jnp.einsum('sif,asfj->aij', rows, w_half, preferred_element_type=jnp.floa...]
    ppermute x15 -> x18, starting transfers between devices: 41.5 us -> 48.9 us  [tensor_shift(): return lax.ppermute(x, 'tensor', perm)]
    ppermute x15 -> x18, waiting for transfers between devices: 48.5 us -> 50.3 us  [tensor_shift(): return lax.ppermute(x, 'tensor', perm)]
  transfers between devices with their start and end apart: 18 -> 22, of which waited for: 8 -> 10; matrix products, arithmetic and copies ran while one was open for 15% -> 17% of each run, Pallas kernels for 0% -> 0%
where the time goes in v12:
time: 246 us; the launch traced here: 245 us
  waiting for transfers between devices  111 us (45%)
  starting transfers between devices  58 us (24%)
  matrix products  36.8 us (15%)
  local copies, waits for them, and re-layouts  17.8 us (7%)
  between operations  13.9 us (6%)
  other arithmetic  7.22 us (3%)
    all_gather x1, waiting for transfers between devices, shards(): gathered = lax.all_gather(pack, 'pool', axis=0, tiled=False)  51.3 us
    ppermute x18, waiting for transfers between devices, tensor_shift(): return lax.ppermute(x, 'tensor', perm)  50.3 us
    ppermute x18, starting transfers between devices, tensor_shift(): return lax.ppermute(x, 'tensor', perm)  48.9 us
    dot_general x8, matrix products, rows_for(): jnp.einsum('sif,asfj->aij', rows, w_half, preferred_element_type=jnp.floa...  35 us
    all_to_all x1, waiting for transfers between devices, shards(): lax.all_to_all(delta, 'tensor', split_axis=0, concat_axis=1, tiled=True)  7.86 us
    all_to_all x1, starting transfers between devices, shards(): lax.all_to_all(delta, 'tensor', split_axis=0, concat_axis=1, tiled=True)  7.11 us
  transfers between devices with their start and end apart: 22, of which 10 were waited for; matrix products, arithmetic and copies ran while one was open for 17% of the time, Pallas kernels for 0%

profile of v12, /device:TPU:0, one launch (start us, length us, event | category | flops | bytes accessed | tf_op | source)
XLA Modules:
  0.0 245.1 jit_solution(8480379816504983041)
XLA Ops:
  6.5 2.0 collective-permute-start
  8.5 0.8 fusion.86
  9.4 1.1 copy.34
  10.7 1.2 copy.33
  12.3 1.1 pad_maximum_fusion
  13.4 14.4 %collective-permute-start.3 = (bf16[512,896]{1,0:T(8,128)(2,1)S(1)}, bf16[512,896]{1,0:T(8,128)(2,1)S(1)}, u32[]{:S(2)}, u32[]{:S(2)}) collective-permute-start(bf16[512,896]{1,0:T(8,128)(2,1)S(1)} %copy-done.4), channel_id=1, source_target_pairs={{0,12},{1,13},{2,14},{3,15},{4,0},{5,1},{6,2},{7,3},{8,4},{9,5},{1... | collective-permute-start | bytes 2752520 | tf_op jit(solution)/shard_map/ppermute | solution.py:24
  27.8 10.4 %collective-permute-start.2 = (bf16[512,896]{1,0:T(8,128)(2,1)S(1)}, bf16[512,896]{1,0:T(8,128)(2,1)S(1)}, u32[]{:S(2)}, u32[]{:S(2)}) collective-permute-start(bf16[512,896]{1,0:T(8,128)(2,1)S(1)} %copy-done.4), channel_id=1, source_target_pairs={{0,8},{1,9},{2,10},{3,11},{4,12},{5,13},{6,14},{7,15},{8,0},{9,1},... | collective-permute-start | bytes 2752520 | tf_op jit(solution)/shard_map/ppermute | solution.py:24
  38.2 1.3 collective-permute-start.1
  40.4 5.2 %collective-permute-done.3 = bf16[512,896]{1,0:T(8,128)(2,1)S(1)} collective-permute-done((bf16[512,896]{1,0:T(8,128)(2,1)S(1)}, bf16[512,896]{1,0:T(8,128)(2,1)S(1)}, u32[]{:S(2)}, u32[]{:S(2)}) %collective-permute-start.3) | collective-permute-done | bytes 917536 | tf_op jit(solution)/shard_map/ppermute | solution.py:24
  45.6 13.4 %collective-permute-done.2 = bf16[512,896]{1,0:T(8,128)(2,1)S(1)} collective-permute-done((bf16[512,896]{1,0:T(8,128)(2,1)S(1)}, bf16[512,896]{1,0:T(8,128)(2,1)S(1)}, u32[]{:S(2)}, u32[]{:S(2)}) %collective-permute-start.2) | collective-permute-done | bytes 917536 | tf_op jit(solution)/shard_map/ppermute | solution.py:24
  59.0 20.1 %collective-permute-done.1 = bf16[512,896]{1,0:T(8,128)(2,1)} collective-permute-done((bf16[512,896]{1,0:T(8,128)(2,1)S(1)}, bf16[512,896]{1,0:T(8,128)(2,1)}, u32[]{:S(2)}, u32[]{:S(2)}) %collective-permute-start.1) | collective-permute-done | bytes 917536 | tf_op jit(solution)/shard_map/ppermute | solution.py:24
  79.1 1.6 maximum_bitcast_fusion
  80.7 2.3 copy.35
  83.0 1.9 all-gather.7.cloned.1.call-done
  84.9 4.6 %fusion.27 = bf16[128,4,256]{2,0,1:T(8,128)(2,1)S(1)} fusion(bf16[4,4,896,256]{3,2,1,0:T(8,128)(2,1)} %bitcast.180, bf16[4,4,128,896]{3,2,1,0:T(8,128)(2,1)} %bitcast.172, s32[]{:T(128)S(6)} %select_n.166), kind=kOutput, calls=%fused_computation.28 | convolution fusion | flops 939655168 | bytes 8519684 | tf_op jit(solution)/shard_map/sif,asfj->aij/dot_general | solution.py:144
  89.6 2.8 %collective-permute-start.9 = (bf16[4,4,32,256]{3,2,1,0:T(8,128)(2,1)S(1)}, bf16[4,4,32,256]{3,2,1,0:T(8,128)(2,1)S(1)}, u32[]{:S(2)}, u32[]{:S(2)}) collective-permute-start(bf16[4,4,32,256]{3,2,1,0:T(8,128)(2,1)S(1)} %bitcast.196), channel_id=1, source_target_pairs={{0,3},{1,0},{2,1},{3,2},{4,7},{5,4},{6,5},{7,6},{8,11},{9,8},{10,9... | collective-permute-start | bytes 786440 | tf_op jit(solution)/shard_map/ppermute | solution.py:24
  92.3 4.3 %fusion.26 = bf16[128,4,256]{2,0,1:T(8,128)(2,1)S(1)} fusion(bf16[4,4,896,256]{3,2,1,0:T(8,128)(2,1)} %bitcast.181, bf16[4,4,128,896]{3,2,1,0:T(8,128)(2,1)S(1)} %bitcast.175, s32[]{:T(128)S(6)} %select_n.164), kind=kOutput, calls=%fused_computation.27 | convolution fusion | flops 939655168 | bytes 8519684 | tf_op jit(solution)/shard_map/sif,asfj->aij/dot_general | solution.py:144
  96.6 1.2 collective-permute-start.8
  97.8 1.1 fusion.25
  99.0 0.8 collective-permute-start.7
  99.8 1.1 fusion.29
  100.9 6.5 %collective-permute-done.8 = bf16[4,4,32,256]{3,2,1,0:T(8,128)(2,1)S(1)} collective-permute-done((bf16[4,4,32,256]{3,2,1,0:T(8,128)(2,1)S(1)}, bf16[4,4,32,256]{3,2,1,0:T(8,128)(2,1)S(1)}, u32[]{:S(2)}, u32[]{:S(2)}) %collective-permute-start.8) | collective-permute-done | bytes 262176 | tf_op jit(solution)/shard_map/ppermute | solution.py:24
  107.4 4.6 %collective-permute-done.7 = bf16[4,4,32,256]{3,2,1,0:T(8,128)(2,1)S(1)} collective-permute-done((bf16[4,4,32,256]{3,2,1,0:T(8,128)(2,1)S(1)}, bf16[4,4,32,256]{3,2,1,0:T(8,128)(2,1)S(1)}, u32[]{:S(2)}, u32[]{:S(2)}) %collective-permute-start.7) | collective-permute-done | bytes 262176 | tf_op jit(solution)/shard_map/ppermute | solution.py:24
  112.2 51.3 %all-gather.5.cloned.1.call-done = bf16[25600,256]{1,0:T(8,128)(2,1)} async-done(((bf16[1600,256]{1,0:T(8,128)(2,1)}), bf16[25600,256]{1,0:T(8,128)(2,1)}) %all-gather.5.cloned.1.call-update) | async-done | bytes 13107216 | tf_op jit(solution)/shard_map/all_gather | solution.py:111
  163.5 7.7 %fusion.36 = bf16[4,256,128]{1,2,0:T(8,128)(2,1)} fusion(bf16[4,4,1600,256]{3,2,1,0:T(8,128)(2,1)} %bitcast.166, s32[]{:T(128)S(6)} %select_n.166, bf16[4,4,128,896]{3,2,1,0:T(8,128)(2,1)} %bitcast.173), kind=kOutput, calls=%fused_computation.33 | convolution fusion | flops 1677852672 | bytes 17039364 | tf_op jit(solution)/shard_map/sif,asfj->aij/dot_general | solution.py:144
  171.2 1.1 copy-done
  172.3 1.0 copy-done.2
  173.3 1.9 fusion.33
  175.2 2.1 slice.24
  177.3 2.6 %gather_fusion.1 = bf16[4,224,256]{2,1,0:T(8,128)(2,1)S(1)} fusion(bf16[32,224,256]{2,1,0:T(8,128)(2,1)} %bitcast.186, s32[1024]{0:T(1024)S(1)} %pad_clamp_fusion), kind=kCustom, calls=%fused_computation.1 | custom fusion | bytes 917520 | tf_op jit(solution)/shard_map/jit(_take)/gather | solution.py:131
  180.9 2.8 %collective-permute-start.15 = (f32[4,128,64]{1,2,0:T(8,128)S(1)}, f32[4,128,64]{1,2,0:T(8,128)S(1)}, u32[]{:S(2)}, u32[]{:S(2)}) collective-permute-start(f32[4,128,64]{1,2,0:T(8,128)S(1)} %convolution_bitcast_fusion.4), channel_id=1, source_target_pairs={{0,3},{1,0},{2,1},{3,2},{4,7},{5,4},{6,5},{7,6},{8,11},{9,8},{10,9... | collective-permute-start | bytes 393224 | tf_op jit(solution)/shard_map/ppermute | solution.py:24
  183.7 7.6 %fusion.30 = bf16[4,256,128]{1,2,0:T(8,128)(2,1)} fusion(bf16[4,4,1600,256]{3,2,1,0:T(8,128)(2,1)} %bitcast.167, s32[]{:T(128)S(6)} %select_n.162, bf16[4,4,128,896]{3,2,1,0:T(8,128)(2,1)} %bitcast.174), kind=kOutput, calls=%fused_computation.31 | convolution fusion | flops 1677852672 | bytes 17039364 | tf_op jit(solution)/shard_map/sif,asfj->aij/dot_general | solution.py:144
  191.3 2.5 collective-permute-start.14
  193.7 1.3 collective-permute-start.6
  195.1 2.4 collective-permute-start.5
  197.5 6.7 %fusion.42 = f32[4,256,128]{1,2,0:T(8,128)S(1)} fusion(bf16[4,4,1600,256]{3,2,1,0:T(8,128)(2,1)} %bitcast.168, s32[]{:T(128)S(6)} %select_n.167, bf16[4,4,128,896]{3,2,1,0:T(8,128)(2,1)S(1)} %bitcast.179), kind=kOutput, calls=%fused_computation.35 | convolution fusion | flops 1677983744 | bytes 17301508 | tf_op jit(solution)/shard_map/sif,asfj->aij/dot_general | solution.py:144
  204.2 1.7 slice.25
  206.9 1.1 add_add_fusion
  207.9 2.8 %collective-permute-start.18 = (f32[4,128,64]{1,2,0:T(8,128)S(1)}, f32[4,128,64]{1,2,0:T(8,128)S(1)}, u32[]{:S(2)}, u32[]{:S(2)}) collective-permute-start(f32[4,128,64]{1,2,0:T(8,128)S(1)} %add_add_fusion), channel_id=1, source_target_pairs={{0,12},{1,13},{2,14},{3,15},{4,0},{5,1},{6,2},{7,3},{8,4},{9,5},{1... | collective-permute-start | bytes 393224 | tf_op jit(solution)/shard_map/ppermute | solution.py:24
  210.7 2.3 collective-permute-start.17
  213.0 1.3 add_convert_fusion.2
  214.3 1.8 collective-permute-start.12
  216.2 2.1 collective-permute-start.11
  218.6 1.2 fusion.12
  219.8 7.1 %all-to-all-start = ((bf16[16,32,512]{2,1,0:T(8,128)(2,1)}), bf16[16,32,512]{2,1,0:T(8,128)(2,1)S(1)}, u32[]{:S(2)}, u32[]{:S(2)}) async-start(bf16[16,32,512]{2,1,0:T(8,128)(2,1)} %bitcast.70), calls=%async_computation | async-start | bytes 1048576 | tf_op jit(solution)/shard_map/all_to_all | solution.py:164
  228.5 0.7 reshape.183
  229.2 7.9 %all-to-all-done = bf16[16,32,512]{2,1,0:T(8,128)(2,1)S(1)} async-done(((bf16[16,32,512]{2,1,0:T(8,128)(2,1)}), bf16[16,32,512]{2,1,0:T(8,128)(2,1)S(1)}, u32[]{:S(2)}, u32[]{:S(2)}) %all-to-all-start) | async-done | bytes 524320 | tf_op jit(solution)/shard_map/all_to_all | solution.py:164
  237.3 0.9 fusion.55
  (65 shorter events, 5.6 us)
Async XLA Ops:
  6.5 6.8 %copy-start.4 = (bf16[512,896]{1,0:T(8,128)(2,1)S(1)}, bf16[512,896]{1,0:T(8,128)(2,1)}, u32[]{:S(2)}) copy-start(bf16[512,896]{1,0:T(8,128)(2,1)} %param.6) | copy-start | bytes 2752516
  6.5 33.1 %copy-start.6 = (s32[4]{0:T(128)S(1)}, s32[4]{0:T(128)}, u32[]{:S(2)}) copy-start(s32[4]{0:T(128)} %param.10) | copy-start | bytes 52
  6.5 33.2 %copy-start.8 = (s32[4]{0:T(128)S(1)}, s32[4]{0:T(128)}, u32[]{:S(2)}) copy-start(s32[4]{0:T(128)} %param.11) | copy-start | bytes 52
  6.5 78.4 %all-gather.7.cloned.1.call-start = ((), (), s32[]{:S(2)}) async-start(), calls=%async_computation.2 | async-start | bytes 7798784 | tf_op jit(solution)/shard_map/all_gather | solution.py:120
  6.5 2.0 collective-permute-start
  9.4 154.1 %all-gather.5.cloned.1.call-start = ((), (), s32[]{:S(2)}) async-start(), calls=%async_computation.1 | async-start | bytes 13926400 | tf_op jit(solution)/shard_map/all_gather | solution.py:111
  13.4 32.3 %collective-permute-start.3 = (bf16[512,896]{1,0:T(8,128)(2,1)S(1)}, bf16[512,896]{1,0:T(8,128)(2,1)S(1)}, u32[]{:S(2)}, u32[]{:S(2)}) collective-permute-start(bf16[512,896]{1,0:T(8,128)(2,1)S(1)} %copy-done.4), channel_id=1, source_target_pairs={{0,12},{1,13},{2,14},{3,15},{4,0},{5,1},{6,2},{7,3},{8,4},{9,5},{1... | collective-permute-start | bytes 2752520 | tf_op jit(solution)/shard_map/ppermute | solution.py:24
  27.8 31.2 %collective-permute-start.2 = (bf16[512,896]{1,0:T(8,128)(2,1)S(1)}, bf16[512,896]{1,0:T(8,128)(2,1)S(1)}, u32[]{:S(2)}, u32[]{:S(2)}) collective-permute-start(bf16[512,896]{1,0:T(8,128)(2,1)S(1)} %copy-done.4), channel_id=1, source_target_pairs={{0,8},{1,9},{2,10},{3,11},{4,12},{5,13},{6,14},{7,15},{8,0},{9,1},... | collective-permute-start | bytes 2752520 | tf_op jit(solution)/shard_map/ppermute | solution.py:24
  38.2 41.0 %collective-permute-start.1 = (bf16[512,896]{1,0:T(8,128)(2,1)S(1)}, bf16[512,896]{1,0:T(8,128)(2,1)}, u32[]{:S(2)}, u32[]{:S(2)}) collective-permute-start(bf16[512,896]{1,0:T(8,128)(2,1)S(1)} %copy-done.4), channel_id=1, source_target_pairs={{0,4},{1,5},{2,6},{3,7},{4,8},{5,9},{6,10},{7,11},{8,12},{9,13},{1... | collective-permute-start | bytes 2752520 | tf_op jit(solution)/shard_map/ppermute | solution.py:24
  84.9 7.4 %copy-start.1 = (bf16[4,4,4,32,896]{4,3,2,1,0:T(8,128)(2,1)S(1)}, bf16[4,4,4,32,896]{4,3,2,1,0:T(8,128)(2,1)}, u32[]{:S(2)}) copy-start(bf16[4,4,4,32,896]{4,3,2,1,0:T(8,128)(2,1)} %copy.35) | copy-start | bytes 11010052
  84.9 12.9 %slice-start = ((s8[7340032]{0:T(1024)(128)(4,1)}), s8[4194304]{0:T(1024)(128)(4,1)S(1)}, s32[]{:S(2)}) async-start(s8[7340032]{0:T(1024)(128)(4,1)} %bitcast.182), calls=%async_computation.3 | async-start | bytes 8388608
  89.5 8.3 %slice-start.1 = ((s8[7340032]{0:T(1024)(128)(4,1)}), s8[3145728]{0:T(1024)(128)(4,1)S(1)}, s32[]{:S(2)}) async-start(s8[7340032]{0:T(1024)(128)(4,1)} %bitcast.182), calls=%async_computation.4 | async-start | bytes 6291456
  89.6 11.4 %collective-permute-start.9 = (bf16[4,4,32,256]{3,2,1,0:T(8,128)(2,1)S(1)}, bf16[4,4,32,256]{3,2,1,0:T(8,128)(2,1)S(1)}, u32[]{:S(2)}, u32[]{:S(2)}) collective-permute-start(bf16[4,4,32,256]{3,2,1,0:T(8,128)(2,1)S(1)} %bitcast.196), channel_id=1, source_target_pairs={{0,3},{1,0},{2,1},{3,2},{4,7},{5,4},{6,5},{7,6},{8,11},{9,8},{10,9... | collective-permute-start | bytes 786440 | tf_op jit(solution)/shard_map/ppermute | solution.py:24
  96.6 10.8 %collective-permute-start.8 = (bf16[4,4,32,256]{3,2,1,0:T(8,128)(2,1)S(1)}, bf16[4,4,32,256]{3,2,1,0:T(8,128)(2,1)S(1)}, u32[]{:S(2)}, u32[]{:S(2)}) collective-permute-start(bf16[4,4,32,256]{3,2,1,0:T(8,128)(2,1)S(1)} %bitcast.197), channel_id=1, source_target_pairs={{0,2},{1,3},{2,0},{3,1},{4,6},{5,7},{6,4},{7,5},{8,10},{9,11},{10,... | collective-permute-start | bytes 786440 | tf_op jit(solution)/shard_map/ppermute | solution.py:24
  99.0 13.1 %collective-permute-start.7 = (bf16[4,4,32,256]{3,2,1,0:T(8,128)(2,1)S(1)}, bf16[4,4,32,256]{3,2,1,0:T(8,128)(2,1)S(1)}, u32[]{:S(2)}, u32[]{:S(2)}) collective-permute-start(bf16[4,4,32,256]{3,2,1,0:T(8,128)(2,1)S(1)} %bitcast.198), channel_id=1, source_target_pairs={{0,1},{1,2},{2,3},{3,0},{4,5},{5,6},{6,7},{7,4},{8,9},{9,10},{10,1... | collective-permute-start | bytes 786440 | tf_op jit(solution)/shard_map/ppermute | solution.py:24
  163.5 8.8 %copy-start = (bf16[25600,256]{1,0:T(8,128)(2,1)S(1)}, bf16[25600,256]{1,0:T(8,128)(2,1)}, u32[]{:S(2)}) copy-start(bf16[25600,256]{1,0:T(8,128)(2,1)} %all-gather.5.cloned.1.call-done) | copy-start | bytes 39321604
  163.5 9.9 %copy-start.2 = (bf16[4,4,4,32,896]{4,3,2,1,0:T(8,128)(2,1)S(1)}, bf16[4,4,4,32,896]{4,3,2,1,0:T(8,128)(2,1)}, u32[]{:S(2)}) copy-start(bf16[4,4,4,32,896]{4,3,2,1,0:T(8,128)(2,1)} %copy.35) | copy-start | bytes 11010052
  180.9 16.6 %copy-start.3 = (bf16[4,4,4,32,896]{4,3,2,1,0:T(8,128)(2,1)S(1)}, bf16[4,4,4,32,896]{4,3,2,1,0:T(8,128)(2,1)}, u32[]{:S(2)}) copy-start(bf16[4,4,4,32,896]{4,3,2,1,0:T(8,128)(2,1)} %copy.35) | copy-start | bytes 11010052
  180.9 16.5 %collective-permute-start.15 = (f32[4,128,64]{1,2,0:T(8,128)S(1)}, f32[4,128,64]{1,2,0:T(8,128)S(1)}, u32[]{:S(2)}, u32[]{:S(2)}) collective-permute-start(f32[4,128,64]{1,2,0:T(8,128)S(1)} %convolution_bitcast_fusion.4), channel_id=1, source_target_pairs={{0,3},{1,0},{2,1},{3,2},{4,7},{5,4},{6,5},{7,6},{8,11},{9,8},{10,9... | collective-permute-start | bytes 393224 | tf_op jit(solution)/shard_map/ppermute | solution.py:24
  191.3 15.6 %collective-permute-start.13 = (f32[4,128,64]{1,2,0:T(8,128)S(1)}, f32[4,128,64]{1,2,0:T(8,128)}, u32[]{:S(2)}, u32[]{:S(2)}) collective-permute-start(f32[4,128,64]{1,2,0:T(8,128)S(1)} %convolution_bitcast_fusion.4), channel_id=1, source_target_pairs={{0,1},{1,2},{2,3},{3,0},{4,5},{5,6},{6,7},{7,4},{8,9},{9,10},{10,1... | collective-permute-start | bytes 393224 | tf_op jit(solution)/shard_map/ppermute | solution.py:24
  191.3 15.6 %collective-permute-start.14 = (f32[4,128,64]{1,2,0:T(8,128)S(1)}, f32[4,128,64]{1,2,0:T(8,128)}, u32[]{:S(2)}, u32[]{:S(2)}) collective-permute-start(f32[4,128,64]{1,2,0:T(8,128)S(1)} %convolution_bitcast_fusion.4), channel_id=1, source_target_pairs={{0,2},{1,3},{2,0},{3,1},{4,6},{5,7},{6,4},{7,5},{8,10},{9,11},{10,... | collective-permute-start | bytes 393224 | tf_op jit(solution)/shard_map/ppermute | solution.py:24
  193.7 17.0 %collective-permute-start.6 = (bf16[4,4,32,256]{3,2,1,0:T(8,128)(2,1)}, bf16[4,4,32,256]{3,2,1,0:T(8,128)(2,1)}, u32[]{:S(2)}, u32[]{:S(2)}) collective-permute-start(bf16[4,4,32,256]{3,2,1,0:T(8,128)(2,1)} %bitcast.24), channel_id=1, source_target_pairs={{0,3},{1,0},{2,1},{3,2},{4,7},{5,4},{6,5},{7,6},{8,11},{9,8},{10,9... | collective-permute-start | bytes 786440 | tf_op jit(solution)/shard_map/ppermute | solution.py:24
  195.1 17.9 %collective-permute-start.5 = (bf16[4,4,32,256]{3,2,1,0:T(8,128)(2,1)S(1)}, bf16[4,4,32,256]{3,2,1,0:T(8,128)(2,1)}, u32[]{:S(2)}, u32[]{:S(2)}) collective-permute-start(bf16[4,4,32,256]{3,2,1,0:T(8,128)(2,1)S(1)} %bitcast.195), channel_id=1, source_target_pairs={{0,2},{1,3},{2,0},{3,1},{4,6},{5,7},{6,4},{7,5},{8,10},{9,11},{10,... | collective-permute-start | bytes 786440 | tf_op jit(solution)/shard_map/ppermute | solution.py:24
  197.5 6.7 %copy-start.5 = (f32[4,128,64]{1,2,0:T(8,128)}, f32[4,128,64]{1,2,0:T(8,128)S(1)}, u32[]{:S(2)}) copy-start(f32[4,128,64]{1,2,0:T(8,128)S(1)} %collective-permute-done.15) | copy-start | bytes 393220
  197.5 15.6 %collective-permute-start.4 = (bf16[4,4,32,256]{3,2,1,0:T(8,128)(2,1)}, bf16[4,4,32,256]{3,2,1,0:T(8,128)(2,1)}, u32[]{:S(2)}, u32[]{:S(2)}) collective-permute-start(bf16[4,4,32,256]{3,2,1,0:T(8,128)(2,1)} %bitcast.12), channel_id=1, source_target_pairs={{0,1},{1,2},{2,3},{3,0},{4,5},{5,6},{6,7},{7,4},{8,9},{9,10},{10,1... | collective-permute-start | bytes 786440 | tf_op jit(solution)/shard_map/ppermute | solution.py:24
  207.9 10.3 %collective-permute-start.18 = (f32[4,128,64]{1,2,0:T(8,128)S(1)}, f32[4,128,64]{1,2,0:T(8,128)S(1)}, u32[]{:S(2)}, u32[]{:S(2)}) collective-permute-start(f32[4,128,64]{1,2,0:T(8,128)S(1)} %add_add_fusion), channel_id=1, source_target_pairs={{0,12},{1,13},{2,14},{3,15},{4,0},{5,1},{6,2},{7,3},{8,4},{9,5},{1... | collective-permute-start | bytes 393224 | tf_op jit(solution)/shard_map/ppermute | solution.py:24
  210.7 7.9 %collective-permute-start.16 = (f32[4,128,64]{1,2,0:T(8,128)S(1)}, f32[4,128,64]{1,2,0:T(8,128)S(1)}, u32[]{:S(2)}, u32[]{:S(2)}) collective-permute-start(f32[4,128,64]{1,2,0:T(8,128)S(1)} %add_add_fusion), channel_id=1, source_target_pairs={{0,4},{1,5},{2,6},{3,7},{4,8},{5,9},{6,10},{7,11},{8,12},{9,13},{1... | collective-permute-start | bytes 393224 | tf_op jit(solution)/shard_map/ppermute | solution.py:24
  210.7 7.9 %collective-permute-start.17 = (f32[4,128,64]{1,2,0:T(8,128)S(1)}, f32[4,128,64]{1,2,0:T(8,128)S(1)}, u32[]{:S(2)}, u32[]{:S(2)}) collective-permute-start(f32[4,128,64]{1,2,0:T(8,128)S(1)} %add_add_fusion), channel_id=1, source_target_pairs={{0,8},{1,9},{2,10},{3,11},{4,12},{5,13},{6,14},{7,15},{8,0},{9,1},... | collective-permute-start | bytes 393224 | tf_op jit(solution)/shard_map/ppermute | solution.py:24
  214.3 12.6 %collective-permute-start.12 = (bf16[4,32,512]{2,1,0:T(8,128)(2,1)S(1)}, bf16[4,32,512]{2,1,0:T(8,128)(2,1)S(1)}, u32[]{:S(2)}, u32[]{:S(2)}) collective-permute-start(bf16[4,32,512]{2,1,0:T(8,128)(2,1)S(1)} %get-tuple-element.10), channel_id=1, source_target_pairs={{0,12},{1,13},{2,14},{3,15},{4,0},{5,1},{6,2},{7,3},{8,4},{9,5},{1... | collective-permute-start | bytes 393224 | tf_op jit(solution)/shard_map/ppermute | solution.py:24
  216.2 10.8 %collective-permute-start.11 = (bf16[4,32,512]{2,1,0:T(8,128)(2,1)S(1)}, bf16[4,32,512]{2,1,0:T(8,128)(2,1)S(1)}, u32[]{:S(2)}, u32[]{:S(2)}) collective-permute-start(bf16[4,32,512]{2,1,0:T(8,128)(2,1)S(1)} %get-tuple-element.9), channel_id=1, source_target_pairs={{0,8},{1,9},{2,10},{3,11},{4,12},{5,13},{6,14},{7,15},{8,0},{9,1},... | collective-permute-start | bytes 393224 | tf_op jit(solution)/shard_map/ppermute | solution.py:24
  218.3 8.7 %collective-permute-start.10 = (bf16[4,32,512]{2,1,0:T(8,128)(2,1)S(1)}, bf16[4,32,512]{2,1,0:T(8,128)(2,1)S(1)}, u32[]{:S(2)}, u32[]{:S(2)}) collective-permute-start(bf16[4,32,512]{2,1,0:T(8,128)(2,1)S(1)} %get-tuple-element.8), channel_id=1, source_target_pairs={{0,4},{1,5},{2,6},{3,7},{4,8},{5,9},{6,10},{7,11},{8,12},{9,13},{1... | collective-permute-start | bytes 393224 | tf_op jit(solution)/shard_map/ppermute | solution.py:24
  219.8 17.3 %all-to-all-start = ((bf16[16,32,512]{2,1,0:T(8,128)(2,1)}), bf16[16,32,512]{2,1,0:T(8,128)(2,1)S(1)}, u32[]{:S(2)}, u32[]{:S(2)}) async-start(bf16[16,32,512]{2,1,0:T(8,128)(2,1)} %bitcast.70), calls=%async_computation | async-start | bytes 1048576 | tf_op jit(solution)/shard_map/all_to_all | solution.py:164
  227.8 9.5 %copy-start.7 = (pred[32]{0:T(512)(128)(4,1)S(1)}, pred[32]{0:T(512)(128)(4,1)}, u32[]{:S(2)}) copy-start(pred[32]{0:T(512)(128)(4,1)} %fusion.76) | copy-start | bytes 100
Sparse Core Ops, SparseCore 0:
  9.5 75.3 all-gather.6
  86.7 76.6 all-gather.4

commit v13 on v12

--- a/solution.py
+++ b/solution.py
@@ -109,6 +109,7 @@
         axis=0,
     )
     gathered = lax.all_gather(pack, "pool", axis=0, tiled=False)
+    later, gathered = lax.optimization_barrier((moved[:, half:], gathered))
     plane_rows = gathered.shape[1]
     w_first = gathered.reshape(quarter, side, plane_rows, half)
     shrink_all = gathered[:, feat:feat + shrink_rows, :].reshape(
@@ -117,7 +118,7 @@
     expand_all = gathered[:, feat + shrink_rows:, :].reshape(
         pool_count * held, expand_rows // held, half
     )
-    w_second = lax.all_gather(moved[:, half:], "pool", axis=0, tiled=False).reshape(
+    w_second = lax.all_gather(later, "pool", axis=0, tiled=False).reshape(
         quarter, side, feat, half
     )
 

time: 246 us -> 260 us (1.057)
  waiting for transfers between devices: 111 us -> 158 us
  starting transfers between devices: 58 us -> 32.2 us
  matrix products: 36.8 us -> 32.6 us
    all_gather x1, waiting for transfers between devices: 51.3 us -> 99.8 us  [shards(): gathered = lax.all_gather(pack, 'pool', axis=0, tiled=False)]
    ppermute x18, starting transfers between devices: 48.9 us -> 25.9 us  [tensor_shift(): return lax.ppermute(x, 'tensor', perm)]
    ppermute x18, waiting for transfers between devices: 50.3 us -> 58.3 us  [tensor_shift(): return lax.ppermute(x, 'tensor', perm)]
    all_to_all x1, waiting for transfers between devices: 7.86 us -> 0.01 us  [shards(): lax.all_to_all(delta, 'tensor', split_axis=0, concat_axis=1, tiled=True)]
    dot_general x8, matrix products: 35 us -> 29.8 us  [rows_for(): jnp.einsum('sif,asfj->aij', rows, w_half, preferred_element_type=jnp.floa...]
    all_to_all x1, starting transfers between devices: 7.11 us -> 4.34 us  [shards(): lax.all_to_all(delta, 'tensor', split_axis=0, concat_axis=1, tiled=True)]
  transfers between devices with their start and end apart: 22 -> 22, of which waited for: 10 -> 10; matrix products, arithmetic and copies ran while one was open for 17% -> 19% of each run, Pallas kernels for 0% -> 0%
where the time goes in v13:
time: 260 us; the launch traced here: 259 us
  waiting for transfers between devices  158 us (61%)
  matrix products  32.6 us (13%)
  starting transfers between devices  32.2 us (12%)
  local copies, waits for them, and re-layouts  16.2 us (6%)
  between operations  14 us (5%)
  other arithmetic  6 us (2%)
    all_gather x1, waiting for transfers between devices, shards(): gathered = lax.all_gather(pack, 'pool', axis=0, tiled=False)  99.8 us
    ppermute x18, waiting for transfers between devices, tensor_shift(): return lax.ppermute(x, 'tensor', perm)  58.3 us
    dot_general x8, matrix products, rows_for(): jnp.einsum('sif,asfj->aij', rows, w_half, preferred_element_type=jnp.floa...  29.8 us
    ppermute x18, starting transfers between devices, tensor_shift(): return lax.ppermute(x, 'tensor', perm)  25.9 us
  transfers between devices with their start and end apart: 22, of which 10 were waited for; matrix products, arithmetic and copies ran while one was open for 19% of the time, Pallas kernels for 0%

profile of v13, /device:TPU:0, one launch (start us, length us, event | category | flops | bytes accessed | tf_op | source)
XLA Modules:
  0.0 259.3 jit_solution(1261437775978724266)
XLA Ops:
  6.5 2.0 collective-permute-start
  8.5 1.1 copy.34
  9.8 1.2 copy.33
  11.4 0.8 fusion.86
  12.2 1.0 pad_maximum_fusion
  13.2 99.8 %all-gather.5.cloned.1.call-done = bf16[25600,256]{1,0:T(8,128)(2,1)} async-done(((bf16[1600,256]{1,0:T(8,128)(2,1)}), bf16[25600,256]{1,0:T(8,128)(2,1)}) %all-gather.5.cloned.1.call-update) | async-done | bytes 13107216 | tf_op jit(solution)/shard_map/all_gather | solution.py:111
  113.1 2.8 %collective-permute-start.3 = (bf16[512,896]{1,0:T(8,128)(2,1)S(1)}, bf16[512,896]{1,0:T(8,128)(2,1)S(1)}, u32[]{:S(2)}, u32[]{:S(2)}) collective-permute-start(bf16[512,896]{1,0:T(8,128)(2,1)S(1)} %copy-done.2), channel_id=1, source_target_pairs={{0,12},{1,13},{2,14},{3,15},{4,0},{5,1},{6,2},{7,3},{8,4},{9,5},{1... | collective-permute-start | bytes 2752520 | tf_op jit(solution)/shard_map/ppermute | solution.py:24
  115.9 0.8 collective-permute-start.2
  116.7 0.9 collective-permute-start.1
  118.5 37.1 %collective-permute-done.3 = bf16[512,896]{1,0:T(8,128)(2,1)S(1)} collective-permute-done((bf16[512,896]{1,0:T(8,128)(2,1)S(1)}, bf16[512,896]{1,0:T(8,128)(2,1)S(1)}, u32[]{:S(2)}, u32[]{:S(2)}) %collective-permute-start.3) | collective-permute-done | bytes 917536 | tf_op jit(solution)/shard_map/ppermute | solution.py:24
  155.6 3.8 %collective-permute-done.1 = bf16[512,896]{1,0:T(8,128)(2,1)} collective-permute-done((bf16[512,896]{1,0:T(8,128)(2,1)S(1)}, bf16[512,896]{1,0:T(8,128)(2,1)}, u32[]{:S(2)}, u32[]{:S(2)}) %collective-permute-start.1) | collective-permute-done | bytes 917536 | tf_op jit(solution)/shard_map/ppermute | solution.py:24
  159.4 1.6 maximum_bitcast_fusion
  161.0 2.3 copy.35
  163.2 4.3 %slice.14 = bf16[16,448,256]{2,1,0:T(8,128)(2,1)} slice(bf16[16,1600,256]{2,1,0:T(8,128)(2,1)} %bitcast.166), slice={[0:16], [896:1344], [0:256]} | slice | bytes 7340032 | tf_op jit(solution)/shard_map/slice | solution.py:115
  167.5 2.6 %gather_fusion.1 = bf16[4,224,256]{2,1,0:T(8,128)(2,1)S(1)} fusion(bf16[32,224,256]{2,1,0:T(8,128)(2,1)} %bitcast.188, s32[1024]{0:T(1024)S(1)} %pad_clamp_fusion), kind=kCustom, calls=%fused_computation.1 | custom fusion | bytes 917520 | tf_op jit(solution)/shard_map/jit(_take)/gather | solution.py:132
  171.1 2.8 %collective-permute-start.15 = (f32[4,128,64]{1,2,0:T(8,128)S(1)}, f32[4,128,64]{1,2,0:T(8,128)S(1)}, u32[]{:S(2)}, u32[]{:S(2)}) collective-permute-start(f32[4,128,64]{1,2,0:T(8,128)S(1)} %convolution_bitcast_fusion.4), channel_id=1, source_target_pairs={{0,3},{1,0},{2,1},{3,2},{4,7},{5,4},{6,5},{7,6},{8,11},{9,8},{10,9... | collective-permute-start | bytes 393224 | tf_op jit(solution)/shard_map/ppermute | solution.py:24
  173.9 2.3 collective-permute-start.14
  176.2 7.0 %fusion.36 = bf16[4,256,128]{1,2,0:T(8,128)(2,1)S(1)} fusion(bf16[4,4,1600,256]{3,2,1,0:T(8,128)(2,1)} %bitcast.167, s32[]{:T(128)S(6)} %select_n.166, bf16[4,4,128,896]{3,2,1,0:T(8,128)(2,1)} %bitcast.174), kind=kOutput, calls=%fused_computation.33 | convolution fusion | flops 1677852672 | bytes 17039364 | tf_op jit(solution)/shard_map/sif,asfj->aij/dot_general | solution.py:145
  183.2 1.4 collective-permute-start.6
  184.7 7.0 %fusion.42 = f32[4,256,128]{1,2,0:T(8,128)S(1)} fusion(bf16[4,4,1600,256]{3,2,1,0:T(8,128)(2,1)} %bitcast.168, s32[]{:T(128)S(6)} %select_n.167, bf16[4,4,128,896]{3,2,1,0:T(8,128)(2,1)S(1)} %bitcast.176), kind=kOutput, calls=%fused_computation.35 | convolution fusion | flops 1677983744 | bytes 17301508 | tf_op jit(solution)/shard_map/sif,asfj->aij/dot_general | solution.py:145
  191.7 1.9 fusion.33
  193.6 2.4 collective-permute-start.5
  196.1 0.8 collective-permute-start.18
  196.8 1.3 collective-permute-start.16
  198.2 0.9 collective-permute-start.17
  199.0 2.6 %fusion.30 = bf16[4,256,128]{1,2,0:T(8,128)(2,1)} fusion(bf16[4,4,1600,256]{3,2,1,0:T(8,128)(2,1)S(1)} %bitcast.172, s32[]{:T(128)S(6)} %select_n.162, bf16[4,4,128,896]{3,2,1,0:T(8,128)(2,1)S(1)} %bitcast.178), kind=kOutput, calls=%fused_computation.31 | convolution fusion | flops 1677852672 | bytes 17039364 | tf_op jit(solution)/shard_map/sif,asfj->aij/dot_general | solution.py:145
  202.8 2.4 collective-permute-done.16
  205.1 2.2 fusion.12
  207.3 4.3 %all-to-all-start = ((bf16[16,32,512]{2,1,0:T(8,128)(2,1)}), bf16[16,32,512]{2,1,0:T(8,128)(2,1)S(1)}, u32[]{:S(2)}, u32[]{:S(2)}) async-start(bf16[16,32,512]{2,1,0:T(8,128)(2,1)} %bitcast.70), calls=%async_computation | async-start | bytes 1048576 | tf_op jit(solution)/shard_map/all_to_all | solution.py:165
  211.7 1.2 add_convert_fusion.2
  212.9 4.6 %fusion.27 = bf16[4,256,128]{1,2,0:T(8,128)(2,1)S(1)} fusion(bf16[4,4,896,256]{3,2,1,0:T(8,128)(2,1)} %bitcast.182, bf16[4,4,128,896]{3,2,1,0:T(8,128)(2,1)} %bitcast.175, s32[]{:T(128)S(6)} %select_n.166), kind=kOutput, calls=%fused_computation.28 | convolution fusion | flops 939655168 | bytes 8519684 | tf_op jit(solution)/shard_map/sif,asfj->aij/dot_general | solution.py:145
  217.6 4.4 %fusion.26 = bf16[4,256,128]{1,2,0:T(8,128)(2,1)S(1)} fusion(bf16[4,4,896,256]{3,2,1,0:T(8,128)(2,1)} %bitcast.183, bf16[4,4,128,896]{3,2,1,0:T(8,128)(2,1)S(1)} %bitcast.179, s32[]{:T(128)S(6)} %select_n.164), kind=kOutput, calls=%fused_computation.27 | convolution fusion | flops 939655168 | bytes 8519684 | tf_op jit(solution)/shard_map/sif,asfj->aij/dot_general | solution.py:145
  222.1 1.1 fusion.25
  223.2 3.2 %collective-permute-start.9 = (bf16[4,4,32,256]{3,2,1,0:T(8,128)(2,1)S(1)}, bf16[4,4,32,256]{3,2,1,0:T(8,128)(2,1)S(1)}, u32[]{:S(2)}, u32[]{:S(2)}) collective-permute-start(bf16[4,4,32,256]{3,2,1,0:T(8,128)(2,1)S(1)} %bitcast.202), channel_id=1, source_target_pairs={{0,3},{1,0},{2,1},{3,2},{4,7},{5,4},{6,5},{7,6},{8,11},{9,8},{10,9... | collective-permute-start | bytes 786440 | tf_op jit(solution)/shard_map/ppermute | solution.py:24
  226.4 0.9 collective-permute-start.8
  227.3 0.9 collective-permute-start.7
  228.1 1.1 fusion.29
  229.2 5.4 %collective-permute-done.9 = bf16[4,4,32,256]{3,2,1,0:T(8,128)(2,1)S(1)} collective-permute-done((bf16[4,4,32,256]{3,2,1,0:T(8,128)(2,1)S(1)}, bf16[4,4,32,256]{3,2,1,0:T(8,128)(2,1)S(1)}, u32[]{:S(2)}, u32[]{:S(2)}) %collective-permute-start.9) | collective-permute-done | bytes 262176 | tf_op jit(solution)/shard_map/ppermute | solution.py:24
  234.7 1.0 collective-permute-done.8
  235.7 2.7 %collective-permute-done.7 = bf16[4,4,32,256]{3,2,1,0:T(8,128)(2,1)S(1)} collective-permute-done((bf16[4,4,32,256]{3,2,1,0:T(8,128)(2,1)S(1)}, bf16[4,4,32,256]{3,2,1,0:T(8,128)(2,1)S(1)}, u32[]{:S(2)}, u32[]{:S(2)}) %collective-permute-start.7) | collective-permute-done | bytes 262176 | tf_op jit(solution)/shard_map/ppermute | solution.py:24
  238.6 2.8 %collective-permute-start.12 = (bf16[4,32,512]{2,1,0:T(8,128)(2,1)S(1)}, bf16[4,32,512]{2,1,0:T(8,128)(2,1)S(1)}, u32[]{:S(2)}, u32[]{:S(2)}) collective-permute-start(bf16[4,32,512]{2,1,0:T(8,128)(2,1)S(1)} %get-tuple-element.14), channel_id=1, source_target_pairs={{0,12},{1,13},{2,14},{3,15},{4,0},{5,1},{6,2},{7,3},{8,4},{9,5},{1... | collective-permute-start | bytes 393224 | tf_op jit(solution)/shard_map/ppermute | solution.py:24
  241.4 0.8 collective-permute-start.11
  242.2 0.9 collective-permute-start.10
  243.3 2.1 collective-permute-done.12
  245.4 2.5 collective-permute-done.11
  247.9 1.3 collective-permute-done.10
  250.7 0.7 reshape.183
  251.5 0.9 fusion.55
  (68 shorter events, 5.4 us)
Async XLA Ops:
  6.5 106.5 %copy-start.2 = (bf16[512,896]{1,0:T(8,128)(2,1)S(1)}, bf16[512,896]{1,0:T(8,128)(2,1)}, u32[]{:S(2)}) copy-start(bf16[512,896]{1,0:T(8,128)(2,1)} %param.6) | copy-start | bytes 2752516
  6.5 111.2 %copy-start.3 = (s32[4]{0:T(128)S(1)}, s32[4]{0:T(128)}, u32[]{:S(2)}) copy-start(s32[4]{0:T(128)} %param.10) | copy-start | bytes 52
  6.5 111.3 %copy-start.5 = (s32[4]{0:T(128)S(1)}, s32[4]{0:T(128)}, u32[]{:S(2)}) copy-start(s32[4]{0:T(128)} %param.11) | copy-start | bytes 52
  6.5 106.5 %all-gather.5.cloned.1.call-start = ((), (), s32[]{:S(2)}) async-start(), calls=%async_computation.1 | async-start | bytes 13926400 | tf_op jit(solution)/shard_map/all_gather | solution.py:111
  6.5 4.8 %collective-permute-start = (bf16[896,512]{1,0:T(8,128)(2,1)}, bf16[896,512]{1,0:T(8,128)(2,1)S(1)}, u32[]{:S(2)}, u32[]{:S(2)}) collective-permute-start(bf16[896,512]{1,0:T(8,128)(2,1)} %param.7), channel_id=1, source_target_pairs={{0,0},{1,1},{2,2},{3,3},{4,48},{5,49},{6,50},{7,51},{8,32},{9,33},... | collective-permute-start | bytes 2752520 | tf_op jit(solution)/shard_map/ppermute | solution.py:98
  13.2 199.8 %all-gather.7.cloned.1.call-start = ((), (), s32[]{:S(2)}) async-start(), calls=%async_computation.2 | async-start | bytes 7798784 | tf_op jit(solution)/shard_map/all_gather | solution.py:121
  113.1 42.5 %collective-permute-start.3 = (bf16[512,896]{1,0:T(8,128)(2,1)S(1)}, bf16[512,896]{1,0:T(8,128)(2,1)S(1)}, u32[]{:S(2)}, u32[]{:S(2)}) collective-permute-start(bf16[512,896]{1,0:T(8,128)(2,1)S(1)} %copy-done.2), channel_id=1, source_target_pairs={{0,12},{1,13},{2,14},{3,15},{4,0},{5,1},{6,2},{7,3},{8,4},{9,5},{1... | collective-permute-start | bytes 2752520 | tf_op jit(solution)/shard_map/ppermute | solution.py:24
  115.9 39.7 %collective-permute-start.2 = (bf16[512,896]{1,0:T(8,128)(2,1)S(1)}, bf16[512,896]{1,0:T(8,128)(2,1)S(1)}, u32[]{:S(2)}, u32[]{:S(2)}) collective-permute-start(bf16[512,896]{1,0:T(8,128)(2,1)S(1)} %copy-done.2), channel_id=1, source_target_pairs={{0,8},{1,9},{2,10},{3,11},{4,12},{5,13},{6,14},{7,15},{8,0},{9,1},... | collective-permute-start | bytes 2752520 | tf_op jit(solution)/shard_map/ppermute | solution.py:24
  116.7 42.7 %collective-permute-start.1 = (bf16[512,896]{1,0:T(8,128)(2,1)S(1)}, bf16[512,896]{1,0:T(8,128)(2,1)}, u32[]{:S(2)}, u32[]{:S(2)}) collective-permute-start(bf16[512,896]{1,0:T(8,128)(2,1)S(1)} %copy-done.2), channel_id=1, source_target_pairs={{0,4},{1,5},{2,6},{3,7},{4,8},{5,9},{6,10},{7,11},{8,12},{9,13},{1... | collective-permute-start | bytes 2752520 | tf_op jit(solution)/shard_map/ppermute | solution.py:24
  171.1 24.9 %collective-permute-start.15 = (f32[4,128,64]{1,2,0:T(8,128)S(1)}, f32[4,128,64]{1,2,0:T(8,128)S(1)}, u32[]{:S(2)}, u32[]{:S(2)}) collective-permute-start(f32[4,128,64]{1,2,0:T(8,128)S(1)} %convolution_bitcast_fusion.4), channel_id=1, source_target_pairs={{0,3},{1,0},{2,1},{3,2},{4,7},{5,4},{6,5},{7,6},{8,11},{9,8},{10,9... | collective-permute-start | bytes 393224 | tf_op jit(solution)/shard_map/ppermute | solution.py:24
  173.9 22.1 %collective-permute-start.13 = (f32[4,128,64]{1,2,0:T(8,128)S(1)}, f32[4,128,64]{1,2,0:T(8,128)S(1)}, u32[]{:S(2)}, u32[]{:S(2)}) collective-permute-start(f32[4,128,64]{1,2,0:T(8,128)S(1)} %convolution_bitcast_fusion.4), channel_id=1, source_target_pairs={{0,1},{1,2},{2,3},{3,0},{4,5},{5,6},{6,7},{7,4},{8,9},{9,10},{10,1... | collective-permute-start | bytes 393224 | tf_op jit(solution)/shard_map/ppermute | solution.py:24
  173.9 22.1 %collective-permute-start.14 = (f32[4,128,64]{1,2,0:T(8,128)S(1)}, f32[4,128,64]{1,2,0:T(8,128)S(1)}, u32[]{:S(2)}, u32[]{:S(2)}) collective-permute-start(f32[4,128,64]{1,2,0:T(8,128)S(1)} %convolution_bitcast_fusion.4), channel_id=1, source_target_pairs={{0,2},{1,3},{2,0},{3,1},{4,6},{5,7},{6,4},{7,5},{8,10},{9,11},{10,... | collective-permute-start | bytes 393224 | tf_op jit(solution)/shard_map/ppermute | solution.py:24
  176.2 8.5 %copy-start = (bf16[4,4,4,32,896]{4,3,2,1,0:T(8,128)(2,1)S(1)}, bf16[4,4,4,32,896]{4,3,2,1,0:T(8,128)(2,1)}, u32[]{:S(2)}) copy-start(bf16[4,4,4,32,896]{4,3,2,1,0:T(8,128)(2,1)} %copy.35) | copy-start | bytes 11010052
  176.2 15.5 %slice-start = ((s8[13107200]{0:T(1024)(128)(4,1)}), s8[4194304]{0:T(1024)(128)(4,1)S(1)}, s32[]{:S(2)}) async-start(s8[13107200]{0:T(1024)(128)(4,1)} %bitcast.169), calls=%async_computation.3 | async-start | bytes 8388608
  176.2 15.5 %slice-start.1 = ((s8[13107200]{0:T(1024)(128)(4,1)}), s8[4194304]{0:T(1024)(128)(4,1)S(1)}, s32[]{:S(2)}) async-start(s8[13107200]{0:T(1024)(128)(4,1)} %bitcast.169), calls=%async_computation.4 | async-start | bytes 8388608
  183.2 8.5 %slice-start.2 = ((s8[13107200]{0:T(1024)(128)(4,1)}), s8[4194304]{0:T(1024)(128)(4,1)S(1)}, s32[]{:S(2)}) async-start(s8[13107200]{0:T(1024)(128)(4,1)} %bitcast.169), calls=%async_computation.5 | async-start | bytes 8388608
  183.2 8.5 %slice-start.3 = ((s8[13107200]{0:T(1024)(128)(4,1)}), s8[524288]{0:T(1024)(128)(4,1)S(1)}, s32[]{:S(2)}) async-start(s8[13107200]{0:T(1024)(128)(4,1)} %bitcast.169), calls=%async_computation.6 | async-start | bytes 1048576
  183.2 28.5 %collective-permute-start.6 = (bf16[4,4,32,256]{3,2,1,0:T(8,128)(2,1)S(1)}, bf16[4,4,32,256]{3,2,1,0:T(8,128)(2,1)}, u32[]{:S(2)}, u32[]{:S(2)}) collective-permute-start(bf16[4,4,32,256]{3,2,1,0:T(8,128)(2,1)S(1)} %bitcast.197), channel_id=1, source_target_pairs={{0,3},{1,0},{2,1},{3,2},{4,7},{5,4},{6,5},{7,6},{8,11},{9,8},{10,9... | collective-permute-start | bytes 786440 | tf_op jit(solution)/shard_map/ppermute | solution.py:24
  193.6 18.1 %collective-permute-start.5 = (bf16[4,4,32,256]{3,2,1,0:T(8,128)(2,1)S(1)}, bf16[4,4,32,256]{3,2,1,0:T(8,128)(2,1)}, u32[]{:S(2)}, u32[]{:S(2)}) collective-permute-start(bf16[4,4,32,256]{3,2,1,0:T(8,128)(2,1)S(1)} %bitcast.198), channel_id=1, source_target_pairs={{0,2},{1,3},{2,0},{3,1},{4,6},{5,7},{6,4},{7,5},{8,10},{9,11},{10,... | collective-permute-start | bytes 786440 | tf_op jit(solution)/shard_map/ppermute | solution.py:24
  196.1 6.6 %collective-permute-start.18 = (f32[4,128,64]{1,2,0:T(8,128)S(1)}, f32[4,128,64]{1,2,0:T(8,128)}, u32[]{:S(2)}, u32[]{:S(2)}) collective-permute-start(f32[4,128,64]{1,2,0:T(8,128)S(1)} %add_add_fusion), channel_id=1, source_target_pairs={{0,12},{1,13},{2,14},{3,15},{4,0},{5,1},{6,2},{7,3},{8,4},{9,5},{1... | collective-permute-start | bytes 393224 | tf_op jit(solution)/shard_map/ppermute | solution.py:24
  196.8 8.3 %collective-permute-start.16 = (f32[4,128,64]{1,2,0:T(8,128)S(1)}, f32[4,128,64]{1,2,0:T(8,128)}, u32[]{:S(2)}, u32[]{:S(2)}) collective-permute-start(f32[4,128,64]{1,2,0:T(8,128)S(1)} %add_add_fusion), channel_id=1, source_target_pairs={{0,4},{1,5},{2,6},{3,7},{4,8},{5,9},{6,10},{7,11},{8,12},{9,13},{1... | collective-permute-start | bytes 393224 | tf_op jit(solution)/shard_map/ppermute | solution.py:24
  198.2 7.0 %collective-permute-start.17 = (f32[4,128,64]{1,2,0:T(8,128)S(1)}, f32[4,128,64]{1,2,0:T(8,128)}, u32[]{:S(2)}, u32[]{:S(2)}) collective-permute-start(f32[4,128,64]{1,2,0:T(8,128)S(1)} %add_add_fusion), channel_id=1, source_target_pairs={{0,8},{1,9},{2,10},{3,11},{4,12},{5,13},{6,14},{7,15},{8,0},{9,1},... | collective-permute-start | bytes 393224 | tf_op jit(solution)/shard_map/ppermute | solution.py:24
  202.7 9.0 %collective-permute-start.4 = (bf16[4,4,32,256]{3,2,1,0:T(8,128)(2,1)}, bf16[4,4,32,256]{3,2,1,0:T(8,128)(2,1)S(1)}, u32[]{:S(2)}, u32[]{:S(2)}) collective-permute-start(bf16[4,4,32,256]{3,2,1,0:T(8,128)(2,1)} %bitcast.199), channel_id=1, source_target_pairs={{0,1},{1,2},{2,3},{3,0},{4,5},{5,6},{6,7},{7,4},{8,9},{9,10},{10,1... | collective-permute-start | bytes 786440 | tf_op jit(solution)/shard_map/ppermute | solution.py:24
  207.3 35.7 %all-to-all-start = ((bf16[16,32,512]{2,1,0:T(8,128)(2,1)}), bf16[16,32,512]{2,1,0:T(8,128)(2,1)S(1)}, u32[]{:S(2)}, u32[]{:S(2)}) async-start(bf16[16,32,512]{2,1,0:T(8,128)(2,1)} %bitcast.70), calls=%async_computation | async-start | bytes 1048576 | tf_op jit(solution)/shard_map/all_to_all | solution.py:165
  212.9 4.7 %copy-start.1 = (bf16[4,4,4,32,896]{4,3,2,1,0:T(8,128)(2,1)S(1)}, bf16[4,4,4,32,896]{4,3,2,1,0:T(8,128)(2,1)}, u32[]{:S(2)}) copy-start(bf16[4,4,4,32,896]{4,3,2,1,0:T(8,128)(2,1)} %copy.35) | copy-start | bytes 11010052
  212.9 9.1 %slice-start.4 = ((s8[7340032]{0:T(1024)(128)(4,1)}), s8[4194304]{0:T(1024)(128)(4,1)S(1)}, s32[]{:S(2)}) async-start(s8[7340032]{0:T(1024)(128)(4,1)} %bitcast.184), calls=%async_computation.7 | async-start | bytes 8388608
  217.6 4.5 %slice-start.5 = ((s8[7340032]{0:T(1024)(128)(4,1)}), s8[3145728]{0:T(1024)(128)(4,1)S(1)}, s32[]{:S(2)}) async-start(s8[7340032]{0:T(1024)(128)(4,1)} %bitcast.184), calls=%async_computation.8 | async-start | bytes 6291456
  223.2 11.5 %collective-permute-start.9 = (bf16[4,4,32,256]{3,2,1,0:T(8,128)(2,1)S(1)}, bf16[4,4,32,256]{3,2,1,0:T(8,128)(2,1)S(1)}, u32[]{:S(2)}, u32[]{:S(2)}) collective-permute-start(bf16[4,4,32,256]{3,2,1,0:T(8,128)(2,1)S(1)} %bitcast.202), channel_id=1, source_target_pairs={{0,3},{1,0},{2,1},{3,2},{4,7},{5,4},{6,5},{7,6},{8,11},{9,8},{10,9... | collective-permute-start | bytes 786440 | tf_op jit(solution)/shard_map/ppermute | solution.py:24
  226.4 9.3 %collective-permute-start.8 = (bf16[4,4,32,256]{3,2,1,0:T(8,128)(2,1)S(1)}, bf16[4,4,32,256]{3,2,1,0:T(8,128)(2,1)S(1)}, u32[]{:S(2)}, u32[]{:S(2)}) collective-permute-start(bf16[4,4,32,256]{3,2,1,0:T(8,128)(2,1)S(1)} %bitcast.201), channel_id=1, source_target_pairs={{0,2},{1,3},{2,0},{3,1},{4,6},{5,7},{6,4},{7,5},{8,10},{9,11},{10,... | collective-permute-start | bytes 786440 | tf_op jit(solution)/shard_map/ppermute | solution.py:24
  227.3 11.1 %collective-permute-start.7 = (bf16[4,4,32,256]{3,2,1,0:T(8,128)(2,1)S(1)}, bf16[4,4,32,256]{3,2,1,0:T(8,128)(2,1)S(1)}, u32[]{:S(2)}, u32[]{:S(2)}) collective-permute-start(bf16[4,4,32,256]{3,2,1,0:T(8,128)(2,1)S(1)} %bitcast.200), channel_id=1, source_target_pairs={{0,1},{1,2},{2,3},{3,0},{4,5},{5,6},{6,7},{7,4},{8,9},{9,10},{10,1... | collective-permute-start | bytes 786440 | tf_op jit(solution)/shard_map/ppermute | solution.py:24
  238.6 6.8 %collective-permute-start.12 = (bf16[4,32,512]{2,1,0:T(8,128)(2,1)S(1)}, bf16[4,32,512]{2,1,0:T(8,128)(2,1)S(1)}, u32[]{:S(2)}, u32[]{:S(2)}) collective-permute-start(bf16[4,32,512]{2,1,0:T(8,128)(2,1)S(1)} %get-tuple-element.14), channel_id=1, source_target_pairs={{0,12},{1,13},{2,14},{3,15},{4,0},{5,1},{6,2},{7,3},{8,4},{9,5},{1... | collective-permute-start | bytes 393224 | tf_op jit(solution)/shard_map/ppermute | solution.py:24
  241.4 6.6 %collective-permute-start.11 = (bf16[4,32,512]{2,1,0:T(8,128)(2,1)S(1)}, bf16[4,32,512]{2,1,0:T(8,128)(2,1)S(1)}, u32[]{:S(2)}, u32[]{:S(2)}) collective-permute-start(bf16[4,32,512]{2,1,0:T(8,128)(2,1)S(1)} %get-tuple-element.13), channel_id=1, source_target_pairs={{0,8},{1,9},{2,10},{3,11},{4,12},{5,13},{6,14},{7,15},{8,0},{9,1},... | collective-permute-start | bytes 393224 | tf_op jit(solution)/shard_map/ppermute | solution.py:24
  242.2 7.0 %collective-permute-start.10 = (bf16[4,32,512]{2,1,0:T(8,128)(2,1)S(1)}, bf16[4,32,512]{2,1,0:T(8,128)(2,1)S(1)}, u32[]{:S(2)}, u32[]{:S(2)}) collective-permute-start(bf16[4,32,512]{2,1,0:T(8,128)(2,1)S(1)} %get-tuple-element.12), channel_id=1, source_target_pairs={{0,4},{1,5},{2,6},{3,7},{4,8},{5,9},{6,10},{7,11},{8,12},{9,13},{1... | collective-permute-start | bytes 393224 | tf_op jit(solution)/shard_map/ppermute | solution.py:24
  249.3 2.2 copy-start.4
Sparse Core Ops, SparseCore 0:
  13.3 99.6 all-gather.4
  114.8 49.5 all-gather.6

commit v14 on v13

--- a/solution.py
+++ b/solution.py
@@ -109,7 +109,8 @@
         axis=0,
     )
     gathered = lax.all_gather(pack, "pool", axis=0, tiled=False)
-    later, gathered = lax.optimization_barrier((moved[:, half:], gathered))
+    pieces = [hidden] + [tensor_shift(hidden, side, s, True) for s in range(1, side)]
+    later, gathered, pieces = lax.optimization_barrier((moved[:, half:], gathered, pieces))
     plane_rows = gathered.shape[1]
     w_first = gathered.reshape(quarter, side, plane_rows, half)
     shrink_all = gathered[:, feat:feat + shrink_rows, :].reshape(
@@ -122,7 +123,6 @@
         quarter, side, feat, half
     )
 
-    pieces = [hidden] + [tensor_shift(hidden, side, s, True) for s in range(1, side)]
     hidden_column = jnp.stack(pieces, axis=0).reshape(side, side, side, own_rows, feat)
     hidden_column = jnp.transpose(hidden_column, (2, 0, 1, 3, 4)).reshape(
         side, side, side * own_rows, feat

time: 260 us -> 219 us (0.84); the launches traced: 259 us -> 215 us
  waiting for transfers between devices: 158 us -> 98.5 us
  starting transfers between devices: 32.2 us -> 53.8 us
  matrix products: 32.6 us -> 23.5 us
  local copies, waits for them, and re-layouts: 16.2 us -> 19.6 us
    all_gather x1, waiting for transfers between devices: 99.8 us -> 37.3 us  [shards(): gathered = lax.all_gather(pack, 'pool', axis=0, tiled=False)]
    ppermute x18, starting transfers between devices: 25.9 us -> 48 us  [tensor_shift(): return lax.ppermute(x, 'tensor', perm)]
    dot_general x8, matrix products: 29.8 us -> 19.5 us  [rows_for(): jnp.einsum('sif,asfj->aij', rows, w_half, preferred_element_type=jnp.floa...]
    unnamed x26 -> x20, local copies, waits for them, and re-layouts: 2.33 us -> 6.55 us
where the time goes in v14:
time: 219 us; the launch traced here: 215 us
  waiting for transfers between devices  98.5 us (45%)
  starting transfers between devices  53.8 us (25%)
  matrix products  23.5 us (11%)
  local copies, waits for them, and re-layouts  19.6 us (9%)
  between operations  14 us (6%)
  other arithmetic  6.07 us (3%)
    ppermute x18, waiting for transfers between devices, tensor_shift(): return lax.ppermute(x, 'tensor', perm)  60.3 us
    ppermute x18, starting transfers between devices, tensor_shift(): return lax.ppermute(x, 'tensor', perm)  48 us
    all_gather x1, waiting for transfers between devices, shards(): gathered = lax.all_gather(pack, 'pool', axis=0, tiled=False)  37.3 us
    dot_general x8, matrix products, rows_for(): jnp.einsum('sif,asfj->aij', rows, w_half, preferred_element_type=jnp.floa...  19.5 us
    unnamed x20, local copies, waits for them, and re-layouts  6.55 us
  transfers between devices with their start and end apart: 22, of which 10 were waited for; matrix products, arithmetic and copies ran while one was open for 19% of the time, Pallas kernels for 0%

profile of v14, /device:TPU:0, one launch (start us, length us, event | category | flops | bytes accessed | tf_op | source)
XLA Modules:
  0.0 215.4 jit_solution(16058318189689049198)
XLA Ops:
  6.5 2.0 collective-permute-start
  8.5 1.1 copy.34
  9.8 1.2 copy.33
  11.4 0.9 fusion.86
  12.3 1.0 pad_maximum_fusion
  13.3 9.7 %collective-permute-start.1 = (bf16[512,896]{1,0:T(8,128)(2,1)S(1)}, bf16[512,896]{1,0:T(8,128)(2,1)S(1)}, u32[]{:S(2)}, u32[]{:S(2)}) collective-permute-start(bf16[512,896]{1,0:T(8,128)(2,1)S(1)} %copy-done.3), channel_id=1, source_target_pairs={{0,4},{1,5},{2,6},{3,7},{4,8},{5,9},{6,10},{7,11},{8,12},{9,13},{1... | collective-permute-start | bytes 2752520 | tf_op jit(solution)/shard_map/ppermute | solution.py:24
  23.0 12.3 %collective-permute-start.2 = (bf16[512,896]{1,0:T(8,128)(2,1)S(1)}, bf16[512,896]{1,0:T(8,128)(2,1)S(1)}, u32[]{:S(2)}, u32[]{:S(2)}) collective-permute-start(bf16[512,896]{1,0:T(8,128)(2,1)S(1)} %copy-done.3), channel_id=1, source_target_pairs={{0,8},{1,9},{2,10},{3,11},{4,12},{5,13},{6,14},{7,15},{8,0},{9,1},... | collective-permute-start | bytes 2752520 | tf_op jit(solution)/shard_map/ppermute | solution.py:24
  35.3 2.5 %collective-permute-start.3 = (bf16[512,896]{1,0:T(8,128)(2,1)S(1)}, bf16[512,896]{1,0:T(8,128)(2,1)}, u32[]{:S(2)}, u32[]{:S(2)}) collective-permute-start(bf16[512,896]{1,0:T(8,128)(2,1)S(1)} %copy-done.3), channel_id=1, source_target_pairs={{0,12},{1,13},{2,14},{3,15},{4,0},{5,1},{6,2},{7,3},{8,4},{9,5},{1... | collective-permute-start | bytes 2752520 | tf_op jit(solution)/shard_map/ppermute | solution.py:24
  37.8 5.8 %collective-permute-done.1 = bf16[512,896]{1,0:T(8,128)(2,1)S(1)} collective-permute-done((bf16[512,896]{1,0:T(8,128)(2,1)S(1)}, bf16[512,896]{1,0:T(8,128)(2,1)S(1)}, u32[]{:S(2)}, u32[]{:S(2)}) %collective-permute-start.1) | collective-permute-done | bytes 917536 | tf_op jit(solution)/shard_map/ppermute | solution.py:24
  43.6 32.3 %collective-permute-done.2 = bf16[512,896]{1,0:T(8,128)(2,1)S(1)} collective-permute-done((bf16[512,896]{1,0:T(8,128)(2,1)S(1)}, bf16[512,896]{1,0:T(8,128)(2,1)S(1)}, u32[]{:S(2)}, u32[]{:S(2)}) %collective-permute-start.2) | collective-permute-done | bytes 917536 | tf_op jit(solution)/shard_map/ppermute | solution.py:24
  75.9 37.3 %all-gather.5.cloned.1.call-done = bf16[25600,256]{1,0:T(8,128)(2,1)} async-done(((bf16[1600,256]{1,0:T(8,128)(2,1)}), bf16[25600,256]{1,0:T(8,128)(2,1)}) %all-gather.5.cloned.1.call-update) | async-done | bytes 13107216 | tf_op jit(solution)/shard_map/all_gather | solution.py:111
  114.1 4.2 %slice.14 = bf16[16,448,256]{2,1,0:T(8,128)(2,1)} slice(bf16[16,1600,256]{2,1,0:T(8,128)(2,1)} %bitcast.166), slice={[0:16], [896:1344], [0:256]} | slice | bytes 7340032 | tf_op jit(solution)/shard_map/slice | solution.py:116
  118.3 2.6 %gather_fusion.1 = bf16[4,224,256]{2,1,0:T(8,128)(2,1)S(1)} fusion(bf16[32,224,256]{2,1,0:T(8,128)(2,1)} %bitcast.186, s32[1024]{0:T(1024)S(1)} %pad_clamp_fusion), kind=kCustom, calls=%fused_computation.1 | custom fusion | bytes 917520 | tf_op jit(solution)/shard_map/jit(_take)/gather | solution.py:132
  120.9 1.3 gather.18
  122.2 1.8 convolution_bitcast_fusion.4
  124.0 2.8 %collective-permute-start.15 = (f32[4,128,64]{1,2,0:T(8,128)S(1)}, f32[4,128,64]{1,2,0:T(8,128)S(1)}, u32[]{:S(2)}, u32[]{:S(2)}) collective-permute-start(f32[4,128,64]{1,2,0:T(8,128)S(1)} %convolution_bitcast_fusion.4), channel_id=1, source_target_pairs={{0,3},{1,0},{2,1},{3,2},{4,7},{5,4},{6,5},{7,6},{8,11},{9,8},{10,9... | collective-permute-start | bytes 393224 | tf_op jit(solution)/shard_map/ppermute | solution.py:24
  126.8 2.3 %collective-permute-start.14 = (f32[4,128,64]{1,2,0:T(8,128)S(1)}, f32[4,128,64]{1,2,0:T(8,128)S(1)}, u32[]{:S(2)}, u32[]{:S(2)}) collective-permute-start(f32[4,128,64]{1,2,0:T(8,128)S(1)} %convolution_bitcast_fusion.4), channel_id=1, source_target_pairs={{0,2},{1,3},{2,0},{3,1},{4,6},{5,7},{6,4},{7,5},{8,10},{9,11},{10,... | collective-permute-start | bytes 393224 | tf_op jit(solution)/shard_map/ppermute | solution.py:24
  129.1 1.8 maximum_bitcast_fusion
  131.3 4.2 %copy-done = bf16[25600,256]{1,0:T(8,128)(2,1)S(1)} copy-done((bf16[25600,256]{1,0:T(8,128)(2,1)S(1)}, bf16[25600,256]{1,0:T(8,128)(2,1)}, u32[]{:S(2)}) %copy-start) | copy-done | bytes 13107224
  135.6 1.9 fusion.36
  137.5 1.3 collective-permute-start.6
  138.8 1.9 fusion.42
  140.7 1.9 fusion.33
  142.6 2.9 %collective-permute-start.5 = (bf16[4,4,32,256]{3,2,1,0:T(8,128)(2,1)S(1)}, bf16[4,4,32,256]{3,2,1,0:T(8,128)(2,1)}, u32[]{:S(2)}, u32[]{:S(2)}) collective-permute-start(bf16[4,4,32,256]{3,2,1,0:T(8,128)(2,1)S(1)} %bitcast.196), channel_id=1, source_target_pairs={{0,2},{1,3},{2,0},{3,1},{4,6},{5,7},{6,4},{7,5},{8,10},{9,11},{10,... | collective-permute-start | bytes 786440 | tf_op jit(solution)/shard_map/ppermute | solution.py:24
  145.5 2.8 %collective-permute-start.18 = (f32[4,128,64]{1,2,0:T(8,128)S(1)}, f32[4,128,64]{1,2,0:T(8,128)}, u32[]{:S(2)}, u32[]{:S(2)}) collective-permute-start(f32[4,128,64]{1,2,0:T(8,128)S(1)} %add_add_fusion), channel_id=1, source_target_pairs={{0,12},{1,13},{2,14},{3,15},{4,0},{5,1},{6,2},{7,3},{8,4},{9,5},{1... | collective-permute-start | bytes 393224 | tf_op jit(solution)/shard_map/ppermute | solution.py:24
  148.3 2.3 %collective-permute-start.17 = (f32[4,128,64]{1,2,0:T(8,128)S(1)}, f32[4,128,64]{1,2,0:T(8,128)}, u32[]{:S(2)}, u32[]{:S(2)}) collective-permute-start(f32[4,128,64]{1,2,0:T(8,128)S(1)} %add_add_fusion), channel_id=1, source_target_pairs={{0,8},{1,9},{2,10},{3,11},{4,12},{5,13},{6,14},{7,15},{8,0},{9,1},... | collective-permute-start | bytes 393224 | tf_op jit(solution)/shard_map/ppermute | solution.py:24
  150.6 2.6 %fusion.30 = bf16[4,256,128]{1,2,0:T(8,128)(2,1)} fusion(bf16[4,4,1600,256]{3,2,1,0:T(8,128)(2,1)S(1)} %bitcast.170, s32[]{:T(128)S(6)} %select_n.162, bf16[4,4,128,896]{3,2,1,0:T(8,128)(2,1)S(1)} %bitcast.175), kind=kOutput, calls=%fused_computation.31 | convolution fusion | flops 1677852672 | bytes 17039364 | tf_op jit(solution)/shard_map/sif,asfj->aij/dot_general | solution.py:145
  154.3 2.1 collective-permute-done.16
  156.4 2.2 %fusion.12 = bf16[4,128,512]{2,1,0:T(8,128)(2,1)} fusion(bf16[4,512,64]{2,1,0:T(8,128)(2,1)S(1)} %gather.20, pred[4]{0:T(512)(128)(4,1)S(1)} %get-tuple-element.23, f32[4,128,64]{1,2,0:T(8,128)S(1)} %add_add_fusion, f32[4,128,64]{1,2,0:T(8,128)} %collective-permute-done.18, f32[4,128,64]{1,2,0:T(8,128)} %collective-permute-done.16, ...), kind=kOutput, calls=%fused_computation.17 | convolution fusion | flops 34340864 | bytes 1310724 | tf_op jit(solution)/shard_map/bnr,bcr->bnc/dot_general | solution.py:137
  158.6 3.8 %all-to-all-start = ((bf16[16,32,512]{2,1,0:T(8,128)(2,1)}), bf16[16,32,512]{2,1,0:T(8,128)(2,1)S(1)}, u32[]{:S(2)}, u32[]{:S(2)}) async-start(bf16[16,32,512]{2,1,0:T(8,128)(2,1)} %bitcast.70), calls=%async_computation | async-start | bytes 1048576 | tf_op jit(solution)/shard_map/all_to_all | solution.py:165
  162.5 1.2 add_convert_fusion.2
  163.7 0.9 all-gather.7.cloned.1.call-done
  164.6 4.6 %fusion.27 = bf16[4,256,128]{1,2,0:T(8,128)(2,1)S(1)} fusion(bf16[4,4,896,256]{3,2,1,0:T(8,128)(2,1)} %bitcast.180, bf16[4,4,128,896]{3,2,1,0:T(8,128)(2,1)} %bitcast.176, s32[]{:T(128)S(6)} %select_n.166), kind=kOutput, calls=%fused_computation.28 | convolution fusion | flops 939655168 | bytes 8519684 | tf_op jit(solution)/shard_map/sif,asfj->aij/dot_general | solution.py:145
  169.2 4.4 %fusion.26 = bf16[4,256,128]{1,2,0:T(8,128)(2,1)S(1)} fusion(bf16[4,4,896,256]{3,2,1,0:T(8,128)(2,1)} %bitcast.181, bf16[4,4,128,896]{3,2,1,0:T(8,128)(2,1)S(1)} %bitcast.177, s32[]{:T(128)S(6)} %select_n.164), kind=kOutput, calls=%fused_computation.27 | convolution fusion | flops 939655168 | bytes 8519684 | tf_op jit(solution)/shard_map/sif,asfj->aij/dot_general | solution.py:145
  173.7 1.1 fusion.25
  174.8 2.8 %collective-permute-start.9 = (bf16[4,4,32,256]{3,2,1,0:T(8,128)(2,1)S(1)}, bf16[4,4,32,256]{3,2,1,0:T(8,128)(2,1)S(1)}, u32[]{:S(2)}, u32[]{:S(2)}) collective-permute-start(bf16[4,4,32,256]{3,2,1,0:T(8,128)(2,1)S(1)} %bitcast.200), channel_id=1, source_target_pairs={{0,3},{1,0},{2,1},{3,2},{4,7},{5,4},{6,5},{7,6},{8,11},{9,8},{10,9... | collective-permute-start | bytes 786440 | tf_op jit(solution)/shard_map/ppermute | solution.py:24
  177.6 0.8 collective-permute-start.8
  178.4 0.9 collective-permute-start.7
  179.3 1.1 fusion.29
  180.4 8.8 %collective-permute-done.9 = bf16[4,4,32,256]{3,2,1,0:T(8,128)(2,1)S(1)} collective-permute-done((bf16[4,4,32,256]{3,2,1,0:T(8,128)(2,1)S(1)}, bf16[4,4,32,256]{3,2,1,0:T(8,128)(2,1)S(1)}, u32[]{:S(2)}, u32[]{:S(2)}) %collective-permute-start.9) | collective-permute-done | bytes 262176 | tf_op jit(solution)/shard_map/ppermute | solution.py:24
  189.2 3.7 %collective-permute-done.7 = bf16[4,4,32,256]{3,2,1,0:T(8,128)(2,1)S(1)} collective-permute-done((bf16[4,4,32,256]{3,2,1,0:T(8,128)(2,1)S(1)}, bf16[4,4,32,256]{3,2,1,0:T(8,128)(2,1)S(1)}, u32[]{:S(2)}, u32[]{:S(2)}) %collective-permute-start.7) | collective-permute-done | bytes 262176 | tf_op jit(solution)/shard_map/ppermute | solution.py:24
  193.1 2.8 %collective-permute-start.12 = (bf16[4,32,512]{2,1,0:T(8,128)(2,1)S(1)}, bf16[4,32,512]{2,1,0:T(8,128)(2,1)S(1)}, u32[]{:S(2)}, u32[]{:S(2)}) collective-permute-start(bf16[4,32,512]{2,1,0:T(8,128)(2,1)S(1)} %get-tuple-element.22), channel_id=1, source_target_pairs={{0,12},{1,13},{2,14},{3,15},{4,0},{5,1},{6,2},{7,3},{8,4},{9,5},{1... | collective-permute-start | bytes 393224 | tf_op jit(solution)/shard_map/ppermute | solution.py:24
  195.9 0.8 collective-permute-start.11
  196.8 0.9 collective-permute-start.10
  197.9 3.9 %collective-permute-done.12 = bf16[4,32,512]{2,1,0:T(8,128)(2,1)S(1)} collective-permute-done((bf16[4,32,512]{2,1,0:T(8,128)(2,1)S(1)}, bf16[4,32,512]{2,1,0:T(8,128)(2,1)S(1)}, u32[]{:S(2)}, u32[]{:S(2)}) %collective-permute-start.12) | collective-permute-done | bytes 131104 | tf_op jit(solution)/shard_map/ppermute | solution.py:24
  201.7 2.1 collective-permute-done.11
  203.8 1.5 collective-permute-done.10
  207.6 0.9 fusion.55
  (61 shorter events, 5.5 us)
Async XLA Ops:
  6.5 6.8 %copy-start.3 = (bf16[512,896]{1,0:T(8,128)(2,1)S(1)}, bf16[512,896]{1,0:T(8,128)(2,1)}, u32[]{:S(2)}) copy-start(bf16[512,896]{1,0:T(8,128)(2,1)} %param.6) | copy-start | bytes 2752516
  6.5 106.9 %copy-start.4 = (s32[4]{0:T(128)S(1)}, s32[4]{0:T(128)}, u32[]{:S(2)}) copy-start(s32[4]{0:T(128)} %param.10) | copy-start | bytes 52
  6.5 106.9 %copy-start.6 = (s32[4]{0:T(128)S(1)}, s32[4]{0:T(128)}, u32[]{:S(2)}) copy-start(s32[4]{0:T(128)} %param.11) | copy-start | bytes 52
  6.5 106.7 %all-gather.5.cloned.1.call-start = ((), (), s32[]{:S(2)}) async-start(), calls=%async_computation.1 | async-start | bytes 13926400 | tf_op jit(solution)/shard_map/all_gather | solution.py:111
  6.5 4.8 %collective-permute-start = (bf16[896,512]{1,0:T(8,128)(2,1)}, bf16[896,512]{1,0:T(8,128)(2,1)S(1)}, u32[]{:S(2)}, u32[]{:S(2)}) collective-permute-start(bf16[896,512]{1,0:T(8,128)(2,1)} %param.7), channel_id=1, source_target_pairs={{0,0},{1,1},{2,2},{3,3},{4,48},{5,49},{6,50},{7,51},{8,32},{9,33},... | collective-permute-start | bytes 2752520 | tf_op jit(solution)/shard_map/ppermute | solution.py:98
  13.2 151.3 %all-gather.7.cloned.1.call-start = ((), (), s32[]{:S(2)}) async-start(), calls=%async_computation.2 | async-start | bytes 7798784 | tf_op jit(solution)/shard_map/all_gather | solution.py:122
  13.3 30.3 %collective-permute-start.1 = (bf16[512,896]{1,0:T(8,128)(2,1)S(1)}, bf16[512,896]{1,0:T(8,128)(2,1)S(1)}, u32[]{:S(2)}, u32[]{:S(2)}) collective-permute-start(bf16[512,896]{1,0:T(8,128)(2,1)S(1)} %copy-done.3), channel_id=1, source_target_pairs={{0,4},{1,5},{2,6},{3,7},{4,8},{5,9},{6,10},{7,11},{8,12},{9,13},{1... | collective-permute-start | bytes 2752520 | tf_op jit(solution)/shard_map/ppermute | solution.py:24
  23.0 52.9 %collective-permute-start.2 = (bf16[512,896]{1,0:T(8,128)(2,1)S(1)}, bf16[512,896]{1,0:T(8,128)(2,1)S(1)}, u32[]{:S(2)}, u32[]{:S(2)}) collective-permute-start(bf16[512,896]{1,0:T(8,128)(2,1)S(1)} %copy-done.3), channel_id=1, source_target_pairs={{0,8},{1,9},{2,10},{3,11},{4,12},{5,13},{6,14},{7,15},{8,0},{9,1},... | collective-permute-start | bytes 2752520 | tf_op jit(solution)/shard_map/ppermute | solution.py:24
  35.3 40.6 %collective-permute-start.3 = (bf16[512,896]{1,0:T(8,128)(2,1)S(1)}, bf16[512,896]{1,0:T(8,128)(2,1)}, u32[]{:S(2)}, u32[]{:S(2)}) collective-permute-start(bf16[512,896]{1,0:T(8,128)(2,1)S(1)} %copy-done.3), channel_id=1, source_target_pairs={{0,12},{1,13},{2,14},{3,15},{4,0},{5,1},{6,2},{7,3},{8,4},{9,5},{1... | collective-permute-start | bytes 2752520 | tf_op jit(solution)/shard_map/ppermute | solution.py:24
  124.0 21.5 %collective-permute-start.15 = (f32[4,128,64]{1,2,0:T(8,128)S(1)}, f32[4,128,64]{1,2,0:T(8,128)S(1)}, u32[]{:S(2)}, u32[]{:S(2)}) collective-permute-start(f32[4,128,64]{1,2,0:T(8,128)S(1)} %convolution_bitcast_fusion.4), channel_id=1, source_target_pairs={{0,3},{1,0},{2,1},{3,2},{4,7},{5,4},{6,5},{7,6},{8,11},{9,8},{10,9... | collective-permute-start | bytes 393224 | tf_op jit(solution)/shard_map/ppermute | solution.py:24
  126.8 18.7 %collective-permute-start.13 = (f32[4,128,64]{1,2,0:T(8,128)S(1)}, f32[4,128,64]{1,2,0:T(8,128)S(1)}, u32[]{:S(2)}, u32[]{:S(2)}) collective-permute-start(f32[4,128,64]{1,2,0:T(8,128)S(1)} %convolution_bitcast_fusion.4), channel_id=1, source_target_pairs={{0,1},{1,2},{2,3},{3,0},{4,5},{5,6},{6,7},{7,4},{8,9},{9,10},{10,1... | collective-permute-start | bytes 393224 | tf_op jit(solution)/shard_map/ppermute | solution.py:24
  126.8 18.7 %collective-permute-start.14 = (f32[4,128,64]{1,2,0:T(8,128)S(1)}, f32[4,128,64]{1,2,0:T(8,128)S(1)}, u32[]{:S(2)}, u32[]{:S(2)}) collective-permute-start(f32[4,128,64]{1,2,0:T(8,128)S(1)} %convolution_bitcast_fusion.4), channel_id=1, source_target_pairs={{0,2},{1,3},{2,0},{3,1},{4,6},{5,7},{6,4},{7,5},{8,10},{9,11},{10,... | collective-permute-start | bytes 393224 | tf_op jit(solution)/shard_map/ppermute | solution.py:24
  129.1 6.5 %copy-start = (bf16[25600,256]{1,0:T(8,128)(2,1)S(1)}, bf16[25600,256]{1,0:T(8,128)(2,1)}, u32[]{:S(2)}) copy-start(bf16[25600,256]{1,0:T(8,128)(2,1)} %all-gather.5.cloned.1.call-done) | copy-start | bytes 39321604
  131.3 19.3 %copy-start.1 = (bf16[4,4,4,32,896]{4,3,2,1,0:T(8,128)(2,1)}, bf16[4,4,4,32,896]{4,3,2,1,0:T(8,128)(2,1)S(1)}, u32[]{:S(2)}) copy-start(bf16[4,4,4,32,896]{4,3,2,1,0:T(8,128)(2,1)S(1)} %copy.35) | copy-start | bytes 11010052
  137.5 25.0 %collective-permute-start.6 = (bf16[4,4,32,256]{3,2,1,0:T(8,128)(2,1)S(1)}, bf16[4,4,32,256]{3,2,1,0:T(8,128)(2,1)}, u32[]{:S(2)}, u32[]{:S(2)}) collective-permute-start(bf16[4,4,32,256]{3,2,1,0:T(8,128)(2,1)S(1)} %bitcast.195), channel_id=1, source_target_pairs={{0,3},{1,0},{2,1},{3,2},{4,7},{5,4},{6,5},{7,6},{8,11},{9,8},{10,9... | collective-permute-start | bytes 786440 | tf_op jit(solution)/shard_map/ppermute | solution.py:24
  142.6 19.9 %collective-permute-start.5 = (bf16[4,4,32,256]{3,2,1,0:T(8,128)(2,1)S(1)}, bf16[4,4,32,256]{3,2,1,0:T(8,128)(2,1)}, u32[]{:S(2)}, u32[]{:S(2)}) collective-permute-start(bf16[4,4,32,256]{3,2,1,0:T(8,128)(2,1)S(1)} %bitcast.196), channel_id=1, source_target_pairs={{0,2},{1,3},{2,0},{3,1},{4,6},{5,7},{6,4},{7,5},{8,10},{9,11},{10,... | collective-permute-start | bytes 786440 | tf_op jit(solution)/shard_map/ppermute | solution.py:24
  145.5 8.7 %collective-permute-start.18 = (f32[4,128,64]{1,2,0:T(8,128)S(1)}, f32[4,128,64]{1,2,0:T(8,128)}, u32[]{:S(2)}, u32[]{:S(2)}) collective-permute-start(f32[4,128,64]{1,2,0:T(8,128)S(1)} %add_add_fusion), channel_id=1, source_target_pairs={{0,12},{1,13},{2,14},{3,15},{4,0},{5,1},{6,2},{7,3},{8,4},{9,5},{1... | collective-permute-start | bytes 393224 | tf_op jit(solution)/shard_map/ppermute | solution.py:24
  148.3 8.1 %collective-permute-start.16 = (f32[4,128,64]{1,2,0:T(8,128)S(1)}, f32[4,128,64]{1,2,0:T(8,128)}, u32[]{:S(2)}, u32[]{:S(2)}) collective-permute-start(f32[4,128,64]{1,2,0:T(8,128)S(1)} %add_add_fusion), channel_id=1, source_target_pairs={{0,4},{1,5},{2,6},{3,7},{4,8},{5,9},{6,10},{7,11},{8,12},{9,13},{1... | collective-permute-start | bytes 393224 | tf_op jit(solution)/shard_map/ppermute | solution.py:24
  148.3 8.1 %collective-permute-start.17 = (f32[4,128,64]{1,2,0:T(8,128)S(1)}, f32[4,128,64]{1,2,0:T(8,128)}, u32[]{:S(2)}, u32[]{:S(2)}) collective-permute-start(f32[4,128,64]{1,2,0:T(8,128)S(1)} %add_add_fusion), channel_id=1, source_target_pairs={{0,8},{1,9},{2,10},{3,11},{4,12},{5,13},{6,14},{7,15},{8,0},{9,1},... | collective-permute-start | bytes 393224 | tf_op jit(solution)/shard_map/ppermute | solution.py:24
  154.2 8.3 %collective-permute-start.4 = (bf16[4,4,32,256]{3,2,1,0:T(8,128)(2,1)}, bf16[4,4,32,256]{3,2,1,0:T(8,128)(2,1)S(1)}, u32[]{:S(2)}, u32[]{:S(2)}) collective-permute-start(bf16[4,4,32,256]{3,2,1,0:T(8,128)(2,1)} %bitcast.197), channel_id=1, source_target_pairs={{0,1},{1,2},{2,3},{3,0},{4,5},{5,6},{6,7},{7,4},{8,9},{9,10},{10,1... | collective-permute-start | bytes 786440 | tf_op jit(solution)/shard_map/ppermute | solution.py:24
  158.6 39.0 %all-to-all-start = ((bf16[16,32,512]{2,1,0:T(8,128)(2,1)}), bf16[16,32,512]{2,1,0:T(8,128)(2,1)S(1)}, u32[]{:S(2)}, u32[]{:S(2)}) async-start(bf16[16,32,512]{2,1,0:T(8,128)(2,1)} %bitcast.70), calls=%async_computation | async-start | bytes 1048576 | tf_op jit(solution)/shard_map/all_to_all | solution.py:165
  164.6 4.6 %copy-start.2 = (bf16[4,4,4,32,896]{4,3,2,1,0:T(8,128)(2,1)S(1)}, bf16[4,4,4,32,896]{4,3,2,1,0:T(8,128)(2,1)}, u32[]{:S(2)}) copy-start(bf16[4,4,4,32,896]{4,3,2,1,0:T(8,128)(2,1)} %copy-done.1) | copy-start | bytes 11010052
  164.6 9.1 %slice-start = ((s8[7340032]{0:T(1024)(128)(4,1)}), s8[4194304]{0:T(1024)(128)(4,1)S(1)}, s32[]{:S(2)}) async-start(s8[7340032]{0:T(1024)(128)(4,1)} %bitcast.182), calls=%async_computation.3 | async-start | bytes 8388608
  169.2 4.5 %slice-start.1 = ((s8[7340032]{0:T(1024)(128)(4,1)}), s8[3145728]{0:T(1024)(128)(4,1)S(1)}, s32[]{:S(2)}) async-start(s8[7340032]{0:T(1024)(128)(4,1)} %bitcast.182), calls=%async_computation.4 | async-start | bytes 6291456
  174.8 14.4 %collective-permute-start.9 = (bf16[4,4,32,256]{3,2,1,0:T(8,128)(2,1)S(1)}, bf16[4,4,32,256]{3,2,1,0:T(8,128)(2,1)S(1)}, u32[]{:S(2)}, u32[]{:S(2)}) collective-permute-start(bf16[4,4,32,256]{3,2,1,0:T(8,128)(2,1)S(1)} %bitcast.200), channel_id=1, source_target_pairs={{0,3},{1,0},{2,1},{3,2},{4,7},{5,4},{6,5},{7,6},{8,11},{9,8},{10,9... | collective-permute-start | bytes 786440 | tf_op jit(solution)/shard_map/ppermute | solution.py:24
  177.6 11.6 %collective-permute-start.8 = (bf16[4,4,32,256]{3,2,1,0:T(8,128)(2,1)S(1)}, bf16[4,4,32,256]{3,2,1,0:T(8,128)(2,1)S(1)}, u32[]{:S(2)}, u32[]{:S(2)}) collective-permute-start(bf16[4,4,32,256]{3,2,1,0:T(8,128)(2,1)S(1)} %bitcast.199), channel_id=1, source_target_pairs={{0,2},{1,3},{2,0},{3,1},{4,6},{5,7},{6,4},{7,5},{8,10},{9,11},{10,... | collective-permute-start | bytes 786440 | tf_op jit(solution)/shard_map/ppermute | solution.py:24
  178.4 14.5 %collective-permute-start.7 = (bf16[4,4,32,256]{3,2,1,0:T(8,128)(2,1)S(1)}, bf16[4,4,32,256]{3,2,1,0:T(8,128)(2,1)S(1)}, u32[]{:S(2)}, u32[]{:S(2)}) collective-permute-start(bf16[4,4,32,256]{3,2,1,0:T(8,128)(2,1)S(1)} %bitcast.198), channel_id=1, source_target_pairs={{0,1},{1,2},{2,3},{3,0},{4,5},{5,6},{6,7},{7,4},{8,9},{9,10},{10,1... | collective-permute-start | bytes 786440 | tf_op jit(solution)/shard_map/ppermute | solution.py:24
  193.1 8.6 %collective-permute-start.12 = (bf16[4,32,512]{2,1,0:T(8,128)(2,1)S(1)}, bf16[4,32,512]{2,1,0:T(8,128)(2,1)S(1)}, u32[]{:S(2)}, u32[]{:S(2)}) collective-permute-start(bf16[4,32,512]{2,1,0:T(8,128)(2,1)S(1)} %get-tuple-element.22), channel_id=1, source_target_pairs={{0,12},{1,13},{2,14},{3,15},{4,0},{5,1},{6,2},{7,3},{8,4},{9,5},{1... | collective-permute-start | bytes 393224 | tf_op jit(solution)/shard_map/ppermute | solution.py:24
  195.9 7.9 %collective-permute-start.11 = (bf16[4,32,512]{2,1,0:T(8,128)(2,1)S(1)}, bf16[4,32,512]{2,1,0:T(8,128)(2,1)S(1)}, u32[]{:S(2)}, u32[]{:S(2)}) collective-permute-start(bf16[4,32,512]{2,1,0:T(8,128)(2,1)S(1)} %get-tuple-element.21), channel_id=1, source_target_pairs={{0,8},{1,9},{2,10},{3,11},{4,12},{5,13},{6,14},{7,15},{8,0},{9,1},... | collective-permute-start | bytes 393224 | tf_op jit(solution)/shard_map/ppermute | solution.py:24
  196.8 8.6 %collective-permute-start.10 = (bf16[4,32,512]{2,1,0:T(8,128)(2,1)S(1)}, bf16[4,32,512]{2,1,0:T(8,128)(2,1)S(1)}, u32[]{:S(2)}, u32[]{:S(2)}) collective-permute-start(bf16[4,32,512]{2,1,0:T(8,128)(2,1)S(1)} %get-tuple-element.20), channel_id=1, source_target_pairs={{0,4},{1,5},{2,6},{3,7},{4,8},{5,9},{6,10},{7,11},{8,12},{9,13},{1... | collective-permute-start | bytes 393224 | tf_op jit(solution)/shard_map/ppermute | solution.py:24
  205.5 2.2 %copy-start.5 = (pred[32]{0:T(512)(128)(4,1)S(1)}, pred[32]{0:T(512)(128)(4,1)}, u32[]{:S(2)}) copy-start(pred[32]{0:T(512)(128)(4,1)} %fusion.76) | copy-start | bytes 100
Sparse Core Ops, SparseCore 0:
  13.4 99.7 all-gather.4
  115.0 49.5 all-gather.6

commit v15 on v14

--- a/solution.py
+++ b/solution.py
@@ -151,17 +151,22 @@
             summed = arrived if summed is None else summed + arrived
         return (summed + rows_for(my_x).astype(jnp.float32)).astype(jnp.bfloat16)
 
-    total = jnp.concatenate(
-        [reduce_over_x(hidden_padded, w_first), reduce_over_x(hidden_column, w_second)], axis=3
-    )
+    order = (my_y - jnp.arange(side, dtype=jnp.int32)) % side
 
-    got = [lax.dynamic_index_in_dim(total, my_y, axis=1, keepdims=False)]
-    for s in range(1, side):
-        piece = lax.dynamic_index_in_dim(total, (my_y + s) % side, axis=1, keepdims=False)
-        got.append(tensor_shift(piece, side, s, True))
-    order = (my_y - jnp.arange(side, dtype=jnp.int32)) % side
-    result = jnp.take(jnp.stack(got, axis=0), order, axis=0)
-    result = jnp.transpose(result, (2, 1, 0, 3)).reshape(own_rows, pool_count * width)
+    def exchange_over_y(total):
+        got = [lax.dynamic_index_in_dim(total, my_y, axis=1, keepdims=False)]
+        for s in range(1, side):
+            piece = lax.dynamic_index_in_dim(total, (my_y + s) % side, axis=1, keepdims=False)
+            got.append(tensor_shift(piece, side, s, True))
+        return jnp.transpose(jnp.take(jnp.stack(got, axis=0), order, axis=0), (2, 1, 0, 3))
+
+    result = jnp.concatenate(
+        [
+            exchange_over_y(reduce_over_x(hidden_padded, w_first)),
+            exchange_over_y(reduce_over_x(hidden_column, w_second)),
+        ],
+        axis=3,
+    ).reshape(own_rows, pool_count * width)
     delta_mine = lax.all_to_all(delta, "tensor", split_axis=0, concat_axis=1, tiled=True)
     result = (result.astype(jnp.float32) + delta_mine.astype(jnp.float32)).astype(jnp.bfloat16)
 

time: 219 us -> 217 us (level); the launches traced: 215 us -> 216 us
  starting transfers between devices: 53.8 us -> 61.6 us
  waiting for transfers between devices: 98.5 us -> 90.7 us
    ppermute x18 -> x21, waiting for transfers between devices: 60.3 us -> 53.3 us  [tensor_shift(): return lax.ppermute(x, 'tensor', perm)]
    ppermute x18 -> x21, starting transfers between devices: 48 us -> 52.8 us  [tensor_shift(): return lax.ppermute(x, 'tensor', perm)]
    all_to_all x1, starting transfers between devices: 3.83 us -> 6.83 us  [shards(): lax.all_to_all(delta, 'tensor', split_axis=0, concat_axis=1, tiled=True)]
    unnamed x20 -> x22, local copies, waits for them, and re-layouts: 6.55 us -> 6.56 us
  transfers between devices with their start and end apart: 22 -> 25, of which waited for: 10 -> 10; matrix products, arithmetic and copies ran while one was open for 19% -> 19% of each run, Pallas kernels for 0% -> 0%
where the time goes in v15:
time: 217 us; the launch traced here: 216 us
  waiting for transfers between devices  90.7 us (42%)
  starting transfers between devices  61.6 us (28%)
  matrix products  22.5 us (10%)
  local copies, waits for them, and re-layouts  20.2 us (9%)
  between operations  14.1 us (6%)
  other arithmetic  7.34 us (3%)
    ppermute x21, waiting for transfers between devices, tensor_shift(): return lax.ppermute(x, 'tensor', perm)  53.3 us
    ppermute x21, starting transfers between devices, tensor_shift(): return lax.ppermute(x, 'tensor', perm)  52.8 us
    all_gather x1, waiting for transfers between devices, shards(): gathered = lax.all_gather(pack, 'pool', axis=0, tiled=False)  37.3 us
    dot_general x8, matrix products, rows_for(): jnp.einsum('sif,asfj->aij', rows, w_half, preferred_element_type=jnp.floa...  19.5 us
    all_to_all x1, starting transfers between devices, shards(): lax.all_to_all(delta, 'tensor', split_axis=0, concat_axis=1, tiled=True)  6.83 us
    unnamed x22, local copies, waits for them, and re-layouts  6.56 us
  transfers between devices with their start and end apart: 25, of which 10 were waited for; matrix products, arithmetic and copies ran while one was open for 19% of the time, Pallas kernels for 0%

profile of v15, /device:TPU:0, one launch (start us, length us, event | category | flops | bytes accessed | tf_op | source)
XLA Modules:
  0.0 216.3 jit_solution(12559824699835002346)
XLA Ops:
  6.5 2.0 collective-permute-start
  8.5 1.1 copy.34
  9.8 1.2 copy.33
  12.2 1.0 pad_maximum_fusion
  13.3 9.7 %collective-permute-start.1 = (bf16[512,896]{1,0:T(8,128)(2,1)S(1)}, bf16[512,896]{1,0:T(8,128)(2,1)S(1)}, u32[]{:S(2)}, u32[]{:S(2)}) collective-permute-start(bf16[512,896]{1,0:T(8,128)(2,1)S(1)} %copy-done.3), channel_id=1, source_target_pairs={{0,4},{1,5},{2,6},{3,7},{4,8},{5,9},{6,10},{7,11},{8,12},{9,13},{1... | collective-permute-start | bytes 2752520 | tf_op jit(solution)/shard_map/ppermute | solution.py:24
  22.9 12.3 %collective-permute-start.2 = (bf16[512,896]{1,0:T(8,128)(2,1)S(1)}, bf16[512,896]{1,0:T(8,128)(2,1)S(1)}, u32[]{:S(2)}, u32[]{:S(2)}) collective-permute-start(bf16[512,896]{1,0:T(8,128)(2,1)S(1)} %copy-done.3), channel_id=1, source_target_pairs={{0,8},{1,9},{2,10},{3,11},{4,12},{5,13},{6,14},{7,15},{8,0},{9,1},... | collective-permute-start | bytes 2752520 | tf_op jit(solution)/shard_map/ppermute | solution.py:24
  35.2 2.5 %collective-permute-start.3 = (bf16[512,896]{1,0:T(8,128)(2,1)S(1)}, bf16[512,896]{1,0:T(8,128)(2,1)}, u32[]{:S(2)}, u32[]{:S(2)}) collective-permute-start(bf16[512,896]{1,0:T(8,128)(2,1)S(1)} %copy-done.3), channel_id=1, source_target_pairs={{0,12},{1,13},{2,14},{3,15},{4,0},{5,1},{6,2},{7,3},{8,4},{9,5},{1... | collective-permute-start | bytes 2752520 | tf_op jit(solution)/shard_map/ppermute | solution.py:24
  37.8 5.8 %collective-permute-done.1 = bf16[512,896]{1,0:T(8,128)(2,1)S(1)} collective-permute-done((bf16[512,896]{1,0:T(8,128)(2,1)S(1)}, bf16[512,896]{1,0:T(8,128)(2,1)S(1)}, u32[]{:S(2)}, u32[]{:S(2)}) %collective-permute-start.1) | collective-permute-done | bytes 917536 | tf_op jit(solution)/shard_map/ppermute | solution.py:24
  43.6 32.3 %collective-permute-done.2 = bf16[512,896]{1,0:T(8,128)(2,1)S(1)} collective-permute-done((bf16[512,896]{1,0:T(8,128)(2,1)S(1)}, bf16[512,896]{1,0:T(8,128)(2,1)S(1)}, u32[]{:S(2)}, u32[]{:S(2)}) %collective-permute-start.2) | collective-permute-done | bytes 917536 | tf_op jit(solution)/shard_map/ppermute | solution.py:24
  75.9 37.3 %all-gather.5.cloned.1.call-done = bf16[25600,256]{1,0:T(8,128)(2,1)} async-done(((bf16[1600,256]{1,0:T(8,128)(2,1)}), bf16[25600,256]{1,0:T(8,128)(2,1)}) %all-gather.5.cloned.1.call-update) | async-done | bytes 13107216 | tf_op jit(solution)/shard_map/all_gather | solution.py:111
  114.1 4.2 %slice.14 = bf16[16,448,256]{2,1,0:T(8,128)(2,1)} slice(bf16[16,1600,256]{2,1,0:T(8,128)(2,1)} %bitcast.177), slice={[0:16], [896:1344], [0:256]} | slice | bytes 7340032 | tf_op jit(solution)/shard_map/slice | solution.py:116
  118.3 2.6 %gather_fusion = bf16[4,224,256]{2,1,0:T(8,128)(2,1)S(1)} fusion(bf16[32,224,256]{2,1,0:T(8,128)(2,1)} %bitcast.197, s32[1024]{0:T(1024)S(1)} %pad_clamp_fusion), kind=kCustom, calls=%fused_computation.2 | custom fusion | bytes 917520 | tf_op jit(solution)/shard_map/jit(_take)/gather | solution.py:132
  120.9 1.3 gather.16
  122.2 1.8 convolution_bitcast_fusion.4
  124.0 2.8 %collective-permute-start.18 = (f32[4,128,64]{1,2,0:T(8,128)S(1)}, f32[4,128,64]{1,2,0:T(8,128)S(1)}, u32[]{:S(2)}, u32[]{:S(2)}) collective-permute-start(f32[4,128,64]{1,2,0:T(8,128)S(1)} %convolution_bitcast_fusion.4), channel_id=1, source_target_pairs={{0,3},{1,0},{2,1},{3,2},{4,7},{5,4},{6,5},{7,6},{8,11},{9,8},{10,9... | collective-permute-start | bytes 393224 | tf_op jit(solution)/shard_map/ppermute | solution.py:24
  126.8 2.3 %collective-permute-start.17 = (f32[4,128,64]{1,2,0:T(8,128)S(1)}, f32[4,128,64]{1,2,0:T(8,128)}, u32[]{:S(2)}, u32[]{:S(2)}) collective-permute-start(f32[4,128,64]{1,2,0:T(8,128)S(1)} %convolution_bitcast_fusion.4), channel_id=1, source_target_pairs={{0,2},{1,3},{2,0},{3,1},{4,6},{5,7},{6,4},{7,5},{8,10},{9,11},{10,... | collective-permute-start | bytes 393224 | tf_op jit(solution)/shard_map/ppermute | solution.py:24
  129.1 1.8 maximum_bitcast_fusion
  131.4 4.2 %copy-done = bf16[25600,256]{1,0:T(8,128)(2,1)S(1)} copy-done((bf16[25600,256]{1,0:T(8,128)(2,1)S(1)}, bf16[25600,256]{1,0:T(8,128)(2,1)}, u32[]{:S(2)}) %copy-start) | copy-done | bytes 13107224
  135.6 2.6 %fusion.36 = bf16[4,256,128]{1,2,0:T(8,128)(2,1)} fusion(bf16[4,4,1600,256]{3,2,1,0:T(8,128)(2,1)S(1)} %bitcast.178, s32[]{:T(128)S(6)} %select_n.147, bf16[4,4,128,896]{3,2,1,0:T(8,128)(2,1)S(1)} %bitcast.183), kind=kOutput, calls=%fused_computation.34 | convolution fusion | flops 1677852672 | bytes 17039364 | tf_op jit(solution)/shard_map/sif,asfj->aij/dot_general | solution.py:145
  138.2 1.1 collective-permute-start.6
  139.3 1.9 fusion.33
  141.2 3.1 %collective-permute-start.5 = (bf16[4,4,32,256]{3,2,1,0:T(8,128)(2,1)S(1)}, bf16[4,4,32,256]{3,2,1,0:T(8,128)(2,1)}, u32[]{:S(2)}, u32[]{:S(2)}) collective-permute-start(bf16[4,4,32,256]{3,2,1,0:T(8,128)(2,1)S(1)} %bitcast.206), channel_id=1, source_target_pairs={{0,2},{1,3},{2,0},{3,1},{4,6},{5,7},{6,4},{7,5},{8,10},{9,11},{10,... | collective-permute-start | bytes 786440 | tf_op jit(solution)/shard_map/ppermute | solution.py:24
  144.3 1.9 fusion.30
  146.3 1.9 fusion.42
  149.1 1.1 add_add_fusion
  150.2 2.8 %collective-permute-start.21 = (f32[4,128,64]{1,2,0:T(8,128)S(1)}, f32[4,128,64]{1,2,0:T(8,128)S(1)}, u32[]{:S(2)}, u32[]{:S(2)}) collective-permute-start(f32[4,128,64]{1,2,0:T(8,128)S(1)} %add_add_fusion), channel_id=1, source_target_pairs={{0,12},{1,13},{2,14},{3,15},{4,0},{5,1},{6,2},{7,3},{8,4},{9,5},{1... | collective-permute-start | bytes 393224 | tf_op jit(solution)/shard_map/ppermute | solution.py:24
  153.0 2.3 %collective-permute-start.20 = (f32[4,128,64]{1,2,0:T(8,128)S(1)}, f32[4,128,64]{1,2,0:T(8,128)S(1)}, u32[]{:S(2)}, u32[]{:S(2)}) collective-permute-start(f32[4,128,64]{1,2,0:T(8,128)S(1)} %add_add_fusion), channel_id=1, source_target_pairs={{0,8},{1,9},{2,10},{3,11},{4,12},{5,13},{6,14},{7,15},{8,0},{9,1},... | collective-permute-start | bytes 393224 | tf_op jit(solution)/shard_map/ppermute | solution.py:24
  155.3 0.9 collective-permute-done.4
  156.3 1.3 add_convert_fusion.2
  157.6 2.8 %collective-permute-start.9 = (bf16[4,32,256]{2,1,0:T(8,128)(2,1)S(1)}, bf16[4,32,256]{2,1,0:T(8,128)(2,1)S(1)}, u32[]{:S(2)}, u32[]{:S(2)}) collective-permute-start(bf16[4,32,256]{2,1,0:T(8,128)(2,1)S(1)} %get-tuple-element.21), channel_id=1, source_target_pairs={{0,12},{1,13},{2,14},{3,15},{4,0},{5,1},{6,2},{7,3},{8,4},{9,5},{1... | collective-permute-start | bytes 196616 | tf_op jit(solution)/shard_map/ppermute | solution.py:24
  161.2 0.9 collective-permute-start.7
  162.1 1.2 fusion.12
  163.3 6.8 %all-to-all-start = ((bf16[16,32,512]{2,1,0:T(8,128)(2,1)}), bf16[16,32,512]{2,1,0:T(8,128)(2,1)S(1)}, u32[]{:S(2)}, u32[]{:S(2)}) async-start(bf16[16,32,512]{2,1,0:T(8,128)(2,1)} %bitcast.77), calls=%async_computation | async-start | bytes 1048576 | tf_op jit(solution)/shard_map/all_to_all | solution.py:170
  170.8 4.6 %fusion.27 = bf16[4,256,128]{1,2,0:T(8,128)(2,1)S(1)} fusion(bf16[4,4,896,256]{3,2,1,0:T(8,128)(2,1)} %bitcast.191, bf16[4,4,128,896]{3,2,1,0:T(8,128)(2,1)} %bitcast.187, s32[]{:T(128)S(6)} %select_n.147), kind=kOutput, calls=%fused_computation.29 | convolution fusion | flops 939655168 | bytes 8519684 | tf_op jit(solution)/shard_map/sif,asfj->aij/dot_general | solution.py:145
  175.5 4.4 %fusion.26 = bf16[4,256,128]{1,2,0:T(8,128)(2,1)S(1)} fusion(bf16[4,4,896,256]{3,2,1,0:T(8,128)(2,1)} %bitcast.192, bf16[4,4,128,896]{3,2,1,0:T(8,128)(2,1)S(1)} %bitcast.188, s32[]{:T(128)S(6)} %select_n.145), kind=kOutput, calls=%fused_computation.28 | convolution fusion | flops 939655168 | bytes 8519684 | tf_op jit(solution)/shard_map/sif,asfj->aij/dot_general | solution.py:145
  179.9 1.1 fusion.25
  181.1 3.2 %collective-permute-start.12 = (bf16[4,4,32,256]{3,2,1,0:T(8,128)(2,1)S(1)}, bf16[4,4,32,256]{3,2,1,0:T(8,128)(2,1)S(1)}, u32[]{:S(2)}, u32[]{:S(2)}) collective-permute-start(bf16[4,4,32,256]{3,2,1,0:T(8,128)(2,1)S(1)} %bitcast.210), channel_id=1, source_target_pairs={{0,3},{1,0},{2,1},{3,2},{4,7},{5,4},{6,5},{7,6},{8,11},{9,8},{10,9... | collective-permute-start | bytes 786440 | tf_op jit(solution)/shard_map/ppermute | solution.py:24
  184.3 0.9 collective-permute-start.11
  185.1 0.9 collective-permute-start.10
  186.0 1.1 fusion.29
  187.1 6.0 %collective-permute-done.12 = bf16[4,4,32,256]{3,2,1,0:T(8,128)(2,1)S(1)} collective-permute-done((bf16[4,4,32,256]{3,2,1,0:T(8,128)(2,1)S(1)}, bf16[4,4,32,256]{3,2,1,0:T(8,128)(2,1)S(1)}, u32[]{:S(2)}, u32[]{:S(2)}) %collective-permute-start.12) | collective-permute-done | bytes 262176 | tf_op jit(solution)/shard_map/ppermute | solution.py:24
  193.1 1.0 collective-permute-done.11
  194.1 2.7 %collective-permute-done.10 = bf16[4,4,32,256]{3,2,1,0:T(8,128)(2,1)S(1)} collective-permute-done((bf16[4,4,32,256]{3,2,1,0:T(8,128)(2,1)S(1)}, bf16[4,4,32,256]{3,2,1,0:T(8,128)(2,1)S(1)}, u32[]{:S(2)}, u32[]{:S(2)}) %collective-permute-start.10) | collective-permute-done | bytes 262176 | tf_op jit(solution)/shard_map/ppermute | solution.py:24
  197.0 2.8 %collective-permute-start.15 = (bf16[4,32,256]{2,1,0:T(8,128)(2,1)S(1)}, bf16[4,32,256]{2,1,0:T(8,128)(2,1)S(1)}, u32[]{:S(2)}, u32[]{:S(2)}) collective-permute-start(bf16[4,32,256]{2,1,0:T(8,128)(2,1)S(1)} %get-tuple-element.25), channel_id=1, source_target_pairs={{0,12},{1,13},{2,14},{3,15},{4,0},{5,1},{6,2},{7,3},{8,4},{9,5},{1... | collective-permute-start | bytes 196616 | tf_op jit(solution)/shard_map/ppermute | solution.py:24
  199.8 0.8 collective-permute-start.14
  200.7 0.9 collective-permute-start.13
  202.0 3.6 %collective-permute-done.14 = bf16[4,32,256]{2,1,0:T(8,128)(2,1)S(1)} collective-permute-done((bf16[4,32,256]{2,1,0:T(8,128)(2,1)S(1)}, bf16[4,32,256]{2,1,0:T(8,128)(2,1)S(1)}, u32[]{:S(2)}, u32[]{:S(2)}) %collective-permute-start.14) | collective-permute-done | bytes 65568 | tf_op jit(solution)/shard_map/ppermute | solution.py:24
  208.6 0.9 fusion.55
  (73 shorter events, 8.8 us)
Async XLA Ops:
  6.5 6.7 %copy-start.3 = (bf16[512,896]{1,0:T(8,128)(2,1)S(1)}, bf16[512,896]{1,0:T(8,128)(2,1)}, u32[]{:S(2)}) copy-start(bf16[512,896]{1,0:T(8,128)(2,1)} %param.8) | copy-start | bytes 2752516
  6.5 106.9 %copy-start.5 = (s32[4]{0:T(128)S(1)}, s32[4]{0:T(128)}, u32[]{:S(2)}) copy-start(s32[4]{0:T(128)} %param.12) | copy-start | bytes 52
  6.5 106.9 %copy-start.7 = (s32[4]{0:T(128)S(1)}, s32[4]{0:T(128)}, u32[]{:S(2)}) copy-start(s32[4]{0:T(128)} %param.13) | copy-start | bytes 52
  6.5 106.6 %all-gather.5.cloned.1.call-start = ((), (), s32[]{:S(2)}) async-start(), calls=%async_computation.1 | async-start | bytes 13926400 | tf_op jit(solution)/shard_map/all_gather | solution.py:111
  6.5 4.8 %collective-permute-start = (bf16[896,512]{1,0:T(8,128)(2,1)}, bf16[896,512]{1,0:T(8,128)(2,1)S(1)}, u32[]{:S(2)}, u32[]{:S(2)}) collective-permute-start(bf16[896,512]{1,0:T(8,128)(2,1)} %param.9), channel_id=1, source_target_pairs={{0,0},{1,1},{2,2},{3,3},{4,48},{5,49},{6,50},{7,51},{8,32},{9,33},... | collective-permute-start | bytes 2752520 | tf_op jit(solution)/shard_map/ppermute | solution.py:98
  13.2 157.6 %all-gather.7.cloned.1.call-start = ((), (), s32[]{:S(2)}) async-start(), calls=%async_computation.2 | async-start | bytes 7798784 | tf_op jit(solution)/shard_map/all_gather | solution.py:122
  13.3 30.3 %collective-permute-start.1 = (bf16[512,896]{1,0:T(8,128)(2,1)S(1)}, bf16[512,896]{1,0:T(8,128)(2,1)S(1)}, u32[]{:S(2)}, u32[]{:S(2)}) collective-permute-start(bf16[512,896]{1,0:T(8,128)(2,1)S(1)} %copy-done.3), channel_id=1, source_target_pairs={{0,4},{1,5},{2,6},{3,7},{4,8},{5,9},{6,10},{7,11},{8,12},{9,13},{1... | collective-permute-start | bytes 2752520 | tf_op jit(solution)/shard_map/ppermute | solution.py:24
  22.9 52.9 %collective-permute-start.2 = (bf16[512,896]{1,0:T(8,128)(2,1)S(1)}, bf16[512,896]{1,0:T(8,128)(2,1)S(1)}, u32[]{:S(2)}, u32[]{:S(2)}) collective-permute-start(bf16[512,896]{1,0:T(8,128)(2,1)S(1)} %copy-done.3), channel_id=1, source_target_pairs={{0,8},{1,9},{2,10},{3,11},{4,12},{5,13},{6,14},{7,15},{8,0},{9,1},... | collective-permute-start | bytes 2752520 | tf_op jit(solution)/shard_map/ppermute | solution.py:24
  35.2 40.6 %collective-permute-start.3 = (bf16[512,896]{1,0:T(8,128)(2,1)S(1)}, bf16[512,896]{1,0:T(8,128)(2,1)}, u32[]{:S(2)}, u32[]{:S(2)}) collective-permute-start(bf16[512,896]{1,0:T(8,128)(2,1)S(1)} %copy-done.3), channel_id=1, source_target_pairs={{0,12},{1,13},{2,14},{3,15},{4,0},{5,1},{6,2},{7,3},{8,4},{9,5},{1... | collective-permute-start | bytes 2752520 | tf_op jit(solution)/shard_map/ppermute | solution.py:24
  124.0 22.1 %collective-permute-start.18 = (f32[4,128,64]{1,2,0:T(8,128)S(1)}, f32[4,128,64]{1,2,0:T(8,128)S(1)}, u32[]{:S(2)}, u32[]{:S(2)}) collective-permute-start(f32[4,128,64]{1,2,0:T(8,128)S(1)} %convolution_bitcast_fusion.4), channel_id=1, source_target_pairs={{0,3},{1,0},{2,1},{3,2},{4,7},{5,4},{6,5},{7,6},{8,11},{9,8},{10,9... | collective-permute-start | bytes 393224 | tf_op jit(solution)/shard_map/ppermute | solution.py:24
  126.8 22.3 %collective-permute-start.16 = (f32[4,128,64]{1,2,0:T(8,128)S(1)}, f32[4,128,64]{1,2,0:T(8,128)}, u32[]{:S(2)}, u32[]{:S(2)}) collective-permute-start(f32[4,128,64]{1,2,0:T(8,128)S(1)} %convolution_bitcast_fusion.4), channel_id=1, source_target_pairs={{0,1},{1,2},{2,3},{3,0},{4,5},{5,6},{6,7},{7,4},{8,9},{9,10},{10,1... | collective-permute-start | bytes 393224 | tf_op jit(solution)/shard_map/ppermute | solution.py:24
  126.8 22.3 %collective-permute-start.17 = (f32[4,128,64]{1,2,0:T(8,128)S(1)}, f32[4,128,64]{1,2,0:T(8,128)}, u32[]{:S(2)}, u32[]{:S(2)}) collective-permute-start(f32[4,128,64]{1,2,0:T(8,128)S(1)} %convolution_bitcast_fusion.4), channel_id=1, source_target_pairs={{0,2},{1,3},{2,0},{3,1},{4,6},{5,7},{6,4},{7,5},{8,10},{9,11},{10,... | collective-permute-start | bytes 393224 | tf_op jit(solution)/shard_map/ppermute | solution.py:24
  129.1 6.5 %copy-start = (bf16[25600,256]{1,0:T(8,128)(2,1)S(1)}, bf16[25600,256]{1,0:T(8,128)(2,1)}, u32[]{:S(2)}) copy-start(bf16[25600,256]{1,0:T(8,128)(2,1)} %all-gather.5.cloned.1.call-done) | copy-start | bytes 39321604
  131.4 14.9 %copy-start.1 = (bf16[4,4,4,32,896]{4,3,2,1,0:T(8,128)(2,1)}, bf16[4,4,4,32,896]{4,3,2,1,0:T(8,128)(2,1)S(1)}, u32[]{:S(2)}) copy-start(bf16[4,4,4,32,896]{4,3,2,1,0:T(8,128)(2,1)S(1)} %copy.35) | copy-start | bytes 11010052
  138.2 14.8 %collective-permute-start.6 = (bf16[4,4,32,256]{3,2,1,0:T(8,128)(2,1)}, bf16[4,4,32,256]{3,2,1,0:T(8,128)(2,1)}, u32[]{:S(2)}, u32[]{:S(2)}) collective-permute-start(bf16[4,4,32,256]{3,2,1,0:T(8,128)(2,1)} %bitcast.25), channel_id=1, source_target_pairs={{0,3},{1,0},{2,1},{3,2},{4,7},{5,4},{6,5},{7,6},{8,11},{9,8},{10,9... | collective-permute-start | bytes 786440 | tf_op jit(solution)/shard_map/ppermute | solution.py:24
  141.2 14.2 %collective-permute-start.5 = (bf16[4,4,32,256]{3,2,1,0:T(8,128)(2,1)S(1)}, bf16[4,4,32,256]{3,2,1,0:T(8,128)(2,1)}, u32[]{:S(2)}, u32[]{:S(2)}) collective-permute-start(bf16[4,4,32,256]{3,2,1,0:T(8,128)(2,1)S(1)} %bitcast.206), channel_id=1, source_target_pairs={{0,2},{1,3},{2,0},{3,1},{4,6},{5,7},{6,4},{7,5},{8,10},{9,11},{10,... | collective-permute-start | bytes 786440 | tf_op jit(solution)/shard_map/ppermute | solution.py:24
  146.1 2.0 copy-start.4
  146.2 10.1 %collective-permute-start.4 = (bf16[4,4,32,256]{3,2,1,0:T(8,128)(2,1)S(1)}, bf16[4,4,32,256]{3,2,1,0:T(8,128)(2,1)}, u32[]{:S(2)}, u32[]{:S(2)}) collective-permute-start(bf16[4,4,32,256]{3,2,1,0:T(8,128)(2,1)S(1)} %bitcast.207), channel_id=1, source_target_pairs={{0,1},{1,2},{2,3},{3,0},{4,5},{5,6},{6,7},{7,4},{8,9},{9,10},{10,1... | collective-permute-start | bytes 786440 | tf_op jit(solution)/shard_map/ppermute | solution.py:24
  150.2 11.0 %collective-permute-start.21 = (f32[4,128,64]{1,2,0:T(8,128)S(1)}, f32[4,128,64]{1,2,0:T(8,128)S(1)}, u32[]{:S(2)}, u32[]{:S(2)}) collective-permute-start(f32[4,128,64]{1,2,0:T(8,128)S(1)} %add_add_fusion), channel_id=1, source_target_pairs={{0,12},{1,13},{2,14},{3,15},{4,0},{5,1},{6,2},{7,3},{8,4},{9,5},{1... | collective-permute-start | bytes 393224 | tf_op jit(solution)/shard_map/ppermute | solution.py:24
  153.0 9.1 %collective-permute-start.19 = (f32[4,128,64]{1,2,0:T(8,128)S(1)}, f32[4,128,64]{1,2,0:T(8,128)S(1)}, u32[]{:S(2)}, u32[]{:S(2)}) collective-permute-start(f32[4,128,64]{1,2,0:T(8,128)S(1)} %add_add_fusion), channel_id=1, source_target_pairs={{0,4},{1,5},{2,6},{3,7},{4,8},{5,9},{6,10},{7,11},{8,12},{9,13},{1... | collective-permute-start | bytes 393224 | tf_op jit(solution)/shard_map/ppermute | solution.py:24
  153.0 9.0 %collective-permute-start.20 = (f32[4,128,64]{1,2,0:T(8,128)S(1)}, f32[4,128,64]{1,2,0:T(8,128)S(1)}, u32[]{:S(2)}, u32[]{:S(2)}) collective-permute-start(f32[4,128,64]{1,2,0:T(8,128)S(1)} %add_add_fusion), channel_id=1, source_target_pairs={{0,8},{1,9},{2,10},{3,11},{4,12},{5,13},{6,14},{7,15},{8,0},{9,1},... | collective-permute-start | bytes 393224 | tf_op jit(solution)/shard_map/ppermute | solution.py:24
  157.6 12.5 %collective-permute-start.9 = (bf16[4,32,256]{2,1,0:T(8,128)(2,1)S(1)}, bf16[4,32,256]{2,1,0:T(8,128)(2,1)S(1)}, u32[]{:S(2)}, u32[]{:S(2)}) collective-permute-start(bf16[4,32,256]{2,1,0:T(8,128)(2,1)S(1)} %get-tuple-element.21), channel_id=1, source_target_pairs={{0,12},{1,13},{2,14},{3,15},{4,0},{5,1},{6,2},{7,3},{8,4},{9,5},{1... | collective-permute-start | bytes 196616 | tf_op jit(solution)/shard_map/ppermute | solution.py:24
  160.4 9.7 %collective-permute-start.8 = (bf16[4,32,256]{2,1,0:T(8,128)(2,1)S(1)}, bf16[4,32,256]{2,1,0:T(8,128)(2,1)S(1)}, u32[]{:S(2)}, u32[]{:S(2)}) collective-permute-start(bf16[4,32,256]{2,1,0:T(8,128)(2,1)S(1)} %get-tuple-element.22), channel_id=1, source_target_pairs={{0,8},{1,9},{2,10},{3,11},{4,12},{5,13},{6,14},{7,15},{8,0},{9,1},... | collective-permute-start | bytes 196616 | tf_op jit(solution)/shard_map/ppermute | solution.py:24
  161.2 8.9 %collective-permute-start.7 = (bf16[4,32,256]{2,1,0:T(8,128)(2,1)S(1)}, bf16[4,32,256]{2,1,0:T(8,128)(2,1)S(1)}, u32[]{:S(2)}, u32[]{:S(2)}) collective-permute-start(bf16[4,32,256]{2,1,0:T(8,128)(2,1)S(1)} %get-tuple-element.23), channel_id=1, source_target_pairs={{0,4},{1,5},{2,6},{3,7},{4,8},{5,9},{6,10},{7,11},{8,12},{9,13},{1... | collective-permute-start | bytes 196616 | tf_op jit(solution)/shard_map/ppermute | solution.py:24
  163.3 38.2 %all-to-all-start = ((bf16[16,32,512]{2,1,0:T(8,128)(2,1)}), bf16[16,32,512]{2,1,0:T(8,128)(2,1)S(1)}, u32[]{:S(2)}, u32[]{:S(2)}) async-start(bf16[16,32,512]{2,1,0:T(8,128)(2,1)} %bitcast.77), calls=%async_computation | async-start | bytes 1048576 | tf_op jit(solution)/shard_map/all_to_all | solution.py:170
  170.8 4.7 %copy-start.2 = (bf16[4,4,4,32,896]{4,3,2,1,0:T(8,128)(2,1)S(1)}, bf16[4,4,4,32,896]{4,3,2,1,0:T(8,128)(2,1)}, u32[]{:S(2)}) copy-start(bf16[4,4,4,32,896]{4,3,2,1,0:T(8,128)(2,1)} %copy-done.1) | copy-start | bytes 11010052
  170.8 9.1 %slice-start = ((s8[7340032]{0:T(1024)(128)(4,1)}), s8[4194304]{0:T(1024)(128)(4,1)S(1)}, s32[]{:S(2)}) async-start(s8[7340032]{0:T(1024)(128)(4,1)} %bitcast.193), calls=%async_computation.3 | async-start | bytes 8388608
  175.5 4.5 %slice-start.1 = ((s8[7340032]{0:T(1024)(128)(4,1)}), s8[3145728]{0:T(1024)(128)(4,1)S(1)}, s32[]{:S(2)}) async-start(s8[7340032]{0:T(1024)(128)(4,1)} %bitcast.193), calls=%async_computation.4 | async-start | bytes 6291456
  181.1 12.1 %collective-permute-start.12 = (bf16[4,4,32,256]{3,2,1,0:T(8,128)(2,1)S(1)}, bf16[4,4,32,256]{3,2,1,0:T(8,128)(2,1)S(1)}, u32[]{:S(2)}, u32[]{:S(2)}) collective-permute-start(bf16[4,4,32,256]{3,2,1,0:T(8,128)(2,1)S(1)} %bitcast.210), channel_id=1, source_target_pairs={{0,3},{1,0},{2,1},{3,2},{4,7},{5,4},{6,5},{7,6},{8,11},{9,8},{10,9... | collective-permute-start | bytes 786440 | tf_op jit(solution)/shard_map/ppermute | solution.py:24
  184.3 9.9 %collective-permute-start.11 = (bf16[4,4,32,256]{3,2,1,0:T(8,128)(2,1)S(1)}, bf16[4,4,32,256]{3,2,1,0:T(8,128)(2,1)S(1)}, u32[]{:S(2)}, u32[]{:S(2)}) collective-permute-start(bf16[4,4,32,256]{3,2,1,0:T(8,128)(2,1)S(1)} %bitcast.209), channel_id=1, source_target_pairs={{0,2},{1,3},{2,0},{3,1},{4,6},{5,7},{6,4},{7,5},{8,10},{9,11},{10,... | collective-permute-start | bytes 786440 | tf_op jit(solution)/shard_map/ppermute | solution.py:24
  185.1 11.7 %collective-permute-start.10 = (bf16[4,4,32,256]{3,2,1,0:T(8,128)(2,1)S(1)}, bf16[4,4,32,256]{3,2,1,0:T(8,128)(2,1)S(1)}, u32[]{:S(2)}, u32[]{:S(2)}) collective-permute-start(bf16[4,4,32,256]{3,2,1,0:T(8,128)(2,1)S(1)} %bitcast.208), channel_id=1, source_target_pairs={{0,1},{1,2},{2,3},{3,0},{4,5},{5,6},{6,7},{7,4},{8,9},{9,10},{10,1... | collective-permute-start | bytes 786440 | tf_op jit(solution)/shard_map/ppermute | solution.py:24
  197.0 5.0 %collective-permute-start.15 = (bf16[4,32,256]{2,1,0:T(8,128)(2,1)S(1)}, bf16[4,32,256]{2,1,0:T(8,128)(2,1)S(1)}, u32[]{:S(2)}, u32[]{:S(2)}) collective-permute-start(bf16[4,32,256]{2,1,0:T(8,128)(2,1)S(1)} %get-tuple-element.25), channel_id=1, source_target_pairs={{0,12},{1,13},{2,14},{3,15},{4,0},{5,1},{6,2},{7,3},{8,4},{9,5},{1... | collective-permute-start | bytes 196616 | tf_op jit(solution)/shard_map/ppermute | solution.py:24
  199.8 5.8 %collective-permute-start.14 = (bf16[4,32,256]{2,1,0:T(8,128)(2,1)S(1)}, bf16[4,32,256]{2,1,0:T(8,128)(2,1)S(1)}, u32[]{:S(2)}, u32[]{:S(2)}) collective-permute-start(bf16[4,32,256]{2,1,0:T(8,128)(2,1)S(1)} %get-tuple-element.26), channel_id=1, source_target_pairs={{0,8},{1,9},{2,10},{3,11},{4,12},{5,13},{6,14},{7,15},{8,0},{9,1},... | collective-permute-start | bytes 196616 | tf_op jit(solution)/shard_map/ppermute | solution.py:24
  200.7 5.6 %collective-permute-start.13 = (bf16[4,32,256]{2,1,0:T(8,128)(2,1)S(1)}, bf16[4,32,256]{2,1,0:T(8,128)(2,1)S(1)}, u32[]{:S(2)}, u32[]{:S(2)}) collective-permute-start(bf16[4,32,256]{2,1,0:T(8,128)(2,1)S(1)} %get-tuple-element.27), channel_id=1, source_target_pairs={{0,4},{1,5},{2,6},{3,7},{4,8},{5,9},{6,10},{7,11},{8,12},{9,13},{1... | collective-permute-start | bytes 196616 | tf_op jit(solution)/shard_map/ppermute | solution.py:24
  206.3 2.2 %copy-start.6 = (pred[32]{0:T(512)(128)(4,1)S(1)}, pred[32]{0:T(512)(128)(4,1)}, u32[]{:S(2)}) copy-start(pred[32]{0:T(512)(128)(4,1)} %fusion.68) | copy-start | bytes 100
Sparse Core Ops, SparseCore 0:
  13.3 99.7 all-gather.4
  115.0 49.5 all-gather.6

commit v16 on v15

--- a/solution.py
+++ b/solution.py
@@ -113,12 +113,6 @@
     later, gathered, pieces = lax.optimization_barrier((moved[:, half:], gathered, pieces))
     plane_rows = gathered.shape[1]
     w_first = gathered.reshape(quarter, side, plane_rows, half)
-    shrink_all = gathered[:, feat:feat + shrink_rows, :].reshape(
-        pool_count * held, shrink_rows // held, half
-    )
-    expand_all = gathered[:, feat + shrink_rows:, :].reshape(
-        pool_count * held, expand_rows // held, half
-    )
     w_second = lax.all_gather(later, "pool", axis=0, tiled=False).reshape(
         quarter, side, feat, half
     )
@@ -129,8 +123,24 @@
     )
     hidden_padded = jnp.pad(hidden_column, ((0, 0), (0, 0), (0, 0), (0, plane_rows - feat)))
 
-    first = jnp.take(shrink_all, block_adapter, axis=0).reshape(block_count, feat, rank)
-    second = jnp.take(expand_all, block_adapter, axis=0).reshape(block_count, column_span, rank)
+    shrink_part = shrink_rows // held
+    expand_part = expand_rows // held
+    first = jnp.stack([
+        lax.dynamic_slice(
+            gathered,
+            (block_adapter[b] // held, feat + (block_adapter[b] % held) * shrink_part, 0),
+            (1, shrink_part, half),
+        )[0]
+        for b in range(block_count)
+    ]).reshape(block_count, feat, rank)
+    second = jnp.stack([
+        lax.dynamic_slice(
+            gathered,
+            (block_adapter[b] // held, feat + shrink_rows + (block_adapter[b] % held) * expand_part, 0),
+            (1, expand_part, half),
+        )[0]
+        for b in range(block_count)
+    ]).reshape(block_count, column_span, rank)
     blocks = hidden.reshape(block_count, BLOCK, feat)
     shrink = jnp.einsum("bnf,bfr->bnr", blocks, first, preferred_element_type=jnp.float32)
     summed_shrink = tensor_allsum(shrink, side).astype(jnp.bfloat16)

time: 217 us -> 218 us (level)
  between operations: 14.1 us -> 23.9 us
  local copies, waits for them, and re-layouts: 20.2 us -> 14.4 us
    gather x4 -> x0, local copies, waits for them, and re-layouts: 4.72 us -> none  [the longest x2 3.92 us: shards(): jnp.take(shrink_all, block_adapter, axis=0).reshape(block_count, feat, rank)]
    slice x2 -> x1, local copies, waits for them, and re-layouts: 4.35 us -> 0.66 us  [shards(): block_adapter[b] // held]
    unnamed x22 -> x18, local copies, waits for them, and re-layouts: 6.56 us -> 7.45 us
  transfers between devices with their start and end apart: 25 -> 25, of which waited for: 10 -> 9; matrix products, arithmetic and copies ran while one was open for 19% -> 14% of each run, Pallas kernels for 0% -> 0%
where the time goes in v16:
time: 218 us; the launch traced here: 217 us
  waiting for transfers between devices  90.7 us (42%)
  starting transfers between devices  62 us (28%)
  between operations  23.9 us (11%)
  matrix products  20.5 us (9%)
  local copies, waits for them, and re-layouts  14.4 us (7%)
  other arithmetic  5.73 us (3%)
    ppermute x21, waiting for transfers between devices, tensor_shift(): return lax.ppermute(x, 'tensor', perm)  53.4 us
    ppermute x21, starting transfers between devices, tensor_shift(): return lax.ppermute(x, 'tensor', perm)  53.1 us
    all_gather x1, waiting for transfers between devices, shards(): gathered = lax.all_gather(pack, 'pool', axis=0, tiled=False)  37.3 us
    dot_general x8, matrix products, rows_for(): jnp.einsum('sif,asfj->aij', rows, w_half, preferred_element_type=jnp.floa...  18.8 us
    unnamed x18, local copies, waits for them, and re-layouts  7.45 us
    all_to_all x1, starting transfers between devices, shards(): lax.all_to_all(delta, 'tensor', split_axis=0, concat_axis=1, tiled=True)  6.95 us
  transfers between devices with their start and end apart: 25, of which 9 were waited for; matrix products, arithmetic and copies ran while one was open for 14% of the time, Pallas kernels for 0%

profile of v16, /device:TPU:0, one launch (start us, length us, event | category | flops | bytes accessed | tf_op | source)
XLA Modules:
  0.0 217.4 jit_solution(5782270389027730301)
XLA Ops:
  6.5 2.0 collective-permute-start
  8.5 1.1 copy.34
  9.8 1.2 copy.33
  11.4 0.9 fusion.68
  12.2 1.0 pad_maximum_fusion
  13.3 9.7 %collective-permute-start.1 = (bf16[512,896]{1,0:T(8,128)(2,1)S(1)}, bf16[512,896]{1,0:T(8,128)(2,1)S(1)}, u32[]{:S(2)}, u32[]{:S(2)}) collective-permute-start(bf16[512,896]{1,0:T(8,128)(2,1)S(1)} %copy-done.4), channel_id=1, source_target_pairs={{0,4},{1,5},{2,6},{3,7},{4,8},{5,9},{6,10},{7,11},{8,12},{9,13},{1... | collective-permute-start | bytes 2752520 | tf_op jit(solution)/shard_map/ppermute | solution.py:24
  22.9 12.3 %collective-permute-start.2 = (bf16[512,896]{1,0:T(8,128)(2,1)S(1)}, bf16[512,896]{1,0:T(8,128)(2,1)S(1)}, u32[]{:S(2)}, u32[]{:S(2)}) collective-permute-start(bf16[512,896]{1,0:T(8,128)(2,1)S(1)} %copy-done.4), channel_id=1, source_target_pairs={{0,8},{1,9},{2,10},{3,11},{4,12},{5,13},{6,14},{7,15},{8,0},{9,1},... | collective-permute-start | bytes 2752520 | tf_op jit(solution)/shard_map/ppermute | solution.py:24
  35.2 2.5 %collective-permute-start.3 = (bf16[512,896]{1,0:T(8,128)(2,1)S(1)}, bf16[512,896]{1,0:T(8,128)(2,1)}, u32[]{:S(2)}, u32[]{:S(2)}) collective-permute-start(bf16[512,896]{1,0:T(8,128)(2,1)S(1)} %copy-done.4), channel_id=1, source_target_pairs={{0,12},{1,13},{2,14},{3,15},{4,0},{5,1},{6,2},{7,3},{8,4},{9,5},{1... | collective-permute-start | bytes 2752520 | tf_op jit(solution)/shard_map/ppermute | solution.py:24
  37.8 5.8 %collective-permute-done.1 = bf16[512,896]{1,0:T(8,128)(2,1)S(1)} collective-permute-done((bf16[512,896]{1,0:T(8,128)(2,1)S(1)}, bf16[512,896]{1,0:T(8,128)(2,1)S(1)}, u32[]{:S(2)}, u32[]{:S(2)}) %collective-permute-start.1) | collective-permute-done | bytes 917536 | tf_op jit(solution)/shard_map/ppermute | solution.py:24
  43.6 32.3 %collective-permute-done.2 = bf16[512,896]{1,0:T(8,128)(2,1)S(1)} collective-permute-done((bf16[512,896]{1,0:T(8,128)(2,1)S(1)}, bf16[512,896]{1,0:T(8,128)(2,1)S(1)}, u32[]{:S(2)}, u32[]{:S(2)}) %collective-permute-start.2) | collective-permute-done | bytes 917536 | tf_op jit(solution)/shard_map/ppermute | solution.py:24
  75.9 37.3 %all-gather.5.cloned.1.call-done = bf16[25600,256]{1,0:T(8,128)(2,1)} async-done(((bf16[1600,256]{1,0:T(8,128)(2,1)}), bf16[25600,256]{1,0:T(8,128)(2,1)}) %all-gather.5.cloned.1.call-update) | async-done | bytes 13107216 | tf_op jit(solution)/shard_map/all_gather | solution.py:111
  124.1 1.1 constant_dynamic-slice_fusion.7
  126.2 3.0 %collective-permute-start.18 = (f32[4,128,64]{1,2,0:T(8,128)S(1)}, f32[4,128,64]{1,2,0:T(8,128)S(1)}, u32[]{:S(2)}, u32[]{:S(2)}) collective-permute-start(f32[4,128,64]{1,2,0:T(8,128)S(1)} %convolution_bitcast_fusion.4), channel_id=1, source_target_pairs={{0,3},{1,0},{2,1},{3,2},{4,7},{5,4},{6,5},{7,6},{8,11},{9,8},{10,9... | collective-permute-start | bytes 393224 | tf_op jit(solution)/shard_map/ppermute | solution.py:24
  129.2 2.3 %collective-permute-start.17 = (f32[4,128,64]{1,2,0:T(8,128)S(1)}, f32[4,128,64]{1,2,0:T(8,128)}, u32[]{:S(2)}, u32[]{:S(2)}) collective-permute-start(f32[4,128,64]{1,2,0:T(8,128)S(1)} %convolution_bitcast_fusion.4), channel_id=1, source_target_pairs={{0,2},{1,3},{2,0},{3,1},{4,6},{5,7},{6,4},{7,5},{8,10},{9,11},{10,... | collective-permute-start | bytes 393224 | tf_op jit(solution)/shard_map/ppermute | solution.py:24
  131.5 1.9 maximum_bitcast_fusion
  134.0 4.4 %copy-done = bf16[25600,256]{1,0:T(8,128)(2,1)S(1)} copy-done((bf16[25600,256]{1,0:T(8,128)(2,1)S(1)}, bf16[25600,256]{1,0:T(8,128)(2,1)}, u32[]{:S(2)}) %copy-start) | copy-done | bytes 13107224
  138.4 1.9 fusion.36
  140.3 1.3 collective-permute-start.6
  141.5 1.9 fusion.33
  143.4 2.9 %collective-permute-start.5 = (bf16[4,4,32,256]{3,2,1,0:T(8,128)(2,1)S(1)}, bf16[4,4,32,256]{3,2,1,0:T(8,128)(2,1)S(1)}, u32[]{:S(2)}, u32[]{:S(2)}) collective-permute-start(bf16[4,4,32,256]{3,2,1,0:T(8,128)(2,1)S(1)} %bitcast.206), channel_id=1, source_target_pairs={{0,2},{1,3},{2,0},{3,1},{4,6},{5,7},{6,4},{7,5},{8,10},{9,11},{10,... | collective-permute-start | bytes 786440 | tf_op jit(solution)/shard_map/ppermute | solution.py:24
  146.3 1.9 fusion.42
  148.2 1.9 fusion.30
  150.6 0.9 add_add_fusion
  151.5 2.8 %collective-permute-start.21 = (f32[4,128,64]{1,2,0:T(8,128)S(1)}, f32[4,128,64]{1,2,0:T(8,128)S(1)}, u32[]{:S(2)}, u32[]{:S(2)}) collective-permute-start(f32[4,128,64]{1,2,0:T(8,128)S(1)} %add_add_fusion), channel_id=1, source_target_pairs={{0,12},{1,13},{2,14},{3,15},{4,0},{5,1},{6,2},{7,3},{8,4},{9,5},{1... | collective-permute-start | bytes 393224 | tf_op jit(solution)/shard_map/ppermute | solution.py:24
  154.4 2.3 %collective-permute-start.20 = (f32[4,128,64]{1,2,0:T(8,128)S(1)}, f32[4,128,64]{1,2,0:T(8,128)S(1)}, u32[]{:S(2)}, u32[]{:S(2)}) collective-permute-start(f32[4,128,64]{1,2,0:T(8,128)S(1)} %add_add_fusion), channel_id=1, source_target_pairs={{0,8},{1,9},{2,10},{3,11},{4,12},{5,13},{6,14},{7,15},{8,0},{9,1},... | collective-permute-start | bytes 393224 | tf_op jit(solution)/shard_map/ppermute | solution.py:24
  156.7 1.9 collective-permute-done.4
  158.8 2.8 %collective-permute-start.9 = (bf16[4,32,256]{2,1,0:T(8,128)(2,1)S(1)}, bf16[4,32,256]{2,1,0:T(8,128)(2,1)S(1)}, u32[]{:S(2)}, u32[]{:S(2)}) collective-permute-start(bf16[4,32,256]{2,1,0:T(8,128)(2,1)S(1)} %get-tuple-element.29), channel_id=1, source_target_pairs={{0,12},{1,13},{2,14},{3,15},{4,0},{5,1},{6,2},{7,3},{8,4},{9,5},{1... | collective-permute-start | bytes 196616 | tf_op jit(solution)/shard_map/ppermute | solution.py:24
  161.6 0.8 collective-permute-start.8
  162.4 0.9 collective-permute-start.7
  163.3 1.1 fusion.12
  164.4 6.9 %all-to-all-start = ((bf16[16,32,512]{2,1,0:T(8,128)(2,1)}), bf16[16,32,512]{2,1,0:T(8,128)(2,1)S(1)}, u32[]{:S(2)}, u32[]{:S(2)}) async-start(bf16[16,32,512]{2,1,0:T(8,128)(2,1)} %bitcast.79), calls=%async_computation | async-start | bytes 1048576 | tf_op jit(solution)/shard_map/all_to_all | solution.py:180
  172.1 4.6 %fusion.27 = bf16[4,256,128]{1,2,0:T(8,128)(2,1)S(1)} fusion(bf16[4,4,896,256]{3,2,1,0:T(8,128)(2,1)} %bitcast.195, bf16[4,4,128,896]{3,2,1,0:T(8,128)(2,1)} %bitcast.191, s32[]{:T(128)S(6)} %select_n.211), kind=kOutput, calls=%fused_computation.27 | convolution fusion | flops 939655168 | bytes 8519684 | tf_op jit(solution)/shard_map/sif,asfj->aij/dot_general | solution.py:155
  176.7 4.4 %fusion.26 = bf16[4,256,128]{1,2,0:T(8,128)(2,1)S(1)} fusion(bf16[4,4,896,256]{3,2,1,0:T(8,128)(2,1)} %bitcast.196, bf16[4,4,128,896]{3,2,1,0:T(8,128)(2,1)S(1)} %bitcast.192, s32[]{:T(128)S(6)} %select_n.209), kind=kOutput, calls=%fused_computation.26 | convolution fusion | flops 939655168 | bytes 8519684 | tf_op jit(solution)/shard_map/sif,asfj->aij/dot_general | solution.py:155
  181.2 0.7 copy-done.3
  181.9 1.1 fusion.25
  183.0 3.2 %collective-permute-start.12 = (bf16[4,4,32,256]{3,2,1,0:T(8,128)(2,1)S(1)}, bf16[4,4,32,256]{3,2,1,0:T(8,128)(2,1)S(1)}, u32[]{:S(2)}, u32[]{:S(2)}) collective-permute-start(bf16[4,4,32,256]{3,2,1,0:T(8,128)(2,1)S(1)} %bitcast.211), channel_id=1, source_target_pairs={{0,3},{1,0},{2,1},{3,2},{4,7},{5,4},{6,5},{7,6},{8,11},{9,8},{10,9... | collective-permute-start | bytes 786440 | tf_op jit(solution)/shard_map/ppermute | solution.py:24
  186.2 0.9 collective-permute-start.11
  187.1 0.9 collective-permute-start.10
  187.9 1.1 fusion.29
  189.1 5.1 %collective-permute-done.12 = bf16[4,4,32,256]{3,2,1,0:T(8,128)(2,1)S(1)} collective-permute-done((bf16[4,4,32,256]{3,2,1,0:T(8,128)(2,1)S(1)}, bf16[4,4,32,256]{3,2,1,0:T(8,128)(2,1)S(1)}, u32[]{:S(2)}, u32[]{:S(2)}) %collective-permute-start.12) | collective-permute-done | bytes 262176 | tf_op jit(solution)/shard_map/ppermute | solution.py:24
  194.2 1.0 collective-permute-done.11
  195.2 2.7 %collective-permute-done.10 = bf16[4,4,32,256]{3,2,1,0:T(8,128)(2,1)S(1)} collective-permute-done((bf16[4,4,32,256]{3,2,1,0:T(8,128)(2,1)S(1)}, bf16[4,4,32,256]{3,2,1,0:T(8,128)(2,1)S(1)}, u32[]{:S(2)}, u32[]{:S(2)}) %collective-permute-start.10) | collective-permute-done | bytes 262176 | tf_op jit(solution)/shard_map/ppermute | solution.py:24
  198.1 2.8 %collective-permute-start.15 = (bf16[4,32,256]{2,1,0:T(8,128)(2,1)S(1)}, bf16[4,32,256]{2,1,0:T(8,128)(2,1)S(1)}, u32[]{:S(2)}, u32[]{:S(2)}) collective-permute-start(bf16[4,32,256]{2,1,0:T(8,128)(2,1)S(1)} %get-tuple-element.33), channel_id=1, source_target_pairs={{0,12},{1,13},{2,14},{3,15},{4,0},{5,1},{6,2},{7,3},{8,4},{9,5},{1... | collective-permute-start | bytes 196616 | tf_op jit(solution)/shard_map/ppermute | solution.py:24
  200.8 0.9 collective-permute-start.14
  201.7 0.9 collective-permute-start.13
  202.8 3.8 %collective-permute-done.14 = bf16[4,32,256]{2,1,0:T(8,128)(2,1)S(1)} collective-permute-done((bf16[4,32,256]{2,1,0:T(8,128)(2,1)S(1)}, bf16[4,32,256]{2,1,0:T(8,128)(2,1)S(1)}, u32[]{:S(2)}, u32[]{:S(2)}) %collective-permute-start.14) | collective-permute-done | bytes 65568 | tf_op jit(solution)/shard_map/ppermute | solution.py:24
  208.9 0.7 reshape.126
  209.6 0.9 fusion.53
  (67 shorter events, 6.7 us)
Async XLA Ops:
  6.5 6.7 %copy-start.4 = (bf16[512,896]{1,0:T(8,128)(2,1)S(1)}, bf16[512,896]{1,0:T(8,128)(2,1)}, u32[]{:S(2)}) copy-start(bf16[512,896]{1,0:T(8,128)(2,1)} %param.8) | copy-start | bytes 2752516
  6.5 106.8 %copy-start.6 = (s32[4]{0:T(128)S(1)}, s32[4]{0:T(128)}, u32[]{:S(2)}) copy-start(s32[4]{0:T(128)} %param.12) | copy-start | bytes 52
  6.5 117.5 %copy-start.7 = (s32[4]{0:T(128)S(1)}, s32[4]{0:T(128)}, u32[]{:S(2)}) copy-start(s32[4]{0:T(128)} %param.13) | copy-start | bytes 52
  6.5 106.6 %all-gather.5.cloned.1.call-start = ((), (), s32[]{:S(2)}) async-start(), calls=%async_computation.1 | async-start | bytes 13926400 | tf_op jit(solution)/shard_map/all_gather | solution.py:111
  6.5 4.8 %collective-permute-start = (bf16[896,512]{1,0:T(8,128)(2,1)}, bf16[896,512]{1,0:T(8,128)(2,1)S(1)}, u32[]{:S(2)}, u32[]{:S(2)}) collective-permute-start(bf16[896,512]{1,0:T(8,128)(2,1)} %param.9), channel_id=1, source_target_pairs={{0,0},{1,1},{2,2},{3,3},{4,48},{5,49},{6,50},{7,51},{8,32},{9,33},... | collective-permute-start | bytes 2752520 | tf_op jit(solution)/shard_map/ppermute | solution.py:98
  13.2 158.8 %all-gather.7.cloned.1.call-start = ((), (), s32[]{:S(2)}) async-start(), calls=%async_computation.2 | async-start | bytes 7798784 | tf_op jit(solution)/shard_map/all_gather | solution.py:116
  13.3 30.3 %collective-permute-start.1 = (bf16[512,896]{1,0:T(8,128)(2,1)S(1)}, bf16[512,896]{1,0:T(8,128)(2,1)S(1)}, u32[]{:S(2)}, u32[]{:S(2)}) collective-permute-start(bf16[512,896]{1,0:T(8,128)(2,1)S(1)} %copy-done.4), channel_id=1, source_target_pairs={{0,4},{1,5},{2,6},{3,7},{4,8},{5,9},{6,10},{7,11},{8,12},{9,13},{1... | collective-permute-start | bytes 2752520 | tf_op jit(solution)/shard_map/ppermute | solution.py:24
  22.9 52.9 %collective-permute-start.2 = (bf16[512,896]{1,0:T(8,128)(2,1)S(1)}, bf16[512,896]{1,0:T(8,128)(2,1)S(1)}, u32[]{:S(2)}, u32[]{:S(2)}) collective-permute-start(bf16[512,896]{1,0:T(8,128)(2,1)S(1)} %copy-done.4), channel_id=1, source_target_pairs={{0,8},{1,9},{2,10},{3,11},{4,12},{5,13},{6,14},{7,15},{8,0},{9,1},... | collective-permute-start | bytes 2752520 | tf_op jit(solution)/shard_map/ppermute | solution.py:24
  35.2 40.6 %collective-permute-start.3 = (bf16[512,896]{1,0:T(8,128)(2,1)S(1)}, bf16[512,896]{1,0:T(8,128)(2,1)}, u32[]{:S(2)}, u32[]{:S(2)}) collective-permute-start(bf16[512,896]{1,0:T(8,128)(2,1)S(1)} %copy-done.4), channel_id=1, source_target_pairs={{0,12},{1,13},{2,14},{3,15},{4,0},{5,1},{6,2},{7,3},{8,4},{9,5},{1... | collective-permute-start | bytes 2752520 | tf_op jit(solution)/shard_map/ppermute | solution.py:24
  75.9 49.4 %copy-start.5 = (bf16[512,896]{1,0:T(8,128)(2,1)}, bf16[512,896]{1,0:T(8,128)(2,1)S(1)}, u32[]{:S(2)}) copy-start(bf16[512,896]{1,0:T(8,128)(2,1)S(1)} %collective-permute-done.2) | copy-start | bytes 2752516
  126.2 23.9 %collective-permute-start.18 = (f32[4,128,64]{1,2,0:T(8,128)S(1)}, f32[4,128,64]{1,2,0:T(8,128)S(1)}, u32[]{:S(2)}, u32[]{:S(2)}) collective-permute-start(f32[4,128,64]{1,2,0:T(8,128)S(1)} %convolution_bitcast_fusion.4), channel_id=1, source_target_pairs={{0,3},{1,0},{2,1},{3,2},{4,7},{5,4},{6,5},{7,6},{8,11},{9,8},{10,9... | collective-permute-start | bytes 393224 | tf_op jit(solution)/shard_map/ppermute | solution.py:24
  129.2 21.3 %collective-permute-start.16 = (f32[4,128,64]{1,2,0:T(8,128)S(1)}, f32[4,128,64]{1,2,0:T(8,128)S(1)}, u32[]{:S(2)}, u32[]{:S(2)}) collective-permute-start(f32[4,128,64]{1,2,0:T(8,128)S(1)} %convolution_bitcast_fusion.4), channel_id=1, source_target_pairs={{0,1},{1,2},{2,3},{3,0},{4,5},{5,6},{6,7},{7,4},{8,9},{9,10},{10,1... | collective-permute-start | bytes 393224 | tf_op jit(solution)/shard_map/ppermute | solution.py:24
  129.2 21.4 %collective-permute-start.17 = (f32[4,128,64]{1,2,0:T(8,128)S(1)}, f32[4,128,64]{1,2,0:T(8,128)}, u32[]{:S(2)}, u32[]{:S(2)}) collective-permute-start(f32[4,128,64]{1,2,0:T(8,128)S(1)} %convolution_bitcast_fusion.4), channel_id=1, source_target_pairs={{0,2},{1,3},{2,0},{3,1},{4,6},{5,7},{6,4},{7,5},{8,10},{9,11},{10,... | collective-permute-start | bytes 393224 | tf_op jit(solution)/shard_map/ppermute | solution.py:24
  131.5 6.9 %copy-start = (bf16[25600,256]{1,0:T(8,128)(2,1)S(1)}, bf16[25600,256]{1,0:T(8,128)(2,1)}, u32[]{:S(2)}) copy-start(bf16[25600,256]{1,0:T(8,128)(2,1)} %all-gather.5.cloned.1.call-done) | copy-start | bytes 39321604
  134.0 14.3 %copy-start.1 = (bf16[4,4,4,32,896]{4,3,2,1,0:T(8,128)(2,1)}, bf16[4,4,4,32,896]{4,3,2,1,0:T(8,128)(2,1)S(1)}, u32[]{:S(2)}) copy-start(bf16[4,4,4,32,896]{4,3,2,1,0:T(8,128)(2,1)S(1)} %copy.35) | copy-start | bytes 11010052
  140.3 14.1 %collective-permute-start.6 = (bf16[4,4,32,256]{3,2,1,0:T(8,128)(2,1)S(1)}, bf16[4,4,32,256]{3,2,1,0:T(8,128)(2,1)S(1)}, u32[]{:S(2)}, u32[]{:S(2)}) collective-permute-start(bf16[4,4,32,256]{3,2,1,0:T(8,128)(2,1)S(1)} %bitcast.208), channel_id=1, source_target_pairs={{0,3},{1,0},{2,1},{3,2},{4,7},{5,4},{6,5},{7,6},{8,11},{9,8},{10,9... | collective-permute-start | bytes 786440 | tf_op jit(solution)/shard_map/ppermute | solution.py:24
  143.4 13.2 %collective-permute-start.5 = (bf16[4,4,32,256]{3,2,1,0:T(8,128)(2,1)S(1)}, bf16[4,4,32,256]{3,2,1,0:T(8,128)(2,1)S(1)}, u32[]{:S(2)}, u32[]{:S(2)}) collective-permute-start(bf16[4,4,32,256]{3,2,1,0:T(8,128)(2,1)S(1)} %bitcast.206), channel_id=1, source_target_pairs={{0,2},{1,3},{2,0},{3,1},{4,6},{5,7},{6,4},{7,5},{8,10},{9,11},{10,... | collective-permute-start | bytes 786440 | tf_op jit(solution)/shard_map/ppermute | solution.py:24
  150.2 8.4 %collective-permute-start.4 = (bf16[4,4,32,256]{3,2,1,0:T(8,128)(2,1)S(1)}, bf16[4,4,32,256]{3,2,1,0:T(8,128)(2,1)S(1)}, u32[]{:S(2)}, u32[]{:S(2)}) collective-permute-start(bf16[4,4,32,256]{3,2,1,0:T(8,128)(2,1)S(1)} %bitcast.207), channel_id=1, source_target_pairs={{0,1},{1,2},{2,3},{3,0},{4,5},{5,6},{6,7},{7,4},{8,9},{9,10},{10,1... | collective-permute-start | bytes 786440 | tf_op jit(solution)/shard_map/ppermute | solution.py:24
  151.5 10.9 %collective-permute-start.21 = (f32[4,128,64]{1,2,0:T(8,128)S(1)}, f32[4,128,64]{1,2,0:T(8,128)S(1)}, u32[]{:S(2)}, u32[]{:S(2)}) collective-permute-start(f32[4,128,64]{1,2,0:T(8,128)S(1)} %add_add_fusion), channel_id=1, source_target_pairs={{0,12},{1,13},{2,14},{3,15},{4,0},{5,1},{6,2},{7,3},{8,4},{9,5},{1... | collective-permute-start | bytes 393224 | tf_op jit(solution)/shard_map/ppermute | solution.py:24
  154.4 8.9 %collective-permute-start.19 = (f32[4,128,64]{1,2,0:T(8,128)S(1)}, f32[4,128,64]{1,2,0:T(8,128)S(1)}, u32[]{:S(2)}, u32[]{:S(2)}) collective-permute-start(f32[4,128,64]{1,2,0:T(8,128)S(1)} %add_add_fusion), channel_id=1, source_target_pairs={{0,4},{1,5},{2,6},{3,7},{4,8},{5,9},{6,10},{7,11},{8,12},{9,13},{1... | collective-permute-start | bytes 393224 | tf_op jit(solution)/shard_map/ppermute | solution.py:24
  154.4 8.9 %collective-permute-start.20 = (f32[4,128,64]{1,2,0:T(8,128)S(1)}, f32[4,128,64]{1,2,0:T(8,128)S(1)}, u32[]{:S(2)}, u32[]{:S(2)}) collective-permute-start(f32[4,128,64]{1,2,0:T(8,128)S(1)} %add_add_fusion), channel_id=1, source_target_pairs={{0,8},{1,9},{2,10},{3,11},{4,12},{5,13},{6,14},{7,15},{8,0},{9,1},... | collective-permute-start | bytes 393224 | tf_op jit(solution)/shard_map/ppermute | solution.py:24
  158.8 12.6 %collective-permute-start.9 = (bf16[4,32,256]{2,1,0:T(8,128)(2,1)S(1)}, bf16[4,32,256]{2,1,0:T(8,128)(2,1)S(1)}, u32[]{:S(2)}, u32[]{:S(2)}) collective-permute-start(bf16[4,32,256]{2,1,0:T(8,128)(2,1)S(1)} %get-tuple-element.29), channel_id=1, source_target_pairs={{0,12},{1,13},{2,14},{3,15},{4,0},{5,1},{6,2},{7,3},{8,4},{9,5},{1... | collective-permute-start | bytes 196616 | tf_op jit(solution)/shard_map/ppermute | solution.py:24
  161.6 9.8 %collective-permute-start.8 = (bf16[4,32,256]{2,1,0:T(8,128)(2,1)S(1)}, bf16[4,32,256]{2,1,0:T(8,128)(2,1)S(1)}, u32[]{:S(2)}, u32[]{:S(2)}) collective-permute-start(bf16[4,32,256]{2,1,0:T(8,128)(2,1)S(1)} %get-tuple-element.30), channel_id=1, source_target_pairs={{0,8},{1,9},{2,10},{3,11},{4,12},{5,13},{6,14},{7,15},{8,0},{9,1},... | collective-permute-start | bytes 196616 | tf_op jit(solution)/shard_map/ppermute | solution.py:24
  162.4 9.0 %collective-permute-start.7 = (bf16[4,32,256]{2,1,0:T(8,128)(2,1)S(1)}, bf16[4,32,256]{2,1,0:T(8,128)(2,1)S(1)}, u32[]{:S(2)}, u32[]{:S(2)}) collective-permute-start(bf16[4,32,256]{2,1,0:T(8,128)(2,1)S(1)} %get-tuple-element.31), channel_id=1, source_target_pairs={{0,4},{1,5},{2,6},{3,7},{4,8},{5,9},{6,10},{7,11},{8,12},{9,13},{1... | collective-permute-start | bytes 196616 | tf_op jit(solution)/shard_map/ppermute | solution.py:24
  164.4 38.1 %all-to-all-start = ((bf16[16,32,512]{2,1,0:T(8,128)(2,1)}), bf16[16,32,512]{2,1,0:T(8,128)(2,1)S(1)}, u32[]{:S(2)}, u32[]{:S(2)}) async-start(bf16[16,32,512]{2,1,0:T(8,128)(2,1)} %bitcast.79), calls=%async_computation | async-start | bytes 1048576 | tf_op jit(solution)/shard_map/all_to_all | solution.py:180
  172.1 4.7 %copy-start.2 = (bf16[4,4,4,32,896]{4,3,2,1,0:T(8,128)(2,1)S(1)}, bf16[4,4,4,32,896]{4,3,2,1,0:T(8,128)(2,1)}, u32[]{:S(2)}) copy-start(bf16[4,4,4,32,896]{4,3,2,1,0:T(8,128)(2,1)} %copy-done.1) | copy-start | bytes 11010052
  176.7 5.2 %copy-start.3 = (bf16[14336,256]{1,0:T(8,128)(2,1)S(1)}, bf16[14336,256]{1,0:T(8,128)(2,1)}, u32[]{:S(2)}) copy-start(bf16[14336,256]{1,0:T(8,128)(2,1)} %all-gather.7.cloned.1.call-done) | copy-start | bytes 22020100
  183.0 11.2 %collective-permute-start.12 = (bf16[4,4,32,256]{3,2,1,0:T(8,128)(2,1)S(1)}, bf16[4,4,32,256]{3,2,1,0:T(8,128)(2,1)S(1)}, u32[]{:S(2)}, u32[]{:S(2)}) collective-permute-start(bf16[4,4,32,256]{3,2,1,0:T(8,128)(2,1)S(1)} %bitcast.211), channel_id=1, source_target_pairs={{0,3},{1,0},{2,1},{3,2},{4,7},{5,4},{6,5},{7,6},{8,11},{9,8},{10,9... | collective-permute-start | bytes 786440 | tf_op jit(solution)/shard_map/ppermute | solution.py:24
  186.2 9.0 %collective-permute-start.11 = (bf16[4,4,32,256]{3,2,1,0:T(8,128)(2,1)S(1)}, bf16[4,4,32,256]{3,2,1,0:T(8,128)(2,1)S(1)}, u32[]{:S(2)}, u32[]{:S(2)}) collective-permute-start(bf16[4,4,32,256]{3,2,1,0:T(8,128)(2,1)S(1)} %bitcast.210), channel_id=1, source_target_pairs={{0,2},{1,3},{2,0},{3,1},{4,6},{5,7},{6,4},{7,5},{8,10},{9,11},{10,... | collective-permute-start | bytes 786440 | tf_op jit(solution)/shard_map/ppermute | solution.py:24
  187.1 10.8 %collective-permute-start.10 = (bf16[4,4,32,256]{3,2,1,0:T(8,128)(2,1)S(1)}, bf16[4,4,32,256]{3,2,1,0:T(8,128)(2,1)S(1)}, u32[]{:S(2)}, u32[]{:S(2)}) collective-permute-start(bf16[4,4,32,256]{3,2,1,0:T(8,128)(2,1)S(1)} %bitcast.209), channel_id=1, source_target_pairs={{0,1},{1,2},{2,3},{3,0},{4,5},{5,6},{6,7},{7,4},{8,9},{9,10},{10,1... | collective-permute-start | bytes 786440 | tf_op jit(solution)/shard_map/ppermute | solution.py:24
  198.1 4.7 %collective-permute-start.15 = (bf16[4,32,256]{2,1,0:T(8,128)(2,1)S(1)}, bf16[4,32,256]{2,1,0:T(8,128)(2,1)S(1)}, u32[]{:S(2)}, u32[]{:S(2)}) collective-permute-start(bf16[4,32,256]{2,1,0:T(8,128)(2,1)S(1)} %get-tuple-element.33), channel_id=1, source_target_pairs={{0,12},{1,13},{2,14},{3,15},{4,0},{5,1},{6,2},{7,3},{8,4},{9,5},{1... | collective-permute-start | bytes 196616 | tf_op jit(solution)/shard_map/ppermute | solution.py:24
  200.8 5.8 %collective-permute-start.14 = (bf16[4,32,256]{2,1,0:T(8,128)(2,1)S(1)}, bf16[4,32,256]{2,1,0:T(8,128)(2,1)S(1)}, u32[]{:S(2)}, u32[]{:S(2)}) collective-permute-start(bf16[4,32,256]{2,1,0:T(8,128)(2,1)S(1)} %get-tuple-element.34), channel_id=1, source_target_pairs={{0,8},{1,9},{2,10},{3,11},{4,12},{5,13},{6,14},{7,15},{8,0},{9,1},... | collective-permute-start | bytes 196616 | tf_op jit(solution)/shard_map/ppermute | solution.py:24
  201.7 5.6 %collective-permute-start.13 = (bf16[4,32,256]{2,1,0:T(8,128)(2,1)S(1)}, bf16[4,32,256]{2,1,0:T(8,128)(2,1)S(1)}, u32[]{:S(2)}, u32[]{:S(2)}) collective-permute-start(bf16[4,32,256]{2,1,0:T(8,128)(2,1)S(1)} %get-tuple-element.35), channel_id=1, source_target_pairs={{0,4},{1,5},{2,6},{3,7},{4,8},{5,9},{6,10},{7,11},{8,12},{9,13},{1... | collective-permute-start | bytes 196616 | tf_op jit(solution)/shard_map/ppermute | solution.py:24
Sparse Core Ops, SparseCore 0:
  13.3 99.7 all-gather.4
  115.0 49.5 all-gather.6

commit v17 on v15

--- a/solution.py
+++ b/solution.py
@@ -110,7 +110,16 @@
     )
     gathered = lax.all_gather(pack, "pool", axis=0, tiled=False)
     pieces = [hidden] + [tensor_shift(hidden, side, s, True) for s in range(1, side)]
-    later, gathered, pieces = lax.optimization_barrier((moved[:, half:], gathered, pieces))
+    hidden_column = jnp.stack(pieces, axis=0).reshape(side, side, side, own_rows, feat)
+    hidden_column = jnp.transpose(hidden_column, (2, 0, 1, 3, 4)).reshape(
+        side, side, side * own_rows, feat
+    )
+    hidden_padded = jnp.pad(
+        hidden_column, ((0, 0), (0, 0), (0, 0), (0, pack.shape[0] - feat))
+    )
+    later, gathered, hidden_column, hidden_padded = lax.optimization_barrier(
+        (moved[:, half:], gathered, hidden_column, hidden_padded)
+    )
     plane_rows = gathered.shape[1]
     w_first = gathered.reshape(quarter, side, plane_rows, half)
     shrink_all = gathered[:, feat:feat + shrink_rows, :].reshape(
@@ -123,11 +132,6 @@
         quarter, side, feat, half
     )
 
-    hidden_column = jnp.stack(pieces, axis=0).reshape(side, side, side, own_rows, feat)
-    hidden_column = jnp.transpose(hidden_column, (2, 0, 1, 3, 4)).reshape(
-        side, side, side * own_rows, feat
-    )
-    hidden_padded = jnp.pad(hidden_column, ((0, 0), (0, 0), (0, 0), (0, plane_rows - feat)))
 
     first = jnp.take(shrink_all, block_adapter, axis=0).reshape(block_count, feat, rank)
     second = jnp.take(expand_all, block_adapter, axis=0).reshape(block_count, column_span, rank)

time: 217 us -> 214 us (0.986)
  matrix products: 22.5 us -> 27.2 us
  waiting for transfers between devices: 90.7 us -> 86.3 us
  starting transfers between devices: 61.6 us -> 58.3 us
    all_gather x1, waiting for transfers between devices: 37.3 us -> 30.3 us  [shards(): gathered = lax.all_gather(pack, 'pool', axis=0, tiled=False)]
    dot_general x8, matrix products: 19.5 us -> 25.4 us  [rows_for(): jnp.einsum('sif,asfj->aij', rows, w_half, preferred_element_type=jnp.floa...]
    pad x0 -> x1, local copies, waits for them, and re-layouts: none -> 3.51 us  [shards(): jnp.pad(hidden_column, ((0, 0), (0, 0), (0, 0), (0, pack.shape[0] - feat)))]
    ppermute x21, waiting for transfers between devices: 53.3 us -> 56 us  [tensor_shift(): return lax.ppermute(x, 'tensor', perm)]
    ppermute x21, starting transfers between devices: 52.8 us -> 50.5 us  [tensor_shift(): return lax.ppermute(x, 'tensor', perm)]
    unnamed x22 -> x24, local copies, waits for them, and re-layouts: 6.56 us -> 5.23 us
  transfers between devices with their start and end apart: 25 -> 25, of which waited for: 10 -> 11; matrix products, arithmetic and copies ran while one was open for 19% -> 22% of each run, Pallas kernels for 0% -> 0%
where the time goes in v17:
time: 214 us; the launch traced here: 213 us
  waiting for transfers between devices  86.3 us (40%)
  starting transfers between devices  58.3 us (27%)
  matrix products  27.2 us (13%)
  local copies, waits for them, and re-layouts  21.4 us (10%)
  between operations  14 us (7%)
  other arithmetic  6.15 us (3%)
    ppermute x21, waiting for transfers between devices, tensor_shift(): return lax.ppermute(x, 'tensor', perm)  56 us
    ppermute x21, starting transfers between devices, tensor_shift(): return lax.ppermute(x, 'tensor', perm)  50.5 us
    all_gather x1, waiting for transfers between devices, shards(): gathered = lax.all_gather(pack, 'pool', axis=0, tiled=False)  30.3 us
    dot_general x8, matrix products, rows_for(): jnp.einsum('sif,asfj->aij', rows, w_half, preferred_element_type=jnp.floa...  25.4 us
    all_to_all x1, starting transfers between devices, shards(): lax.all_to_all(delta, 'tensor', split_axis=0, concat_axis=1, tiled=True)  5.8 us
    unnamed x24, local copies, waits for them, and re-layouts  5.23 us
  transfers between devices with their start and end apart: 25, of which 11 were waited for; matrix products, arithmetic and copies ran while one was open for 22% of the time, Pallas kernels for 0%

profile of v17, /device:TPU:0, one launch (start us, length us, event | category | flops | bytes accessed | tf_op | source)
XLA Modules:
  0.0 213.3 jit_solution(3434217343288727105)
XLA Ops:
  6.5 2.0 collective-permute-start
  8.5 1.1 copy.34
  9.8 1.2 copy.33
  11.3 0.8 fusion.72
  12.2 1.0 pad_maximum_fusion
  13.2 11.6 %collective-permute-start.3 = (bf16[512,896]{1,0:T(8,128)(2,1)}, bf16[512,896]{1,0:T(8,128)(2,1)S(1)}, u32[]{:S(2)}, u32[]{:S(2)}) collective-permute-start(bf16[512,896]{1,0:T(8,128)(2,1)} %param.8), channel_id=1, source_target_pairs={{0,12},{1,13},{2,14},{3,15},{4,0},{5,1},{6,2},{7,3},{8,4},{9,5},{1... | collective-permute-start | bytes 2752520 | tf_op jit(solution)/shard_map/ppermute | solution.py:24
  24.8 10.4 %collective-permute-start.2 = (bf16[512,896]{1,0:T(8,128)(2,1)}, bf16[512,896]{1,0:T(8,128)(2,1)S(1)}, u32[]{:S(2)}, u32[]{:S(2)}) collective-permute-start(bf16[512,896]{1,0:T(8,128)(2,1)} %param.8), channel_id=1, source_target_pairs={{0,8},{1,9},{2,10},{3,11},{4,12},{5,13},{6,14},{7,15},{8,0},{9,1},... | collective-permute-start | bytes 2752520 | tf_op jit(solution)/shard_map/ppermute | solution.py:24
  35.2 1.3 collective-permute-start.1
  36.5 6.3 %collective-permute-done.3 = bf16[512,896]{1,0:T(8,128)(2,1)S(1)} collective-permute-done((bf16[512,896]{1,0:T(8,128)(2,1)}, bf16[512,896]{1,0:T(8,128)(2,1)S(1)}, u32[]{:S(2)}, u32[]{:S(2)}) %collective-permute-start.3) | collective-permute-done | bytes 917536 | tf_op jit(solution)/shard_map/ppermute | solution.py:24
  42.8 13.5 %collective-permute-done.2 = bf16[512,896]{1,0:T(8,128)(2,1)S(1)} collective-permute-done((bf16[512,896]{1,0:T(8,128)(2,1)}, bf16[512,896]{1,0:T(8,128)(2,1)S(1)}, u32[]{:S(2)}, u32[]{:S(2)}) %collective-permute-start.2) | collective-permute-done | bytes 917536 | tf_op jit(solution)/shard_map/ppermute | solution.py:24
  56.3 19.9 %collective-permute-done.1 = bf16[512,896]{1,0:T(8,128)(2,1)S(1)} collective-permute-done((bf16[512,896]{1,0:T(8,128)(2,1)}, bf16[512,896]{1,0:T(8,128)(2,1)S(1)}, u32[]{:S(2)}, u32[]{:S(2)}) %collective-permute-start.1) | collective-permute-done | bytes 917536 | tf_op jit(solution)/shard_map/ppermute | solution.py:24
  77.3 1.9 copy-done.2
  79.2 3.5 %pad.4 = bf16[4,4,128,1600]{3,2,1,0:T(8,128)(2,1)} pad(bf16[4,4,128,896]{3,2,1,0:T(8,128)(2,1)S(1)} %bitcast.187, bf16[]{:T(256)} %constant.177.clone.1), padding=0_0x0_0x0_0x0_704 | pad | bytes 10223618 | tf_op jit(solution)/shard_map/jit(_pad)/pad | solution.py:117
  82.7 30.3 %all-gather.5.cloned.1.call-done = bf16[25600,256]{1,0:T(8,128)(2,1)} async-done(((bf16[1600,256]{1,0:T(8,128)(2,1)}), bf16[25600,256]{1,0:T(8,128)(2,1)}) %all-gather.5.cloned.1.call-update) | async-done | bytes 13107216 | tf_op jit(solution)/shard_map/all_gather | solution.py:111
  114.0 4.2 %slice.14 = bf16[16,448,256]{2,1,0:T(8,128)(2,1)} slice(bf16[16,1600,256]{2,1,0:T(8,128)(2,1)} %bitcast.177), slice={[0:16], [896:1344], [0:256]} | slice | bytes 7340032 | tf_op jit(solution)/shard_map/slice | solution.py:125
  118.1 2.6 %gather_fusion = bf16[4,224,256]{2,1,0:T(8,128)(2,1)S(1)} fusion(bf16[32,224,256]{2,1,0:T(8,128)(2,1)} %bitcast.194, s32[1024]{0:T(1024)S(1)} %pad_clamp_fusion), kind=kCustom, calls=%fused_computation.2 | custom fusion | bytes 917520 | tf_op jit(solution)/shard_map/jit(_take)/gather | solution.py:136
  121.7 2.8 %collective-permute-start.18 = (f32[4,128,64]{1,2,0:T(8,128)S(1)}, f32[4,128,64]{1,2,0:T(8,128)S(1)}, u32[]{:S(2)}, u32[]{:S(2)}) collective-permute-start(f32[4,128,64]{1,2,0:T(8,128)S(1)} %convolution_bitcast_fusion.4), channel_id=1, source_target_pairs={{0,3},{1,0},{2,1},{3,2},{4,7},{5,4},{6,5},{7,6},{8,11},{9,8},{10,9... | collective-permute-start | bytes 393224 | tf_op jit(solution)/shard_map/ppermute | solution.py:24
  124.5 2.3 %collective-permute-start.17 = (f32[4,128,64]{1,2,0:T(8,128)S(1)}, f32[4,128,64]{1,2,0:T(8,128)}, u32[]{:S(2)}, u32[]{:S(2)}) collective-permute-start(f32[4,128,64]{1,2,0:T(8,128)S(1)} %convolution_bitcast_fusion.4), channel_id=1, source_target_pairs={{0,2},{1,3},{2,0},{3,1},{4,6},{5,7},{6,4},{7,5},{8,10},{9,11},{10,... | collective-permute-start | bytes 393224 | tf_op jit(solution)/shard_map/ppermute | solution.py:24
  126.8 8.1 %fusion.36 = bf16[4,256,128]{1,2,0:T(8,128)(2,1)} fusion(bf16[4,4,1600,256]{3,2,1,0:T(8,128)(2,1)} %bitcast.178, bf16[4,4,128,1600]{3,2,1,0:T(8,128)(2,1)} %pad.4, s32[]{:T(128)S(6)} %select_n.147), kind=kOutput, calls=%fused_computation.34 | convolution fusion | flops 1677852672 | bytes 15073284 | tf_op jit(solution)/shard_map/sif,asfj->aij/dot_general | solution.py:149
  134.9 1.1 collective-permute-start.6
  136.2 4.3 %fusion.39 = bf16[4,256,128]{1,2,0:T(8,128)(2,1)S(1)} fusion(bf16[4,4,1600,256]{3,2,1,0:T(8,128)(2,1)S(1)} %bitcast.179, bf16[4,4,128,1600]{3,2,1,0:T(8,128)(2,1)} %pad.4, s32[]{:T(128)S(6)} %select_n.145), kind=kOutput, calls=%fused_computation.35 | convolution fusion | flops 1677852672 | bytes 15073284 | tf_op jit(solution)/shard_map/sif,asfj->aij/dot_general | solution.py:149
  140.5 1.8 collective-permute-start.5
  142.3 1.9 fusion.42
  144.4 1.9 fusion.33
  147.4 1.1 add_add_fusion
  148.5 2.8 %collective-permute-start.21 = (f32[4,128,64]{1,2,0:T(8,128)S(1)}, f32[4,128,64]{1,2,0:T(8,128)S(1)}, u32[]{:S(2)}, u32[]{:S(2)}) collective-permute-start(f32[4,128,64]{1,2,0:T(8,128)S(1)} %add_add_fusion), channel_id=1, source_target_pairs={{0,12},{1,13},{2,14},{3,15},{4,0},{5,1},{6,2},{7,3},{8,4},{9,5},{1... | collective-permute-start | bytes 393224 | tf_op jit(solution)/shard_map/ppermute | solution.py:24
  151.3 2.3 %collective-permute-start.20 = (f32[4,128,64]{1,2,0:T(8,128)S(1)}, f32[4,128,64]{1,2,0:T(8,128)S(1)}, u32[]{:S(2)}, u32[]{:S(2)}) collective-permute-start(f32[4,128,64]{1,2,0:T(8,128)S(1)} %add_add_fusion), channel_id=1, source_target_pairs={{0,8},{1,9},{2,10},{3,11},{4,12},{5,13},{6,14},{7,15},{8,0},{9,1},... | collective-permute-start | bytes 393224 | tf_op jit(solution)/shard_map/ppermute | solution.py:24
  153.6 1.7 collective-permute-done.4
  155.4 1.3 add_convert_fusion.2
  156.7 2.8 %collective-permute-start.9 = (bf16[4,32,256]{2,1,0:T(8,128)(2,1)S(1)}, bf16[4,32,256]{2,1,0:T(8,128)(2,1)S(1)}, u32[]{:S(2)}, u32[]{:S(2)}) collective-permute-start(bf16[4,32,256]{2,1,0:T(8,128)(2,1)S(1)} %get-tuple-element.17), channel_id=1, source_target_pairs={{0,12},{1,13},{2,14},{3,15},{4,0},{5,1},{6,2},{7,3},{8,4},{9,5},{1... | collective-permute-start | bytes 196616 | tf_op jit(solution)/shard_map/ppermute | solution.py:24
  160.3 0.9 collective-permute-start.7
  161.2 1.2 fusion.12
  162.4 5.8 %all-to-all-start = ((bf16[16,32,512]{2,1,0:T(8,128)(2,1)}), bf16[16,32,512]{2,1,0:T(8,128)(2,1)S(1)}, u32[]{:S(2)}, u32[]{:S(2)}) async-start(bf16[16,32,512]{2,1,0:T(8,128)(2,1)} %bitcast.77), calls=%async_computation | async-start | bytes 1048576 | tf_op jit(solution)/shard_map/all_to_all | solution.py:174
  168.9 4.6 %fusion.27 = bf16[4,256,128]{1,2,0:T(8,128)(2,1)S(1)} fusion(bf16[4,4,896,256]{3,2,1,0:T(8,128)(2,1)} %bitcast.183, bf16[4,4,128,896]{3,2,1,0:T(8,128)(2,1)} %bitcast.188, s32[]{:T(128)S(6)} %select_n.147), kind=kOutput, calls=%fused_computation.29 | convolution fusion | flops 939655168 | bytes 8519684 | tf_op jit(solution)/shard_map/sif,asfj->aij/dot_general | solution.py:149
  174.3 2.4 %fusion.26 = bf16[4,256,128]{1,2,0:T(8,128)(2,1)S(1)} fusion(bf16[4,4,896,256]{3,2,1,0:T(8,128)(2,1)S(1)} %bitcast.184, bf16[4,4,128,896]{3,2,1,0:T(8,128)(2,1)} %bitcast.189, s32[]{:T(128)S(6)} %select_n.145), kind=kOutput, calls=%fused_computation.28 | convolution fusion | flops 939655168 | bytes 8519684 | tf_op jit(solution)/shard_map/sif,asfj->aij/dot_general | solution.py:149
  176.8 1.1 fusion.25
  177.9 3.2 %collective-permute-start.12 = (bf16[4,4,32,256]{3,2,1,0:T(8,128)(2,1)S(1)}, bf16[4,4,32,256]{3,2,1,0:T(8,128)(2,1)S(1)}, u32[]{:S(2)}, u32[]{:S(2)}) collective-permute-start(bf16[4,4,32,256]{3,2,1,0:T(8,128)(2,1)S(1)} %bitcast.208), channel_id=1, source_target_pairs={{0,3},{1,0},{2,1},{3,2},{4,7},{5,4},{6,5},{7,6},{8,11},{9,8},{10,9... | collective-permute-start | bytes 786440 | tf_op jit(solution)/shard_map/ppermute | solution.py:24
  181.1 0.9 collective-permute-start.11
  181.9 0.9 collective-permute-start.10
  182.8 1.1 fusion.29
  183.9 6.2 %collective-permute-done.12 = bf16[4,4,32,256]{3,2,1,0:T(8,128)(2,1)S(1)} collective-permute-done((bf16[4,4,32,256]{3,2,1,0:T(8,128)(2,1)S(1)}, bf16[4,4,32,256]{3,2,1,0:T(8,128)(2,1)S(1)}, u32[]{:S(2)}, u32[]{:S(2)}) %collective-permute-start.12) | collective-permute-done | bytes 262176 | tf_op jit(solution)/shard_map/ppermute | solution.py:24
  190.1 1.0 collective-permute-done.11
  191.1 2.7 %collective-permute-done.10 = bf16[4,4,32,256]{3,2,1,0:T(8,128)(2,1)S(1)} collective-permute-done((bf16[4,4,32,256]{3,2,1,0:T(8,128)(2,1)S(1)}, bf16[4,4,32,256]{3,2,1,0:T(8,128)(2,1)S(1)}, u32[]{:S(2)}, u32[]{:S(2)}) %collective-permute-start.10) | collective-permute-done | bytes 262176 | tf_op jit(solution)/shard_map/ppermute | solution.py:24
  194.0 2.8 %collective-permute-start.15 = (bf16[4,32,256]{2,1,0:T(8,128)(2,1)S(1)}, bf16[4,32,256]{2,1,0:T(8,128)(2,1)S(1)}, u32[]{:S(2)}, u32[]{:S(2)}) collective-permute-start(bf16[4,32,256]{2,1,0:T(8,128)(2,1)S(1)} %get-tuple-element.21), channel_id=1, source_target_pairs={{0,12},{1,13},{2,14},{3,15},{4,0},{5,1},{6,2},{7,3},{8,4},{9,5},{1... | collective-permute-start | bytes 196616 | tf_op jit(solution)/shard_map/ppermute | solution.py:24
  196.8 0.8 collective-permute-start.14
  197.6 0.9 collective-permute-start.13
  199.0 3.6 %collective-permute-done.14 = bf16[4,32,256]{2,1,0:T(8,128)(2,1)S(1)} collective-permute-done((bf16[4,32,256]{2,1,0:T(8,128)(2,1)S(1)}, bf16[4,32,256]{2,1,0:T(8,128)(2,1)S(1)}, u32[]{:S(2)}, u32[]{:S(2)}) %collective-permute-start.14) | collective-permute-done | bytes 65568 | tf_op jit(solution)/shard_map/ppermute | solution.py:24
  205.5 0.9 fusion.55
  (76 shorter events, 10.7 us)
Async XLA Ops:
  6.5 69.7 %copy-start.4 = (bf16[512,896]{1,0:T(8,128)(2,1)S(1)}, bf16[512,896]{1,0:T(8,128)(2,1)}, u32[]{:S(2)}) copy-start(bf16[512,896]{1,0:T(8,128)(2,1)} %param.8) | copy-start | bytes 2752516
  6.5 106.5 %all-gather.5.cloned.1.call-start = ((), (), s32[]{:S(2)}) async-start(), calls=%async_computation.1 | async-start | bytes 13926400 | tf_op jit(solution)/shard_map/all_gather | solution.py:111
  6.5 4.8 %collective-permute-start = (bf16[896,512]{1,0:T(8,128)(2,1)}, bf16[896,512]{1,0:T(8,128)(2,1)S(1)}, u32[]{:S(2)}, u32[]{:S(2)}) collective-permute-start(bf16[896,512]{1,0:T(8,128)(2,1)} %param.9), channel_id=1, source_target_pairs={{0,0},{1,1},{2,2},{3,3},{4,48},{5,49},{6,50},{7,51},{8,32},{9,33},... | collective-permute-start | bytes 2752520 | tf_op jit(solution)/shard_map/ppermute | solution.py:98
  13.2 155.7 %all-gather.7.cloned.1.call-start = ((), (), s32[]{:S(2)}) async-start(), calls=%async_computation.2 | async-start | bytes 7798784 | tf_op jit(solution)/shard_map/all_gather | solution.py:131
  13.2 29.6 %collective-permute-start.3 = (bf16[512,896]{1,0:T(8,128)(2,1)}, bf16[512,896]{1,0:T(8,128)(2,1)S(1)}, u32[]{:S(2)}, u32[]{:S(2)}) collective-permute-start(bf16[512,896]{1,0:T(8,128)(2,1)} %param.8), channel_id=1, source_target_pairs={{0,12},{1,13},{2,14},{3,15},{4,0},{5,1},{6,2},{7,3},{8,4},{9,5},{1... | collective-permute-start | bytes 2752520 | tf_op jit(solution)/shard_map/ppermute | solution.py:24
  24.8 31.5 %collective-permute-start.2 = (bf16[512,896]{1,0:T(8,128)(2,1)}, bf16[512,896]{1,0:T(8,128)(2,1)S(1)}, u32[]{:S(2)}, u32[]{:S(2)}) collective-permute-start(bf16[512,896]{1,0:T(8,128)(2,1)} %param.8), channel_id=1, source_target_pairs={{0,8},{1,9},{2,10},{3,11},{4,12},{5,13},{6,14},{7,15},{8,0},{9,1},... | collective-permute-start | bytes 2752520 | tf_op jit(solution)/shard_map/ppermute | solution.py:24
  35.2 41.1 %collective-permute-start.1 = (bf16[512,896]{1,0:T(8,128)(2,1)}, bf16[512,896]{1,0:T(8,128)(2,1)S(1)}, u32[]{:S(2)}, u32[]{:S(2)}) collective-permute-start(bf16[512,896]{1,0:T(8,128)(2,1)} %param.8), channel_id=1, source_target_pairs={{0,4},{1,5},{2,6},{3,7},{4,8},{5,9},{6,10},{7,11},{8,12},{9,13},{1... | collective-permute-start | bytes 2752520 | tf_op jit(solution)/shard_map/ppermute | solution.py:24
  77.3 1.9 copy-start.2
  77.3 35.9 %copy-start.6 = (s32[4]{0:T(128)S(1)}, s32[4]{0:T(128)}, u32[]{:S(2)}) copy-start(s32[4]{0:T(128)} %param.12) | copy-start | bytes 52
  77.3 35.9 %copy-start.8 = (s32[4]{0:T(128)S(1)}, s32[4]{0:T(128)}, u32[]{:S(2)}) copy-start(s32[4]{0:T(128)} %param.13) | copy-start | bytes 52
  121.7 22.5 %collective-permute-start.18 = (f32[4,128,64]{1,2,0:T(8,128)S(1)}, f32[4,128,64]{1,2,0:T(8,128)S(1)}, u32[]{:S(2)}, u32[]{:S(2)}) collective-permute-start(f32[4,128,64]{1,2,0:T(8,128)S(1)} %convolution_bitcast_fusion.4), channel_id=1, source_target_pairs={{0,3},{1,0},{2,1},{3,2},{4,7},{5,4},{6,5},{7,6},{8,11},{9,8},{10,9... | collective-permute-start | bytes 393224 | tf_op jit(solution)/shard_map/ppermute | solution.py:24
  124.5 22.9 %collective-permute-start.16 = (f32[4,128,64]{1,2,0:T(8,128)S(1)}, f32[4,128,64]{1,2,0:T(8,128)}, u32[]{:S(2)}, u32[]{:S(2)}) collective-permute-start(f32[4,128,64]{1,2,0:T(8,128)S(1)} %convolution_bitcast_fusion.4), channel_id=1, source_target_pairs={{0,1},{1,2},{2,3},{3,0},{4,5},{5,6},{6,7},{7,4},{8,9},{9,10},{10,1... | collective-permute-start | bytes 393224 | tf_op jit(solution)/shard_map/ppermute | solution.py:24
  124.5 22.9 %collective-permute-start.17 = (f32[4,128,64]{1,2,0:T(8,128)S(1)}, f32[4,128,64]{1,2,0:T(8,128)}, u32[]{:S(2)}, u32[]{:S(2)}) collective-permute-start(f32[4,128,64]{1,2,0:T(8,128)S(1)} %convolution_bitcast_fusion.4), channel_id=1, source_target_pairs={{0,2},{1,3},{2,0},{3,1},{4,6},{5,7},{6,4},{7,5},{8,10},{9,11},{10,... | collective-permute-start | bytes 393224 | tf_op jit(solution)/shard_map/ppermute | solution.py:24
  126.8 9.4 %copy-start = (bf16[25600,256]{1,0:T(8,128)(2,1)S(1)}, bf16[25600,256]{1,0:T(8,128)(2,1)}, u32[]{:S(2)}) copy-start(bf16[25600,256]{1,0:T(8,128)(2,1)} %all-gather.5.cloned.1.call-done) | copy-start | bytes 39321604
  134.9 7.4 %slice-start = ((s8[6815744]{0:T(1024)(128)(4,1)}), s8[4194304]{0:T(1024)(128)(4,1)S(1)}, s32[]{:S(2)}) async-start(s8[6815744]{0:T(1024)(128)(4,1)} %bitcast.192), calls=%async_computation.3 | async-start | bytes 8388608
  134.9 7.4 %slice-start.1 = ((s8[6815744]{0:T(1024)(128)(4,1)}), s8[2621440]{0:T(1024)(128)(4,1)S(1)}, s32[]{:S(2)}) async-start(s8[6815744]{0:T(1024)(128)(4,1)} %bitcast.192), calls=%async_computation.4 | async-start | bytes 5242880
  134.9 16.5 %collective-permute-start.6 = (bf16[4,4,32,256]{3,2,1,0:T(8,128)(2,1)}, bf16[4,4,32,256]{3,2,1,0:T(8,128)(2,1)}, u32[]{:S(2)}, u32[]{:S(2)}) collective-permute-start(bf16[4,4,32,256]{3,2,1,0:T(8,128)(2,1)} %bitcast.25), channel_id=1, source_target_pairs={{0,3},{1,0},{2,1},{3,2},{4,7},{5,4},{6,5},{7,6},{8,11},{9,8},{10,9... | collective-permute-start | bytes 786440 | tf_op jit(solution)/shard_map/ppermute | solution.py:24
  140.5 13.1 %collective-permute-start.5 = (bf16[4,4,32,256]{3,2,1,0:T(8,128)(2,1)S(1)}, bf16[4,4,32,256]{3,2,1,0:T(8,128)(2,1)}, u32[]{:S(2)}, u32[]{:S(2)}) collective-permute-start(bf16[4,4,32,256]{3,2,1,0:T(8,128)(2,1)S(1)} %bitcast.204), channel_id=1, source_target_pairs={{0,2},{1,3},{2,0},{3,1},{4,6},{5,7},{6,4},{7,5},{8,10},{9,11},{10,... | collective-permute-start | bytes 786440 | tf_op jit(solution)/shard_map/ppermute | solution.py:24
  144.2 2.1 %copy-start.5 = (f32[4,128,64]{1,2,0:T(8,128)}, f32[4,128,64]{1,2,0:T(8,128)S(1)}, u32[]{:S(2)}) copy-start(f32[4,128,64]{1,2,0:T(8,128)S(1)} %collective-permute-done.18) | copy-start | bytes 393220
  144.2 11.2 %collective-permute-start.4 = (bf16[4,4,32,256]{3,2,1,0:T(8,128)(2,1)S(1)}, bf16[4,4,32,256]{3,2,1,0:T(8,128)(2,1)}, u32[]{:S(2)}, u32[]{:S(2)}) collective-permute-start(bf16[4,4,32,256]{3,2,1,0:T(8,128)(2,1)S(1)} %bitcast.205), channel_id=1, source_target_pairs={{0,1},{1,2},{2,3},{3,0},{4,5},{5,6},{6,7},{7,4},{8,9},{9,10},{10,1... | collective-permute-start | bytes 786440 | tf_op jit(solution)/shard_map/ppermute | solution.py:24
  148.5 11.8 %collective-permute-start.21 = (f32[4,128,64]{1,2,0:T(8,128)S(1)}, f32[4,128,64]{1,2,0:T(8,128)S(1)}, u32[]{:S(2)}, u32[]{:S(2)}) collective-permute-start(f32[4,128,64]{1,2,0:T(8,128)S(1)} %add_add_fusion), channel_id=1, source_target_pairs={{0,12},{1,13},{2,14},{3,15},{4,0},{5,1},{6,2},{7,3},{8,4},{9,5},{1... | collective-permute-start | bytes 393224 | tf_op jit(solution)/shard_map/ppermute | solution.py:24
  151.3 9.9 %collective-permute-start.19 = (f32[4,128,64]{1,2,0:T(8,128)S(1)}, f32[4,128,64]{1,2,0:T(8,128)S(1)}, u32[]{:S(2)}, u32[]{:S(2)}) collective-permute-start(f32[4,128,64]{1,2,0:T(8,128)S(1)} %add_add_fusion), channel_id=1, source_target_pairs={{0,4},{1,5},{2,6},{3,7},{4,8},{5,9},{6,10},{7,11},{8,12},{9,13},{1... | collective-permute-start | bytes 393224 | tf_op jit(solution)/shard_map/ppermute | solution.py:24
  151.3 9.9 %collective-permute-start.20 = (f32[4,128,64]{1,2,0:T(8,128)S(1)}, f32[4,128,64]{1,2,0:T(8,128)S(1)}, u32[]{:S(2)}, u32[]{:S(2)}) collective-permute-start(f32[4,128,64]{1,2,0:T(8,128)S(1)} %add_add_fusion), channel_id=1, source_target_pairs={{0,8},{1,9},{2,10},{3,11},{4,12},{5,13},{6,14},{7,15},{8,0},{9,1},... | collective-permute-start | bytes 393224 | tf_op jit(solution)/shard_map/ppermute | solution.py:24
  156.7 11.5 %collective-permute-start.9 = (bf16[4,32,256]{2,1,0:T(8,128)(2,1)S(1)}, bf16[4,32,256]{2,1,0:T(8,128)(2,1)S(1)}, u32[]{:S(2)}, u32[]{:S(2)}) collective-permute-start(bf16[4,32,256]{2,1,0:T(8,128)(2,1)S(1)} %get-tuple-element.17), channel_id=1, source_target_pairs={{0,12},{1,13},{2,14},{3,15},{4,0},{5,1},{6,2},{7,3},{8,4},{9,5},{1... | collective-permute-start | bytes 196616 | tf_op jit(solution)/shard_map/ppermute | solution.py:24
  159.5 8.7 %collective-permute-start.8 = (bf16[4,32,256]{2,1,0:T(8,128)(2,1)S(1)}, bf16[4,32,256]{2,1,0:T(8,128)(2,1)S(1)}, u32[]{:S(2)}, u32[]{:S(2)}) collective-permute-start(bf16[4,32,256]{2,1,0:T(8,128)(2,1)S(1)} %get-tuple-element.18), channel_id=1, source_target_pairs={{0,8},{1,9},{2,10},{3,11},{4,12},{5,13},{6,14},{7,15},{8,0},{9,1},... | collective-permute-start | bytes 196616 | tf_op jit(solution)/shard_map/ppermute | solution.py:24
  160.3 7.9 %collective-permute-start.7 = (bf16[4,32,256]{2,1,0:T(8,128)(2,1)S(1)}, bf16[4,32,256]{2,1,0:T(8,128)(2,1)S(1)}, u32[]{:S(2)}, u32[]{:S(2)}) collective-permute-start(bf16[4,32,256]{2,1,0:T(8,128)(2,1)S(1)} %get-tuple-element.19), channel_id=1, source_target_pairs={{0,4},{1,5},{2,6},{3,7},{4,8},{5,9},{6,10},{7,11},{8,12},{9,13},{1... | collective-permute-start | bytes 196616 | tf_op jit(solution)/shard_map/ppermute | solution.py:24
  162.4 36.1 %all-to-all-start = ((bf16[16,32,512]{2,1,0:T(8,128)(2,1)}), bf16[16,32,512]{2,1,0:T(8,128)(2,1)S(1)}, u32[]{:S(2)}, u32[]{:S(2)}) async-start(bf16[16,32,512]{2,1,0:T(8,128)(2,1)} %bitcast.77), calls=%async_computation | async-start | bytes 1048576 | tf_op jit(solution)/shard_map/all_to_all | solution.py:174
  168.9 5.4 %copy-start.1 = (bf16[14336,256]{1,0:T(8,128)(2,1)S(1)}, bf16[14336,256]{1,0:T(8,128)(2,1)}, u32[]{:S(2)}) copy-start(bf16[14336,256]{1,0:T(8,128)(2,1)} %all-gather.7.cloned.1.call-done) | copy-start | bytes 22020100
  168.9 7.9 %copy-start.3 = (bf16[4,4,4,32,896]{4,3,2,1,0:T(8,128)(2,1)S(1)}, bf16[4,4,4,32,896]{4,3,2,1,0:T(8,128)(2,1)}, u32[]{:S(2)}) copy-start(bf16[4,4,4,32,896]{4,3,2,1,0:T(8,128)(2,1)} %copy-done.2) | copy-start | bytes 11010052
  177.9 12.2 %collective-permute-start.12 = (bf16[4,4,32,256]{3,2,1,0:T(8,128)(2,1)S(1)}, bf16[4,4,32,256]{3,2,1,0:T(8,128)(2,1)S(1)}, u32[]{:S(2)}, u32[]{:S(2)}) collective-permute-start(bf16[4,4,32,256]{3,2,1,0:T(8,128)(2,1)S(1)} %bitcast.208), channel_id=1, source_target_pairs={{0,3},{1,0},{2,1},{3,2},{4,7},{5,4},{6,5},{7,6},{8,11},{9,8},{10,9... | collective-permute-start | bytes 786440 | tf_op jit(solution)/shard_map/ppermute | solution.py:24
  181.1 10.0 %collective-permute-start.11 = (bf16[4,4,32,256]{3,2,1,0:T(8,128)(2,1)S(1)}, bf16[4,4,32,256]{3,2,1,0:T(8,128)(2,1)S(1)}, u32[]{:S(2)}, u32[]{:S(2)}) collective-permute-start(bf16[4,4,32,256]{3,2,1,0:T(8,128)(2,1)S(1)} %bitcast.207), channel_id=1, source_target_pairs={{0,2},{1,3},{2,0},{3,1},{4,6},{5,7},{6,4},{7,5},{8,10},{9,11},{10,... | collective-permute-start | bytes 786440 | tf_op jit(solution)/shard_map/ppermute | solution.py:24
  181.9 11.9 %collective-permute-start.10 = (bf16[4,4,32,256]{3,2,1,0:T(8,128)(2,1)S(1)}, bf16[4,4,32,256]{3,2,1,0:T(8,128)(2,1)S(1)}, u32[]{:S(2)}, u32[]{:S(2)}) collective-permute-start(bf16[4,4,32,256]{3,2,1,0:T(8,128)(2,1)S(1)} %bitcast.206), channel_id=1, source_target_pairs={{0,1},{1,2},{2,3},{3,0},{4,5},{5,6},{6,7},{7,4},{8,9},{9,10},{10,1... | collective-permute-start | bytes 786440 | tf_op jit(solution)/shard_map/ppermute | solution.py:24
  193.8 11.7 %copy-start.7 = (pred[32]{0:T(512)(128)(4,1)S(1)}, pred[32]{0:T(512)(128)(4,1)}, u32[]{:S(2)}) copy-start(pred[32]{0:T(512)(128)(4,1)} %fusion.68) | copy-start | bytes 100
  194.0 5.0 %collective-permute-start.15 = (bf16[4,32,256]{2,1,0:T(8,128)(2,1)S(1)}, bf16[4,32,256]{2,1,0:T(8,128)(2,1)S(1)}, u32[]{:S(2)}, u32[]{:S(2)}) collective-permute-start(bf16[4,32,256]{2,1,0:T(8,128)(2,1)S(1)} %get-tuple-element.21), channel_id=1, source_target_pairs={{0,12},{1,13},{2,14},{3,15},{4,0},{5,1},{6,2},{7,3},{8,4},{9,5},{1... | collective-permute-start | bytes 196616 | tf_op jit(solution)/shard_map/ppermute | solution.py:24
  196.8 5.8 %collective-permute-start.14 = (bf16[4,32,256]{2,1,0:T(8,128)(2,1)S(1)}, bf16[4,32,256]{2,1,0:T(8,128)(2,1)S(1)}, u32[]{:S(2)}, u32[]{:S(2)}) collective-permute-start(bf16[4,32,256]{2,1,0:T(8,128)(2,1)S(1)} %get-tuple-element.22), channel_id=1, source_target_pairs={{0,8},{1,9},{2,10},{3,11},{4,12},{5,13},{6,14},{7,15},{8,0},{9,1},... | collective-permute-start | bytes 196616 | tf_op jit(solution)/shard_map/ppermute | solution.py:24
  197.6 5.6 %collective-permute-start.13 = (bf16[4,32,256]{2,1,0:T(8,128)(2,1)S(1)}, bf16[4,32,256]{2,1,0:T(8,128)(2,1)S(1)}, u32[]{:S(2)}, u32[]{:S(2)}) collective-permute-start(bf16[4,32,256]{2,1,0:T(8,128)(2,1)S(1)} %get-tuple-element.23), channel_id=1, source_target_pairs={{0,4},{1,5},{2,6},{3,7},{4,8},{5,9},{6,10},{7,11},{8,12},{9,13},{1... | collective-permute-start | bytes 196616 | tf_op jit(solution)/shard_map/ppermute | solution.py:24
Sparse Core Ops, SparseCore 0:
  13.3 99.6 all-gather.4
  114.8 49.5 all-gather.6

commit v18 on v16

--- a/solution.py
+++ b/solution.py
@@ -110,18 +110,22 @@
     )
     gathered = lax.all_gather(pack, "pool", axis=0, tiled=False)
     pieces = [hidden] + [tensor_shift(hidden, side, s, True) for s in range(1, side)]
-    later, gathered, pieces = lax.optimization_barrier((moved[:, half:], gathered, pieces))
+    hidden_column = jnp.stack(pieces, axis=0).reshape(side, side, side, own_rows, feat)
+    hidden_column = jnp.transpose(hidden_column, (2, 0, 1, 3, 4)).reshape(
+        side, side, side * own_rows, feat
+    )
+    hidden_padded = jnp.pad(
+        hidden_column, ((0, 0), (0, 0), (0, 0), (0, pack.shape[0] - feat))
+    )
+    later, gathered, hidden_column, hidden_padded = lax.optimization_barrier(
+        (moved[:, half:], gathered, hidden_column, hidden_padded)
+    )
     plane_rows = gathered.shape[1]
     w_first = gathered.reshape(quarter, side, plane_rows, half)
     w_second = lax.all_gather(later, "pool", axis=0, tiled=False).reshape(
         quarter, side, feat, half
     )
 
-    hidden_column = jnp.stack(pieces, axis=0).reshape(side, side, side, own_rows, feat)
-    hidden_column = jnp.transpose(hidden_column, (2, 0, 1, 3, 4)).reshape(
-        side, side, side * own_rows, feat
-    )
-    hidden_padded = jnp.pad(hidden_column, ((0, 0), (0, 0), (0, 0), (0, plane_rows - feat)))
 
     shrink_part = shrink_rows // held
     expand_part = expand_rows // held

time: 218 us -> 218 us (level)
  matrix products: 20.5 us -> 26.7 us
  starting transfers between devices: 62 us -> 57.7 us
  waiting for transfers between devices: 90.7 us -> 88.2 us
  other arithmetic: 5.73 us -> 3.48 us
    all_gather x1, waiting for transfers between devices: 37.3 us -> 30.3 us  [shards(): gathered = lax.all_gather(pack, 'pool', axis=0, tiled=False)]
    dot_general x8, matrix products: 18.8 us -> 25 us  [rows_for(): jnp.einsum('sif,asfj->aij', rows, w_half, preferred_element_type=jnp.floa...]
    ppermute x21, waiting for transfers between devices: 53.4 us -> 57.9 us  [tensor_shift(): return lax.ppermute(x, 'tensor', perm)]
    pad x0 -> x1, local copies, waits for them, and re-layouts: none -> 3.51 us  [shards(): jnp.pad(hidden_column, ((0, 0), (0, 0), (0, 0), (0, pack.shape[0] - feat)))]
    ppermute x21, starting transfers between devices: 53.1 us -> 50.9 us  [tensor_shift(): return lax.ppermute(x, 'tensor', perm)]
    unnamed x18 -> x20, local copies, waits for them, and re-layouts: 7.45 us -> 5.49 us
  transfers between devices with their start and end apart: 25 -> 25, of which waited for: 9 -> 11; matrix products, arithmetic and copies ran while one was open for 14% -> 18% of each run, Pallas kernels for 0% -> 0%
where the time goes in v18:
time: 218 us; the launch traced here: 217 us
  waiting for transfers between devices  88.2 us (40%)
  starting transfers between devices  57.7 us (26%)
  matrix products  26.7 us (12%)
  between operations  24.7 us (11%)
  local copies, waits for them, and re-layouts  16 us (7%)
  other arithmetic  3.48 us (2%)
    ppermute x21, waiting for transfers between devices, tensor_shift(): return lax.ppermute(x, 'tensor', perm)  57.9 us
    ppermute x21, starting transfers between devices, tensor_shift(): return lax.ppermute(x, 'tensor', perm)  50.9 us
    all_gather x1, waiting for transfers between devices, shards(): gathered = lax.all_gather(pack, 'pool', axis=0, tiled=False)  30.3 us
    dot_general x8, matrix products, rows_for(): jnp.einsum('sif,asfj->aij', rows, w_half, preferred_element_type=jnp.floa...  25 us
    unnamed x20, local copies, waits for them, and re-layouts  5.49 us
    all_to_all x1, starting transfers between devices, shards(): lax.all_to_all(delta, 'tensor', split_axis=0, concat_axis=1, tiled=True)  4.86 us
  transfers between devices with their start and end apart: 25, of which 11 were waited for; matrix products, arithmetic and copies ran while one was open for 18% of the time, Pallas kernels for 0%

profile of v18, /device:TPU:0, one launch (start us, length us, event | category | flops | bytes accessed | tf_op | source)
XLA Modules:
  0.0 216.7 jit_solution(14110291543875139063)
XLA Ops:
  6.5 2.0 collective-permute-start
  8.5 1.1 copy.34
  9.8 1.2 copy.33
  11.3 0.8 fusion.64
  12.2 1.0 pad_maximum_fusion
  13.2 11.6 %collective-permute-start.3 = (bf16[512,896]{1,0:T(8,128)(2,1)}, bf16[512,896]{1,0:T(8,128)(2,1)S(1)}, u32[]{:S(2)}, u32[]{:S(2)}) collective-permute-start(bf16[512,896]{1,0:T(8,128)(2,1)} %param.8), channel_id=1, source_target_pairs={{0,12},{1,13},{2,14},{3,15},{4,0},{5,1},{6,2},{7,3},{8,4},{9,5},{1... | collective-permute-start | bytes 2752520 | tf_op jit(solution)/shard_map/ppermute | solution.py:24
  24.8 10.4 %collective-permute-start.2 = (bf16[512,896]{1,0:T(8,128)(2,1)}, bf16[512,896]{1,0:T(8,128)(2,1)S(1)}, u32[]{:S(2)}, u32[]{:S(2)}) collective-permute-start(bf16[512,896]{1,0:T(8,128)(2,1)} %param.8), channel_id=1, source_target_pairs={{0,8},{1,9},{2,10},{3,11},{4,12},{5,13},{6,14},{7,15},{8,0},{9,1},... | collective-permute-start | bytes 2752520 | tf_op jit(solution)/shard_map/ppermute | solution.py:24
  35.2 1.3 collective-permute-start.1
  36.5 6.3 %collective-permute-done.3 = bf16[512,896]{1,0:T(8,128)(2,1)S(1)} collective-permute-done((bf16[512,896]{1,0:T(8,128)(2,1)}, bf16[512,896]{1,0:T(8,128)(2,1)S(1)}, u32[]{:S(2)}, u32[]{:S(2)}) %collective-permute-start.3) | collective-permute-done | bytes 917536 | tf_op jit(solution)/shard_map/ppermute | solution.py:24
  42.8 13.5 %collective-permute-done.2 = bf16[512,896]{1,0:T(8,128)(2,1)S(1)} collective-permute-done((bf16[512,896]{1,0:T(8,128)(2,1)}, bf16[512,896]{1,0:T(8,128)(2,1)S(1)}, u32[]{:S(2)}, u32[]{:S(2)}) %collective-permute-start.2) | collective-permute-done | bytes 917536 | tf_op jit(solution)/shard_map/ppermute | solution.py:24
  56.3 19.9 %collective-permute-done.1 = bf16[512,896]{1,0:T(8,128)(2,1)S(1)} collective-permute-done((bf16[512,896]{1,0:T(8,128)(2,1)}, bf16[512,896]{1,0:T(8,128)(2,1)S(1)}, u32[]{:S(2)}, u32[]{:S(2)}) %collective-permute-start.1) | collective-permute-done | bytes 917536 | tf_op jit(solution)/shard_map/ppermute | solution.py:24
  77.3 1.9 copy-done.2
  79.2 3.5 %pad.4 = bf16[4,4,128,1600]{3,2,1,0:T(8,128)(2,1)} pad(bf16[4,4,128,896]{3,2,1,0:T(8,128)(2,1)S(1)} %bitcast.191, bf16[]{:T(256)} %constant.230.clone.1), padding=0_0x0_0x0_0x0_704 | pad | bytes 10223618 | tf_op jit(solution)/shard_map/jit(_pad)/pad | solution.py:117
  82.7 30.3 %all-gather.5.cloned.1.call-done = bf16[25600,256]{1,0:T(8,128)(2,1)} async-done(((bf16[1600,256]{1,0:T(8,128)(2,1)}), bf16[25600,256]{1,0:T(8,128)(2,1)}) %all-gather.5.cloned.1.call-update) | async-done | bytes 13107216 | tf_op jit(solution)/shard_map/all_gather | solution.py:111
  124.7 1.1 constant_dynamic-slice_fusion.7
  126.8 2.7 %collective-permute-start.18 = (f32[4,128,64]{1,2,0:T(8,128)S(1)}, f32[4,128,64]{1,2,0:T(8,128)S(1)}, u32[]{:S(2)}, u32[]{:S(2)}) collective-permute-start(f32[4,128,64]{1,2,0:T(8,128)S(1)} %convolution_bitcast_fusion.4), channel_id=1, source_target_pairs={{0,3},{1,0},{2,1},{3,2},{4,7},{5,4},{6,5},{7,6},{8,11},{9,8},{10,9... | collective-permute-start | bytes 393224 | tf_op jit(solution)/shard_map/ppermute | solution.py:24
  129.6 2.3 %collective-permute-start.17 = (f32[4,128,64]{1,2,0:T(8,128)S(1)}, f32[4,128,64]{1,2,0:T(8,128)S(1)}, u32[]{:S(2)}, u32[]{:S(2)}) collective-permute-start(f32[4,128,64]{1,2,0:T(8,128)S(1)} %convolution_bitcast_fusion.4), channel_id=1, source_target_pairs={{0,2},{1,3},{2,0},{3,1},{4,6},{5,7},{6,4},{7,5},{8,10},{9,11},{10,... | collective-permute-start | bytes 393224 | tf_op jit(solution)/shard_map/ppermute | solution.py:24
  131.9 7.6 %fusion.36 = bf16[4,256,128]{1,2,0:T(8,128)(2,1)S(1)} fusion(bf16[4,4,1600,256]{3,2,1,0:T(8,128)(2,1)} %bitcast.182, bf16[4,4,128,1600]{3,2,1,0:T(8,128)(2,1)} %pad.4, s32[]{:T(128)S(6)} %select_n.211), kind=kOutput, calls=%fused_computation.32 | convolution fusion | flops 1677852672 | bytes 15073284 | tf_op jit(solution)/shard_map/sif,asfj->aij/dot_general | solution.py:159
  139.4 1.4 collective-permute-start.6
  141.4 4.4 %fusion.39 = bf16[4,256,128]{1,2,0:T(8,128)(2,1)S(1)} fusion(bf16[4,4,1600,256]{3,2,1,0:T(8,128)(2,1)S(1)} %bitcast.183, bf16[4,4,128,1600]{3,2,1,0:T(8,128)(2,1)} %pad.4, s32[]{:T(128)S(6)} %select_n.209), kind=kOutput, calls=%fused_computation.33 | convolution fusion | flops 1677852672 | bytes 15073284 | tf_op jit(solution)/shard_map/sif,asfj->aij/dot_general | solution.py:159
  145.7 1.5 collective-permute-start.5
  147.2 1.9 fusion.33
  149.1 1.9 fusion.42
  152.1 2.8 %collective-permute-start.21 = (f32[4,128,64]{1,2,0:T(8,128)S(1)}, f32[4,128,64]{1,2,0:T(8,128)S(1)}, u32[]{:S(2)}, u32[]{:S(2)}) collective-permute-start(f32[4,128,64]{1,2,0:T(8,128)S(1)} %add_add_fusion), channel_id=1, source_target_pairs={{0,12},{1,13},{2,14},{3,15},{4,0},{5,1},{6,2},{7,3},{8,4},{9,5},{1... | collective-permute-start | bytes 393224 | tf_op jit(solution)/shard_map/ppermute | solution.py:24
  154.9 2.3 %collective-permute-start.20 = (f32[4,128,64]{1,2,0:T(8,128)S(1)}, f32[4,128,64]{1,2,0:T(8,128)S(1)}, u32[]{:S(2)}, u32[]{:S(2)}) collective-permute-start(f32[4,128,64]{1,2,0:T(8,128)S(1)} %add_add_fusion), channel_id=1, source_target_pairs={{0,8},{1,9},{2,10},{3,11},{4,12},{5,13},{6,14},{7,15},{8,0},{9,1},... | collective-permute-start | bytes 393224 | tf_op jit(solution)/shard_map/ppermute | solution.py:24
  157.2 3.4 %collective-permute-done.4 = bf16[4,4,32,256]{3,2,1,0:T(8,128)(2,1)S(1)} collective-permute-done((bf16[4,4,32,256]{3,2,1,0:T(8,128)(2,1)S(1)}, bf16[4,4,32,256]{3,2,1,0:T(8,128)(2,1)S(1)}, u32[]{:S(2)}, u32[]{:S(2)}) %collective-permute-start.4) | collective-permute-done | bytes 262176 | tf_op jit(solution)/shard_map/ppermute | solution.py:24
  160.8 2.8 %collective-permute-start.9 = (bf16[4,32,256]{2,1,0:T(8,128)(2,1)S(1)}, bf16[4,32,256]{2,1,0:T(8,128)(2,1)S(1)}, u32[]{:S(2)}, u32[]{:S(2)}) collective-permute-start(bf16[4,32,256]{2,1,0:T(8,128)(2,1)S(1)} %get-tuple-element.25), channel_id=1, source_target_pairs={{0,12},{1,13},{2,14},{3,15},{4,0},{5,1},{6,2},{7,3},{8,4},{9,5},{1... | collective-permute-start | bytes 196616 | tf_op jit(solution)/shard_map/ppermute | solution.py:24
  163.6 0.8 collective-permute-start.8
  164.4 0.9 collective-permute-start.7
  165.3 1.1 fusion.12
  166.5 4.9 %all-to-all-start = ((bf16[16,32,512]{2,1,0:T(8,128)(2,1)}), bf16[16,32,512]{2,1,0:T(8,128)(2,1)S(1)}, u32[]{:S(2)}, u32[]{:S(2)}) async-start(bf16[16,32,512]{2,1,0:T(8,128)(2,1)} %bitcast.79), calls=%async_computation | async-start | bytes 1048576 | tf_op jit(solution)/shard_map/all_to_all | solution.py:184
  172.0 4.6 %fusion.27 = bf16[4,256,128]{1,2,0:T(8,128)(2,1)S(1)} fusion(bf16[4,4,896,256]{3,2,1,0:T(8,128)(2,1)} %bitcast.187, bf16[4,4,128,896]{3,2,1,0:T(8,128)(2,1)} %bitcast.192, s32[]{:T(128)S(6)} %select_n.211), kind=kOutput, calls=%fused_computation.27 | convolution fusion | flops 939655168 | bytes 8519684 | tf_op jit(solution)/shard_map/sif,asfj->aij/dot_general | solution.py:159
  176.7 0.8 copy-done.1
  177.5 2.4 %fusion.26 = bf16[4,256,128]{1,2,0:T(8,128)(2,1)S(1)} fusion(bf16[4,4,896,256]{3,2,1,0:T(8,128)(2,1)S(1)} %bitcast.188, bf16[4,4,128,896]{3,2,1,0:T(8,128)(2,1)} %bitcast.193, s32[]{:T(128)S(6)} %select_n.209), kind=kOutput, calls=%fused_computation.26 | convolution fusion | flops 939655168 | bytes 8519684 | tf_op jit(solution)/shard_map/sif,asfj->aij/dot_general | solution.py:159
  179.9 1.1 fusion.25
  181.0 3.2 %collective-permute-start.12 = (bf16[4,4,32,256]{3,2,1,0:T(8,128)(2,1)S(1)}, bf16[4,4,32,256]{3,2,1,0:T(8,128)(2,1)S(1)}, u32[]{:S(2)}, u32[]{:S(2)}) collective-permute-start(bf16[4,4,32,256]{3,2,1,0:T(8,128)(2,1)S(1)} %bitcast.211), channel_id=1, source_target_pairs={{0,3},{1,0},{2,1},{3,2},{4,7},{5,4},{6,5},{7,6},{8,11},{9,8},{10,9... | collective-permute-start | bytes 786440 | tf_op jit(solution)/shard_map/ppermute | solution.py:24
  184.2 0.9 collective-permute-start.11
  185.1 0.9 collective-permute-start.10
  185.9 1.1 fusion.29
  187.1 6.5 %collective-permute-done.12 = bf16[4,4,32,256]{3,2,1,0:T(8,128)(2,1)S(1)} collective-permute-done((bf16[4,4,32,256]{3,2,1,0:T(8,128)(2,1)S(1)}, bf16[4,4,32,256]{3,2,1,0:T(8,128)(2,1)S(1)}, u32[]{:S(2)}, u32[]{:S(2)}) %collective-permute-start.12) | collective-permute-done | bytes 262176 | tf_op jit(solution)/shard_map/ppermute | solution.py:24
  193.5 1.0 collective-permute-done.11
  194.5 2.7 %collective-permute-done.10 = bf16[4,4,32,256]{3,2,1,0:T(8,128)(2,1)S(1)} collective-permute-done((bf16[4,4,32,256]{3,2,1,0:T(8,128)(2,1)S(1)}, bf16[4,4,32,256]{3,2,1,0:T(8,128)(2,1)S(1)}, u32[]{:S(2)}, u32[]{:S(2)}) %collective-permute-start.10) | collective-permute-done | bytes 262176 | tf_op jit(solution)/shard_map/ppermute | solution.py:24
  197.4 2.8 %collective-permute-start.15 = (bf16[4,32,256]{2,1,0:T(8,128)(2,1)S(1)}, bf16[4,32,256]{2,1,0:T(8,128)(2,1)S(1)}, u32[]{:S(2)}, u32[]{:S(2)}) collective-permute-start(bf16[4,32,256]{2,1,0:T(8,128)(2,1)S(1)} %get-tuple-element.29), channel_id=1, source_target_pairs={{0,12},{1,13},{2,14},{3,15},{4,0},{5,1},{6,2},{7,3},{8,4},{9,5},{1... | collective-permute-start | bytes 196616 | tf_op jit(solution)/shard_map/ppermute | solution.py:24
  200.2 0.9 collective-permute-start.14
  201.0 0.9 collective-permute-start.13
  202.2 3.8 %collective-permute-done.14 = bf16[4,32,256]{2,1,0:T(8,128)(2,1)S(1)} collective-permute-done((bf16[4,32,256]{2,1,0:T(8,128)(2,1)S(1)}, bf16[4,32,256]{2,1,0:T(8,128)(2,1)S(1)}, u32[]{:S(2)}, u32[]{:S(2)}) %collective-permute-start.14) | collective-permute-done | bytes 65568 | tf_op jit(solution)/shard_map/ppermute | solution.py:24
  208.2 0.7 reshape.126
  208.9 0.9 fusion.53
  (71 shorter events, 8.5 us)
Async XLA Ops:
  6.5 69.7 %copy-start.4 = (bf16[512,896]{1,0:T(8,128)(2,1)S(1)}, bf16[512,896]{1,0:T(8,128)(2,1)}, u32[]{:S(2)}) copy-start(bf16[512,896]{1,0:T(8,128)(2,1)} %param.8) | copy-start | bytes 2752516
  6.5 106.5 %all-gather.5.cloned.1.call-start = ((), (), s32[]{:S(2)}) async-start(), calls=%async_computation.1 | async-start | bytes 13926400 | tf_op jit(solution)/shard_map/all_gather | solution.py:111
  6.5 4.8 %collective-permute-start = (bf16[896,512]{1,0:T(8,128)(2,1)}, bf16[896,512]{1,0:T(8,128)(2,1)S(1)}, u32[]{:S(2)}, u32[]{:S(2)}) collective-permute-start(bf16[896,512]{1,0:T(8,128)(2,1)} %param.9), channel_id=1, source_target_pairs={{0,0},{1,1},{2,2},{3,3},{4,48},{5,49},{6,50},{7,51},{8,32},{9,33},... | collective-permute-start | bytes 2752520 | tf_op jit(solution)/shard_map/ppermute | solution.py:98
  13.1 158.9 %all-gather.7.cloned.1.call-start = ((), (), s32[]{:S(2)}) async-start(), calls=%async_computation.2 | async-start | bytes 7798784 | tf_op jit(solution)/shard_map/all_gather | solution.py:125
  13.2 29.6 %collective-permute-start.3 = (bf16[512,896]{1,0:T(8,128)(2,1)}, bf16[512,896]{1,0:T(8,128)(2,1)S(1)}, u32[]{:S(2)}, u32[]{:S(2)}) collective-permute-start(bf16[512,896]{1,0:T(8,128)(2,1)} %param.8), channel_id=1, source_target_pairs={{0,12},{1,13},{2,14},{3,15},{4,0},{5,1},{6,2},{7,3},{8,4},{9,5},{1... | collective-permute-start | bytes 2752520 | tf_op jit(solution)/shard_map/ppermute | solution.py:24
  24.8 31.5 %collective-permute-start.2 = (bf16[512,896]{1,0:T(8,128)(2,1)}, bf16[512,896]{1,0:T(8,128)(2,1)S(1)}, u32[]{:S(2)}, u32[]{:S(2)}) collective-permute-start(bf16[512,896]{1,0:T(8,128)(2,1)} %param.8), channel_id=1, source_target_pairs={{0,8},{1,9},{2,10},{3,11},{4,12},{5,13},{6,14},{7,15},{8,0},{9,1},... | collective-permute-start | bytes 2752520 | tf_op jit(solution)/shard_map/ppermute | solution.py:24
  35.2 41.1 %collective-permute-start.1 = (bf16[512,896]{1,0:T(8,128)(2,1)}, bf16[512,896]{1,0:T(8,128)(2,1)S(1)}, u32[]{:S(2)}, u32[]{:S(2)}) collective-permute-start(bf16[512,896]{1,0:T(8,128)(2,1)} %param.8), channel_id=1, source_target_pairs={{0,4},{1,5},{2,6},{3,7},{4,8},{5,9},{6,10},{7,11},{8,12},{9,13},{1... | collective-permute-start | bytes 2752520 | tf_op jit(solution)/shard_map/ppermute | solution.py:24
  77.3 1.9 copy-start.2
  77.3 35.8 %copy-start.5 = (s32[4]{0:T(128)S(1)}, s32[4]{0:T(128)}, u32[]{:S(2)}) copy-start(s32[4]{0:T(128)} %param.12) | copy-start | bytes 52
  77.3 47.3 %copy-start.6 = (s32[4]{0:T(128)S(1)}, s32[4]{0:T(128)}, u32[]{:S(2)}) copy-start(s32[4]{0:T(128)} %param.13) | copy-start | bytes 52
  126.8 24.2 %collective-permute-start.18 = (f32[4,128,64]{1,2,0:T(8,128)S(1)}, f32[4,128,64]{1,2,0:T(8,128)S(1)}, u32[]{:S(2)}, u32[]{:S(2)}) collective-permute-start(f32[4,128,64]{1,2,0:T(8,128)S(1)} %convolution_bitcast_fusion.4), channel_id=1, source_target_pairs={{0,3},{1,0},{2,1},{3,2},{4,7},{5,4},{6,5},{7,6},{8,11},{9,8},{10,9... | collective-permute-start | bytes 393224 | tf_op jit(solution)/shard_map/ppermute | solution.py:24
  129.6 22.5 %collective-permute-start.16 = (f32[4,128,64]{1,2,0:T(8,128)S(1)}, f32[4,128,64]{1,2,0:T(8,128)S(1)}, u32[]{:S(2)}, u32[]{:S(2)}) collective-permute-start(f32[4,128,64]{1,2,0:T(8,128)S(1)} %convolution_bitcast_fusion.4), channel_id=1, source_target_pairs={{0,1},{1,2},{2,3},{3,0},{4,5},{5,6},{6,7},{7,4},{8,9},{9,10},{10,1... | collective-permute-start | bytes 393224 | tf_op jit(solution)/shard_map/ppermute | solution.py:24
  129.6 22.5 %collective-permute-start.17 = (f32[4,128,64]{1,2,0:T(8,128)S(1)}, f32[4,128,64]{1,2,0:T(8,128)S(1)}, u32[]{:S(2)}, u32[]{:S(2)}) collective-permute-start(f32[4,128,64]{1,2,0:T(8,128)S(1)} %convolution_bitcast_fusion.4), channel_id=1, source_target_pairs={{0,2},{1,3},{2,0},{3,1},{4,6},{5,7},{6,4},{7,5},{8,10},{9,11},{10,... | collective-permute-start | bytes 393224 | tf_op jit(solution)/shard_map/ppermute | solution.py:24
  131.9 9.5 %copy-start = (bf16[25600,256]{1,0:T(8,128)(2,1)S(1)}, bf16[25600,256]{1,0:T(8,128)(2,1)}, u32[]{:S(2)}) copy-start(bf16[25600,256]{1,0:T(8,128)(2,1)} %all-gather.5.cloned.1.call-done) | copy-start | bytes 39321604
  139.4 7.8 %slice-start = ((s8[6815744]{0:T(1024)(128)(4,1)}), s8[4194304]{0:T(1024)(128)(4,1)S(1)}, s32[]{:S(2)}) async-start(s8[6815744]{0:T(1024)(128)(4,1)} %bitcast.196), calls=%async_computation.3 | async-start | bytes 8388608
  139.4 7.8 %slice-start.1 = ((s8[6815744]{0:T(1024)(128)(4,1)}), s8[2621440]{0:T(1024)(128)(4,1)S(1)}, s32[]{:S(2)}) async-start(s8[6815744]{0:T(1024)(128)(4,1)} %bitcast.196), calls=%async_computation.4 | async-start | bytes 5242880
  139.4 15.5 %collective-permute-start.6 = (bf16[4,4,32,256]{3,2,1,0:T(8,128)(2,1)S(1)}, bf16[4,4,32,256]{3,2,1,0:T(8,128)(2,1)S(1)}, u32[]{:S(2)}, u32[]{:S(2)}) collective-permute-start(bf16[4,4,32,256]{3,2,1,0:T(8,128)(2,1)S(1)} %bitcast.208), channel_id=1, source_target_pairs={{0,3},{1,0},{2,1},{3,2},{4,7},{5,4},{6,5},{7,6},{8,11},{9,8},{10,9... | collective-permute-start | bytes 786440 | tf_op jit(solution)/shard_map/ppermute | solution.py:24
  145.7 11.5 %collective-permute-start.5 = (bf16[4,4,32,256]{3,2,1,0:T(8,128)(2,1)S(1)}, bf16[4,4,32,256]{3,2,1,0:T(8,128)(2,1)S(1)}, u32[]{:S(2)}, u32[]{:S(2)}) collective-permute-start(bf16[4,4,32,256]{3,2,1,0:T(8,128)(2,1)S(1)} %bitcast.206), channel_id=1, source_target_pairs={{0,2},{1,3},{2,0},{3,1},{4,6},{5,7},{6,4},{7,5},{8,10},{9,11},{10,... | collective-permute-start | bytes 786440 | tf_op jit(solution)/shard_map/ppermute | solution.py:24
  151.1 9.6 %collective-permute-start.4 = (bf16[4,4,32,256]{3,2,1,0:T(8,128)(2,1)S(1)}, bf16[4,4,32,256]{3,2,1,0:T(8,128)(2,1)S(1)}, u32[]{:S(2)}, u32[]{:S(2)}) collective-permute-start(bf16[4,4,32,256]{3,2,1,0:T(8,128)(2,1)S(1)} %bitcast.207), channel_id=1, source_target_pairs={{0,1},{1,2},{2,3},{3,0},{4,5},{5,6},{6,7},{7,4},{8,9},{9,10},{10,1... | collective-permute-start | bytes 786440 | tf_op jit(solution)/shard_map/ppermute | solution.py:24
  152.1 12.4 %collective-permute-start.21 = (f32[4,128,64]{1,2,0:T(8,128)S(1)}, f32[4,128,64]{1,2,0:T(8,128)S(1)}, u32[]{:S(2)}, u32[]{:S(2)}) collective-permute-start(f32[4,128,64]{1,2,0:T(8,128)S(1)} %add_add_fusion), channel_id=1, source_target_pairs={{0,12},{1,13},{2,14},{3,15},{4,0},{5,1},{6,2},{7,3},{8,4},{9,5},{1... | collective-permute-start | bytes 393224 | tf_op jit(solution)/shard_map/ppermute | solution.py:24
  154.9 10.4 %collective-permute-start.19 = (f32[4,128,64]{1,2,0:T(8,128)S(1)}, f32[4,128,64]{1,2,0:T(8,128)S(1)}, u32[]{:S(2)}, u32[]{:S(2)}) collective-permute-start(f32[4,128,64]{1,2,0:T(8,128)S(1)} %add_add_fusion), channel_id=1, source_target_pairs={{0,4},{1,5},{2,6},{3,7},{4,8},{5,9},{6,10},{7,11},{8,12},{9,13},{1... | collective-permute-start | bytes 393224 | tf_op jit(solution)/shard_map/ppermute | solution.py:24
  154.9 10.4 %collective-permute-start.20 = (f32[4,128,64]{1,2,0:T(8,128)S(1)}, f32[4,128,64]{1,2,0:T(8,128)S(1)}, u32[]{:S(2)}, u32[]{:S(2)}) collective-permute-start(f32[4,128,64]{1,2,0:T(8,128)S(1)} %add_add_fusion), channel_id=1, source_target_pairs={{0,8},{1,9},{2,10},{3,11},{4,12},{5,13},{6,14},{7,15},{8,0},{9,1},... | collective-permute-start | bytes 393224 | tf_op jit(solution)/shard_map/ppermute | solution.py:24
  160.8 10.5 %collective-permute-start.9 = (bf16[4,32,256]{2,1,0:T(8,128)(2,1)S(1)}, bf16[4,32,256]{2,1,0:T(8,128)(2,1)S(1)}, u32[]{:S(2)}, u32[]{:S(2)}) collective-permute-start(bf16[4,32,256]{2,1,0:T(8,128)(2,1)S(1)} %get-tuple-element.25), channel_id=1, source_target_pairs={{0,12},{1,13},{2,14},{3,15},{4,0},{5,1},{6,2},{7,3},{8,4},{9,5},{1... | collective-permute-start | bytes 196616 | tf_op jit(solution)/shard_map/ppermute | solution.py:24
  163.6 7.7 %collective-permute-start.8 = (bf16[4,32,256]{2,1,0:T(8,128)(2,1)S(1)}, bf16[4,32,256]{2,1,0:T(8,128)(2,1)S(1)}, u32[]{:S(2)}, u32[]{:S(2)}) collective-permute-start(bf16[4,32,256]{2,1,0:T(8,128)(2,1)S(1)} %get-tuple-element.26), channel_id=1, source_target_pairs={{0,8},{1,9},{2,10},{3,11},{4,12},{5,13},{6,14},{7,15},{8,0},{9,1},... | collective-permute-start | bytes 196616 | tf_op jit(solution)/shard_map/ppermute | solution.py:24
  164.4 6.9 %collective-permute-start.7 = (bf16[4,32,256]{2,1,0:T(8,128)(2,1)S(1)}, bf16[4,32,256]{2,1,0:T(8,128)(2,1)S(1)}, u32[]{:S(2)}, u32[]{:S(2)}) collective-permute-start(bf16[4,32,256]{2,1,0:T(8,128)(2,1)S(1)} %get-tuple-element.27), channel_id=1, source_target_pairs={{0,4},{1,5},{2,6},{3,7},{4,8},{5,9},{6,10},{7,11},{8,12},{9,13},{1... | collective-permute-start | bytes 196616 | tf_op jit(solution)/shard_map/ppermute | solution.py:24
  166.5 35.4 %all-to-all-start = ((bf16[16,32,512]{2,1,0:T(8,128)(2,1)}), bf16[16,32,512]{2,1,0:T(8,128)(2,1)S(1)}, u32[]{:S(2)}, u32[]{:S(2)}) async-start(bf16[16,32,512]{2,1,0:T(8,128)(2,1)} %bitcast.79), calls=%async_computation | async-start | bytes 1048576 | tf_op jit(solution)/shard_map/all_to_all | solution.py:184
  172.0 5.4 %copy-start.1 = (bf16[14336,256]{1,0:T(8,128)(2,1)S(1)}, bf16[14336,256]{1,0:T(8,128)(2,1)}, u32[]{:S(2)}) copy-start(bf16[14336,256]{1,0:T(8,128)(2,1)} %all-gather.7.cloned.1.call-done) | copy-start | bytes 22020100
  172.0 7.9 %copy-start.3 = (bf16[4,4,4,32,896]{4,3,2,1,0:T(8,128)(2,1)S(1)}, bf16[4,4,4,32,896]{4,3,2,1,0:T(8,128)(2,1)}, u32[]{:S(2)}) copy-start(bf16[4,4,4,32,896]{4,3,2,1,0:T(8,128)(2,1)} %copy-done.2) | copy-start | bytes 11010052
  181.0 12.5 %collective-permute-start.12 = (bf16[4,4,32,256]{3,2,1,0:T(8,128)(2,1)S(1)}, bf16[4,4,32,256]{3,2,1,0:T(8,128)(2,1)S(1)}, u32[]{:S(2)}, u32[]{:S(2)}) collective-permute-start(bf16[4,4,32,256]{3,2,1,0:T(8,128)(2,1)S(1)} %bitcast.211), channel_id=1, source_target_pairs={{0,3},{1,0},{2,1},{3,2},{4,7},{5,4},{6,5},{7,6},{8,11},{9,8},{10,9... | collective-permute-start | bytes 786440 | tf_op jit(solution)/shard_map/ppermute | solution.py:24
  184.2 10.3 %collective-permute-start.11 = (bf16[4,4,32,256]{3,2,1,0:T(8,128)(2,1)S(1)}, bf16[4,4,32,256]{3,2,1,0:T(8,128)(2,1)S(1)}, u32[]{:S(2)}, u32[]{:S(2)}) collective-permute-start(bf16[4,4,32,256]{3,2,1,0:T(8,128)(2,1)S(1)} %bitcast.210), channel_id=1, source_target_pairs={{0,2},{1,3},{2,0},{3,1},{4,6},{5,7},{6,4},{7,5},{8,10},{9,11},{10,... | collective-permute-start | bytes 786440 | tf_op jit(solution)/shard_map/ppermute | solution.py:24
  185.1 12.1 %collective-permute-start.10 = (bf16[4,4,32,256]{3,2,1,0:T(8,128)(2,1)S(1)}, bf16[4,4,32,256]{3,2,1,0:T(8,128)(2,1)S(1)}, u32[]{:S(2)}, u32[]{:S(2)}) collective-permute-start(bf16[4,4,32,256]{3,2,1,0:T(8,128)(2,1)S(1)} %bitcast.209), channel_id=1, source_target_pairs={{0,1},{1,2},{2,3},{3,0},{4,5},{5,6},{6,7},{7,4},{8,9},{9,10},{10,1... | collective-permute-start | bytes 786440 | tf_op jit(solution)/shard_map/ppermute | solution.py:24
  197.4 4.8 %collective-permute-start.15 = (bf16[4,32,256]{2,1,0:T(8,128)(2,1)S(1)}, bf16[4,32,256]{2,1,0:T(8,128)(2,1)S(1)}, u32[]{:S(2)}, u32[]{:S(2)}) collective-permute-start(bf16[4,32,256]{2,1,0:T(8,128)(2,1)S(1)} %get-tuple-element.29), channel_id=1, source_target_pairs={{0,12},{1,13},{2,14},{3,15},{4,0},{5,1},{6,2},{7,3},{8,4},{9,5},{1... | collective-permute-start | bytes 196616 | tf_op jit(solution)/shard_map/ppermute | solution.py:24
  200.2 5.8 %collective-permute-start.14 = (bf16[4,32,256]{2,1,0:T(8,128)(2,1)S(1)}, bf16[4,32,256]{2,1,0:T(8,128)(2,1)S(1)}, u32[]{:S(2)}, u32[]{:S(2)}) collective-permute-start(bf16[4,32,256]{2,1,0:T(8,128)(2,1)S(1)} %get-tuple-element.30), channel_id=1, source_target_pairs={{0,8},{1,9},{2,10},{3,11},{4,12},{5,13},{6,14},{7,15},{8,0},{9,1},... | collective-permute-start | bytes 196616 | tf_op jit(solution)/shard_map/ppermute | solution.py:24
  201.0 5.6 %collective-permute-start.13 = (bf16[4,32,256]{2,1,0:T(8,128)(2,1)S(1)}, bf16[4,32,256]{2,1,0:T(8,128)(2,1)S(1)}, u32[]{:S(2)}, u32[]{:S(2)}) collective-permute-start(bf16[4,32,256]{2,1,0:T(8,128)(2,1)S(1)} %get-tuple-element.31), channel_id=1, source_target_pairs={{0,4},{1,5},{2,6},{3,7},{4,8},{5,9},{6,10},{7,11},{8,12},{9,13},{1... | collective-permute-start | bytes 196616 | tf_op jit(solution)/shard_map/ppermute | solution.py:24
Sparse Core Ops, SparseCore 0:
  13.3 99.6 all-gather.4
  114.8 49.5 all-gather.6
